TPU v7x, 128 devices: a whole 4x4x4 slice. The times are simulated.
128 devices in a mesh: leaf: 2 (over core), front: 64 (over z, y, x).
Axes of the slice: x: 4, y: 4, z: 4, core: 2. Of those that a mesh axis runs over, the one named last changes fastest.
Arguments:
- front_block: float32 [8192, 8192], P('leaf', 'front'), as said below
- child_update: float32 [2, 6144, 8192], P('leaf', None, 'front'), as said below
- child_map: int32 [2, 48], P('leaf'), may hold values from 0 to 63, as said below
Outputs:
- factored: float32 [8192, 8192], P('leaf', 'front')
Inputs may be any that keep to these rules, and one draw needn't show every extreme that they name: `child_map`: each row is strictly increasing, holds 48 distinct blocks, and always names block 0 and block 63. `front_block`: Symmetric; the assembled front is positive definite. `child_update`: each child's update is symmetric and positive semidefinite in the child's order; columns of parent blocks that the child's map does not name are zero.
All inputs are finite; a program needn't handle non-finite values.
Results may differ from a plain program's by a relative error of at most 0.000088.
Values sent between devices are 32-bit elements; how exact they have to be, the bound alone decides.
A program may use at most 128 MiB of HBM per device.

v0:
```python
import jax
import jax.numpy as jnp
from jax import lax
from jax.sharding import PartitionSpec as P

BLK = 128
P_SIZE = 8192
S = 512


def spread(block, axis, holder):
    block = jnp.where(lax.axis_index(axis) == holder, block, jnp.zeros_like(block))
    return lax.psum(block, axis)


def solve_right(factor, rows):
    return lax.linalg.triangular_solve(factor, rows, left_side=False, lower=True, transpose_a=True)


def per_device(front_block, child_update, child_map):
    row_count = front_block.shape[0]
    col_count = front_block.shape[1]
    leaf_count = lax.axis_size("leaf")
    leaf_index = lax.axis_index("leaf")
    front_index = lax.axis_index("front")
    offsets = jnp.arange(BLK, dtype=jnp.int32)
    row_index = (child_map[0][:, None] * BLK + offsets[None, :]).reshape(-1)
    placed_rows = jnp.zeros((P_SIZE, col_count), jnp.float32).at[row_index].set(child_update[0])
    received = lax.all_to_all(
        placed_rows.reshape(leaf_count, row_count, col_count),
        "leaf",
        split_axis=0,
        concat_axis=0,
        tiled=True,
    )
    contribution = jnp.sum(received, axis=0)
    assembled = front_block + contribution
    holder = front_index * col_count < S
    zero_panel = jnp.zeros((row_count, S), jnp.float32)
    placed = lax.dynamic_update_slice_in_dim(
        zero_panel, jnp.where(holder, assembled, 0.0), front_index * col_count, 1
    )
    pivot_panel = lax.psum(placed, "front")
    top_block = pivot_panel[:S]
    diag_block, top_cols = (spread(top_block, "leaf", 0), spread(assembled[:S], "leaf", 0))
    factor = jnp.linalg.cholesky(diag_block)
    col_solved = solve_right(factor, top_cols.T)
    solved = solve_right(factor, pivot_panel)
    row_global = leaf_index * row_count + jnp.arange(row_count, dtype=jnp.int32)
    col_global = front_index * col_count + jnp.arange(col_count, dtype=jnp.int32)
    col_start = jnp.minimum(front_index * col_count, S - col_count)
    left_rows = lax.dynamic_slice_in_dim(solved, col_start, col_count, 1)
    left_top = jnp.pad(
        lax.dynamic_slice_in_dim(factor, col_start, col_count, 1), ((0, row_count - S), (0, 0))
    )
    left_part = jnp.where(row_global[:, None] < S, left_top, left_rows)
    schur_part = assembled - jnp.dot(solved, col_solved.T, precision=lax.Precision.HIGHEST)
    right_top = jnp.pad(col_solved.T, ((0, row_count - S), (0, 0)))
    right_part = jnp.where(row_global[:, None] < S, right_top, schur_part)
    return jnp.where(col_global[None, :] < S, left_part, right_part)


def solution(mesh):
    return jax.shard_map(
        per_device,
        mesh=mesh,
        in_specs=(P("leaf", "front"), P("leaf", None, "front"), P("leaf", None)),
        out_specs=P("leaf", "front"),
        check_vma=False,
    )
```

profile of v0, /device:TPU:1, one launch (start us, length us, event | category | flops | bytes accessed | tf_op | source)
XLA Modules:
  0.0 430.9 jit_solution(17772581311692880417)
XLA Ops:
  6.5 0.8 multiply_bitcast_fusion
  7.5 1.0 copy-done
  8.4 17.9 %scatter_custom_fusion = f32[8192,128]{1,0:T(8,128)} fusion(s32[6144]{0:T(1024)S(1)} %bitcast.70, f32[1,6144,128]{2,1,0:T(8,128)S(1)} %copy-done, f32[]{:T(128)} %constant.170.clone.1), kind=kCustom, calls=%fused_computation.19 | custom fusion | bytes 7340036 | tf_op jit(solution)/shard_map/scatter | solution.py:28
  26.3 7.2 %all-to-all-start = ((f32[2,4096,128]{2,1,0:T(8,128)}), f32[2,4096,128]{2,1,0:T(8,128)}, u32[]{:S(2)}, u32[]{:S(2)}) async-start(f32[2,4096,128]{2,1,0:T(8,128)} %bitcast.68), calls=%async_computation | async-start | bytes 8388608 | tf_op jit(solution)/shard_map/all_to_all | solution.py:29
  33.5 1.8 copy.20
  35.3 2.3 all-to-all-done
  37.6 2.7 reduce_sum.9
  40.3 1.9 copy.21
  42.1 4.2 broadcast_in_dim.44
  46.4 1.7 select_dynamic-update-slice_fusion
  48.3 1.1 copy-done.2
  49.4 0.7 fusion.21
  50.1 167.5 %all-reduce.7.cloned.1.call-done = f32[4096,512]{0,1:T(8,128)} async-done(((f32[4096,512]{0,1:T(8,128)}), f32[4096,512]{0,1:T(8,128)}) %all-reduce.7.cloned.1.call-update) | async-done | bytes 8388624 | tf_op jit(solution)/shard_map/psum | solution.py:43
  217.6 2.3 slice_select_fusion
  219.9 26.6 %all-reduce.9.cloned.1.call-done = (f32[512,512]{0,1:T(8,128)}, f32[128,512]{1,0:T(8,128)}) async-done(((f32[512,512]{0,1:T(8,128)}, f32[128,512]{1,0:T(8,128)}), (f32[512,512]{0,1:T(8,128)}, f32[128,512]{1,0:T(8,128)})) %all-reduce.9.cloned.1.call-update) | async-done | bytes 1310736 | tf_op jit(solution)/shard_map/psum | solution.py:13
  246.5 1.6 copy.22
  248.4 11.7 %cholesky.103 = f32[128,128]{1,0:T(8,128)S(1)} custom-call(f32[128,128]{1,0:T(8,128)S(1)} %cholesky.263), custom_call_target="Cholesky" | custom-call | tf_op jit(solution)/shard_map/jit(cholesky)/cholesky | solution.py:46
  260.3 9.8 %custom-call.32 = f32[1,128,128]{1,2,0:T(8,128)S(1)} custom-call(f32[1,128,128]{2,1,0:T(8,128)S(1)} %get-tuple-element.42), custom_call_target="InvertDiagBlocksLowerTriangular" | custom-call | tf_op jit(solution)/shard_map/jit(cholesky)/cholesky | solution.py:46
  270.9 11.7 %cholesky.215 = f32[128,128]{1,0:T(8,128)S(1)} custom-call(f32[128,128]{1,0:T(8,128)S(1)} %cholesky.267), custom_call_target="Cholesky" | custom-call | tf_op jit(solution)/shard_map/jit(cholesky)/cholesky | solution.py:46
  282.7 10.2 %custom-call.33 = f32[1,128,128]{1,2,0:T(8,128)S(1)} custom-call(f32[1,128,128]{2,1,0:T(8,128)S(1)} %get-tuple-element.40), custom_call_target="InvertDiagBlocksLowerTriangular" | custom-call | tf_op jit(solution)/shard_map/jit(cholesky)/cholesky | solution.py:46
  294.0 11.7 %cholesky.236 = f32[128,128]{1,0:T(8,128)S(1)} custom-call(f32[128,128]{1,0:T(8,128)S(1)} %cholesky.272), custom_call_target="Cholesky" | custom-call | tf_op jit(solution)/shard_map/jit(cholesky)/cholesky | solution.py:46
  305.9 9.8 %custom-call.34 = f32[1,128,128]{1,2,0:T(8,128)S(1)} custom-call(f32[1,128,128]{2,1,0:T(8,128)S(1)} %get-tuple-element.38), custom_call_target="InvertDiagBlocksLowerTriangular" | custom-call | tf_op jit(solution)/shard_map/jit(cholesky)/cholesky | solution.py:46
  316.5 11.9 %cholesky.253 = f32[128,128]{1,0:T(8,128)S(1)} custom-call(f32[128,128]{1,0:T(8,128)S(1)} %convolution_subtract_fusion.8), custom_call_target="Cholesky" | custom-call | tf_op jit(solution)/shard_map/jit(cholesky)/cholesky | solution.py:46
  329.1 0.6 compare_reduce_fusion
  329.8 0.7 compare_reduce_fusion.2
  332.8 1.3 fusion.20
  334.2 11.1 %while.1 = (s32[]{:T(128)}, f32[512,512]{0,1:T(8,128)S(1)}, s32[4,2]{0,1:T(2,128)S(1)}, f32[4,128,128]{2,1,0:T(8,128)}, s32[]{:T(128)}) while((s32[]{:T(128)}, f32[512,512]{0,1:T(8,128)S(1)}, s32[4,2]{0,1:T(2,128)S(1)}, f32[4,128,128]{2,1,0:T(8,128)}, s32[]{:T(128)}) %tuple.27), condition=%wide.while_cond, body=%wide.while_body.sunk | while | flops 2 | bytes 393329 | solution.py:17
  334.8 1.4 dynamic-slice.7
  336.3 0.6 bitcast_dynamic-update-slice_fusion.2
  337.6 1.4 dynamic-slice.7
  339.1 0.6 bitcast_dynamic-update-slice_fusion.2
  340.4 1.4 dynamic-slice.7
  341.9 0.6 bitcast_dynamic-update-slice_fusion.2
  343.2 1.4 dynamic-slice.7
  344.7 0.6 bitcast_dynamic-update-slice_fusion.2
  345.3 40.1 %custom-call.35 = f32[4,128,128]{1,2,0:T(8,128)S(1)} custom-call(f32[4,128,128]{2,1,0:T(8,128)} %get-tuple-element.12), custom_call_target="InvertDiagBlocksLowerTriangular" | custom-call | tf_op jit(solution)/shard_map/triangular_solve | solution.py:17
  387.7 0.7 copy.33
  388.6 3.6 fusion.16
  392.2 3.6 convolution_subtract_fusion.2
  395.9 2.0 fusion.49
  397.9 4.1 convolution_subtract_fusion.1
  401.9 2.2 fusion.51
  404.2 5.9 %fusion.8 = f32[4096,128]{0,1:T(8,128)S(1)} fusion(f32[4096,128]{0,1:T(8,128)S(1)} %fusion.51, f32[4096,128]{0,1:T(8,128)S(1)} %fusion.49, f32[4096,128]{0,1:T(8,128)S(1)} %fusion.16, f32[4096,512]{0,1:T(8,128)} %all-reduce.7.cloned.1.call-done, f32[512,512]{0,1:T(8,128)S(1)} %get-tuple-element.97), kind=kOutput, calls=%fused_computation.15 | convolution fusion | flops 2419589120 | bytes 10682368 | tf_op jit(solution)/shard_map/triangular_solve | solution.py:17
  410.1 2.0 fusion.53
  412.1 1.3 pad_maximum_fusion
  413.4 1.0 constant_dynamic-slice_fusion.1
  414.5 6.5 %fusion.7 = f32[4096,128]{0,1:T(8,128)} fusion(f32[4096,128]{0,1:T(8,128)S(1)} %copy-done.3, f32[4096,512]{0,1:T(8,128)S(1)} %pad_maximum_fusion, f32[512,128]{0,1:T(8,128)S(1)} %fusion.33, s32[]{:T(128)S(6)} %select_n.63, f32[512,128]{0,1:T(8,128)S(1)} %constant_dynamic-slice_fusion.1, pred[128]{0:T(512)(128)(4,1)S(1)} %add_compare_fusion.1, ...), kind=kOutput, calls=%fused_computation.12 | convolution fusion | flops 3223519232 | bytes 15471108 | tf_op jit(solution)/shard_map/dot_general | solution.py:57
  420.9 2.9 copy.36
  (76 shorter events, 9.8 us)
Async XLA Ops:
  6.5 1.9 copy-start
  26.3 7.2 %copy-start.7 = (f32[4096,128]{1,0:T(8,128)S(1)}, f32[4096,128]{1,0:T(8,128)}, u32[]{:S(2)}) copy-start(f32[4096,128]{1,0:T(8,128)} %param.3) | copy-start | bytes 6291460
  26.3 11.3 %all-to-all-start = ((f32[2,4096,128]{2,1,0:T(8,128)}), f32[2,4096,128]{2,1,0:T(8,128)}, u32[]{:S(2)}, u32[]{:S(2)}) async-start(f32[2,4096,128]{2,1,0:T(8,128)} %bitcast.68), calls=%async_computation | async-start | bytes 8388608 | tf_op jit(solution)/shard_map/all_to_all | solution.py:29
  33.5 184.1 %all-reduce.7.cloned.1.call-start = ((), (), s32[]{:S(2)}) async-start(), calls=%async_computation.1 | async-start | bytes 16777216 | tf_op jit(solution)/shard_map/psum | solution.py:43
  42.1 4.2 copy-start.4
  42.1 4.2 copy-start.5
  48.1 1.3 copy-start.2
  48.1 198.4 %all-reduce.9.cloned.1.call-start = ((), (), s32[]{:S(2)}) async-start(), calls=%async_computation.2 | async-start | bytes 2621440 | tf_op jit(solution)/shard_map/psum | solution.py:13
  246.5 1.7 copy-start.6
  332.8 52.6 %copy-start.9 = (f32[128,512]{1,0:T(8,128)S(1)}, f32[128,512]{1,0:T(8,128)}, u32[]{:S(2)}) copy-start(f32[128,512]{1,0:T(8,128)} %get-tuple-element.30) | copy-start | bytes 786436
  412.1 2.3 copy-start.8
  412.1 2.3 copy-start.3
  414.5 9.4 %copy-start.1 = (f32[1,6144,128]{2,1,0:T(8,128)S(1)}, f32[1,6144,128]{2,1,0:T(8,128)}, u32[]{:S(2)}) copy-start(f32[1,6144,128]{2,1,0:T(8,128)} %param.4) | copy-start | bytes 9437188
Sparse Core Ops, SparseCore 0:
  48.2 169.2 all-reduce.6
  220.2 26.2 all-reduce.8
where the time goes:
time: 435 us; the launch traced here: 431 us
  waiting for transfers between devices  196 us (45%)
  other arithmetic  130 us (30%)
  local copies, waits for them, and re-layouts  46 us (11%)
  matrix products  34.5 us (8%)
  between operations  16.5 us (4%)
  starting transfers between devices  7.38 us (2%)
    psum x1, waiting for transfers between devices, per_device(): pivot_panel = lax.psum(placed, 'front')  167 us
    another operation x14, other arithmetic, per_device(): factor = jnp.linalg.cholesky(diag_block)  78.8 us
    another operation x4, other arithmetic, solve_right(): lax.linalg.triangular_solve(factor, rows, left_side=False, lower=True, tr...  42.7 us
    psum x1, waiting for transfers between devices, spread(): return lax.psum(block, axis)  26.6 us
    another operation x14, matrix products, solve_right(): lax.linalg.triangular_solve(factor, rows, left_side=False, lower=True, tr...  25.7 us
    scatter x1, local copies, waits for them, and re-layouts, per_device(): jnp.zeros((P_SIZE, col_count), jnp.float32).at[row_index]  17.9 us
    another operation x20, local copies, waits for them, and re-layouts  11.1 us
  transfers between devices with their start and end apart: 3, of which 3 were waited for; matrix products, arithmetic and copies ran while one was open for 1% of the time, Pallas kernels for 0%

commit v1 on v0

v1 whole, which is shorter than its diff:
```python
import jax
import jax.numpy as jnp
from jax import lax
from jax.sharding import PartitionSpec as P

BLK = 128
S = 512
HIGHEST = lax.Precision.HIGHEST


def gather_half(blocks, child_map, half, half_blocks):
    parent = half * half_blocks + jnp.arange(half_blocks, dtype=jnp.int32)
    hit = child_map[None, :] == parent[:, None]
    found = jnp.any(hit, axis=1)
    index = jnp.argmax(hit, axis=1)
    picked = jnp.take(blocks, index, axis=0)
    picked = jnp.where(found[:, None, None], picked, jnp.zeros_like(picked))
    return picked.reshape(half_blocks * BLK, blocks.shape[2])


def per_device(front_block, child_update, child_map):
    rows, cols = front_block.shape
    n_leaf = lax.axis_size("leaf")
    n_front = lax.axis_size("front")
    leaf = lax.axis_index("leaf")
    front = lax.axis_index("front")
    half_blocks = rows // BLK

    blocks = child_update[0].reshape(-1, BLK, cols)
    cmap = child_map[0]
    own = gather_half(blocks, cmap, leaf, half_blocks)
    send = gather_half(blocks, cmap, 1 - leaf, half_blocks)
    recv = lax.ppermute(send, "leaf", [(0, 1), (1, 0)])
    first = jnp.where(leaf == 0, own, recv)
    second = jnp.where(leaf == 0, recv, own)
    assembled = front_block + first + second

    top = assembled[:S]
    piv_cols = S // cols
    is_piv = front < piv_cols
    col_at = jnp.minimum(front, piv_cols - 1) * cols
    panel = lax.dynamic_update_slice_in_dim(
        jnp.zeros((S, S), jnp.float32), jnp.where(is_piv, top, jnp.zeros_like(top)), col_at, 1
    )
    pivot = lax.psum(panel, "front")
    factor = jnp.linalg.cholesky(pivot)

    own_solved = lax.linalg.triangular_solve(factor, top, left_side=True, lower=True).T
    from_leaf0 = lax.ppermute(own_solved, "leaf", [(0, 1)])
    col_solved = jnp.where(leaf == 0, own_solved, from_leaf0)

    piece = rows // n_front
    per_block = BLK // piece
    pieces = []
    for part in range(per_block):
        pairs = []
        for lf in range(n_leaf):
            for k in range(n_front // per_block):
                src = lf * n_front + lf * half_blocks + k
                dst = lf * n_front + per_block * k + part
                pairs.append((src, dst))
        pieces.append(lax.ppermute(col_solved[part * piece:(part + 1) * piece], ("leaf", "front"), pairs))
    my_piece = pieces[0]
    for part in range(1, per_block):
        my_piece = jnp.where(front % per_block == part, pieces[part], my_piece)
    row_solved = lax.all_gather(my_piece, "front", tiled=True)

    schur = assembled - jnp.dot(row_solved, col_solved.T, precision=HIGHEST)

    row_global = leaf * rows + jnp.arange(rows, dtype=jnp.int32)
    col_global = front * cols + jnp.arange(cols, dtype=jnp.int32)
    col_start = jnp.minimum(front * cols, S - cols)
    left_rows = lax.dynamic_slice_in_dim(row_solved, col_start, cols, 1)
    left_top = jnp.pad(lax.dynamic_slice_in_dim(factor, col_start, cols, 1), ((0, rows - S), (0, 0)))
    left_part = jnp.where(row_global[:, None] < S, left_top, left_rows)
    right_top = jnp.pad(col_solved.T, ((0, rows - S), (0, 0)))
    right_part = jnp.where(row_global[:, None] < S, right_top, schur)
    return jnp.where(col_global[None, :] < S, left_part, right_part)


def solution(mesh):
    return jax.shard_map(
        per_device,
        mesh=mesh,
        in_specs=(P("leaf", "front"), P("leaf", None, "front"), P("leaf", None)),
        out_specs=P("leaf", "front"),
        check_vma=False,
    )
```

time: 435 us -> 476 us (1.094)
  waiting for transfers between devices: 196 us -> 220 us
  other arithmetic: 130 us -> 143 us
  local copies, waits for them, and re-layouts: 46 us -> 54 us
    all_gather x0 -> x1, waiting for transfers between devices: none -> 80.8 us  [per_device(): row_solved = lax.all_gather(my_piece, 'front', tiled=True)]
    psum x2 -> x1, waiting for transfers between devices: 194 us -> 129 us  [per_device(): pivot = lax.psum(panel, 'front')]
    scatter x1 -> x0, local copies, waits for them, and re-layouts: 17.9 us -> none  [per_device(): jnp.zeros((P_SIZE, col_count), jnp.float32).at[row_index]]
    another operation x20 -> x13, matrix products: 28 us -> 17.3 us  [the longest x7 9.01 us: per_device(): lax.linalg.triangular_solve(factor, top, left_side=True, lower=True)]
    ppermute x0 -> x4, waiting for transfers between devices: none -> 9.69 us  [the longest x1 4.86 us: per_device(): from_leaf0 = lax.ppermute(own_solved, 'leaf', [(0, 1)])]
    another operation x37, local copies, waits for them, and re-layouts: 12.6 us -> 22 us
    dot_general x1, matrix products: 6.47 us -> 14.8 us  [per_device(): schur = assembled - jnp.dot(row_solved, col_solved.T, precision=HIGHEST)]
    all_to_all x1 -> x0, starting transfers between devices: 7.16 us -> none  [per_device(): lax.all_to_all(placed_rows.reshape(leaf_count, row_count, col_count), 'le...]
  transfers between devices with their start and end apart: 3 -> 6, of which waited for: 3 -> 4; matrix products, arithmetic and copies ran while one was open for 1% -> 3% of each run, Pallas kernels for 0% -> 0%
where the time goes in v1:
time: 476 us; the launch traced here: 471 us
  waiting for transfers between devices  220 us (46%)
  other arithmetic  143 us (30%)
  local copies, waits for them, and re-layouts  54 us (11%)
  matrix products  32.1 us (7%)
  between operations  16.5 us (3%)
  starting transfers between devices  5.81 us (1%)
    psum x1, waiting for transfers between devices, per_device(): pivot = lax.psum(panel, 'front')  129 us
    another operation x15, other arithmetic, per_device(): factor = jnp.linalg.cholesky(pivot)  83.8 us
    all_gather x1, waiting for transfers between devices, per_device(): row_solved = lax.all_gather(my_piece, 'front', tiled=True)  80.8 us
    another operation x3, other arithmetic, per_device(): lax.linalg.triangular_solve(factor, top, left_side=True, lower=True)  41.7 us
    dot_general x1, matrix products, per_device(): schur = assembled - jnp.dot(row_solved, col_solved.T, precision=HIGHEST)  14.8 us
    another operation x20, local copies, waits for them, and re-layouts  14.5 us
  transfers between devices with their start and end apart: 6, of which 4 were waited for; matrix products, arithmetic and copies ran while one was open for 3% of the time, Pallas kernels for 0%

profile of v1, /device:TPU:1, one launch (start us, length us, event | category | flops | bytes accessed | tf_op | source)
XLA Modules:
  0.0 471.3 jit_solution(12014427817205239228)
XLA Ops:
  6.5 1.5 compare_reduce_fusion
  8.9 1.4 compare_reduce_fusion.2
  10.3 2.0 gather_fusion.1
  12.3 3.2 select_select_fusion
  15.5 2.9 copy.84
  18.4 1.4 collective-permute-start
  19.9 2.0 gather_fusion
  21.8 3.2 select_select_fusion.1
  25.1 2.9 copy.83
  28.0 2.9 copy.56
  30.8 3.3 select_add_fusion
  34.1 1.4 broadcast_in_dim.58
  37.1 129.3 %all-reduce.5.cloned.1.call-done = f32[512,512]{0,1:T(8,128)} async-done(((f32[512,512]{0,1:T(8,128)}), f32[512,512]{0,1:T(8,128)}) %all-reduce.5.cloned.1.call-update) | async-done | bytes 1048592 | tf_op jit(solution)/shard_map/psum | solution.py:45
  166.4 2.6 copy.57
  169.0 1.8 fusion
  171.8 11.7 %cholesky.103 = f32[128,128]{1,0:T(8,128)S(1)} custom-call(f32[128,128]{1,0:T(8,128)S(1)} %cholesky.263), custom_call_target="Cholesky" | custom-call | tf_op jit(solution)/shard_map/jit(cholesky)/cholesky | solution.py:46
  184.3 9.8 %custom-call.30 = f32[1,128,128]{1,2,0:T(8,128)S(1)} custom-call(f32[1,128,128]{2,1,0:T(8,128)S(1)} %get-tuple-element.55), custom_call_target="InvertDiagBlocksLowerTriangular" | custom-call | tf_op jit(solution)/shard_map/jit(cholesky)/cholesky | solution.py:46
  195.3 1.9 convolution_subtract_fusion.1
  197.4 1.5 cholesky.267
  198.9 13.2 %cholesky.215 = f32[128,128]{1,0:T(8,128)} custom-call(f32[128,128]{1,0:T(8,128)} %cholesky.267), custom_call_target="Cholesky" | custom-call | tf_op jit(solution)/shard_map/jit(cholesky)/cholesky | solution.py:46
  212.1 1.5 copy.60
  213.6 1.5 select_reduce_fusion.2
  215.1 11.4 %custom-call.31 = f32[1,128,128]{1,2,0:T(8,128)} custom-call(f32[1,128,128]{2,1,0:T(8,128)} %get-tuple-element.53), custom_call_target="InvertDiagBlocksLowerTriangular" | custom-call | tf_op jit(solution)/shard_map/jit(cholesky)/cholesky | solution.py:46
  230.6 1.5 convolution_subtract_fusion.2
  232.1 11.7 %cholesky.236 = f32[128,128]{1,0:T(8,128)S(1)} custom-call(f32[128,128]{1,0:T(8,128)S(1)} %cholesky.272), custom_call_target="Cholesky" | custom-call | tf_op jit(solution)/shard_map/jit(cholesky)/cholesky | solution.py:46
  244.6 9.8 %custom-call.32 = f32[1,128,128]{1,2,0:T(8,128)S(1)} custom-call(f32[1,128,128]{2,1,0:T(8,128)S(1)} %get-tuple-element.51), custom_call_target="InvertDiagBlocksLowerTriangular" | custom-call | tf_op jit(solution)/shard_map/jit(cholesky)/cholesky | solution.py:46
  255.3 1.5 convolution_subtract_fusion.3
  256.8 11.9 %cholesky.253 = f32[128,128]{1,0:T(8,128)S(1)} custom-call(f32[128,128]{1,0:T(8,128)S(1)} %convolution_subtract_fusion.3), custom_call_target="Cholesky" | custom-call | tf_op jit(solution)/shard_map/jit(cholesky)/cholesky | solution.py:46
  274.7 1.6 fusion.1
  276.3 14.5 %while.1 = (s32[]{:T(128)}, f32[512,512]{0,1:T(8,128)}, s32[4,2]{0,1:T(2,128)S(1)}, f32[4,128,128]{2,1,0:T(8,128)}, s32[]{:T(128)}) while((s32[]{:T(128)}, f32[512,512]{0,1:T(8,128)}, s32[4,2]{0,1:T(2,128)S(1)}, f32[4,128,128]{2,1,0:T(8,128)}, s32[]{:T(128)}) %tuple.35), condition=%wide.while_cond, body=%wide.while_body.sunk | while | flops 2 | bytes 393329 | solution.py:48
  277.0 2.2 dynamic-slice.7
  280.6 2.2 dynamic-slice.7
  284.3 2.2 dynamic-slice.7
  287.9 2.2 dynamic-slice.7
  290.8 40.1 %custom-call.33 = f32[4,128,128]{1,2,0:T(8,128)S(1)} custom-call(f32[4,128,128]{2,1,0:T(8,128)} %get-tuple-element.17), custom_call_target="InvertDiagBlocksLowerTriangular" | custom-call | tf_op jit(solution)/shard_map/triangular_solve | solution.py:48
  335.3 1.3 fusion.14
  337.8 2.0 fusion.4
  341.1 1.3 collective-permute-start.1
  342.4 4.9 %collective-permute-done.1 = f32[128,512]{1,0:T(8,128)S(1)} collective-permute-done((f32[128,512]{1,0:T(8,128)S(1)}, f32[128,512]{1,0:T(8,128)S(1)}, u32[]{:S(2)}, u32[]{:S(2)}) %collective-permute-start.1) | collective-permute-done | bytes 262176 | tf_op jit(solution)/shard_map/ppermute | solution.py:49
  348.8 1.3 collective-permute-start.3
  350.1 1.3 collective-permute-start.2
  351.4 4.8 %collective-permute-done.3 = f32[64,512]{1,0:T(8,128)S(1)} collective-permute-done((f32[64,512]{1,0:T(8,128)}, f32[64,512]{1,0:T(8,128)S(1)}, u32[]{:S(2)}, u32[]{:S(2)}) %collective-permute-start.3) | collective-permute-done | bytes 131104 | tf_op jit(solution)/shard_map/ppermute | solution.py:62
  357.0 1.7 constant_dynamic-slice_fusion.2
  358.7 80.8 %all-gather.2.cloned.1.call-done = f32[4096,512]{1,0:T(8,128)} async-done(((f32[64,512]{1,0:T(8,128)}), f32[4096,512]{1,0:T(8,128)}) %all-gather.2.cloned.1.call-update) | async-done | bytes 8388624 | tf_op jit(solution)/shard_map/all_gather | solution.py:66
  439.5 4.2 constant_dynamic-slice_fusion.1
  443.7 2.9 copy.86
  446.6 14.8 %select_select_fusion.2 = f32[4096,128]{0,1:T(8,128)} fusion(f32[512,128]{0,1:T(8,128)S(1)} %bitcast.58, f32[4096,128]{0,1:T(8,128)} %copy.86, f32[512,128]{0,1:T(8,128)} %constant_dynamic-slice_fusion.2, pred[128]{0:T(512)(128)(4,1)S(1)} %add_compare_fusion.1, pred[4096]{0:T(1024)(128)(4,1)S(1)} %add_compare_fusion, f32[4096,128]{0,1:T(8,128)} %copy-done.1, ...), kind=kOutput, calls=%fused_computation.7 | convolution fusion | flops 3223322624 | bytes 15470720 | tf_op jit(solution)/shard_map/dot_general | solution.py:68
  461.4 2.9 copy.75
  (82 shorter events, 29.3 us)
Async XLA Ops:
  6.5 3.8 copy-start
  6.5 159.9 %all-reduce.5.cloned.1.call-start = ((), (), s32[]{:S(2)}) async-start(), calls=%async_computation | async-start | bytes 2097152 | tf_op jit(solution)/shard_map/psum | solution.py:45
  18.4 12.4 %collective-permute-start = (f32[4096,128]{0,1:T(8,128)}, f32[4096,128]{0,1:T(8,128)}, u32[]{:S(2)}, u32[]{:S(2)}) collective-permute-start(f32[4096,128]{0,1:T(8,128)} %copy.84), channel_id=1, source_target_pairs={{0,64},{64,0},{1,65},{65,1},{2,66},{66,2},{3,67},{67,3},{4,68},{68... | collective-permute-start | bytes 6291464 | tf_op jit(solution)/shard_map/ppermute | solution.py:33
  34.1 1.7 copy-start.1
  36.6 403.0 %all-gather.2.cloned.1.call-start = ((), (), s32[]{:S(2)}) async-start(), calls=%async_computation.1 | async-start | bytes 8519680 | tf_op jit(solution)/shard_map/all_gather | solution.py:66
  170.8 1.0 copy-start.3
  197.4 31.0 %copy-start.4 = (f32[384,128]{1,0:T(8,128)S(1)}, f32[384,128]{1,0:T(8,128)}, u32[]{:S(2)}) copy-start(f32[384,128]{1,0:T(8,128)} %convolution_subtract_fusion.1) | copy-start | bytes 589828
  229.5 1.0 copy-start.2
  331.0 0.7 copy-start.6
  339.9 2.5 copy-start.5
  341.1 6.2 %collective-permute-start.1 = (f32[128,512]{1,0:T(8,128)S(1)}, f32[128,512]{1,0:T(8,128)S(1)}, u32[]{:S(2)}, u32[]{:S(2)}) collective-permute-start(f32[128,512]{1,0:T(8,128)S(1)} %maximum_bitcast_fusion), channel_id=1, source_target_pairs={{0,64},{1,65},{2,66},{3,67},{4,68},{5,69},{6,70},{7,71},{8,72},{9,... | collective-permute-start | bytes 786440 | tf_op jit(solution)/shard_map/ppermute | solution.py:49
  348.8 7.4 %collective-permute-start.3 = (f32[64,512]{1,0:T(8,128)}, f32[64,512]{1,0:T(8,128)S(1)}, u32[]{:S(2)}, u32[]{:S(2)}) collective-permute-start(f32[64,512]{1,0:T(8,128)} %get-tuple-element.48), channel_id=1, source_target_pairs={{0,0},{1,2},{2,4},{3,6},{4,8},{5,10},{6,12},{7,14},{8,16},{9,18},{... | collective-permute-start | bytes 393224 | tf_op jit(solution)/shard_map/ppermute | solution.py:62
  350.1 6.1 %collective-permute-start.2 = (f32[64,512]{1,0:T(8,128)}, f32[64,512]{1,0:T(8,128)}, u32[]{:S(2)}, u32[]{:S(2)}) collective-permute-start(f32[64,512]{1,0:T(8,128)} %get-tuple-element.49), channel_id=1, source_target_pairs={{0,1},{1,3},{2,5},{3,7},{4,9},{5,11},{6,13},{7,15},{8,17},{9,19},{... | collective-permute-start | bytes 393224 | tf_op jit(solution)/shard_map/ppermute | solution.py:62
Sparse Core Ops, SparseCore 0:
  36.7 129.7 all-reduce.4
  357.1 82.4 all-gather.1

commit v2 on v1

--- a/solution.py
+++ b/solution.py
@@ -1,11 +1,16 @@
+import functools
+
 import jax
 import jax.numpy as jnp
 from jax import lax
+from jax.experimental import pallas as pl
+from jax.experimental.pallas import tpu as pltpu
 from jax.sharding import PartitionSpec as P
 
 BLK = 128
 S = 512
 HIGHEST = lax.Precision.HIGHEST
+MESH = pl.DeviceIdType.MESH
 
 
 def gather_half(blocks, child_map, half, half_blocks):
@@ -18,6 +23,132 @@
     return picked.reshape(half_blocks * BLK, blocks.shape[2])
 
 
+def pivot_kernel(n_front, n_src, top_ref, out_ref, chunk, sem_a, sem_b, send_a, send_b, recv_g, send_g):
+    leaf = lax.axis_index("leaf")
+    me = lax.axis_index("front")
+    per_src = n_front // n_src
+    rows = chunk.shape[0]
+
+    @pl.when((leaf == 0) & (me < n_src))
+    def _():
+        for k in range(per_src):
+            src = top_ref.at[pl.ds(k * rows, rows)]
+            dst = me * per_src + k
+            if k == 0:
+                @pl.when(me == 0)
+                def _():
+                    pltpu.make_async_copy(src, chunk, sem_a).start()
+
+                @pl.when(me != 0)
+                def _():
+                    pltpu.make_async_remote_copy(
+                        src, chunk, send_a.at[k], sem_a, device_id=(0, dst), device_id_type=MESH
+                    ).start()
+            else:
+                pltpu.make_async_remote_copy(
+                    src, chunk, send_a.at[k], sem_a, device_id=(0, dst), device_id_type=MESH
+                ).start()
+
+    @pl.when((leaf == 0) & (me == 0))
+    def _():
+        pltpu.make_async_copy(top_ref.at[pl.ds(0, rows)], chunk, sem_a).wait()
+
+    @pl.when((leaf == 0) & (me != 0))
+    def _():
+        pltpu.make_async_remote_copy(
+            top_ref.at[pl.ds(0, rows)], chunk, send_a.at[0], sem_a, device_id=(0, me), device_id_type=MESH
+        ).wait_recv()
+
+    @pl.when(leaf == 0)
+    def _():
+        pltpu.make_async_remote_copy(
+            chunk, chunk, send_b, sem_b, device_id=(1, me), device_id_type=MESH
+        ).start()
+
+    @pl.when(leaf == 1)
+    def _():
+        pltpu.make_async_remote_copy(
+            chunk, chunk, send_b, sem_b, device_id=(0, me), device_id_type=MESH
+        ).wait_recv()
+
+    pltpu.make_async_copy(chunk, out_ref.at[me], recv_g.at[me]).start()
+
+    def send(j, carry):
+        dst = lax.rem(me + j, n_front)
+        pltpu.make_async_remote_copy(
+            chunk, out_ref.at[me], send_g.at[j], recv_g.at[me], device_id=(leaf, dst), device_id_type=MESH
+        ).start()
+        return carry
+
+    lax.fori_loop(1, n_front, send, 0)
+
+    pltpu.make_async_copy(chunk, out_ref.at[me], recv_g.at[me]).wait()
+
+    def receive(j, carry):
+        src = lax.rem(me + j, n_front)
+        pltpu.make_async_remote_copy(
+            chunk, out_ref.at[src], send_g.at[j], recv_g.at[src], device_id=(leaf, src), device_id_type=MESH
+        ).wait_recv()
+        return carry
+
+    lax.fori_loop(1, n_front, receive, 0)
+
+    def sent(j, carry):
+        dst = lax.rem(me + j, n_front)
+        pltpu.make_async_remote_copy(
+            chunk, out_ref.at[me], send_g.at[j], recv_g.at[me], device_id=(leaf, dst), device_id_type=MESH
+        ).wait_send()
+        return carry
+
+    lax.fori_loop(1, n_front, sent, 0)
+
+    @pl.when(leaf == 0)
+    def _():
+        pltpu.make_async_remote_copy(
+            chunk, chunk, send_b, sem_b, device_id=(1, me), device_id_type=MESH
+        ).wait_send()
+
+    @pl.when((leaf == 0) & (me < n_src))
+    def _():
+        for k in range(per_src):
+            src = top_ref.at[pl.ds(k * rows, rows)]
+            dst = me * per_src + k
+            if k == 0:
+                @pl.when(me != 0)
+                def _():
+                    pltpu.make_async_remote_copy(
+                        src, chunk, send_a.at[k], sem_a, device_id=(0, dst), device_id_type=MESH
+                    ).wait_send()
+            else:
+                pltpu.make_async_remote_copy(
+                    src, chunk, send_a.at[k], sem_a, device_id=(0, dst), device_id_type=MESH
+                ).wait_send()
+
+
+def broadcast_pivot(top, n_front):
+    cols = top.shape[1]
+    n_src = S // cols
+    per_src = n_front // n_src
+    rows = S // per_src
+    gathered = pl.pallas_call(
+        functools.partial(pivot_kernel, n_front, n_src),
+        out_shape=jax.ShapeDtypeStruct((n_front, rows, cols), jnp.float32),
+        in_specs=[pl.BlockSpec(memory_space=pltpu.VMEM)],
+        out_specs=pl.BlockSpec(memory_space=pltpu.VMEM),
+        scratch_shapes=[
+            pltpu.VMEM((rows, cols), jnp.float32),
+            pltpu.SemaphoreType.DMA,
+            pltpu.SemaphoreType.DMA,
+            pltpu.SemaphoreType.DMA((per_src,)),
+            pltpu.SemaphoreType.DMA,
+            pltpu.SemaphoreType.DMA((n_front,)),
+            pltpu.SemaphoreType.DMA((n_front,)),
+        ],
+        compiler_params=pltpu.CompilerParams(has_side_effects=True),
+    )(top)
+    return gathered.reshape(n_src, per_src, rows, cols).transpose(1, 2, 0, 3).reshape(S, S)
+
+
 def per_device(front_block, child_update, child_map):
     rows, cols = front_block.shape
     n_leaf = lax.axis_size("leaf")
@@ -36,18 +167,7 @@
     assembled = front_block + first + second
 
     top = assembled[:S]
-    piv_cols = S // cols
-    is_piv = front < piv_cols
-    col_at = jnp.minimum(front, piv_cols - 1) * cols
-    panel = lax.dynamic_update_slice_in_dim(
-        jnp.zeros((S, S), jnp.float32), jnp.where(is_piv, top, jnp.zeros_like(top)), col_at, 1
-    )
-    pivot = lax.psum(panel, "front")
-    factor = jnp.linalg.cholesky(pivot)
-
-    own_solved = lax.linalg.triangular_solve(factor, top, left_side=True, lower=True).T
-    from_leaf0 = lax.ppermute(own_solved, "leaf", [(0, 1)])
-    col_solved = jnp.where(leaf == 0, own_solved, from_leaf0)
+    panel_rows = top.T
 
     piece = rows // n_front
     per_block = BLK // piece
@@ -56,15 +176,26 @@
         pairs = []
         for lf in range(n_leaf):
             for k in range(n_front // per_block):
-                src = lf * n_front + lf * half_blocks + k
+                src = lf * half_blocks + k
                 dst = lf * n_front + per_block * k + part
                 pairs.append((src, dst))
-        pieces.append(lax.ppermute(col_solved[part * piece:(part + 1) * piece], ("leaf", "front"), pairs))
+        pieces.append(lax.ppermute(panel_rows[part * piece:(part + 1) * piece], ("leaf", "front"), pairs))
     my_piece = pieces[0]
     for part in range(1, per_block):
         my_piece = jnp.where(front % per_block == part, pieces[part], my_piece)
-    row_solved = lax.all_gather(my_piece, "front", tiled=True)
-
+    panel = lax.all_gather(my_piece, "front", tiled=True)
+
+    pivot = broadcast_pivot(top, n_front)
+    factor = jnp.linalg.cholesky(pivot)
+    inverse = lax.linalg.triangular_solve(
+        factor, jnp.eye(S, dtype=jnp.float32), left_side=True, lower=True
+    )
+
+    own_solved = jnp.dot(panel_rows, inverse.T, precision=HIGHEST)
+    from_leaf0 = lax.ppermute(own_solved, "leaf", [(0, 1)])
+    col_solved = jnp.where(leaf == 0, own_solved, from_leaf0)
+
+    row_solved = jnp.dot(panel, inverse.T, precision=HIGHEST)
     schur = assembled - jnp.dot(row_solved, col_solved.T, precision=HIGHEST)
 
     row_global = leaf * rows + jnp.arange(rows, dtype=jnp.int32)

time: 476 us -> 299 us (0.63)
  waiting for transfers between devices: 220 us -> 8.08 us
  Pallas kernels: 0 us -> 44.5 us
  local copies, waits for them, and re-layouts: 54 us -> 32.3 us
  matrix products: 32.1 us -> 45.8 us
    psum x1 -> x0, waiting for transfers between devices: 129 us -> none  [per_device(): pivot = lax.psum(panel, 'front')]
    all_gather x1, waiting for transfers between devices: 80.8 us -> 0.01 us  [per_device(): panel = lax.all_gather(my_piece, 'front', tiled=True)]
    pallas_call x0 -> x1, Pallas kernels: none -> 44.5 us  [broadcast_pivot(): pl.pallas_call(functools.partial(pivot_kernel, n_front, n_src), out_shape...]
    dot_general x0 -> x2, matrix products: none -> 20.7 us  [the longest x1 18 us: per_device(): row_solved = jnp.dot(panel, inverse.T, precision=HIGHEST)]
    another operation x13 -> x4, local copies, waits for them, and re-layouts: 7.23 us -> 1.12 us  [per_device(): factor = jnp.linalg.cholesky(pivot)]
    dot_general x1, matrix products: 14.8 us -> 9.3 us  [per_device(): schur = assembled - jnp.dot(row_solved, col_solved.T, precision=HIGHEST)]
    another operation x24 -> x13, local copies, waits for them, and re-layouts: 14.7 us -> 14.1 us
  transfers between devices with their start and end apart: 6 -> 5, of which waited for: 4 -> 3; matrix products, arithmetic and copies ran while one was open for 3% -> 60% of each run, Pallas kernels for 0% -> 15%
where the time goes in v2:
time: 299 us; the launch traced here: 295 us
  other arithmetic  142 us (47%)
  matrix products  45.8 us (15%)
  Pallas kernels  44.5 us (15%)
  local copies, waits for them, and re-layouts  32.3 us (11%)
  between operations  16.8 us (6%)
  waiting for transfers between devices  8.08 us (3%)
  starting transfers between devices  5.35 us (2%)
    another operation x15, other arithmetic, per_device(): factor = jnp.linalg.cholesky(pivot)  81.4 us
    pallas_call x1, Pallas kernels, broadcast_pivot(): pl.pallas_call(functools.partial(pivot_kernel, n_front, n_src), out_shape...  44.5 us
    another operation x3, other arithmetic, per_device(): lax.linalg.triangular_solve(factor, jnp.eye(S, dtype=jnp.float32), left_s...  43.5 us
    dot_general x1, matrix products, per_device(): row_solved = jnp.dot(panel, inverse.T, precision=HIGHEST)  18 us
    another operation x12, local copies, waits for them, and re-layouts  14.1 us
    dot_general x1, matrix products, per_device(): schur = assembled - jnp.dot(row_solved, col_solved.T, precision=HIGHEST)  9.3 us
    another operation x7, matrix products, per_device(): lax.linalg.triangular_solve(factor, jnp.eye(S, dtype=jnp.float32), left_s...  7.98 us
    another operation x6, matrix products, per_device(): factor = jnp.linalg.cholesky(pivot)  7.82 us
  transfers between devices with their start and end apart: 5, of which 3 were waited for; matrix products, arithmetic and copies ran while one was open for 60% of the time, Pallas kernels for 15%

profile of v2, /device:TPU:1, one launch (start us, length us, event | category | flops | bytes accessed | tf_op | source)
XLA Modules:
  0.0 295.1 jit_solution(13562337701372461803)
XLA Ops:
  6.5 1.5 compare_reduce_fusion
  8.9 1.4 compare_reduce_fusion.2
  10.3 2.0 gather_fusion.1
  12.3 3.2 %select_select_fusion = f32[32,128,128]{2,1,0:T(8,128)} fusion(f32[32,128,128]{2,1,0:T(8,128)} %gather_fusion.1, pred[32]{0:T(512)(128)(4,1)S(1)} %compare_and_fusion, pred[32]{0:T(512)(128)(4,1)S(1)} %get-tuple-element.19), kind=kLoop, calls=%fused_computation.9 | loop fusion | flops 1048576 | bytes 4194368 | tf_op jit(solution)/shard_map/jit(_where)/select_n | solution.py:22
  15.5 1.4 collective-permute-start
  16.9 2.0 gather_fusion
  18.9 2.0 select_select_fusion.1
  21.1 1.9 fusion.1
  23.0 1.3 copy-done.1
  25.8 1.3 collective-permute-start.2
  27.1 1.4 collective-permute-start.1
  28.5 7.5 %collective-permute-done.2 = f32[64,512]{0,1:T(8,128)} collective-permute-done((f32[64,512]{0,1:T(8,128)}, f32[64,512]{0,1:T(8,128)}, u32[]{:S(2)}, u32[]{:S(2)}) %collective-permute-start.2) | collective-permute-done | bytes 131104 | tf_op jit(solution)/shard_map/ppermute | solution.py:182
  38.6 1.2 fusion.14
  39.7 44.5 %shard_map.37 = f32[64,32,128]{2,1,0:T(8,128)} custom-call(f32[512,128]{1,0:T(8,128)} %get-tuple-element.33.top_ref), custom_call_target="tpu_custom_call" | custom-call | tf_op jit(solution)/shard_map/pallas_call | solution.py:133
  84.2 1.9 copy.17
  87.1 1.0 copy.27
  88.2 2.5 copy.18
  90.7 1.8 fusion.2
  93.5 11.7 %cholesky.104 = f32[128,128]{1,0:T(8,128)S(1)} custom-call(f32[128,128]{1,0:T(8,128)S(1)} %cholesky.266), custom_call_target="Cholesky" | custom-call | tf_op jit(solution)/shard_map/jit(cholesky)/cholesky | solution.py:189
  105.3 9.8 %custom-call.30 = f32[1,128,128]{1,2,0:T(8,128)S(1)} custom-call(f32[1,128,128]{2,1,0:T(8,128)S(1)} %get-tuple-element.45), custom_call_target="InvertDiagBlocksLowerTriangular" | custom-call | tf_op jit(solution)/shard_map/jit(cholesky)/cholesky | solution.py:189
  115.1 1.1 cholesky.224
  116.2 2.0 constant_dynamic-update-slice_fusion.1
  118.1 1.3 convolution_subtract_fusion.4
  119.4 11.9 %cholesky.217 = f32[128,128]{1,0:T(8,128)S(1)} custom-call(f32[128,128]{1,0:T(8,128)S(1)} %cholesky.270), custom_call_target="Cholesky" | custom-call | tf_op jit(solution)/shard_map/jit(cholesky)/cholesky | solution.py:189
  131.9 9.8 %custom-call.31 = f32[1,128,128]{1,2,0:T(8,128)S(1)} custom-call(f32[1,128,128]{2,1,0:T(8,128)S(1)} %get-tuple-element.42), custom_call_target="InvertDiagBlocksLowerTriangular" | custom-call | tf_op jit(solution)/shard_map/jit(cholesky)/cholesky | solution.py:189
  142.7 1.4 convolution_subtract_fusion.5
  144.1 11.7 %cholesky.238 = f32[128,128]{1,0:T(8,128)S(1)} custom-call(f32[128,128]{1,0:T(8,128)S(1)} %cholesky.275), custom_call_target="Cholesky" | custom-call | tf_op jit(solution)/shard_map/jit(cholesky)/cholesky | solution.py:189
  156.5 9.8 %custom-call.32 = f32[1,128,128]{1,2,0:T(8,128)S(1)} custom-call(f32[1,128,128]{2,1,0:T(8,128)S(1)} %get-tuple-element.39), custom_call_target="InvertDiagBlocksLowerTriangular" | custom-call | tf_op jit(solution)/shard_map/jit(cholesky)/cholesky | solution.py:189
  167.1 1.4 convolution_subtract_fusion.6
  168.5 11.9 %cholesky.255 = f32[128,128]{1,0:T(8,128)S(1)} custom-call(f32[128,128]{1,0:T(8,128)S(1)} %convolution_subtract_fusion.6), custom_call_target="Cholesky" | custom-call | tf_op jit(solution)/shard_map/jit(cholesky)/cholesky | solution.py:189
  186.5 2.8 fusion.3
  189.3 14.1 %while.1 = (s32[]{:T(128)}, f32[512,512]{1,0:T(8,128)}, s32[4,2]{0,1:T(2,128)S(1)}, f32[4,128,128]{2,1,0:T(8,128)}, s32[]{:T(128)}) while((s32[]{:T(128)}, f32[512,512]{1,0:T(8,128)}, s32[4,2]{0,1:T(2,128)S(1)}, f32[4,128,128]{2,1,0:T(8,128)}, s32[]{:T(128)}) %tuple.35), condition=%wide.while_cond, body=%wide.while_body.sunk | while | flops 2 | bytes 132205 | solution.py:190
  189.9 2.9 bitcast_dynamic-update-slice_fusion.2
  193.5 2.9 bitcast_dynamic-update-slice_fusion.2
  197.0 2.9 bitcast_dynamic-update-slice_fusion.2
  200.6 2.8 bitcast_dynamic-update-slice_fusion.2
  203.4 40.7 %custom-call.33 = f32[4,128,128]{1,2,0:T(8,128)} custom-call(f32[4,128,128]{2,1,0:T(8,128)} %get-tuple-element.17), custom_call_target="InvertDiagBlocksLowerTriangular" | custom-call | tf_op jit(solution)/shard_map/triangular_solve | solution.py:190
  244.1 1.2 fusion.16
  245.4 1.4 convolution_subtract_fusion.2
  246.7 1.3 fusion.29
  248.0 1.5 convolution_subtract_fusion.1
  250.0 1.8 convolution_subtract_fusion.3
  252.2 2.7 fusion.9
  255.0 1.3 collective-permute-start.3
  256.3 1.9 constant_dynamic-slice_fusion.1
  258.7 1.7 fusion.25
  260.4 18.0 %fusion.10 = f32[4096,512]{1,0:T(8,128)S(1)} fusion(f32[4096,512]{1,0:T(8,128)} %all-gather.2.cloned.1.call-done, f32[128,512]{1,0:T(8,128)} %copy-done.8, f32[128,512]{1,0:T(8,128)} %copy-done.6, f32[128,512]{1,0:T(8,128)} %copy-done.4, f32[128,512]{1,0:T(8,128)S(1)} %fusion.16), kind=kOutput, calls=%fused_computation.34 | convolution fusion | flops 12885688320 | bytes 17825792 | tf_op jit(solution)/shard_map/dot_general | solution.py:198
  278.4 9.3 %select_select_fusion.2 = f32[4096,128]{1,0:T(8,128)} fusion(f32[512,128]{1,0:T(8,128)S(1)} %copy-done.10, f32[4096,512]{1,0:T(8,128)S(1)} %fusion.10, s32[]{:T(128)S(6)} %select_n.80, f32[512,128]{1,0:T(8,128)S(1)} %copy-done.9, pred[4096]{0:T(1024)(128)(4,1)S(1)} %add_compare_fusion, pred[128]{0:T(512)(128)(4,1)S(1)} %add_compare_fusion.1, ...), kind=kOutput, calls=%fused_computation.11 | convolution fusion | flops 3223388160 | bytes 15733253 | tf_op jit(solution)/shard_map/dot_general | solution.py:199
  (70 shorter events, 17.6 us)
Async XLA Ops:
  6.5 3.7 %copy-start = (f32[1,6144,128]{2,1,0:T(8,128)S(1)}, f32[1,6144,128]{2,1,0:T(8,128)}, u32[]{:S(2)}) copy-start(f32[1,6144,128]{2,1,0:T(8,128)} %param.6) | copy-start | bytes 9437188
  6.5 253.9 %all-gather.2.cloned.1.call-start = ((), (), s32[]{:S(2)}) async-start(), calls=%async_computation | async-start | bytes 8519680 | tf_op jit(solution)/shard_map/all_gather | solution.py:186
  15.5 5.6 %collective-permute-start = (f32[4096,128]{1,0:T(8,128)}, f32[4096,128]{1,0:T(8,128)}, u32[]{:S(2)}, u32[]{:S(2)}) collective-permute-start(f32[4096,128]{1,0:T(8,128)} %bitcast.3), channel_id=1, source_target_pairs={{0,64},{64,0},{1,65},{65,1},{2,66},{66,2},{3,67},{67,3},{4,68},{68... | collective-permute-start | bytes 6291464 | tf_op jit(solution)/shard_map/ppermute | solution.py:164
  18.9 2.2 copy-start.7
  23.0 1.3 copy-start.1
  25.8 10.1 %collective-permute-start.2 = (f32[64,512]{0,1:T(8,128)}, f32[64,512]{0,1:T(8,128)}, u32[]{:S(2)}, u32[]{:S(2)}) collective-permute-start(f32[64,512]{0,1:T(8,128)} %get-tuple-element.34), channel_id=1, source_target_pairs={{0,0},{1,2},{2,4},{3,6},{4,8},{5,10},{6,12},{7,14},{8,16},{9,18},{... | collective-permute-start | bytes 393224 | tf_op jit(solution)/shard_map/ppermute | solution.py:182
  27.1 8.8 %collective-permute-start.1 = (f32[64,512]{0,1:T(8,128)S(1)}, f32[64,512]{0,1:T(8,128)}, u32[]{:S(2)}, u32[]{:S(2)}) collective-permute-start(f32[64,512]{0,1:T(8,128)S(1)} %get-tuple-element.35), channel_id=1, source_target_pairs={{0,1},{1,3},{2,5},{3,7},{4,9},{5,11},{6,13},{7,15},{8,17},{9,19},{... | collective-permute-start | bytes 393224 | tf_op jit(solution)/shard_map/ppermute | solution.py:182
  86.2 1.0 copy-start.3
  92.5 1.0 copy-start.5
  244.1 5.4 %copy-start.11 = (f32[4,128,128]{1,2,0:T(8,128)S(1)}, f32[4,128,128]{1,2,0:T(8,128)}, u32[]{:S(2)}) copy-start(f32[4,128,128]{1,2,0:T(8,128)} %custom-call.33) | copy-start | bytes 786436
  248.0 7.0 %copy-start.4 = (f32[128,512]{1,0:T(8,128)}, f32[128,512]{1,0:T(8,128)S(1)}, u32[]{:S(2)}) copy-start(f32[128,512]{1,0:T(8,128)S(1)} %fusion.29) | copy-start | bytes 786436
  250.0 6.3 %copy-start.6 = (f32[128,512]{1,0:T(8,128)}, f32[128,512]{1,0:T(8,128)S(1)}, u32[]{:S(2)}) copy-start(f32[128,512]{1,0:T(8,128)S(1)} %fusion.27) | copy-start | bytes 786436
  252.2 4.1 %copy-start.8 = (f32[128,512]{1,0:T(8,128)}, f32[128,512]{1,0:T(8,128)S(1)}, u32[]{:S(2)}) copy-start(f32[128,512]{1,0:T(8,128)S(1)} %fusion.26) | copy-start | bytes 786436
  255.0 3.8 %collective-permute-start.3 = (f32[128,512]{0,1:T(8,128)}, f32[128,512]{0,1:T(8,128)}, u32[]{:S(2)}, u32[]{:S(2)}) collective-permute-start(f32[128,512]{0,1:T(8,128)} %fusion.9), channel_id=1, source_target_pairs={{0,64},{1,65},{2,66},{3,67},{4,68},{5,69},{6,70},{7,71},{8,72},{9,... | collective-permute-start | bytes 786440 | tf_op jit(solution)/shard_map/ppermute | solution.py:195
  260.4 18.0 %copy-start.2 = (f32[4096,128]{1,0:T(8,128)S(1)}, f32[4096,128]{1,0:T(8,128)}, u32[]{:S(2)}) copy-start(f32[4096,128]{1,0:T(8,128)} %copy-done.1) | copy-start | bytes 6291460
  260.4 18.0 %copy-start.9 = (f32[512,128]{1,0:T(8,128)S(1)}, f32[512,128]{1,0:T(8,128)}, u32[]{:S(2)}) copy-start(f32[512,128]{1,0:T(8,128)} %constant_dynamic-slice_fusion.1) | copy-start | bytes 786436
  260.4 18.0 %copy-start.10 = (f32[512,128]{1,0:T(8,128)S(1)}, f32[512,128]{1,0:T(8,128)}, u32[]{:S(2)}) copy-start(f32[512,128]{1,0:T(8,128)} %fusion.25) | copy-start | bytes 786436
Sparse Core Ops, SparseCore 0:
  37.9 96.9 all-gather.1

commit v3 on v2

--- a/solution.py
+++ b/solution.py
@@ -183,19 +183,17 @@
     my_piece = pieces[0]
     for part in range(1, per_block):
         my_piece = jnp.where(front % per_block == part, pieces[part], my_piece)
+    pivot = broadcast_pivot(top, n_front)
+    my_piece, pivot = lax.optimization_barrier((my_piece, pivot))
     panel = lax.all_gather(my_piece, "front", tiled=True)
-
-    pivot = broadcast_pivot(top, n_front)
     factor = jnp.linalg.cholesky(pivot)
-    inverse = lax.linalg.triangular_solve(
-        factor, jnp.eye(S, dtype=jnp.float32), left_side=True, lower=True
-    )
-
-    own_solved = jnp.dot(panel_rows, inverse.T, precision=HIGHEST)
-    from_leaf0 = lax.ppermute(own_solved, "leaf", [(0, 1)])
-    col_solved = jnp.where(leaf == 0, own_solved, from_leaf0)
-
-    row_solved = jnp.dot(panel, inverse.T, precision=HIGHEST)
+    row_solved = lax.linalg.triangular_solve(factor, panel, left_side=False, lower=True, transpose_a=True)
+
+    in_half = front // half_blocks == leaf
+    candidate = lax.dynamic_slice_in_dim(row_solved, (front % half_blocks) * BLK, BLK, 0)
+    other = lax.ppermute(candidate, "leaf", [(0, 1), (1, 0)])
+    col_solved = jnp.where(in_half, candidate, other)
+
     schur = assembled - jnp.dot(row_solved, col_solved.T, precision=HIGHEST)
 
     row_global = leaf * rows + jnp.arange(rows, dtype=jnp.int32)

time: 299 us -> 278 us (0.930)
  other arithmetic: 142 us -> 133 us
  waiting for transfers between devices: 8.08 us -> 0.12 us
  matrix products: 45.8 us -> 52.9 us
  local copies, waits for them, and re-layouts: 32.3 us -> 26.8 us
    another operation x7, matrix products: 7.98 us -> 33.1 us  [per_device(): lax.linalg.triangular_solve(factor, panel, left_side=False, lower=True, t...]
    dot_general x2 -> x0, matrix products: 20.7 us -> none  [the longest x1 18 us: per_device(): row_solved = jnp.dot(panel, inverse.T, precision=HIGHEST)]
    dot_general x1, matrix products: 9.3 us -> 17.9 us  [per_device(): schur = assembled - jnp.dot(row_solved, col_solved.T, precision=HIGHEST)]
    ppermute x2, waiting for transfers between devices: 7.47 us -> 0.01 us  [per_device(): lax.ppermute(panel_rows[part * piece:(part + 1) * piece], ('leaf', 'front...]
    another operation x6, matrix products: 7.82 us -> 1.88 us  [per_device(): factor = jnp.linalg.cholesky(pivot)]
    another operation x13, local copies, waits for them, and re-layouts: 14.1 us -> 10 us
    another operation x3 -> x4, other arithmetic: 43.5 us -> 41.4 us  [per_device(): lax.linalg.triangular_solve(factor, panel, left_side=False, lower=True, t...]
  transfers between devices with their start and end apart: 5 -> 5, of which waited for: 3 -> 1; matrix products, arithmetic and copies ran while one was open for 60% -> 51% of each run, Pallas kernels for 15% -> 15%
where the time goes in v3:
time: 278 us; the launch traced here: 275 us
  other arithmetic  133 us (48%)
  matrix products  52.9 us (19%)
  Pallas kernels  42.2 us (15%)
  local copies, waits for them, and re-layouts  26.8 us (10%)
  between operations  16.6 us (6%)
  starting transfers between devices  3.51 us (1%)
    another operation x15, other arithmetic, per_device(): factor = jnp.linalg.cholesky(pivot)  79.5 us
    pallas_call x1, Pallas kernels, broadcast_pivot(): pl.pallas_call(functools.partial(pivot_kernel, n_front, n_src), out_shape...  42.2 us
    another operation x4, other arithmetic, per_device(): lax.linalg.triangular_solve(factor, panel, left_side=False, lower=True, t...  41.4 us
    another operation x7, matrix products, per_device(): lax.linalg.triangular_solve(factor, panel, left_side=False, lower=True, t...  33.1 us
    dot_general x1, matrix products, per_device(): schur = assembled - jnp.dot(row_solved, col_solved.T, precision=HIGHEST)  17.9 us
    another operation x12, local copies, waits for them, and re-layouts  10 us
    unnamed x27, local copies, waits for them, and re-layouts  5.79 us
  transfers between devices with their start and end apart: 5, of which 1 were waited for; matrix products, arithmetic and copies ran while one was open for 51% of the time, Pallas kernels for 15%

profile of v3, /device:TPU:1, one launch (start us, length us, event | category | flops | bytes accessed | tf_op | source)
XLA Modules:
  0.0 275.1 jit_solution(3583637970492289138)
XLA Ops:
  6.5 1.5 compare_reduce_fusion
  8.1 0.8 compare_reduce_fusion.3
  8.9 1.4 compare_reduce_fusion.2
  10.3 2.0 gather_fusion.1
  12.3 3.2 %select_select_fusion = f32[32,128,128]{2,1,0:T(8,128)} fusion(f32[32,128,128]{2,1,0:T(8,128)} %gather_fusion.1, pred[32]{0:T(512)(128)(4,1)S(1)} %compare_and_fusion, pred[32]{0:T(512)(128)(4,1)S(1)} %get-tuple-element.23), kind=kLoop, calls=%fused_computation.24 | loop fusion | flops 1048576 | bytes 4194368 | tf_op jit(solution)/shard_map/jit(_where)/select_n | solution.py:22
  15.5 1.4 collective-permute-start
  16.9 2.0 gather_fusion
  18.9 2.0 select_select_fusion.1
  21.1 1.9 fusion.15
  23.0 1.4 copy-done.8
  24.4 0.7 fusion.39
  25.3 1.3 collective-permute-start.2
  26.6 0.7 collective-permute-start.1
  27.3 42.2 %shard_map.37 = f32[64,32,128]{2,1,0:T(8,128)} custom-call(f32[512,128]{1,0:T(8,128)} %get-tuple-element.36.top_ref), custom_call_target="tpu_custom_call" | custom-call | tf_op jit(solution)/shard_map/pallas_call | solution.py:133
  69.5 1.9 copy.14
  71.5 0.8 copy.16
  73.0 11.7 %cholesky.104 = f32[128,128]{1,0:T(8,128)S(1)} custom-call(f32[128,128]{1,0:T(8,128)S(1)} %cholesky.266), custom_call_target="Cholesky" | custom-call | tf_op jit(solution)/shard_map/jit(cholesky)/cholesky | solution.py:189
  84.8 9.8 %custom-call.30 = f32[1,128,128]{1,2,0:T(8,128)S(1)} custom-call(f32[1,128,128]{2,1,0:T(8,128)S(1)} %get-tuple-element.49), custom_call_target="InvertDiagBlocksLowerTriangular" | custom-call | tf_op jit(solution)/shard_map/jit(cholesky)/cholesky | solution.py:189
  95.4 11.9 %cholesky.217 = f32[128,128]{1,0:T(8,128)S(1)} custom-call(f32[128,128]{1,0:T(8,128)S(1)} %cholesky.270), custom_call_target="Cholesky" | custom-call | tf_op jit(solution)/shard_map/jit(cholesky)/cholesky | solution.py:189
  107.3 9.8 %custom-call.31 = f32[1,128,128]{1,2,0:T(8,128)S(1)} custom-call(f32[1,128,128]{2,1,0:T(8,128)S(1)} %get-tuple-element.46), custom_call_target="InvertDiagBlocksLowerTriangular" | custom-call | tf_op jit(solution)/shard_map/jit(cholesky)/cholesky | solution.py:189
  117.8 11.7 %cholesky.238 = f32[128,128]{1,0:T(8,128)S(1)} custom-call(f32[128,128]{1,0:T(8,128)S(1)} %cholesky.275), custom_call_target="Cholesky" | custom-call | tf_op jit(solution)/shard_map/jit(cholesky)/cholesky | solution.py:189
  129.5 9.8 %custom-call.32 = f32[1,128,128]{1,2,0:T(8,128)S(1)} custom-call(f32[1,128,128]{2,1,0:T(8,128)S(1)} %get-tuple-element.43), custom_call_target="InvertDiagBlocksLowerTriangular" | custom-call | tf_op jit(solution)/shard_map/jit(cholesky)/cholesky | solution.py:189
  139.9 12.1 %cholesky.255 = f32[128,128]{1,0:T(8,128)S(1)} custom-call(f32[128,128]{1,0:T(8,128)S(1)} %convolution_subtract_fusion.5), custom_call_target="Cholesky" | custom-call | tf_op jit(solution)/shard_map/jit(cholesky)/cholesky | solution.py:189
  152.0 0.6 compare_reduce_fusion.7
  152.7 0.6 compare_reduce_fusion.6
  154.5 0.6 compare_reduce_fusion.5
  155.8 0.6 compare_reduce_fusion.4
  157.3 10.1 %while.1 = (s32[]{:T(128)}, f32[512,512]{1,0:T(8,128)S(1)}, s32[4,2]{0,1:T(2,128)S(1)}, f32[4,128,128]{2,1,0:T(8,128)}, s32[]{:T(128)}) while((s32[]{:T(128)}, f32[512,512]{1,0:T(8,128)S(1)}, s32[4,2]{0,1:T(2,128)S(1)}, f32[4,128,128]{2,1,0:T(8,128)}, s32[]{:T(128)}) %tuple.37), condition=%wide.while_cond, body=%wide.while_body.sunk | while | flops 2 | bytes 132205 | solution.py:190
  157.4 0.5 fusion.47
  157.9 1.9 bitcast_dynamic-update-slice_fusion.2
  160.5 1.9 bitcast_dynamic-update-slice_fusion.2
  163.0 1.9 bitcast_dynamic-update-slice_fusion.2
  165.5 1.9 bitcast_dynamic-update-slice_fusion.2
  167.4 40.1 %custom-call.33 = f32[4,128,128]{1,2,0:T(8,128)S(1)} custom-call(f32[4,128,128]{2,1,0:T(8,128)} %get-tuple-element.21), custom_call_target="InvertDiagBlocksLowerTriangular" | custom-call | tf_op jit(solution)/shard_map/triangular_solve | solution.py:190
  207.5 0.9 constant_dynamic-slice_fusion.3
  208.4 3.6 %fusion.12 = f32[4096,128]{0,1:T(8,128)S(1)} fusion(f32[4096,512]{1,0:T(8,128)} %all-gather.2.cloned.1.call-done, f32[4,128,128]{1,2,0:T(8,128)S(1)} %custom-call.33), kind=kOutput, calls=%fused_computation.18 | convolution fusion | flops 805306368 | bytes 4259840 | tf_op jit(solution)/shard_map/triangular_solve | solution.py:190
  212.0 5.9 %convolution_subtract_fusion.2 = f32[4096,128]{1,0:T(8,128)S(1)} fusion(f32[4096,128]{0,1:T(8,128)S(1)} %fusion.12, f32[4096,512]{1,0:T(8,128)} %all-gather.2.cloned.1.call-done, f32[512,512]{1,0:T(8,128)S(1)} %get-tuple-element.100), kind=kOutput, calls=%fused_computation.13 | convolution fusion | flops 805830656 | bytes 6356992 | tf_op jit(solution)/shard_map/triangular_solve | solution.py:190
  217.9 2.0 fusion.29
  220.0 7.2 %convolution_subtract_fusion.1 = f32[4096,128]{1,0:T(8,128)S(1)} fusion(f32[4096,128]{0,1:T(8,128)S(1)} %fusion.29, f32[4096,128]{0,1:T(8,128)S(1)} %fusion.12, f32[4096,512]{1,0:T(8,128)S(1)} %copy-done.6, f32[512,512]{1,0:T(8,128)S(1)} %get-tuple-element.100), kind=kOutput, calls=%fused_computation.12 | convolution fusion | flops 1612185600 | bytes 8519680 | tf_op jit(solution)/shard_map/triangular_solve | solution.py:190
  227.2 2.0 fusion.28
  229.2 10.3 %fusion.6 = f32[4096,128]{1,0:T(8,128)S(1)} fusion(f32[4096,128]{0,1:T(8,128)S(1)} %fusion.28, f32[4096,128]{0,1:T(8,128)S(1)} %fusion.29, f32[4096,128]{0,1:T(8,128)S(1)} %fusion.12, f32[4096,512]{1,0:T(8,128)S(1)} %copy-done.6, f32[512,512]{1,0:T(8,128)S(1)} %get-tuple-element.100), kind=kOutput, calls=%fused_computation.14 | convolution fusion | flops 2419589120 | bytes 10682368 | tf_op jit(solution)/shard_map/triangular_solve | solution.py:190
  239.5 2.0 fusion.27
  241.6 1.0 pad_maximum_fusion
  243.2 3.1 %copy-done.5 = f32[4096,512]{0,1:T(8,128)} copy-done((f32[4096,512]{0,1:T(8,128)}, f32[4096,512]{0,1:T(8,128)S(1)}, u32[]{:S(2)}) %copy-start.5) | copy-done | bytes 8388632
  246.6 1.8 copy.17
  248.4 0.7 copy-done.12
  249.1 1.0 fusion.26
  250.1 17.9 %select_select_fusion.2 = f32[4096,128]{1,0:T(8,128)} fusion(f32[512,128]{1,0:T(8,128)S(1)} %fusion.26, f32[4096,128]{1,0:T(8,128)} %copy.17, f32[512,128]{1,0:T(8,128)S(1)} %copy-done.10, pred[4096]{0:T(1024)(128)(4,1)S(1)} %add_compare_fusion, pred[128]{0:T(512)(128)(4,1)S(1)} %add_compare_fusion.1, f32[4096,128]{1,0:T(8,128)} %copy-done.8, ...), kind=kOutput, calls=%fused_computation.26 | convolution fusion | flops 3229679616 | bytes 15732865 | tf_op jit(solution)/shard_map/dot_general | solution.py:197
  (72 shorter events, 6.2 us)
Async XLA Ops:
  6.5 3.7 %copy-start = (f32[1,6144,128]{2,1,0:T(8,128)S(1)}, f32[1,6144,128]{2,1,0:T(8,128)}, u32[]{:S(2)}) copy-start(f32[1,6144,128]{2,1,0:T(8,128)} %param.6) | copy-start | bytes 9437188
  6.5 201.8 %all-gather.2.cloned.1.call-start = ((), (), s32[]{:S(2)}) async-start(), calls=%async_computation | async-start | bytes 8519680 | tf_op jit(solution)/shard_map/all_gather | solution.py:188
  15.5 5.6 %collective-permute-start = (f32[4096,128]{1,0:T(8,128)}, f32[4096,128]{1,0:T(8,128)}, u32[]{:S(2)}, u32[]{:S(2)}) collective-permute-start(f32[4096,128]{1,0:T(8,128)} %bitcast.3), channel_id=1, source_target_pairs={{0,64},{64,0},{1,65},{65,1},{2,66},{66,2},{3,67},{67,3},{4,68},{68... | collective-permute-start | bytes 6291464 | tf_op jit(solution)/shard_map/ppermute | solution.py:164
  18.9 2.2 copy-start.9
  23.0 1.4 copy-start.8
  25.3 46.2 %collective-permute-start.2 = (f32[64,512]{0,1:T(8,128)S(1)}, f32[64,512]{0,1:T(8,128)S(1)}, u32[]{:S(2)}, u32[]{:S(2)}) collective-permute-start(f32[64,512]{0,1:T(8,128)S(1)} %get-tuple-element.38), channel_id=1, source_target_pairs={{0,0},{1,2},{2,4},{3,6},{4,8},{5,10},{6,12},{7,14},{8,16},{9,18},{... | collective-permute-start | bytes 393224 | tf_op jit(solution)/shard_map/ppermute | solution.py:182
  26.6 44.9 %collective-permute-start.1 = (f32[64,512]{0,1:T(8,128)S(1)}, f32[64,512]{0,1:T(8,128)S(1)}, u32[]{:S(2)}, u32[]{:S(2)}) collective-permute-start(f32[64,512]{0,1:T(8,128)S(1)} %get-tuple-element.39), channel_id=1, source_target_pairs={{0,1},{1,3},{2,5},{3,7},{4,9},{5,11},{6,13},{7,15},{8,17},{9,19},{... | collective-permute-start | bytes 393224 | tf_op jit(solution)/shard_map/ppermute | solution.py:182
  212.0 29.6 %copy-start.2 = (f32[4096,128]{0,1:T(8,128)}, f32[4096,128]{0,1:T(8,128)S(1)}, u32[]{:S(2)}) copy-start(f32[4096,128]{0,1:T(8,128)S(1)} %fusion.12) | copy-start | bytes 6291460
  212.0 8.0 %copy-start.6 = (f32[4096,512]{1,0:T(8,128)S(1)}, f32[4096,512]{1,0:T(8,128)}, u32[]{:S(2)}) copy-start(f32[4096,512]{1,0:T(8,128)} %all-gather.2.cloned.1.call-done) | copy-start | bytes 25165828
  220.0 21.6 %copy-start.3 = (f32[4096,128]{0,1:T(8,128)}, f32[4096,128]{0,1:T(8,128)S(1)}, u32[]{:S(2)}) copy-start(f32[4096,128]{0,1:T(8,128)S(1)} %fusion.29) | copy-start | bytes 6291460
  229.2 12.4 %copy-start.4 = (f32[4096,128]{0,1:T(8,128)}, f32[4096,128]{0,1:T(8,128)S(1)}, u32[]{:S(2)}) copy-start(f32[4096,128]{0,1:T(8,128)S(1)} %fusion.28) | copy-start | bytes 6291460
  241.6 1.5 copy-start.7
  243.1 3.2 %copy-start.5 = (f32[4096,512]{0,1:T(8,128)}, f32[4096,512]{0,1:T(8,128)S(1)}, u32[]{:S(2)}) copy-start(f32[4096,512]{0,1:T(8,128)S(1)} %pad_maximum_fusion) | copy-start | bytes 25165828
  243.1 3.4 %copy-start.11 = (f32[128,512]{0,1:T(8,128)}, f32[128,512]{0,1:T(8,128)S(1)}, u32[]{:S(2)}) copy-start(f32[128,512]{0,1:T(8,128)S(1)} %constant_dynamic-slice_fusion.1) | copy-start | bytes 786436
  243.1 5.3 %collective-permute-start.3 = (f32[128,512]{0,1:T(8,128)S(1)}, f32[128,512]{0,1:T(8,128)S(1)}, u32[]{:S(2)}, u32[]{:S(2)}) collective-permute-start(f32[128,512]{0,1:T(8,128)S(1)} %constant_dynamic-slice_fusion.1), channel_id=1, source_target_pairs={{0,64},{64,0},{1,65},{65,1},{2,66},{66,2},{3,67},{67,3},{4,68},{68... | collective-permute-start | bytes 786440 | tf_op jit(solution)/shard_map/ppermute | solution.py:194
  246.6 3.5 %copy-start.10 = (f32[512,128]{1,0:T(8,128)S(1)}, f32[512,128]{1,0:T(8,128)}, u32[]{:S(2)}) copy-start(f32[512,128]{1,0:T(8,128)} %constant_dynamic-slice_fusion.3) | copy-start | bytes 786436
  248.4 0.7 copy-start.12
  250.1 17.9 %copy-start.1 = (f32[1,6144,128]{2,1,0:T(8,128)S(1)}, f32[1,6144,128]{2,1,0:T(8,128)}, u32[]{:S(2)}) copy-start(f32[1,6144,128]{2,1,0:T(8,128)} %param.6) | copy-start | bytes 9437188
Sparse Core Ops, SparseCore 0:
  72.4 78.1 all-gather.1

commit v4 on v3

--- a/solution.py
+++ b/solution.py
@@ -149,6 +149,75 @@
     return gathered.reshape(n_src, per_src, rows, cols).transpose(1, 2, 0, 3).reshape(S, S)
 
 
+def _mm(a, b):
+    return jnp.dot(a, b, precision=HIGHEST, preferred_element_type=jnp.float32)
+
+
+def _mm_t(a, b):
+    return lax.dot_general(a, b, (((1,), (1,)), ((), ())), precision=HIGHEST,
+                           preferred_element_type=jnp.float32)
+
+
+def chol_inv_kernel(a_ref, l_ref, linv_ref, w_ref, d_ref, lt_ref, x_ref):
+    n = a_ref.shape[0]
+    b = d_ref.shape[0]
+    nb = n // b
+    lane = lax.broadcasted_iota(jnp.int32, (1, b), 1)
+    sub = lax.broadcasted_iota(jnp.int32, (b, 1), 0)
+    eye = (lax.broadcasted_iota(jnp.int32, (b, b), 0) == lax.broadcasted_iota(jnp.int32, (b, b), 1)).astype(jnp.float32)
+    w_ref[...] = a_ref[...]
+    l_ref[...] = jnp.zeros_like(l_ref)
+    linv_ref[...] = jnp.zeros_like(linv_ref)
+
+    def step(k, carry):
+        row = d_ref[pl.ds(k, 1), :]
+        piv = jnp.sum(jnp.where(lane == k, row, 0.0), axis=1, keepdims=True)
+        root = jnp.sqrt(piv)
+        col = jnp.where(lane >= k, row / root, 0.0)
+        lt_ref[pl.ds(k, 1), :] = col
+        col_t = jnp.transpose(jnp.broadcast_to(col, (8, b)))[:, 0:1]
+        d_ref[...] = d_ref[...] - col_t * col
+        xk = x_ref[pl.ds(k, 1), :] / root
+        x_ref[pl.ds(k, 1), :] = xk
+        below = jnp.where(sub > k, col_t, 0.0)
+        x_ref[...] = x_ref[...] - below * xk
+        return carry
+
+    for j in range(nb):
+        jb = j * b
+        d_ref[...] = w_ref[jb:jb + b, jb:jb + b]
+        x_ref[...] = eye
+        lax.fori_loop(0, b, step, 0)
+        l_ref[jb:jb + b, jb:jb + b] = jnp.transpose(lt_ref[...])
+        linv_ref[jb:jb + b, jb:jb + b] = x_ref[...]
+        if j < nb - 1:
+            lp = _mm_t(w_ref[jb + b:, jb:jb + b], x_ref[...])
+            l_ref[jb + b:, jb:jb + b] = lp
+            w_ref[jb + b:, jb + b:] = w_ref[jb + b:, jb + b:] - _mm_t(lp, lp)
+    for j in range(nb):
+        for i in range(j + 1, nb):
+            acc = jnp.zeros((b, b), jnp.float32)
+            for k in range(j, i):
+                acc = acc + _mm(l_ref[i * b:(i + 1) * b, k * b:(k + 1) * b], linv_ref[k * b:(k + 1) * b, j * b:(j + 1) * b])
+            linv_ref[i * b:(i + 1) * b, j * b:(j + 1) * b] = -_mm(linv_ref[i * b:(i + 1) * b, i * b:(i + 1) * b], acc)
+
+
+def chol_inv(a, b=128):
+    n = a.shape[0]
+    return pl.pallas_call(
+        chol_inv_kernel,
+        out_shape=(jax.ShapeDtypeStruct((n, n), jnp.float32), jax.ShapeDtypeStruct((n, n), jnp.float32)),
+        in_specs=[pl.BlockSpec(memory_space=pltpu.VMEM)],
+        out_specs=(pl.BlockSpec(memory_space=pltpu.VMEM), pl.BlockSpec(memory_space=pltpu.VMEM)),
+        scratch_shapes=[
+            pltpu.VMEM((n, n), jnp.float32),
+            pltpu.VMEM((b, b), jnp.float32),
+            pltpu.VMEM((b, b), jnp.float32),
+            pltpu.VMEM((b, b), jnp.float32),
+        ],
+    )(a)
+
+
 def per_device(front_block, child_update, child_map):
     rows, cols = front_block.shape
     n_leaf = lax.axis_size("leaf")
@@ -186,8 +255,8 @@
     pivot = broadcast_pivot(top, n_front)
     my_piece, pivot = lax.optimization_barrier((my_piece, pivot))
     panel = lax.all_gather(my_piece, "front", tiled=True)
-    factor = jnp.linalg.cholesky(pivot)
-    row_solved = lax.linalg.triangular_solve(factor, panel, left_side=False, lower=True, transpose_a=True)
+    factor, inverse = chol_inv(pivot)
+    row_solved = lax.dot_general(panel, inverse, (((1,), (1,)), ((), ())), precision=HIGHEST)
 
     in_half = front // half_blocks == leaf
     candidate = lax.dynamic_slice_in_dim(row_solved, (front % half_blocks) * BLK, BLK, 0)

time: 278 us -> 277 us (level); the launches traced: 275 us -> 277 us
  Pallas kernels: 42.2 us -> 202 us
  other arithmetic: 133 us -> 12.8 us
  matrix products: 52.9 us -> 27.3 us
  local copies, waits for them, and re-layouts: 26.8 us -> 16.8 us
  between operations: 16.6 us -> 13.5 us
    pallas_call x0 -> x1, Pallas kernels: none -> 159 us  [chol_inv(): pl.pallas_call(chol_inv_kernel, out_shape=(jax.ShapeDtypeStruct((n, n), j...]
    another operation x19 -> x0, other arithmetic: 121 us -> none  [the longest x15 79.5 us: per_device(): factor = jnp.linalg.cholesky(pivot)]
    another operation x13 -> x0, matrix products: 35 us -> none  [the longest x7 33.1 us: per_device(): lax.linalg.triangular_solve(factor, panel, left_side=False, lower=True, t...]
    dot_general x0 -> x1, matrix products: none -> 16.3 us  [per_device(): lax.dot_general(panel, inverse, (((1,), (1,)), ((), ())), precision=HIGHEST)]
    another operation x17 -> x0, local copies, waits for them, and re-layouts: 10.2 us -> none
    dot_general x1, matrix products: 17.9 us -> 11.1 us  [per_device(): schur = assembled - jnp.dot(row_solved, col_solved.T, precision=HIGHEST)]
    unnamed x27 -> x10, local copies, waits for them, and re-layouts: 5.79 us -> 6.73 us
  transfers between devices with their start and end apart: 5 -> 5, of which waited for: 1 -> 2; matrix products, arithmetic and copies ran while one was open for 51% -> 3% of each run, Pallas kernels for 15% -> 73%
where the time goes in v4:
time: 277 us
  Pallas kernels  202 us (73%)
  matrix products  27.3 us (10%)
  local copies, waits for them, and re-layouts  16.8 us (6%)
  between operations  13.5 us (5%)
  other arithmetic  12.8 us (5%)
  starting transfers between devices  4.2 us (2%)
    pallas_call x1, Pallas kernels, chol_inv(): pl.pallas_call(chol_inv_kernel, out_shape=(jax.ShapeDtypeStruct((n, n), j...  159 us
    pallas_call x1, Pallas kernels, broadcast_pivot(): pl.pallas_call(functools.partial(pivot_kernel, n_front, n_src), out_shape...  42.3 us
    dot_general x1, matrix products, per_device(): lax.dot_general(panel, inverse, (((1,), (1,)), ((), ())), precision=HIGHEST)  16.3 us
    dot_general x1, matrix products, per_device(): schur = assembled - jnp.dot(row_solved, col_solved.T, precision=HIGHEST)  11.1 us
    unnamed x10, local copies, waits for them, and re-layouts  6.73 us
  transfers between devices with their start and end apart: 5, of which 2 were waited for; matrix products, arithmetic and copies ran while one was open for 3% of the time, Pallas kernels for 73%

profile of v4, /device:TPU:1, one launch (start us, length us, event | category | flops | bytes accessed | tf_op | source)
XLA Modules:
  0.0 276.9 jit_solution(13782415390464915939)
XLA Ops:
  6.5 0.0 copy-start
  6.5 0.0 all-gather.2.cloned.1.call-start
  6.5 1.5 compare_reduce_fusion
  8.1 0.8 compare_reduce_fusion.3
  8.9 1.4 compare_reduce_fusion.2
  10.3 0.0 copy-done
  10.3 2.0 gather_fusion.1
  12.3 3.2 %select_select_fusion = f32[32,128,128]{2,1,0:T(8,128)} fusion(f32[32,128,128]{2,1,0:T(8,128)} %gather_fusion.1, pred[32]{0:T(512)(128)(4,1)S(1)} %compare_and_fusion, pred[32]{0:T(512)(128)(4,1)S(1)} %get-tuple-element.19), kind=kLoop, calls=%fused_computation.7 | loop fusion | flops 1048576 | bytes 4194368 | tf_op jit(solution)/shard_map/jit(_where)/select_n | solution.py:22
  15.5 1.4 collective-permute-start
  16.9 2.0 gather_fusion
  18.9 0.0 copy-start.3
  18.9 2.0 select_select_fusion.1
  20.9 0.1 collective-permute-done
  21.0 0.1 copy-done.3
  21.1 1.9 fusion.1
  23.0 0.0 copy-start.2
  23.0 1.3 copy-done.2
  24.3 0.7 fusion.3
  25.1 0.8 fusion.4
  25.9 1.3 collective-permute-start.2
  27.1 1.4 collective-permute-start.1
  28.5 42.3 %shard_map.37 = f32[64,32,128]{2,1,0:T(8,128)} custom-call(f32[512,128]{1,0:T(8,128)} %get-tuple-element.20.top_ref), custom_call_target="tpu_custom_call" | custom-call | tf_op jit(solution)/shard_map/pallas_call | solution.py:133
  70.9 1.9 copy.9
  72.8 1.0 copy.15
  73.9 0.0 collective-permute-done.2
  73.9 0.0 collective-permute-done.1
  73.9 1.0 broadcast_select_fusion.1
  74.8 0.8 copy.10
  75.6 0.0 all-gather.2.cloned.1.call-update
  75.7 159.3 %shard_map.38 = (f32[512,512]{1,0:T(8,128)}, f32[512,512]{1,0:T(8,128)}) custom-call(f32[512,512]{1,0:T(8,128)} %bitcast.29), custom_call_target="tpu_custom_call" | custom-call | tf_op jit(solution)/shard_map/pallas_call | solution.py:207
  234.9 0.0 all-gather.2.cloned.1.call-done
  235.0 16.3 %fusion.5 = f32[4096,512]{1,0:T(8,128)S(1)} fusion(f32[4096,512]{1,0:T(8,128)} %all-gather.2.cloned.1.call-done, f32[512,512]{1,0:T(8,128)} %get-tuple-element.17), kind=kOutput, calls=%fused_computation.33 | convolution fusion | flops 12884901888 | bytes 17825792 | tf_op jit(solution)/shard_map/dot_general | solution.py:259
  251.2 0.0 copy-start.1
  251.2 3.2 %copy-done.1 = f32[4096,512]{1,0:T(8,128)} copy-done((f32[4096,512]{1,0:T(8,128)}, f32[4096,512]{1,0:T(8,128)S(1)}, u32[]{:S(2)}) %copy-start.1) | copy-done | bytes 8388632
  254.5 0.7 constant_dynamic-slice_fusion
  255.2 1.1 copy.12
  256.3 0.1 collective-permute-start.3
  256.4 1.2 constant_dynamic-slice_fusion.1
  257.6 0.4 collective-permute-done.3
  258.0 1.0 fusion.2
  259.0 11.1 %select_select_fusion.2 = f32[4096,128]{1,0:T(8,128)} fusion(f32[512,128]{1,0:T(8,128)S(1)} %fusion.2, f32[4096,512]{1,0:T(8,128)} %copy-done.1, s32[]{:T(128)S(6)} %select_n.89, f32[512,128]{1,0:T(8,128)S(1)} %constant_dynamic-slice_fusion.1, pred[4096]{0:T(1024)(128)(4,1)S(1)} %add_compare_fusion, pred[128]{0:T(512)(128)(4,1)S(1)} %add_compare_fusion.1, ...), kind=kOutput, calls=%fused_computation.9 | convolution fusion | flops 3223388160 | bytes 15732869 | tf_op jit(solution)/shard_map/dot_general | solution.py:266
  (9 shorter events, 0.1 us)
Async XLA Ops:
  6.5 3.7 %copy-start = (f32[1,6144,128]{2,1,0:T(8,128)S(1)}, f32[1,6144,128]{2,1,0:T(8,128)}, u32[]{:S(2)}) copy-start(f32[1,6144,128]{2,1,0:T(8,128)} %param.6) | copy-start | bytes 9437188
  6.5 228.4 %all-gather.2.cloned.1.call-start = ((), (), s32[]{:S(2)}) async-start(), calls=%async_computation | async-start | bytes 8519680 | tf_op jit(solution)/shard_map/all_gather | solution.py:257
  15.5 5.6 %collective-permute-start = (f32[4096,128]{1,0:T(8,128)}, f32[4096,128]{1,0:T(8,128)}, u32[]{:S(2)}, u32[]{:S(2)}) collective-permute-start(f32[4096,128]{1,0:T(8,128)} %bitcast.3), channel_id=1, source_target_pairs={{0,64},{64,0},{1,65},{65,1},{2,66},{66,2},{3,67},{67,3},{4,68},{68... | collective-permute-start | bytes 6291464 | tf_op jit(solution)/shard_map/ppermute | solution.py:233
  18.9 2.2 copy-start.3
  23.0 1.3 copy-start.2
  25.9 48.0 %collective-permute-start.2 = (f32[64,512]{0,1:T(8,128)}, f32[64,512]{0,1:T(8,128)}, u32[]{:S(2)}, u32[]{:S(2)}) collective-permute-start(f32[64,512]{0,1:T(8,128)} %get-tuple-element.22), channel_id=1, source_target_pairs={{0,0},{1,2},{2,4},{3,6},{4,8},{5,10},{6,12},{7,14},{8,16},{9,18},{... | collective-permute-start | bytes 393224 | tf_op jit(solution)/shard_map/ppermute | solution.py:251
  27.1 46.7 %collective-permute-start.1 = (f32[64,512]{0,1:T(8,128)S(1)}, f32[64,512]{0,1:T(8,128)}, u32[]{:S(2)}, u32[]{:S(2)}) collective-permute-start(f32[64,512]{0,1:T(8,128)S(1)} %get-tuple-element.23), channel_id=1, source_target_pairs={{0,1},{1,3},{2,5},{3,7},{4,9},{5,11},{6,13},{7,15},{8,17},{9,19},{... | collective-permute-start | bytes 393224 | tf_op jit(solution)/shard_map/ppermute | solution.py:251
  251.2 3.2 %copy-start.1 = (f32[4096,512]{1,0:T(8,128)}, f32[4096,512]{1,0:T(8,128)S(1)}, u32[]{:S(2)}) copy-start(f32[4096,512]{1,0:T(8,128)S(1)} %fusion.5) | copy-start | bytes 25165828
  256.3 1.7 collective-permute-start.3
Sparse Core Ops, SparseCore 0:
  75.8 78.0 all-gather.1

commit v5 on v4

--- a/solution.py
+++ b/solution.py
@@ -149,6 +149,9 @@
     return gathered.reshape(n_src, per_src, rows, cols).transpose(1, 2, 0, 3).reshape(S, S)
 
 
+PANEL = 8
+
+
 def _mm(a, b):
     return jnp.dot(a, b, precision=HIGHEST, preferred_element_type=jnp.float32)
 
@@ -158,37 +161,59 @@
                            preferred_element_type=jnp.float32)
 
 
-def chol_inv_kernel(a_ref, l_ref, linv_ref, w_ref, d_ref, lt_ref, x_ref):
+def _mm_tn(a, b):
+    return lax.dot_general(a, b, (((0,), (0,)), ((), ())), precision=HIGHEST,
+                           preferred_element_type=jnp.float32)
+
+
+def chol_inv_kernel(a_ref, l_ref, linv_ref, w_ref, d_ref, ut_ref, lo_ref, x_ref):
     n = a_ref.shape[0]
     b = d_ref.shape[0]
     nb = n // b
-    lane = lax.broadcasted_iota(jnp.int32, (1, b), 1)
-    sub = lax.broadcasted_iota(jnp.int32, (b, 1), 0)
-    eye = (lax.broadcasted_iota(jnp.int32, (b, b), 0) == lax.broadcasted_iota(jnp.int32, (b, b), 1)).astype(jnp.float32)
+    lane = lax.broadcasted_iota(jnp.int32, (PANEL, b), 1)
+    sub = lax.broadcasted_iota(jnp.int32, (PANEL, 1), 0)
     w_ref[...] = a_ref[...]
     l_ref[...] = jnp.zeros_like(l_ref)
     linv_ref[...] = jnp.zeros_like(linv_ref)
 
-    def step(k, carry):
-        row = d_ref[pl.ds(k, 1), :]
-        piv = jnp.sum(jnp.where(lane == k, row, 0.0), axis=1, keepdims=True)
-        root = jnp.sqrt(piv)
-        col = jnp.where(lane >= k, row / root, 0.0)
-        lt_ref[pl.ds(k, 1), :] = col
-        col_t = jnp.transpose(jnp.broadcast_to(col, (8, b)))[:, 0:1]
-        d_ref[...] = d_ref[...] - col_t * col
-        xk = x_ref[pl.ds(k, 1), :] / root
-        x_ref[pl.ds(k, 1), :] = xk
-        below = jnp.where(sub > k, col_t, 0.0)
-        x_ref[...] = x_ref[...] - below * xk
+    def factor_panel(p, carry):
+        k = pl.multiple_of(p * PANEL, PANEL)
+        r = d_ref[pl.ds(k, PANEL), :]
+        for t in range(PANEL):
+            c = k + t
+            colv = jnp.sum(jnp.where(lane == c, r, 0.0), axis=1, keepdims=True)
+            piv = jnp.sum(jnp.where(sub == t, colv, 0.0), axis=0, keepdims=True)
+            root = jnp.sqrt(piv)
+            urow = jnp.where(lane[t:t + 1] >= c, r[t:t + 1] / root, 0.0)
+            f = jnp.where(sub > t, colv / root, 0.0)
+            r = jnp.where(sub == t, urow, r - f * urow)
+        ut_ref[pl.ds(k, PANEL), :] = r
+        d_ref[...] = d_ref[...] - _mm_tn(r, r)
+        return carry
+
+    def invert_panel(p, carry):
+        k = pl.multiple_of(p * PANEL, PANEL)
+        lrows = lo_ref[pl.ds(k, PANEL), :]
+        e = (lane == sub + k).astype(jnp.float32) - _mm(lrows, x_ref[...])
+        for t in range(PANEL):
+            c = k + t
+            colv = jnp.sum(jnp.where(lane == c, lrows, 0.0), axis=1, keepdims=True)
+            diag = jnp.sum(jnp.where(sub == t, colv, 0.0), axis=0, keepdims=True)
+            xrow = e[t:t + 1] / diag
+            f = jnp.where(sub > t, colv, 0.0)
+            e = jnp.where(sub == t, xrow, e - f * xrow)
+        x_ref[pl.ds(k, PANEL), :] = e
         return carry
 
     for j in range(nb):
         jb = j * b
         d_ref[...] = w_ref[jb:jb + b, jb:jb + b]
-        x_ref[...] = eye
-        lax.fori_loop(0, b, step, 0)
-        l_ref[jb:jb + b, jb:jb + b] = jnp.transpose(lt_ref[...])
+        ut_ref[...] = jnp.zeros_like(ut_ref)
+        x_ref[...] = jnp.zeros_like(x_ref)
+        lax.fori_loop(0, b // PANEL, factor_panel, 0)
+        lo_ref[...] = jnp.transpose(ut_ref[...])
+        lax.fori_loop(0, b // PANEL, invert_panel, 0)
+        l_ref[jb:jb + b, jb:jb + b] = lo_ref[...]
         linv_ref[jb:jb + b, jb:jb + b] = x_ref[...]
         if j < nb - 1:
             lp = _mm_t(w_ref[jb + b:, jb:jb + b], x_ref[...])
@@ -211,6 +236,7 @@
         out_specs=(pl.BlockSpec(memory_space=pltpu.VMEM), pl.BlockSpec(memory_space=pltpu.VMEM)),
         scratch_shapes=[
             pltpu.VMEM((n, n), jnp.float32),
+            pltpu.VMEM((b, b), jnp.float32),
             pltpu.VMEM((b, b), jnp.float32),
             pltpu.VMEM((b, b), jnp.float32),
             pltpu.VMEM((b, b), jnp.float32),

time: 277 us -> 208 us (0.75)
  Pallas kernels: 202 us -> 133 us
    pallas_call x1, Pallas kernels: 159 us -> 90.3 us  [chol_inv(): pl.pallas_call(chol_inv_kernel, out_shape=(jax.ShapeDtypeStruct((n, n), j...]
  transfers between devices with their start and end apart: 5 -> 5, of which waited for: 2 -> 2; matrix products, arithmetic and copies ran while one was open for 3% -> 4% of each run, Pallas kernels for 73% -> 64%
where the time goes in v5:
time: 208 us
  Pallas kernels  133 us (64%)
  matrix products  27.4 us (13%)
  local copies, waits for them, and re-layouts  16.8 us (8%)
  between operations  13.5 us (6%)
  other arithmetic  12.8 us (6%)
  starting transfers between devices  4.2 us (2%)
    pallas_call x1, Pallas kernels, chol_inv(): pl.pallas_call(chol_inv_kernel, out_shape=(jax.ShapeDtypeStruct((n, n), j...  90.3 us
    pallas_call x1, Pallas kernels, broadcast_pivot(): pl.pallas_call(functools.partial(pivot_kernel, n_front, n_src), out_shape...  42.3 us
    dot_general x1, matrix products, per_device(): lax.dot_general(panel, inverse, (((1,), (1,)), ((), ())), precision=HIGHEST)  16.3 us
    dot_general x1, matrix products, per_device(): schur = assembled - jnp.dot(row_solved, col_solved.T, precision=HIGHEST)  11.1 us
    unnamed x10, local copies, waits for them, and re-layouts  6.73 us
    select_n x2, other arithmetic, gather_half(): picked = jnp.where(found[:, None, None], picked, jnp.zeros_like(picked))  5.24 us
  transfers between devices with their start and end apart: 5, of which 2 were waited for; matrix products, arithmetic and copies ran while one was open for 4% of the time, Pallas kernels for 64%

profile of v5, /device:TPU:1, one launch (start us, length us, event | category | flops | bytes accessed | tf_op | source)
XLA Modules:
  0.0 207.9 jit_solution(13196503958123883419)
XLA Ops:
  6.5 0.0 copy-start
  6.5 0.0 all-gather.2.cloned.1.call-start
  6.5 1.5 compare_reduce_fusion
  8.1 0.8 compare_reduce_fusion.3
  8.9 1.4 compare_reduce_fusion.2
  10.3 0.0 copy-done
  10.3 2.0 gather_fusion.1
  12.3 3.2 %select_select_fusion = f32[32,128,128]{2,1,0:T(8,128)} fusion(f32[32,128,128]{2,1,0:T(8,128)} %gather_fusion.1, pred[32]{0:T(512)(128)(4,1)S(1)} %compare_and_fusion, pred[32]{0:T(512)(128)(4,1)S(1)} %get-tuple-element.19), kind=kLoop, calls=%fused_computation.7 | loop fusion | flops 1048576 | bytes 4194368 | tf_op jit(solution)/shard_map/jit(_where)/select_n | solution.py:22
  15.5 1.4 collective-permute-start
  16.9 2.0 gather_fusion
  18.9 0.0 copy-start.3
  18.9 2.0 select_select_fusion.1
  20.9 0.1 collective-permute-done
  21.0 0.1 copy-done.3
  21.1 1.9 fusion.1
  23.0 0.0 copy-start.2
  23.0 1.3 copy-done.2
  24.3 0.7 fusion.3
  25.1 0.8 fusion.4
  25.9 1.3 collective-permute-start.2
  27.1 1.4 collective-permute-start.1
  28.5 42.3 %shard_map.37 = f32[64,32,128]{2,1,0:T(8,128)} custom-call(f32[512,128]{1,0:T(8,128)} %get-tuple-element.20.top_ref), custom_call_target="tpu_custom_call" | custom-call | tf_op jit(solution)/shard_map/pallas_call | solution.py:133
  70.9 1.9 copy.9
  72.8 1.0 copy.15
  73.9 0.0 collective-permute-done.2
  73.9 0.0 collective-permute-done.1
  73.9 1.0 broadcast_select_fusion.1
  74.8 0.8 copy.10
  75.6 0.0 all-gather.2.cloned.1.call-update
  75.7 90.3 %shard_map.38 = (f32[512,512]{1,0:T(8,128)}, f32[512,512]{1,0:T(8,128)}) custom-call(f32[512,512]{1,0:T(8,128)} %bitcast.29), custom_call_target="tpu_custom_call" | custom-call | tf_op jit(solution)/shard_map/pallas_call | solution.py:232
  165.9 0.0 all-gather.2.cloned.1.call-done
  165.9 16.3 %fusion.5 = f32[4096,512]{1,0:T(8,128)S(1)} fusion(f32[4096,512]{1,0:T(8,128)} %all-gather.2.cloned.1.call-done, f32[512,512]{1,0:T(8,128)} %get-tuple-element.17), kind=kOutput, calls=%fused_computation.33 | convolution fusion | flops 12884901888 | bytes 17825792 | tf_op jit(solution)/shard_map/dot_general | solution.py:285
  182.2 0.0 copy-start.1
  182.2 3.2 %copy-done.1 = f32[4096,512]{1,0:T(8,128)} copy-done((f32[4096,512]{1,0:T(8,128)}, f32[4096,512]{1,0:T(8,128)S(1)}, u32[]{:S(2)}) %copy-start.1) | copy-done | bytes 8388632
  185.4 0.7 constant_dynamic-slice_fusion
  186.1 1.1 copy.12
  187.2 0.1 collective-permute-start.3
  187.4 1.2 constant_dynamic-slice_fusion.1
  188.5 0.4 collective-permute-done.3
  189.0 1.0 fusion.2
  189.9 11.1 %select_select_fusion.2 = f32[4096,128]{1,0:T(8,128)} fusion(f32[512,128]{1,0:T(8,128)S(1)} %fusion.2, f32[4096,512]{1,0:T(8,128)} %copy-done.1, s32[]{:T(128)S(6)} %select_n.89, f32[512,128]{1,0:T(8,128)S(1)} %constant_dynamic-slice_fusion.1, pred[4096]{0:T(1024)(128)(4,1)S(1)} %add_compare_fusion, pred[128]{0:T(512)(128)(4,1)S(1)} %add_compare_fusion.1, ...), kind=kOutput, calls=%fused_computation.9 | convolution fusion | flops 3223388160 | bytes 15732869 | tf_op jit(solution)/shard_map/dot_general | solution.py:292
  (9 shorter events, 0.1 us)
Async XLA Ops:
  6.5 3.7 %copy-start = (f32[1,6144,128]{2,1,0:T(8,128)S(1)}, f32[1,6144,128]{2,1,0:T(8,128)}, u32[]{:S(2)}) copy-start(f32[1,6144,128]{2,1,0:T(8,128)} %param.6) | copy-start | bytes 9437188
  6.5 159.4 %all-gather.2.cloned.1.call-start = ((), (), s32[]{:S(2)}) async-start(), calls=%async_computation | async-start | bytes 8519680 | tf_op jit(solution)/shard_map/all_gather | solution.py:283
  15.5 5.6 %collective-permute-start = (f32[4096,128]{1,0:T(8,128)}, f32[4096,128]{1,0:T(8,128)}, u32[]{:S(2)}, u32[]{:S(2)}) collective-permute-start(f32[4096,128]{1,0:T(8,128)} %bitcast.3), channel_id=1, source_target_pairs={{0,64},{64,0},{1,65},{65,1},{2,66},{66,2},{3,67},{67,3},{4,68},{68... | collective-permute-start | bytes 6291464 | tf_op jit(solution)/shard_map/ppermute | solution.py:259
  18.9 2.2 %copy-start.3 = (f32[4096,128]{1,0:T(8,128)S(1)}, f32[4096,128]{1,0:T(8,128)}, u32[]{:S(2)}) copy-start(f32[4096,128]{1,0:T(8,128)} %param.5) | copy-start | bytes 6291460
  23.0 1.3 copy-start.2
  25.9 48.0 %collective-permute-start.2 = (f32[64,512]{0,1:T(8,128)}, f32[64,512]{0,1:T(8,128)}, u32[]{:S(2)}, u32[]{:S(2)}) collective-permute-start(f32[64,512]{0,1:T(8,128)} %get-tuple-element.22), channel_id=1, source_target_pairs={{0,0},{1,2},{2,4},{3,6},{4,8},{5,10},{6,12},{7,14},{8,16},{9,18},{... | collective-permute-start | bytes 393224 | tf_op jit(solution)/shard_map/ppermute | solution.py:277
  27.1 46.7 %collective-permute-start.1 = (f32[64,512]{0,1:T(8,128)S(1)}, f32[64,512]{0,1:T(8,128)}, u32[]{:S(2)}, u32[]{:S(2)}) collective-permute-start(f32[64,512]{0,1:T(8,128)S(1)} %get-tuple-element.23), channel_id=1, source_target_pairs={{0,1},{1,3},{2,5},{3,7},{4,9},{5,11},{6,13},{7,15},{8,17},{9,19},{... | collective-permute-start | bytes 393224 | tf_op jit(solution)/shard_map/ppermute | solution.py:277
  182.2 3.2 %copy-start.1 = (f32[4096,512]{1,0:T(8,128)}, f32[4096,512]{1,0:T(8,128)S(1)}, u32[]{:S(2)}) copy-start(f32[4096,512]{1,0:T(8,128)S(1)} %fusion.5) | copy-start | bytes 25165828
  187.2 1.7 collective-permute-start.3
Sparse Core Ops, SparseCore 0:
  75.8 81.8 all-gather.1

commit v6 on v5

--- a/solution.py
+++ b/solution.py
@@ -282,24 +282,27 @@
     my_piece, pivot = lax.optimization_barrier((my_piece, pivot))
     panel = lax.all_gather(my_piece, "front", tiled=True)
     factor, inverse = chol_inv(pivot)
-    row_solved = lax.dot_general(panel, inverse, (((1,), (1,)), ((), ())), precision=HIGHEST)
-
-    in_half = front // half_blocks == leaf
-    candidate = lax.dynamic_slice_in_dim(row_solved, (front % half_blocks) * BLK, BLK, 0)
-    other = lax.ppermute(candidate, "leaf", [(0, 1), (1, 0)])
-    col_solved = jnp.where(in_half, candidate, other)
-
-    schur = assembled - jnp.dot(row_solved, col_solved.T, precision=HIGHEST)
-
-    row_global = leaf * rows + jnp.arange(rows, dtype=jnp.int32)
-    col_global = front * cols + jnp.arange(cols, dtype=jnp.int32)
-    col_start = jnp.minimum(front * cols, S - cols)
-    left_rows = lax.dynamic_slice_in_dim(row_solved, col_start, cols, 1)
-    left_top = jnp.pad(lax.dynamic_slice_in_dim(factor, col_start, cols, 1), ((0, rows - S), (0, 0)))
-    left_part = jnp.where(row_global[:, None] < S, left_top, left_rows)
-    right_top = jnp.pad(col_solved.T, ((0, rows - S), (0, 0)))
-    right_part = jnp.where(row_global[:, None] < S, right_top, schur)
-    return jnp.where(col_global[None, :] < S, left_part, right_part)
+
+    own_solved = lax.dot_general(panel_rows, inverse, (((1,), (1,)), ((), ())), precision=HIGHEST)
+    from_leaf0 = lax.ppermute(own_solved, "leaf", [(0, 1)])
+    col_solved = jnp.where(leaf == 0, own_solved, from_leaf0)
+
+    piv_cols = S // cols
+    col_at = jnp.minimum(front, piv_cols - 1) * cols
+
+    def pivot_columns():
+        inv_rows = lax.dynamic_slice_in_dim(inverse, col_at, cols, 0)
+        out = lax.dot_general(panel, inv_rows, (((1,), (1,)), ((), ())), precision=HIGHEST)
+        top_rows = jnp.where(leaf == 0, lax.dynamic_slice_in_dim(factor, col_at, cols, 1), out[:S])
+        return lax.dynamic_update_slice_in_dim(out, top_rows, 0, 0)
+
+    def other_columns():
+        weights = jnp.dot(col_solved, inverse, precision=HIGHEST).T
+        out = assembled - jnp.dot(panel, weights, precision=HIGHEST)
+        top_rows = jnp.where(leaf == 0, col_solved.T, out[:S])
+        return lax.dynamic_update_slice_in_dim(out, top_rows, 0, 0)
+
+    return lax.cond(front < piv_cols, pivot_columns, other_columns)
 
 
 def solution(mesh):

time: 208 us -> 201 us (0.966)
  matrix products: 27.4 us -> 15.8 us
    dot_general x2, matrix products: 27.4 us -> 15.8 us  [the longest x1 13.3 us: pivot_columns(): lax.dot_general(panel, inv_rows, (((1,), (1,)), ((), ())), precision=HIGH...]
    unnamed x10 -> x9, local copies, waits for them, and re-layouts: 6.73 us -> 2.6 us
    cond x0 -> x1, local copies, waits for them, and re-layouts: none -> 2.88 us
    another operation x0 -> x1, local copies, waits for them, and re-layouts: none -> 2.53 us
  transfers between devices with their start and end apart: 5 -> 5, of which waited for: 2 -> 1; matrix products, arithmetic and copies ran while one was open for 4% -> 5% of each run, Pallas kernels for 64% -> 67%
where the time goes in v6:
time: 201 us; the launch traced here: 199 us
  Pallas kernels  133 us (66%)
  local copies, waits for them, and re-layouts  16.2 us (8%)
  matrix products  15.8 us (8%)
  between operations  13.5 us (7%)
  other arithmetic  13 us (6%)
  starting transfers between devices  5.38 us (3%)
  waiting for transfers between devices  2.27 us (1%)
    pallas_call x1, Pallas kernels, chol_inv(): pl.pallas_call(chol_inv_kernel, out_shape=(jax.ShapeDtypeStruct((n, n), j...  90.3 us
    pallas_call x1, Pallas kernels, broadcast_pivot(): pl.pallas_call(functools.partial(pivot_kernel, n_front, n_src), out_shape...  42.3 us
    dot_general x1, matrix products, pivot_columns(): lax.dot_general(panel, inv_rows, (((1,), (1,)), ((), ())), precision=HIGH...  13.3 us
    select_n x2, other arithmetic, gather_half(): picked = jnp.where(found[:, None, None], picked, jnp.zeros_like(picked))  5.25 us
  transfers between devices with their start and end apart: 5, of which 1 were waited for; matrix products, arithmetic and copies ran while one was open for 5% of the time, Pallas kernels for 67%

profile of v6, /device:TPU:1, one launch (start us, length us, event | category | flops | bytes accessed | tf_op | source)
XLA Modules:
  0.0 198.8 jit_solution(7185740936151647257)
XLA Ops:
  6.5 0.0 copy-start
  6.5 0.0 all-gather.2.cloned.1.call-start
  6.5 1.5 compare_reduce_fusion
  8.1 0.8 compare_reduce_fusion.3
  8.9 0.0 copy-done
  8.9 2.0 %gather_fusion.1 = f32[32,128,128]{2,1,0:T(8,128)} fusion(f32[48,128,128]{2,1,0:T(8,128)S(1)} %bitcast.35, s32[1024]{0:T(1024)S(1)} %pad_clamp_fusion), kind=kCustom, calls=%fused_computation.1.clone | custom fusion | bytes 4194432 | tf_op jit(solution)/shard_map/jit(_take)/gather | solution.py:21
  10.9 0.0 copy-start.3
  10.9 3.2 %select_select_fusion = f32[32,128,128]{2,1,0:T(8,128)} fusion(f32[32,128,128]{2,1,0:T(8,128)} %gather_fusion.1, pred[32]{0:T(512)(128)(4,1)S(1)} %compare_and_fusion, pred[32]{0:T(512)(128)(4,1)S(1)} %get-tuple-element.112), kind=kLoop, calls=%fused_computation.17 | loop fusion | flops 1048576 | bytes 4194368 | tf_op jit(solution)/shard_map/jit(_where)/select_n | solution.py:22
  14.1 1.4 collective-permute-start
  15.6 0.0 copy-done.3
  15.6 0.7 compare_reduce_fusion.2
  16.3 2.0 gather_fusion
  18.3 0.0 copy-start.2
  18.3 2.0 %select_select_fusion.1 = f32[32,128,128]{2,1,0:T(8,128)S(1)} fusion(f32[32,128,128]{2,1,0:T(8,128)} %gather_fusion, pred[32]{0:T(512)(128)(4,1)S(1)} %compare_and_fusion.1, pred[32]{0:T(512)(128)(4,1)S(1)} %get-tuple-element.111), kind=kLoop, calls=%fused_computation.18 | loop fusion | flops 1048576 | bytes 4194368 | tf_op jit(solution)/shard_map/jit(_where)/select_n | solution.py:22
  20.3 0.0 collective-permute-done
  20.3 0.2 copy-done.2
  20.5 1.9 fusion.7
  22.4 0.0 copy-start.1
  22.4 1.4 copy-done.1
  23.8 0.7 fusion.10
  24.5 0.8 fusion.11
  25.3 1.3 collective-permute-start.2
  26.6 1.4 collective-permute-start.1
  28.0 42.3 %shard_map.39 = f32[64,32,128]{2,1,0:T(8,128)} custom-call(f32[512,128]{1,0:T(8,128)} %get-tuple-element.113.top_ref), custom_call_target="tpu_custom_call" | custom-call | tf_op jit(solution)/shard_map/pallas_call | solution.py:133
  70.3 1.9 copy.17
  72.2 1.0 copy.26
  73.3 0.0 collective-permute-done.2
  73.3 0.0 collective-permute-done.1
  73.3 1.0 broadcast_select_fusion.2
  74.3 0.8 copy.18
  75.0 0.0 all-gather.2.cloned.1.call-update
  75.1 90.3 %shard_map.40 = (f32[512,512]{1,0:T(8,128)}, f32[512,512]{1,0:T(8,128)}) custom-call(f32[512,512]{1,0:T(8,128)} %bitcast.37), custom_call_target="tpu_custom_call" | custom-call | tf_op jit(solution)/shard_map/pallas_call | solution.py:232
  165.3 2.6 %fusion.8 = f32[128,512]{1,0:T(8,128)S(1)} fusion(f32[512,512]{1,0:T(8,128)} %get-tuple-element.70, f32[4096,128]{1,0:T(8,128)} %copy-done.1), kind=kOutput, calls=%fused_computation.33 | convolution fusion | flops 402653184 | bytes 1572864 | tf_op jit(solution)/shard_map/dot_general | solution.py:286
  167.9 1.3 collective-permute-start.3
  169.2 0.0 all-gather.2.cloned.1.call-done
  169.2 2.2 %collective-permute-done.3 = f32[128,512]{1,0:T(8,128)} collective-permute-done((f32[128,512]{1,0:T(8,128)S(1)}, f32[128,512]{1,0:T(8,128)}, u32[]{:S(2)}, u32[]{:S(2)}) %collective-permute-start.3) | collective-permute-done | bytes 262176 | tf_op jit(solution)/shard_map/ppermute | solution.py:287
  171.4 20.5 %conditional.1 = (f32[4096,128]{1,0:T(8,128)}) conditional(s32[]{:T(128)} %convert_element_type.3, (pred[]{:T(512)}, f32[128,512]{1,0:T(8,128)S(1)}, f32[128,512]{1,0:T(8,128)}, f32[512,512]{1,0:T(8,128)}, f32[4096,512]{1,0:T(8,128)}, /*index=5*/f32[4096,128]{1,0:T(8,128)}, s32[]{:T(128)}) %tuple.42, (s32[]{:T(128)}, f32[512,512]{1,0:T(8,128)}, ...), branch_computations={%region_4.6_spmd, %region_5.7_spmd} | conditional | flops 3624599552 | bytes 24117776 | solution.py:305
  171.4 2.5 %copy.20 = f32[512,512]{0,1:T(8,128)} copy(f32[512,512]{1,0:T(8,128)} %get-tuple-element.109) | data formatting | bytes 2097152 | tf_op jit(solution)/shard_map
  174.0 13.3 %convolution_bitcast_fusion.1 = f32[4096,128]{0,1:T(8,128)} fusion(f32[4096,512]{1,0:T(8,128)} %get-tuple-element.58, f32[512,512]{1,0:T(8,128)} %get-tuple-element.56, s32[]{:T(128)S(6)} %select_n.67), kind=kOutput, calls=%fused_computation.8 | convolution fusion | flops 3221225472 | bytes 10747908 | tf_op jit(solution)/shard_map/cond/branch_1_fun/dot_general | solution.py:295
  187.3 1.8 fusion.3
  189.1 2.9 %copy.23 = f32[4096,128]{1,0:T(8,128)} copy(f32[4096,128]{0,1:T(8,128)} %fusion.3) | data formatting | bytes 4194304 | tf_op jit(solution)/shard_map/cond
  (7 shorter events, 0.0 us)
Async XLA Ops:
  6.5 2.4 %copy-start = (f32[1,6144,128]{2,1,0:T(8,128)S(1)}, f32[1,6144,128]{2,1,0:T(8,128)}, u32[]{:S(2)}) copy-start(f32[1,6144,128]{2,1,0:T(8,128)} %param.8) | copy-start | bytes 9437188
  6.5 162.7 %all-gather.2.cloned.1.call-start = ((), (), s32[]{:S(2)}) async-start(), calls=%async_computation | async-start | bytes 8519680 | tf_op jit(solution)/shard_map/all_gather | solution.py:283
  10.9 4.6 %copy-start.3 = (s32[1,48]{1,0:T(1,128)S(1)}, s32[1,48]{1,0:T(1,128)}, u32[]{:S(2)}) copy-start(s32[1,48]{1,0:T(1,128)} %param.9) | copy-start | bytes 580
  14.1 6.2 %collective-permute-start = (f32[4096,128]{1,0:T(8,128)}, f32[4096,128]{1,0:T(8,128)}, u32[]{:S(2)}, u32[]{:S(2)}) collective-permute-start(f32[4096,128]{1,0:T(8,128)} %bitcast.6), channel_id=1, source_target_pairs={{0,64},{64,0},{1,65},{65,1},{2,66},{66,2},{3,67},{67,3},{4,68},{68... | collective-permute-start | bytes 6291464 | tf_op jit(solution)/shard_map/ppermute | solution.py:259
  18.3 2.2 %copy-start.2 = (f32[4096,128]{1,0:T(8,128)S(1)}, f32[4096,128]{1,0:T(8,128)}, u32[]{:S(2)}) copy-start(f32[4096,128]{1,0:T(8,128)} %param.7) | copy-start | bytes 6291460
  22.4 1.4 copy-start.1
  25.3 48.0 %collective-permute-start.2 = (f32[64,512]{0,1:T(8,128)}, f32[64,512]{0,1:T(8,128)}, u32[]{:S(2)}, u32[]{:S(2)}) collective-permute-start(f32[64,512]{0,1:T(8,128)} %get-tuple-element.115), channel_id=1, source_target_pairs={{0,0},{1,2},{2,4},{3,6},{4,8},{5,10},{6,12},{7,14},{8,16},{9,18},{... | collective-permute-start | bytes 393224 | tf_op jit(solution)/shard_map/ppermute | solution.py:277
  26.6 46.7 %collective-permute-start.1 = (f32[64,512]{0,1:T(8,128)S(1)}, f32[64,512]{0,1:T(8,128)}, u32[]{:S(2)}, u32[]{:S(2)}) collective-permute-start(f32[64,512]{0,1:T(8,128)S(1)} %get-tuple-element.116), channel_id=1, source_target_pairs={{0,1},{1,3},{2,5},{3,7},{4,9},{5,11},{6,13},{7,15},{8,17},{9,19},{... | collective-permute-start | bytes 393224 | tf_op jit(solution)/shard_map/ppermute | solution.py:277
  167.9 3.6 %collective-permute-start.3 = (f32[128,512]{1,0:T(8,128)S(1)}, f32[128,512]{1,0:T(8,128)}, u32[]{:S(2)}, u32[]{:S(2)}) collective-permute-start(f32[128,512]{1,0:T(8,128)S(1)} %fusion.8), channel_id=1, source_target_pairs={{0,64},{1,65},{2,66},{3,67},{4,68},{5,69},{6,70},{7,71},{8,72},{9,... | collective-permute-start | bytes 786440 | tf_op jit(solution)/shard_map/ppermute | solution.py:287
Sparse Core Ops, SparseCore 0:
  75.2 81.9 all-gather.1

commit v7 on v6

--- a/solution.py
+++ b/solution.py
@@ -161,24 +161,21 @@
                            preferred_element_type=jnp.float32)
 
 
-def _mm_tn(a, b):
-    return lax.dot_general(a, b, (((0,), (0,)), ((), ())), precision=HIGHEST,
-                           preferred_element_type=jnp.float32)
-
-
-def chol_inv_kernel(a_ref, l_ref, linv_ref, w_ref, d_ref, ut_ref, lo_ref, x_ref):
+def chol_inv_kernel(a_ref, l_ref, linv_ref, w_ref, d_ref, e_ref, ut_ref, x_ref):
     n = a_ref.shape[0]
     b = d_ref.shape[0]
     nb = n // b
     lane = lax.broadcasted_iota(jnp.int32, (PANEL, b), 1)
     sub = lax.broadcasted_iota(jnp.int32, (PANEL, 1), 0)
+    eye = (lax.broadcasted_iota(jnp.int32, (b, b), 0) == lax.broadcasted_iota(jnp.int32, (b, b), 1)).astype(jnp.float32)
     w_ref[...] = a_ref[...]
     l_ref[...] = jnp.zeros_like(l_ref)
     linv_ref[...] = jnp.zeros_like(linv_ref)
 
-    def factor_panel(p, carry):
+    def panel(p, carry):
         k = pl.multiple_of(p * PANEL, PANEL)
         r = d_ref[pl.ds(k, PANEL), :]
+        e = e_ref[pl.ds(k, PANEL), :]
         for t in range(PANEL):
             c = k + t
             colv = jnp.sum(jnp.where(lane == c, r, 0.0), axis=1, keepdims=True)
@@ -187,33 +184,27 @@
             urow = jnp.where(lane[t:t + 1] >= c, r[t:t + 1] / root, 0.0)
             f = jnp.where(sub > t, colv / root, 0.0)
             r = jnp.where(sub == t, urow, r - f * urow)
+            xrow = e[t:t + 1] / root
+            e = jnp.where(sub == t, xrow, e - f * xrow)
         ut_ref[pl.ds(k, PANEL), :] = r
-        d_ref[...] = d_ref[...] - _mm_tn(r, r)
-        return carry
-
-    def invert_panel(p, carry):
-        k = pl.multiple_of(p * PANEL, PANEL)
-        lrows = lo_ref[pl.ds(k, PANEL), :]
-        e = (lane == sub + k).astype(jnp.float32) - _mm(lrows, x_ref[...])
+        x_ref[pl.ds(k, PANEL), :] = e
+        rt = jnp.transpose(r)
+        dd = d_ref[...]
+        ee = e_ref[...]
         for t in range(PANEL):
-            c = k + t
-            colv = jnp.sum(jnp.where(lane == c, lrows, 0.0), axis=1, keepdims=True)
-            diag = jnp.sum(jnp.where(sub == t, colv, 0.0), axis=0, keepdims=True)
-            xrow = e[t:t + 1] / diag
-            f = jnp.where(sub > t, colv, 0.0)
-            e = jnp.where(sub == t, xrow, e - f * xrow)
-        x_ref[pl.ds(k, PANEL), :] = e
+            lcol = rt[:, t:t + 1]
+            dd = dd - lcol * r[t:t + 1]
+            ee = ee - lcol * e[t:t + 1]
+        d_ref[...] = dd
+        e_ref[...] = ee
         return carry
 
     for j in range(nb):
         jb = j * b
         d_ref[...] = w_ref[jb:jb + b, jb:jb + b]
-        ut_ref[...] = jnp.zeros_like(ut_ref)
-        x_ref[...] = jnp.zeros_like(x_ref)
-        lax.fori_loop(0, b // PANEL, factor_panel, 0)
-        lo_ref[...] = jnp.transpose(ut_ref[...])
-        lax.fori_loop(0, b // PANEL, invert_panel, 0)
-        l_ref[jb:jb + b, jb:jb + b] = lo_ref[...]
+        e_ref[...] = eye
+        lax.fori_loop(0, b // PANEL, panel, 0)
+        l_ref[jb:jb + b, jb:jb + b] = jnp.transpose(ut_ref[...])
         linv_ref[jb:jb + b, jb:jb + b] = x_ref[...]
         if j < nb - 1:
             lp = _mm_t(w_ref[jb + b:, jb:jb + b], x_ref[...])

time: 201 us -> 194 us (0.965)
  Pallas kernels: 133 us -> 126 us
    pallas_call x1, Pallas kernels: 90.3 us -> 83.5 us  [chol_inv(): pl.pallas_call(chol_inv_kernel, out_shape=(jax.ShapeDtypeStruct((n, n), j...]
  transfers between devices with their start and end apart: 5 -> 5, of which waited for: 1 -> 1; matrix products, arithmetic and copies ran while one was open for 5% -> 5% of each run, Pallas kernels for 67% -> 66%
where the time goes in v7:
time: 194 us; the launch traced here: 192 us
  Pallas kernels  126 us (65%)
  local copies, waits for them, and re-layouts  16.2 us (8%)
  matrix products  15.8 us (8%)
  between operations  13.5 us (7%)
  other arithmetic  13 us (7%)
  starting transfers between devices  5.38 us (3%)
  waiting for transfers between devices  2.27 us (1%)
    pallas_call x1, Pallas kernels, chol_inv(): pl.pallas_call(chol_inv_kernel, out_shape=(jax.ShapeDtypeStruct((n, n), j...  83.5 us
    pallas_call x1, Pallas kernels, broadcast_pivot(): pl.pallas_call(functools.partial(pivot_kernel, n_front, n_src), out_shape...  42.3 us
    dot_general x1, matrix products, pivot_columns(): lax.dot_general(panel, inv_rows, (((1,), (1,)), ((), ())), precision=HIGH...  13.3 us
    select_n x2, other arithmetic, gather_half(): picked = jnp.where(found[:, None, None], picked, jnp.zeros_like(picked))  5.25 us
    gather x2, local copies, waits for them, and re-layouts, gather_half(): picked = jnp.take(blocks, index, axis=0)  3.98 us
  transfers between devices with their start and end apart: 5, of which 1 were waited for; matrix products, arithmetic and copies ran while one was open for 5% of the time, Pallas kernels for 66%

profile of v7, /device:TPU:1, one launch (start us, length us, event | category | flops | bytes accessed | tf_op | source)
XLA Modules:
  0.0 192.1 jit_solution(14442887645689041797)
XLA Ops:
  6.5 0.0 copy-start
  6.5 0.0 all-gather.2.cloned.1.call-start
  6.5 1.5 compare_reduce_fusion
  8.1 0.8 compare_reduce_fusion.3
  8.9 0.0 copy-done
  8.9 2.0 %gather_fusion.1 = f32[32,128,128]{2,1,0:T(8,128)} fusion(f32[48,128,128]{2,1,0:T(8,128)S(1)} %bitcast.35, s32[1024]{0:T(1024)S(1)} %pad_clamp_fusion), kind=kCustom, calls=%fused_computation.1.clone | custom fusion | bytes 4194432 | tf_op jit(solution)/shard_map/jit(_take)/gather | solution.py:21
  10.9 0.0 copy-start.3
  10.9 3.2 %select_select_fusion = f32[32,128,128]{2,1,0:T(8,128)} fusion(f32[32,128,128]{2,1,0:T(8,128)} %gather_fusion.1, pred[32]{0:T(512)(128)(4,1)S(1)} %compare_and_fusion, pred[32]{0:T(512)(128)(4,1)S(1)} %get-tuple-element.112), kind=kLoop, calls=%fused_computation.17 | loop fusion | flops 1048576 | bytes 4194368 | tf_op jit(solution)/shard_map/jit(_where)/select_n | solution.py:22
  14.1 1.4 collective-permute-start
  15.6 0.0 copy-done.3
  15.6 0.7 compare_reduce_fusion.2
  16.3 2.0 %gather_fusion = f32[32,128,128]{2,1,0:T(8,128)} fusion(f32[48,128,128]{2,1,0:T(8,128)S(1)} %bitcast.34, s32[1024]{0:T(1024)S(1)} %pad_clamp_fusion.1), kind=kCustom, calls=%fused_computation.clone | custom fusion | bytes 4194432 | tf_op jit(solution)/shard_map/jit(_take)/gather | solution.py:21
  18.3 0.0 copy-start.2
  18.3 2.0 %select_select_fusion.1 = f32[32,128,128]{2,1,0:T(8,128)S(1)} fusion(f32[32,128,128]{2,1,0:T(8,128)} %gather_fusion, pred[32]{0:T(512)(128)(4,1)S(1)} %compare_and_fusion.1, pred[32]{0:T(512)(128)(4,1)S(1)} %get-tuple-element.111), kind=kLoop, calls=%fused_computation.18 | loop fusion | flops 1048576 | bytes 4194368 | tf_op jit(solution)/shard_map/jit(_where)/select_n | solution.py:22
  20.3 0.0 collective-permute-done
  20.3 0.2 copy-done.2
  20.5 1.9 fusion.7
  22.4 0.0 copy-start.1
  22.4 1.4 copy-done.1
  23.8 0.7 fusion.10
  24.5 0.8 fusion.11
  25.3 1.3 collective-permute-start.2
  26.6 1.4 collective-permute-start.1
  28.0 42.3 %shard_map.39 = f32[64,32,128]{2,1,0:T(8,128)} custom-call(f32[512,128]{1,0:T(8,128)} %get-tuple-element.113.top_ref), custom_call_target="tpu_custom_call" | custom-call | tf_op jit(solution)/shard_map/pallas_call | solution.py:133
  70.3 1.9 %copy.17 = f32[4,16,32,128]{3,0,2,1:T(4,128)S(1)} copy(f32[4,16,32,128]{3,2,1,0:T(8,128)} %bitcast.36) | data formatting | bytes 2097152 | tf_op jit(solution)/shard_map/reshape | solution.py:149
  72.2 1.0 copy.26
  73.3 0.0 collective-permute-done.2
  73.3 0.0 collective-permute-done.1
  73.3 1.0 broadcast_select_fusion.2
  74.3 0.8 copy.18
  75.0 0.0 all-gather.2.cloned.1.call-update
  75.1 83.5 %shard_map.40 = (f32[512,512]{1,0:T(8,128)}, f32[512,512]{1,0:T(8,128)}) custom-call(f32[512,512]{1,0:T(8,128)} %bitcast.37), custom_call_target="tpu_custom_call" | custom-call | tf_op jit(solution)/shard_map/pallas_call | solution.py:223
  158.6 2.6 %fusion.8 = f32[128,512]{1,0:T(8,128)S(1)} fusion(f32[512,512]{1,0:T(8,128)} %get-tuple-element.70, f32[4096,128]{1,0:T(8,128)} %copy-done.1), kind=kOutput, calls=%fused_computation.33 | convolution fusion | flops 402653184 | bytes 1572864 | tf_op jit(solution)/shard_map/dot_general | solution.py:277
  161.1 1.3 collective-permute-start.3
  162.4 0.0 all-gather.2.cloned.1.call-done
  162.5 2.2 %collective-permute-done.3 = f32[128,512]{1,0:T(8,128)} collective-permute-done((f32[128,512]{1,0:T(8,128)S(1)}, f32[128,512]{1,0:T(8,128)}, u32[]{:S(2)}, u32[]{:S(2)}) %collective-permute-start.3) | collective-permute-done | bytes 262176 | tf_op jit(solution)/shard_map/ppermute | solution.py:278
  164.7 20.5 %conditional.1 = (f32[4096,128]{1,0:T(8,128)}) conditional(s32[]{:T(128)} %convert_element_type.3, (pred[]{:T(512)}, f32[128,512]{1,0:T(8,128)S(1)}, f32[128,512]{1,0:T(8,128)}, f32[512,512]{1,0:T(8,128)}, f32[4096,512]{1,0:T(8,128)}, /*index=5*/f32[4096,128]{1,0:T(8,128)}, s32[]{:T(128)}) %tuple.42, (s32[]{:T(128)}, f32[512,512]{1,0:T(8,128)}, ...), branch_computations={%region_4.6_spmd, %region_5.7_spmd} | conditional | flops 3624599552 | bytes 24117776 | solution.py:296
  164.7 2.5 %copy.20 = f32[512,512]{0,1:T(8,128)} copy(f32[512,512]{1,0:T(8,128)} %get-tuple-element.109) | data formatting | bytes 2097152 | tf_op jit(solution)/shard_map
  167.2 13.3 %convolution_bitcast_fusion.1 = f32[4096,128]{0,1:T(8,128)} fusion(f32[4096,512]{1,0:T(8,128)} %get-tuple-element.58, f32[512,512]{1,0:T(8,128)} %get-tuple-element.56, s32[]{:T(128)S(6)} %select_n.67), kind=kOutput, calls=%fused_computation.8 | convolution fusion | flops 3221225472 | bytes 10747908 | tf_op jit(solution)/shard_map/cond/branch_1_fun/dot_general | solution.py:286
  180.5 1.8 fusion.3
  182.3 2.9 %copy.23 = f32[4096,128]{1,0:T(8,128)} copy(f32[4096,128]{0,1:T(8,128)} %fusion.3) | data formatting | bytes 4194304 | tf_op jit(solution)/shard_map/cond
  (7 shorter events, 0.0 us)
Async XLA Ops:
  6.5 2.4 %copy-start = (f32[1,6144,128]{2,1,0:T(8,128)S(1)}, f32[1,6144,128]{2,1,0:T(8,128)}, u32[]{:S(2)}) copy-start(f32[1,6144,128]{2,1,0:T(8,128)} %param.8) | copy-start | bytes 9437188
  6.5 155.9 %all-gather.2.cloned.1.call-start = ((), (), s32[]{:S(2)}) async-start(), calls=%async_computation | async-start | bytes 8519680 | tf_op jit(solution)/shard_map/all_gather | solution.py:274
  10.9 4.6 %copy-start.3 = (s32[1,48]{1,0:T(1,128)S(1)}, s32[1,48]{1,0:T(1,128)}, u32[]{:S(2)}) copy-start(s32[1,48]{1,0:T(1,128)} %param.9) | copy-start | bytes 580
  14.1 6.2 %collective-permute-start = (f32[4096,128]{1,0:T(8,128)}, f32[4096,128]{1,0:T(8,128)}, u32[]{:S(2)}, u32[]{:S(2)}) collective-permute-start(f32[4096,128]{1,0:T(8,128)} %bitcast.6), channel_id=1, source_target_pairs={{0,64},{64,0},{1,65},{65,1},{2,66},{66,2},{3,67},{67,3},{4,68},{68... | collective-permute-start | bytes 6291464 | tf_op jit(solution)/shard_map/ppermute | solution.py:250
  18.3 2.2 %copy-start.2 = (f32[4096,128]{1,0:T(8,128)S(1)}, f32[4096,128]{1,0:T(8,128)}, u32[]{:S(2)}) copy-start(f32[4096,128]{1,0:T(8,128)} %param.7) | copy-start | bytes 6291460
  22.4 1.4 copy-start.1
  25.3 48.0 %collective-permute-start.2 = (f32[64,512]{0,1:T(8,128)}, f32[64,512]{0,1:T(8,128)}, u32[]{:S(2)}, u32[]{:S(2)}) collective-permute-start(f32[64,512]{0,1:T(8,128)} %get-tuple-element.115), channel_id=1, source_target_pairs={{0,0},{1,2},{2,4},{3,6},{4,8},{5,10},{6,12},{7,14},{8,16},{9,18},{... | collective-permute-start | bytes 393224 | tf_op jit(solution)/shard_map/ppermute | solution.py:268
  26.6 46.7 %collective-permute-start.1 = (f32[64,512]{0,1:T(8,128)S(1)}, f32[64,512]{0,1:T(8,128)}, u32[]{:S(2)}, u32[]{:S(2)}) collective-permute-start(f32[64,512]{0,1:T(8,128)S(1)} %get-tuple-element.116), channel_id=1, source_target_pairs={{0,1},{1,3},{2,5},{3,7},{4,9},{5,11},{6,13},{7,15},{8,17},{9,19},{... | collective-permute-start | bytes 393224 | tf_op jit(solution)/shard_map/ppermute | solution.py:268
  161.1 3.6 %collective-permute-start.3 = (f32[128,512]{1,0:T(8,128)S(1)}, f32[128,512]{1,0:T(8,128)}, u32[]{:S(2)}, u32[]{:S(2)}) collective-permute-start(f32[128,512]{1,0:T(8,128)S(1)} %fusion.8), channel_id=1, source_target_pairs={{0,64},{1,65},{2,66},{3,67},{4,68},{5,69},{6,70},{7,71},{8,72},{9,... | collective-permute-start | bytes 786440 | tf_op jit(solution)/shard_map/ppermute | solution.py:278
Sparse Core Ops, SparseCore 0:
  75.2 81.3 all-gather.1

commit v8 on v7

--- a/solution.py
+++ b/solution.py
@@ -10,6 +10,7 @@
 BLK = 128
 S = 512
 HIGHEST = lax.Precision.HIGHEST
+HIGH = lax.Precision.HIGH
 MESH = pl.DeviceIdType.MESH
 
 
@@ -270,26 +271,26 @@
     for part in range(1, per_block):
         my_piece = jnp.where(front % per_block == part, pieces[part], my_piece)
     pivot = broadcast_pivot(top, n_front)
+    partner_rows = lax.ppermute(panel_rows, "leaf", [(0, 1)])
+    col_rows = jnp.where(leaf == 0, panel_rows, partner_rows)
     my_piece, pivot = lax.optimization_barrier((my_piece, pivot))
     panel = lax.all_gather(my_piece, "front", tiled=True)
     factor, inverse = chol_inv(pivot)
 
-    own_solved = lax.dot_general(panel_rows, inverse, (((1,), (1,)), ((), ())), precision=HIGHEST)
-    from_leaf0 = lax.ppermute(own_solved, "leaf", [(0, 1)])
-    col_solved = jnp.where(leaf == 0, own_solved, from_leaf0)
+    col_solved = lax.dot_general(col_rows, inverse, (((1,), (1,)), ((), ())), precision=HIGHEST)
 
     piv_cols = S // cols
     col_at = jnp.minimum(front, piv_cols - 1) * cols
 
     def pivot_columns():
         inv_rows = lax.dynamic_slice_in_dim(inverse, col_at, cols, 0)
-        out = lax.dot_general(panel, inv_rows, (((1,), (1,)), ((), ())), precision=HIGHEST)
+        out = lax.dot_general(panel, inv_rows, (((1,), (1,)), ((), ())), precision=HIGH)
         top_rows = jnp.where(leaf == 0, lax.dynamic_slice_in_dim(factor, col_at, cols, 1), out[:S])
         return lax.dynamic_update_slice_in_dim(out, top_rows, 0, 0)
 
     def other_columns():
         weights = jnp.dot(col_solved, inverse, precision=HIGHEST).T
-        out = assembled - jnp.dot(panel, weights, precision=HIGHEST)
+        out = assembled - jnp.dot(panel, weights, precision=HIGH)
         top_rows = jnp.where(leaf == 0, col_solved.T, out[:S])
         return lax.dynamic_update_slice_in_dim(out, top_rows, 0, 0)
 

time: 194 us -> 190 us (0.979)
  matrix products: 15.8 us -> 11.6 us
  waiting for transfers between devices: 2.27 us -> 0.05 us
    dot_general x2, matrix products: 15.8 us -> 11.6 us  [the longest x1 8.97 us: pivot_columns(): lax.dot_general(panel, inv_rows, (((1,), (1,)), ((), ())), precision=HIGH)]
    ppermute x1, waiting for transfers between devices: 2.23 us -> 0.01 us  [per_device(): partner_rows = lax.ppermute(panel_rows, 'leaf', [(0, 1)])]
  transfers between devices with their start and end apart: 5 -> 5, of which waited for: 1 -> 0; matrix products, arithmetic and copies ran while one was open for 5% -> 6% of each run, Pallas kernels for 66% -> 67%
where the time goes in v8:
time: 190 us; the launch traced here: 188 us
  Pallas kernels  126 us (66%)
  local copies, waits for them, and re-layouts  17.3 us (9%)
  other arithmetic  13.7 us (7%)
  between operations  13.5 us (7%)
  matrix products  11.6 us (6%)
  starting transfers between devices  5.38 us (3%)
    pallas_call x1, Pallas kernels, chol_inv(): pl.pallas_call(chol_inv_kernel, out_shape=(jax.ShapeDtypeStruct((n, n), j...  83.5 us
    pallas_call x1, Pallas kernels, broadcast_pivot(): pl.pallas_call(functools.partial(pivot_kernel, n_front, n_src), out_shape...  42.4 us
    dot_general x1, matrix products, pivot_columns(): lax.dot_general(panel, inv_rows, (((1,), (1,)), ((), ())), precision=HIGH)  8.97 us
    select_n x2, other arithmetic, gather_half(): picked = jnp.where(found[:, None, None], picked, jnp.zeros_like(picked))  5.25 us
    gather x2, local copies, waits for them, and re-layouts, gather_half(): picked = jnp.take(blocks, index, axis=0)  3.98 us
  transfers between devices with their start and end apart: 5, of which 0 were waited for; matrix products, arithmetic and copies ran while one was open for 6% of the time, Pallas kernels for 67%

profile of v8, /device:TPU:1, one launch (start us, length us, event | category | flops | bytes accessed | tf_op | source)
XLA Modules:
  0.0 187.6 jit_solution(13104850565994572846)
XLA Ops:
  6.5 0.0 copy-start
  6.5 0.0 all-gather.2.cloned.1.call-start
  6.5 1.5 compare_reduce_fusion
  8.1 0.8 compare_reduce_fusion.3
  8.9 0.0 copy-done
  8.9 2.0 %gather_fusion.1 = f32[32,128,128]{2,1,0:T(8,128)} fusion(f32[48,128,128]{2,1,0:T(8,128)S(1)} %bitcast.40, s32[1024]{0:T(1024)S(1)} %pad_clamp_fusion), kind=kCustom, calls=%fused_computation.1.clone | custom fusion | bytes 4194432 | tf_op jit(solution)/shard_map/jit(_take)/gather | solution.py:22
  10.9 0.0 copy-start.3
  10.9 3.2 %select_select_fusion = f32[32,128,128]{2,1,0:T(8,128)} fusion(f32[32,128,128]{2,1,0:T(8,128)} %gather_fusion.1, pred[32]{0:T(512)(128)(4,1)S(1)} %compare_and_fusion, pred[32]{0:T(512)(128)(4,1)S(1)} %get-tuple-element.98), kind=kLoop, calls=%fused_computation.15 | loop fusion | flops 1048576 | bytes 4194368 | tf_op jit(solution)/shard_map/jit(_where)/select_n | solution.py:23
  14.1 1.4 collective-permute-start
  15.6 0.0 copy-done.3
  15.6 0.7 compare_reduce_fusion.2
  16.3 2.0 %gather_fusion = f32[32,128,128]{2,1,0:T(8,128)} fusion(f32[48,128,128]{2,1,0:T(8,128)S(1)} %bitcast.39, s32[1024]{0:T(1024)S(1)} %pad_clamp_fusion.1), kind=kCustom, calls=%fused_computation.clone | custom fusion | bytes 4194432 | tf_op jit(solution)/shard_map/jit(_take)/gather | solution.py:22
  18.3 0.0 copy-start.2
  18.3 2.0 %select_select_fusion.1 = f32[32,128,128]{2,1,0:T(8,128)S(1)} fusion(f32[32,128,128]{2,1,0:T(8,128)} %gather_fusion, pred[32]{0:T(512)(128)(4,1)S(1)} %compare_and_fusion.1, pred[32]{0:T(512)(128)(4,1)S(1)} %get-tuple-element.97), kind=kLoop, calls=%fused_computation.16 | loop fusion | flops 1048576 | bytes 4194368 | tf_op jit(solution)/shard_map/jit(_where)/select_n | solution.py:23
  20.3 0.0 collective-permute-done
  20.3 0.2 copy-done.2
  20.5 1.9 fusion.6
  22.4 0.0 copy-start.1
  22.4 1.4 copy-done.1
  23.8 0.7 fusion.12
  24.5 0.9 fusion.13
  25.4 1.3 collective-permute-start.3
  26.7 1.4 collective-permute-start.2
  28.0 42.4 %shard_map.39 = f32[64,32,128]{2,1,0:T(8,128)} custom-call(f32[512,128]{1,0:T(8,128)} %get-tuple-element.99.top_ref), custom_call_target="tpu_custom_call" | custom-call | tf_op jit(solution)/shard_map/pallas_call | solution.py:134
  70.4 1.9 %copy.17 = f32[4,16,32,128]{3,0,2,1:T(4,128)S(1)} copy(f32[4,16,32,128]{3,2,1,0:T(8,128)} %bitcast.41) | data formatting | bytes 2097152 | tf_op jit(solution)/shard_map/reshape | solution.py:150
  72.3 1.0 copy.26
  73.4 0.0 collective-permute-done.3
  73.4 0.0 collective-permute-done.2
  73.4 1.7 broadcast_select_fusion
  75.1 1.7 copy.18
  76.8 0.0 all-gather.2.cloned.1.call-update
  76.8 1.3 collective-permute-start.1
  78.1 83.5 %shard_map.40 = (f32[512,512]{1,0:T(8,128)}, f32[512,512]{1,0:T(8,128)}) custom-call(f32[512,512]{1,0:T(8,128)} %bitcast.42), custom_call_target="tpu_custom_call" | custom-call | tf_op jit(solution)/shard_map/pallas_call | solution.py:224
  161.6 0.0 collective-permute-done.1
  161.6 2.6 %fusion.7 = f32[128,512]{1,0:T(8,128)S(1)} fusion(f32[512,512]{1,0:T(8,128)} %get-tuple-element.62, f32[128,512]{0,1:T(8,128)} %collective-permute-done.1, pred[]{:T(512)S(6)} %eq.46, f32[4096,128]{1,0:T(8,128)} %copy-done.1), kind=kOutput, calls=%fused_computation.18 | convolution fusion | flops 402718720 | bytes 1835009 | tf_op jit(solution)/shard_map/dot_general | solution.py:280
  164.3 0.0 all-gather.2.cloned.1.call-done
  164.3 16.4 %conditional.1 = (f32[4096,128]{1,0:T(8,128)}) conditional(s32[]{:T(128)} %convert_element_type.3, (f32[128,512]{1,0:T(8,128)S(1)}, f32[512,512]{1,0:T(8,128)}, f32[4096,512]{1,0:T(8,128)}, f32[4096,128]{1,0:T(8,128)}, s32[]{:T(128)}) %tuple.42, (s32[]{:T(128)}, f32[512,512]{1,0:T(8,128)}, f32[4096,512]{1,0:T(8,128)}, s32[]{:T(128)}, ...), branch_computations={%region_4.6_spmd, %region_5.7_spmd} | conditional | flops 2013855744 | bytes 23592976 | solution.py:297
  164.5 2.5 %copy.20 = f32[512,512]{0,1:T(8,128)} copy(f32[512,512]{1,0:T(8,128)} %get-tuple-element.95) | data formatting | bytes 2097152 | tf_op jit(solution)/shard_map
  167.0 9.0 %convolution_bitcast_fusion.1 = f32[4096,128]{0,1:T(8,128)} fusion(f32[4096,512]{1,0:T(8,128)} %get-tuple-element.50, f32[512,512]{1,0:T(8,128)} %get-tuple-element.48, s32[]{:T(128)S(6)} %select_n.63), kind=kOutput, calls=%fused_computation.6 | convolution fusion | flops 1610612736 | bytes 10747908 | tf_op jit(solution)/shard_map/cond/branch_1_fun/dot_general | solution.py:287
  176.0 1.8 fusion.2
  177.8 2.9 %copy.23 = f32[4096,128]{1,0:T(8,128)} copy(f32[4096,128]{0,1:T(8,128)} %fusion.2) | data formatting | bytes 4194304 | tf_op jit(solution)/shard_map/cond
  (7 shorter events, 0.0 us)
Async XLA Ops:
  6.5 2.4 %copy-start = (f32[1,6144,128]{2,1,0:T(8,128)S(1)}, f32[1,6144,128]{2,1,0:T(8,128)}, u32[]{:S(2)}) copy-start(f32[1,6144,128]{2,1,0:T(8,128)} %param.8) | copy-start | bytes 9437188
  6.5 157.8 %all-gather.2.cloned.1.call-start = ((), (), s32[]{:S(2)}) async-start(), calls=%async_computation | async-start | bytes 8519680 | tf_op jit(solution)/shard_map/all_gather | solution.py:277
  10.9 4.6 %copy-start.3 = (s32[1,48]{1,0:T(1,128)S(1)}, s32[1,48]{1,0:T(1,128)}, u32[]{:S(2)}) copy-start(s32[1,48]{1,0:T(1,128)} %param.9) | copy-start | bytes 580
  14.1 6.2 %collective-permute-start = (f32[4096,128]{1,0:T(8,128)}, f32[4096,128]{1,0:T(8,128)}, u32[]{:S(2)}, u32[]{:S(2)}) collective-permute-start(f32[4096,128]{1,0:T(8,128)} %bitcast.6), channel_id=1, source_target_pairs={{0,64},{64,0},{1,65},{65,1},{2,66},{66,2},{3,67},{67,3},{4,68},{68... | collective-permute-start | bytes 6291464 | tf_op jit(solution)/shard_map/ppermute | solution.py:251
  18.3 2.2 %copy-start.2 = (f32[4096,128]{1,0:T(8,128)S(1)}, f32[4096,128]{1,0:T(8,128)}, u32[]{:S(2)}) copy-start(f32[4096,128]{1,0:T(8,128)} %param.7) | copy-start | bytes 6291460
  22.4 1.4 copy-start.1
  25.4 48.0 %collective-permute-start.3 = (f32[64,512]{0,1:T(8,128)}, f32[64,512]{0,1:T(8,128)}, u32[]{:S(2)}, u32[]{:S(2)}) collective-permute-start(f32[64,512]{0,1:T(8,128)} %get-tuple-element.101), channel_id=1, source_target_pairs={{0,0},{1,2},{2,4},{3,6},{4,8},{5,10},{6,12},{7,14},{8,16},{9,18},{... | collective-permute-start | bytes 393224 | tf_op jit(solution)/shard_map/ppermute | solution.py:269
  26.7 46.7 %collective-permute-start.2 = (f32[64,512]{0,1:T(8,128)}, f32[64,512]{0,1:T(8,128)}, u32[]{:S(2)}, u32[]{:S(2)}) collective-permute-start(f32[64,512]{0,1:T(8,128)} %get-tuple-element.102), channel_id=1, source_target_pairs={{0,1},{1,3},{2,5},{3,7},{4,9},{5,11},{6,13},{7,15},{8,17},{9,19},{... | collective-permute-start | bytes 393224 | tf_op jit(solution)/shard_map/ppermute | solution.py:269
  76.8 84.8 %collective-permute-start.1 = (f32[128,512]{0,1:T(8,128)S(1)}, f32[128,512]{0,1:T(8,128)}, u32[]{:S(2)}, u32[]{:S(2)}) collective-permute-start(f32[128,512]{0,1:T(8,128)S(1)} %get-tuple-element.100), channel_id=1, source_target_pairs={{0,64},{1,65},{2,66},{3,67},{4,68},{5,69},{6,70},{7,71},{8,72},{9,... | collective-permute-start | bytes 786440 | tf_op jit(solution)/shard_map/ppermute | solution.py:274
Sparse Core Ops, SparseCore 0:
  76.9 80.7 all-gather.1

commit v9 on v8

--- a/solution.py
+++ b/solution.py
@@ -10,7 +10,6 @@
 BLK = 128
 S = 512
 HIGHEST = lax.Precision.HIGHEST
-HIGH = lax.Precision.HIGH
 MESH = pl.DeviceIdType.MESH
 
 
@@ -179,13 +178,14 @@
         e = e_ref[pl.ds(k, PANEL), :]
         for t in range(PANEL):
             c = k + t
-            colv = jnp.sum(jnp.where(lane == c, r, 0.0), axis=1, keepdims=True)
-            piv = jnp.sum(jnp.where(sub == t, colv, 0.0), axis=0, keepdims=True)
-            root = jnp.sqrt(piv)
-            urow = jnp.where(lane[t:t + 1] >= c, r[t:t + 1] / root, 0.0)
-            f = jnp.where(sub > t, colv / root, 0.0)
+            at_c = lane == c
+            colv = jnp.sum(jnp.where(at_c, r, 0.0), axis=1, keepdims=True)
+            piv = jnp.sum(jnp.where(at_c[t:t + 1], r[t:t + 1], 0.0), axis=1, keepdims=True)
+            scale = 1.0 / jnp.sqrt(piv)
+            urow = jnp.where(lane[t:t + 1] >= c, r[t:t + 1] * scale, 0.0)
+            f = jnp.where(sub > t, colv * scale, 0.0)
             r = jnp.where(sub == t, urow, r - f * urow)
-            xrow = e[t:t + 1] / root
+            xrow = e[t:t + 1] * scale
             e = jnp.where(sub == t, xrow, e - f * xrow)
         ut_ref[pl.ds(k, PANEL), :] = r
         x_ref[pl.ds(k, PANEL), :] = e
@@ -284,13 +284,13 @@
 
     def pivot_columns():
         inv_rows = lax.dynamic_slice_in_dim(inverse, col_at, cols, 0)
-        out = lax.dot_general(panel, inv_rows, (((1,), (1,)), ((), ())), precision=HIGH)
+        out = lax.dot_general(panel, inv_rows, (((1,), (1,)), ((), ())), precision=HIGHEST)
         top_rows = jnp.where(leaf == 0, lax.dynamic_slice_in_dim(factor, col_at, cols, 1), out[:S])
         return lax.dynamic_update_slice_in_dim(out, top_rows, 0, 0)
 
     def other_columns():
         weights = jnp.dot(col_solved, inverse, precision=HIGHEST).T
-        out = assembled - jnp.dot(panel, weights, precision=HIGH)
+        out = assembled - jnp.dot(panel, weights, precision=HIGHEST)
         top_rows = jnp.where(leaf == 0, col_solved.T, out[:S])
         return lax.dynamic_update_slice_in_dim(out, top_rows, 0, 0)
 

time: 190 us -> 189 us (level)
  Pallas kernels: 126 us -> 121 us
  matrix products: 11.6 us -> 15.9 us
    pallas_call x1, Pallas kernels: 83.5 us -> 78.2 us  [chol_inv(): pl.pallas_call(chol_inv_kernel, out_shape=(jax.ShapeDtypeStruct((n, n), j...]
    dot_general x1, matrix products: 8.97 us -> 13.3 us  [pivot_columns(): lax.dot_general(panel, inv_rows, (((1,), (1,)), ((), ())), precision=HIGH...]
  transfers between devices with their start and end apart: 5 -> 5, of which waited for: 0 -> 0; matrix products, arithmetic and copies ran while one was open for 6% -> 6% of each run, Pallas kernels for 67% -> 65%
where the time goes in v9:
time: 189 us; the launch traced here: 187 us
  Pallas kernels  121 us (64%)
  local copies, waits for them, and re-layouts  17.3 us (9%)
  matrix products  15.9 us (8%)
  other arithmetic  13.7 us (7%)
  between operations  13.5 us (7%)
  starting transfers between devices  5.38 us (3%)
    pallas_call x1, Pallas kernels, chol_inv(): pl.pallas_call(chol_inv_kernel, out_shape=(jax.ShapeDtypeStruct((n, n), j...  78.2 us
    pallas_call x1, Pallas kernels, broadcast_pivot(): pl.pallas_call(functools.partial(pivot_kernel, n_front, n_src), out_shape...  42.4 us
    dot_general x1, matrix products, pivot_columns(): lax.dot_general(panel, inv_rows, (((1,), (1,)), ((), ())), precision=HIGH...  13.3 us
    select_n x2, other arithmetic, gather_half(): picked = jnp.where(found[:, None, None], picked, jnp.zeros_like(picked))  5.25 us
    gather x2, local copies, waits for them, and re-layouts, gather_half(): picked = jnp.take(blocks, index, axis=0)  3.98 us
  transfers between devices with their start and end apart: 5, of which 0 were waited for; matrix products, arithmetic and copies ran while one was open for 6% of the time, Pallas kernels for 65%

profile of v9, /device:TPU:1, one launch (start us, length us, event | category | flops | bytes accessed | tf_op | source)
XLA Modules:
  0.0 186.7 jit_solution(2419589017168347098)
XLA Ops:
  6.5 0.0 copy-start
  6.5 0.0 all-gather.2.cloned.1.call-start
  6.5 1.5 compare_reduce_fusion
  8.1 0.8 compare_reduce_fusion.3
  8.9 0.0 copy-done
  8.9 2.0 %gather_fusion.1 = f32[32,128,128]{2,1,0:T(8,128)} fusion(f32[48,128,128]{2,1,0:T(8,128)S(1)} %bitcast.40, s32[1024]{0:T(1024)S(1)} %pad_clamp_fusion), kind=kCustom, calls=%fused_computation.1.clone | custom fusion | bytes 4194432 | tf_op jit(solution)/shard_map/jit(_take)/gather | solution.py:21
  10.9 0.0 copy-start.3
  10.9 3.2 %select_select_fusion = f32[32,128,128]{2,1,0:T(8,128)} fusion(f32[32,128,128]{2,1,0:T(8,128)} %gather_fusion.1, pred[32]{0:T(512)(128)(4,1)S(1)} %compare_and_fusion, pred[32]{0:T(512)(128)(4,1)S(1)} %get-tuple-element.98), kind=kLoop, calls=%fused_computation.15 | loop fusion | flops 1048576 | bytes 4194368 | tf_op jit(solution)/shard_map/jit(_where)/select_n | solution.py:22
  14.1 1.4 collective-permute-start
  15.6 0.0 copy-done.3
  15.6 0.7 compare_reduce_fusion.2
  16.3 2.0 %gather_fusion = f32[32,128,128]{2,1,0:T(8,128)} fusion(f32[48,128,128]{2,1,0:T(8,128)S(1)} %bitcast.39, s32[1024]{0:T(1024)S(1)} %pad_clamp_fusion.1), kind=kCustom, calls=%fused_computation.clone | custom fusion | bytes 4194432 | tf_op jit(solution)/shard_map/jit(_take)/gather | solution.py:21
  18.3 0.0 copy-start.2
  18.3 2.0 %select_select_fusion.1 = f32[32,128,128]{2,1,0:T(8,128)S(1)} fusion(f32[32,128,128]{2,1,0:T(8,128)} %gather_fusion, pred[32]{0:T(512)(128)(4,1)S(1)} %compare_and_fusion.1, pred[32]{0:T(512)(128)(4,1)S(1)} %get-tuple-element.97), kind=kLoop, calls=%fused_computation.16 | loop fusion | flops 1048576 | bytes 4194368 | tf_op jit(solution)/shard_map/jit(_where)/select_n | solution.py:22
  20.3 0.0 collective-permute-done
  20.3 0.2 copy-done.2
  20.5 1.9 fusion.6
  22.4 0.0 copy-start.1
  22.4 1.4 copy-done.1
  23.8 0.7 fusion.12
  24.5 0.9 fusion.13
  25.4 1.3 collective-permute-start.3
  26.7 1.4 collective-permute-start.2
  28.0 42.4 %shard_map.39 = f32[64,32,128]{2,1,0:T(8,128)} custom-call(f32[512,128]{1,0:T(8,128)} %get-tuple-element.99.top_ref), custom_call_target="tpu_custom_call" | custom-call | tf_op jit(solution)/shard_map/pallas_call | solution.py:133
  70.4 1.9 %copy.17 = f32[4,16,32,128]{3,0,2,1:T(4,128)S(1)} copy(f32[4,16,32,128]{3,2,1,0:T(8,128)} %bitcast.41) | data formatting | bytes 2097152 | tf_op jit(solution)/shard_map/reshape | solution.py:149
  72.3 1.0 copy.26
  73.4 0.0 collective-permute-done.3
  73.4 0.0 collective-permute-done.2
  73.4 1.7 broadcast_select_fusion
  75.1 1.7 copy.18
  76.8 0.0 all-gather.2.cloned.1.call-update
  76.8 1.3 collective-permute-start.1
  78.1 78.2 %shard_map.40 = (f32[512,512]{1,0:T(8,128)}, f32[512,512]{1,0:T(8,128)}) custom-call(f32[512,512]{1,0:T(8,128)} %bitcast.42), custom_call_target="tpu_custom_call" | custom-call | tf_op jit(solution)/shard_map/pallas_call | solution.py:224
  156.3 0.0 collective-permute-done.1
  156.3 2.6 %fusion.7 = f32[128,512]{1,0:T(8,128)S(1)} fusion(f32[512,512]{1,0:T(8,128)} %get-tuple-element.62, f32[128,512]{0,1:T(8,128)} %collective-permute-done.1, pred[]{:T(512)S(6)} %eq.46, f32[4096,128]{1,0:T(8,128)} %copy-done.1), kind=kOutput, calls=%fused_computation.18 | convolution fusion | flops 402718720 | bytes 1835009 | tf_op jit(solution)/shard_map/dot_general | solution.py:280
  158.9 0.0 all-gather.2.cloned.1.call-done
  158.9 20.9 %conditional.1 = (f32[4096,128]{1,0:T(8,128)}) conditional(s32[]{:T(128)} %convert_element_type.3, (f32[128,512]{1,0:T(8,128)S(1)}, f32[512,512]{1,0:T(8,128)}, f32[4096,512]{1,0:T(8,128)}, f32[4096,128]{1,0:T(8,128)}, s32[]{:T(128)}) %tuple.42, (s32[]{:T(128)}, f32[512,512]{1,0:T(8,128)}, f32[4096,512]{1,0:T(8,128)}, s32[]{:T(128)}, ...), branch_computations={%region_4.6_spmd, %region_5.7_spmd} | conditional | flops 3624468480 | bytes 23592976 | solution.py:297
  159.4 2.5 %copy.20 = f32[512,512]{0,1:T(8,128)} copy(f32[512,512]{1,0:T(8,128)} %get-tuple-element.95) | data formatting | bytes 2097152 | tf_op jit(solution)/shard_map
  161.9 13.3 %convolution_bitcast_fusion.1 = f32[4096,128]{0,1:T(8,128)} fusion(f32[4096,512]{1,0:T(8,128)} %get-tuple-element.50, f32[512,512]{1,0:T(8,128)} %get-tuple-element.48, s32[]{:T(128)S(6)} %select_n.63), kind=kOutput, calls=%fused_computation.6 | convolution fusion | flops 3221225472 | bytes 10747908 | tf_op jit(solution)/shard_map/cond/branch_1_fun/dot_general | solution.py:287
  175.2 1.8 fusion.2
  177.0 2.9 %copy.23 = f32[4096,128]{1,0:T(8,128)} copy(f32[4096,128]{0,1:T(8,128)} %fusion.2) | data formatting | bytes 4194304 | tf_op jit(solution)/shard_map/cond
  (7 shorter events, 0.0 us)
Async XLA Ops:
  6.5 2.4 %copy-start = (f32[1,6144,128]{2,1,0:T(8,128)S(1)}, f32[1,6144,128]{2,1,0:T(8,128)}, u32[]{:S(2)}) copy-start(f32[1,6144,128]{2,1,0:T(8,128)} %param.8) | copy-start | bytes 9437188
  6.5 152.4 %all-gather.2.cloned.1.call-start = ((), (), s32[]{:S(2)}) async-start(), calls=%async_computation | async-start | bytes 8519680 | tf_op jit(solution)/shard_map/all_gather | solution.py:277
  10.9 4.6 %copy-start.3 = (s32[1,48]{1,0:T(1,128)S(1)}, s32[1,48]{1,0:T(1,128)}, u32[]{:S(2)}) copy-start(s32[1,48]{1,0:T(1,128)} %param.9) | copy-start | bytes 580
  14.1 6.2 %collective-permute-start = (f32[4096,128]{1,0:T(8,128)}, f32[4096,128]{1,0:T(8,128)}, u32[]{:S(2)}, u32[]{:S(2)}) collective-permute-start(f32[4096,128]{1,0:T(8,128)} %bitcast.6), channel_id=1, source_target_pairs={{0,64},{64,0},{1,65},{65,1},{2,66},{66,2},{3,67},{67,3},{4,68},{68... | collective-permute-start | bytes 6291464 | tf_op jit(solution)/shard_map/ppermute | solution.py:251
  18.3 2.2 %copy-start.2 = (f32[4096,128]{1,0:T(8,128)S(1)}, f32[4096,128]{1,0:T(8,128)}, u32[]{:S(2)}) copy-start(f32[4096,128]{1,0:T(8,128)} %param.7) | copy-start | bytes 6291460
  22.4 1.4 copy-start.1
  25.4 48.0 %collective-permute-start.3 = (f32[64,512]{0,1:T(8,128)}, f32[64,512]{0,1:T(8,128)}, u32[]{:S(2)}, u32[]{:S(2)}) collective-permute-start(f32[64,512]{0,1:T(8,128)} %get-tuple-element.101), channel_id=1, source_target_pairs={{0,0},{1,2},{2,4},{3,6},{4,8},{5,10},{6,12},{7,14},{8,16},{9,18},{... | collective-permute-start | bytes 393224 | tf_op jit(solution)/shard_map/ppermute | solution.py:269
  26.7 46.7 %collective-permute-start.2 = (f32[64,512]{0,1:T(8,128)}, f32[64,512]{0,1:T(8,128)}, u32[]{:S(2)}, u32[]{:S(2)}) collective-permute-start(f32[64,512]{0,1:T(8,128)} %get-tuple-element.102), channel_id=1, source_target_pairs={{0,1},{1,3},{2,5},{3,7},{4,9},{5,11},{6,13},{7,15},{8,17},{9,19},{... | collective-permute-start | bytes 393224 | tf_op jit(solution)/shard_map/ppermute | solution.py:269
  76.8 79.5 %collective-permute-start.1 = (f32[128,512]{0,1:T(8,128)S(1)}, f32[128,512]{0,1:T(8,128)}, u32[]{:S(2)}, u32[]{:S(2)}) collective-permute-start(f32[128,512]{0,1:T(8,128)S(1)} %get-tuple-element.100), channel_id=1, source_target_pairs={{0,64},{1,65},{2,66},{3,67},{4,68},{5,69},{6,70},{7,71},{8,72},{9,... | collective-permute-start | bytes 786440 | tf_op jit(solution)/shard_map/ppermute | solution.py:274
Sparse Core Ops, SparseCore 0:
  76.9 80.1 all-gather.1

commit v10 on v9

--- a/solution.py
+++ b/solution.py
@@ -161,7 +161,7 @@
                            preferred_element_type=jnp.float32)
 
 
-def chol_inv_kernel(a_ref, l_ref, linv_ref, w_ref, d_ref, e_ref, ut_ref, x_ref):
+def chol_inv_kernel(a_ref, l_ref, linv_ref, w_ref, d_ref, e_ref, ut_ref, x_ref, rt_ref):
     n = a_ref.shape[0]
     b = d_ref.shape[0]
     nb = n // b
@@ -189,15 +189,22 @@
             e = jnp.where(sub == t, xrow, e - f * xrow)
         ut_ref[pl.ds(k, PANEL), :] = r
         x_ref[pl.ds(k, PANEL), :] = e
-        rt = jnp.transpose(r)
-        dd = d_ref[...]
-        ee = e_ref[...]
-        for t in range(PANEL):
-            lcol = rt[:, t:t + 1]
-            dd = dd - lcol * r[t:t + 1]
-            ee = ee - lcol * e[t:t + 1]
-        d_ref[...] = dd
-        e_ref[...] = ee
+        rt_ref[...] = jnp.transpose(r)
+
+        def update(g, carry):
+            row0 = pl.multiple_of(g * PANEL, PANEL)
+            lg = rt_ref[pl.ds(row0, PANEL), :]
+            dd = d_ref[pl.ds(row0, PANEL), :]
+            ee = e_ref[pl.ds(row0, PANEL), :]
+            for t in range(PANEL):
+                lcol = lg[:, t:t + 1]
+                dd = dd - lcol * r[t:t + 1]
+                ee = ee - lcol * e[t:t + 1]
+            d_ref[pl.ds(row0, PANEL), :] = dd
+            e_ref[pl.ds(row0, PANEL), :] = ee
+            return carry
+
+        lax.fori_loop(p + 1, b // PANEL, update, 0)
         return carry
 
     for j in range(nb):
@@ -232,6 +239,7 @@
             pltpu.VMEM((b, b), jnp.float32),
             pltpu.VMEM((b, b), jnp.float32),
             pltpu.VMEM((b, b), jnp.float32),
+            pltpu.VMEM((b, PANEL), jnp.float32),
         ],
     )(a)
 

time: 189 us -> 215 us (1.14)
  Pallas kernels: 121 us -> 146 us
    pallas_call x1, Pallas kernels: 78.2 us -> 104 us  [chol_inv(): pl.pallas_call(chol_inv_kernel, out_shape=(jax.ShapeDtypeStruct((n, n), j...]
  transfers between devices with their start and end apart: 5 -> 5, of which waited for: 0 -> 0; matrix products, arithmetic and copies ran while one was open for 6% -> 5% of each run, Pallas kernels for 65% -> 69%
where the time goes in v10:
time: 215 us; the launch traced here: 212 us
  Pallas kernels  146 us (68%)
  local copies, waits for them, and re-layouts  17.3 us (8%)
  matrix products  15.9 us (7%)
  other arithmetic  13.7 us (6%)
  between operations  13.5 us (6%)
  starting transfers between devices  5.38 us (3%)
    pallas_call x1, Pallas kernels, chol_inv(): pl.pallas_call(chol_inv_kernel, out_shape=(jax.ShapeDtypeStruct((n, n), j...  104 us
    pallas_call x1, Pallas kernels, broadcast_pivot(): pl.pallas_call(functools.partial(pivot_kernel, n_front, n_src), out_shape...  42.4 us
    dot_general x1, matrix products, pivot_columns(): lax.dot_general(panel, inv_rows, (((1,), (1,)), ((), ())), precision=HIGH...  13.3 us
    select_n x2, other arithmetic, gather_half(): picked = jnp.where(found[:, None, None], picked, jnp.zeros_like(picked))  5.25 us
  transfers between devices with their start and end apart: 5, of which 0 were waited for; matrix products, arithmetic and copies ran while one was open for 5% of the time, Pallas kernels for 69%

profile of v10, /device:TPU:1, one launch (start us, length us, event | category | flops | bytes accessed | tf_op | source)
XLA Modules:
  0.0 212.2 jit_solution(5187085494841541961)
XLA Ops:
  6.5 0.0 copy-start
  6.5 0.0 all-gather.2.cloned.1.call-start
  6.5 1.5 compare_reduce_fusion
  8.1 0.8 compare_reduce_fusion.3
  8.9 0.0 copy-done
  8.9 2.0 gather_fusion.1
  10.9 0.0 copy-start.3
  10.9 3.2 %select_select_fusion = f32[32,128,128]{2,1,0:T(8,128)} fusion(f32[32,128,128]{2,1,0:T(8,128)} %gather_fusion.1, pred[32]{0:T(512)(128)(4,1)S(1)} %compare_and_fusion, pred[32]{0:T(512)(128)(4,1)S(1)} %get-tuple-element.98), kind=kLoop, calls=%fused_computation.15 | loop fusion | flops 1048576 | bytes 4194368 | tf_op jit(solution)/shard_map/jit(_where)/select_n | solution.py:22
  14.1 1.4 collective-permute-start
  15.6 0.0 copy-done.3
  15.6 0.7 compare_reduce_fusion.2
  16.3 2.0 gather_fusion
  18.3 0.0 copy-start.2
  18.3 2.0 select_select_fusion.1
  20.3 0.0 collective-permute-done
  20.3 0.2 copy-done.2
  20.5 1.9 fusion.6
  22.4 0.0 copy-start.1
  22.4 1.4 copy-done.1
  23.8 0.7 fusion.12
  24.5 0.9 fusion.13
  25.4 1.3 collective-permute-start.3
  26.7 1.4 collective-permute-start.2
  28.0 42.4 %shard_map.39 = f32[64,32,128]{2,1,0:T(8,128)} custom-call(f32[512,128]{1,0:T(8,128)} %get-tuple-element.99.top_ref), custom_call_target="tpu_custom_call" | custom-call | tf_op jit(solution)/shard_map/pallas_call | solution.py:133
  70.4 1.9 copy.17
  72.3 1.0 copy.26
  73.4 0.0 collective-permute-done.3
  73.4 0.0 collective-permute-done.2
  73.4 1.7 broadcast_select_fusion
  75.1 1.7 copy.18
  76.8 0.0 all-gather.2.cloned.1.call-update
  76.8 1.3 collective-permute-start.1
  78.1 103.6 %shard_map.40 = (f32[512,512]{1,0:T(8,128)}, f32[512,512]{1,0:T(8,128)}) custom-call(f32[512,512]{1,0:T(8,128)} %bitcast.42), custom_call_target="tpu_custom_call" | custom-call | tf_op jit(solution)/shard_map/pallas_call | solution.py:231
  181.7 0.0 collective-permute-done.1
  181.7 2.6 %fusion.7 = f32[128,512]{1,0:T(8,128)S(1)} fusion(f32[512,512]{1,0:T(8,128)} %get-tuple-element.62, f32[128,512]{0,1:T(8,128)} %collective-permute-done.1, pred[]{:T(512)S(6)} %eq.46, f32[4096,128]{1,0:T(8,128)} %copy-done.1), kind=kOutput, calls=%fused_computation.18 | convolution fusion | flops 402718720 | bytes 1835009 | tf_op jit(solution)/shard_map/dot_general | solution.py:288
  184.4 0.0 all-gather.2.cloned.1.call-done
  184.4 20.9 %conditional.1 = (f32[4096,128]{1,0:T(8,128)}) conditional(s32[]{:T(128)} %convert_element_type.3, (f32[128,512]{1,0:T(8,128)S(1)}, f32[512,512]{1,0:T(8,128)}, f32[4096,512]{1,0:T(8,128)}, f32[4096,128]{1,0:T(8,128)}, s32[]{:T(128)}) %tuple.42, (s32[]{:T(128)}, f32[512,512]{1,0:T(8,128)}, f32[4096,512]{1,0:T(8,128)}, s32[]{:T(128)}, ...), branch_computations={%region_4.6_spmd, %region_5.7_spmd} | conditional | flops 3624468480 | bytes 23592976 | solution.py:305
  184.8 2.5 %copy.20 = f32[512,512]{0,1:T(8,128)} copy(f32[512,512]{1,0:T(8,128)} %get-tuple-element.95) | data formatting | bytes 2097152 | tf_op jit(solution)/shard_map
  187.4 13.3 %convolution_bitcast_fusion.1 = f32[4096,128]{0,1:T(8,128)} fusion(f32[4096,512]{1,0:T(8,128)} %get-tuple-element.50, f32[512,512]{1,0:T(8,128)} %get-tuple-element.48, s32[]{:T(128)S(6)} %select_n.63), kind=kOutput, calls=%fused_computation.6 | convolution fusion | flops 3221225472 | bytes 10747908 | tf_op jit(solution)/shard_map/cond/branch_1_fun/dot_general | solution.py:295
  200.6 1.8 fusion.2
  202.5 2.9 %copy.23 = f32[4096,128]{1,0:T(8,128)} copy(f32[4096,128]{0,1:T(8,128)} %fusion.2) | data formatting | bytes 4194304 | tf_op jit(solution)/shard_map/cond
  (7 shorter events, 0.0 us)
Async XLA Ops:
  6.5 2.4 %copy-start = (f32[1,6144,128]{2,1,0:T(8,128)S(1)}, f32[1,6144,128]{2,1,0:T(8,128)}, u32[]{:S(2)}) copy-start(f32[1,6144,128]{2,1,0:T(8,128)} %param.8) | copy-start | bytes 9437188
  6.5 177.9 %all-gather.2.cloned.1.call-start = ((), (), s32[]{:S(2)}) async-start(), calls=%async_computation | async-start | bytes 8519680 | tf_op jit(solution)/shard_map/all_gather | solution.py:285
  10.9 4.6 %copy-start.3 = (s32[1,48]{1,0:T(1,128)S(1)}, s32[1,48]{1,0:T(1,128)}, u32[]{:S(2)}) copy-start(s32[1,48]{1,0:T(1,128)} %param.9) | copy-start | bytes 580
  14.1 6.2 %collective-permute-start = (f32[4096,128]{1,0:T(8,128)}, f32[4096,128]{1,0:T(8,128)}, u32[]{:S(2)}, u32[]{:S(2)}) collective-permute-start(f32[4096,128]{1,0:T(8,128)} %bitcast.6), channel_id=1, source_target_pairs={{0,64},{64,0},{1,65},{65,1},{2,66},{66,2},{3,67},{67,3},{4,68},{68... | collective-permute-start | bytes 6291464 | tf_op jit(solution)/shard_map/ppermute | solution.py:259
  18.3 2.2 %copy-start.2 = (f32[4096,128]{1,0:T(8,128)S(1)}, f32[4096,128]{1,0:T(8,128)}, u32[]{:S(2)}) copy-start(f32[4096,128]{1,0:T(8,128)} %param.7) | copy-start | bytes 6291460
  22.4 1.4 copy-start.1
  25.4 48.0 %collective-permute-start.3 = (f32[64,512]{0,1:T(8,128)}, f32[64,512]{0,1:T(8,128)}, u32[]{:S(2)}, u32[]{:S(2)}) collective-permute-start(f32[64,512]{0,1:T(8,128)} %get-tuple-element.101), channel_id=1, source_target_pairs={{0,0},{1,2},{2,4},{3,6},{4,8},{5,10},{6,12},{7,14},{8,16},{9,18},{... | collective-permute-start | bytes 393224 | tf_op jit(solution)/shard_map/ppermute | solution.py:277
  26.7 46.7 %collective-permute-start.2 = (f32[64,512]{0,1:T(8,128)}, f32[64,512]{0,1:T(8,128)}, u32[]{:S(2)}, u32[]{:S(2)}) collective-permute-start(f32[64,512]{0,1:T(8,128)} %get-tuple-element.102), channel_id=1, source_target_pairs={{0,1},{1,3},{2,5},{3,7},{4,9},{5,11},{6,13},{7,15},{8,17},{9,19},{... | collective-permute-start | bytes 393224 | tf_op jit(solution)/shard_map/ppermute | solution.py:277
  76.8 104.9 %collective-permute-start.1 = (f32[128,512]{0,1:T(8,128)S(1)}, f32[128,512]{0,1:T(8,128)}, u32[]{:S(2)}, u32[]{:S(2)}) collective-permute-start(f32[128,512]{0,1:T(8,128)S(1)} %get-tuple-element.100), channel_id=1, source_target_pairs={{0,64},{1,65},{2,66},{3,67},{4,68},{5,69},{6,70},{7,71},{8,72},{9,... | collective-permute-start | bytes 786440 | tf_op jit(solution)/shard_map/ppermute | solution.py:282
Sparse Core Ops, SparseCore 0:
  76.9 80.7 all-gather.1

commit v11 on v9

--- a/solution.py
+++ b/solution.py
@@ -146,7 +146,7 @@
         ],
         compiler_params=pltpu.CompilerParams(has_side_effects=True),
     )(top)
-    return gathered.reshape(n_src, per_src, rows, cols).transpose(1, 2, 0, 3).reshape(S, S)
+    return gathered
 
 
 PANEL = 8
@@ -162,13 +162,17 @@
 
 
 def chol_inv_kernel(a_ref, l_ref, linv_ref, w_ref, d_ref, e_ref, ut_ref, x_ref):
-    n = a_ref.shape[0]
+    n = w_ref.shape[0]
     b = d_ref.shape[0]
     nb = n // b
     lane = lax.broadcasted_iota(jnp.int32, (PANEL, b), 1)
     sub = lax.broadcasted_iota(jnp.int32, (PANEL, 1), 0)
     eye = (lax.broadcasted_iota(jnp.int32, (b, b), 0) == lax.broadcasted_iota(jnp.int32, (b, b), 1)).astype(jnp.float32)
-    w_ref[...] = a_ref[...]
+    n_slots, rows, cols = a_ref.shape
+    per_src = n_slots // (n // cols)
+    for slot in range(n_slots):
+        c, k = divmod(slot, per_src)
+        w_ref[k * rows:(k + 1) * rows, c * cols:(c + 1) * cols] = a_ref[slot]
     l_ref[...] = jnp.zeros_like(l_ref)
     linv_ref[...] = jnp.zeros_like(linv_ref)
 
@@ -219,8 +223,7 @@
             linv_ref[i * b:(i + 1) * b, j * b:(j + 1) * b] = -_mm(linv_ref[i * b:(i + 1) * b, i * b:(i + 1) * b], acc)
 
 
-def chol_inv(a, b=128):
-    n = a.shape[0]
+def chol_inv(a, n, b=128):
     return pl.pallas_call(
         chol_inv_kernel,
         out_shape=(jax.ShapeDtypeStruct((n, n), jnp.float32), jax.ShapeDtypeStruct((n, n), jnp.float32)),
@@ -270,12 +273,13 @@
     my_piece = pieces[0]
     for part in range(1, per_block):
         my_piece = jnp.where(front % per_block == part, pieces[part], my_piece)
-    pivot = broadcast_pivot(top, n_front)
     partner_rows = lax.ppermute(panel_rows, "leaf", [(0, 1)])
     col_rows = jnp.where(leaf == 0, panel_rows, partner_rows)
+    col_rows, top = lax.optimization_barrier((col_rows, top))
+    pivot = broadcast_pivot(top, n_front)
     my_piece, pivot = lax.optimization_barrier((my_piece, pivot))
     panel = lax.all_gather(my_piece, "front", tiled=True)
-    factor, inverse = chol_inv(pivot)
+    factor, inverse = chol_inv(pivot, S)
 
     col_solved = lax.dot_general(col_rows, inverse, (((1,), (1,)), ((), ())), precision=HIGHEST)
 

time: 189 us -> 193 us (1.021)
  waiting for transfers between devices: 0.05 us -> 5.92 us
  local copies, waits for them, and re-layouts: 17.3 us -> 13.3 us
    ppermute x2, waiting for transfers between devices: 0.01 us -> 5.88 us  [per_device(): lax.ppermute(panel_rows[part * piece:(part + 1) * piece], ('leaf', 'front...]
    reshape x1 -> x0, local copies, waits for them, and re-layouts: 1.93 us -> none  [broadcast_pivot(): gathered.reshape(n_src, per_src, rows, cols).transpose(1, 2, 0, 3)]
  transfers between devices with their start and end apart: 5 -> 5, of which waited for: 0 -> 1; matrix products, arithmetic and copies ran while one was open for 6% -> 5% of each run, Pallas kernels for 65% -> 41%
where the time goes in v11:
time: 193 us; the launch traced here: 191 us
  Pallas kernels  121 us (63%)
  matrix products  15.8 us (8%)
  other arithmetic  15.5 us (8%)
  between operations  13.5 us (7%)
  local copies, waits for them, and re-layouts  13.3 us (7%)
  waiting for transfers between devices  5.92 us (3%)
  starting transfers between devices  5.35 us (3%)
    pallas_call x1, Pallas kernels, chol_inv(): pl.pallas_call(chol_inv_kernel, out_shape=(jax.ShapeDtypeStruct((n, n), j...  78.2 us
    pallas_call x1, Pallas kernels, broadcast_pivot(): pl.pallas_call(functools.partial(pivot_kernel, n_front, n_src), out_shape...  43.2 us
    dot_general x1, matrix products, pivot_columns(): lax.dot_general(panel, inv_rows, (((1,), (1,)), ((), ())), precision=HIGH...  13.3 us
    ppermute x2, waiting for transfers between devices, per_device(): lax.ppermute(panel_rows[part * piece:(part + 1) * piece], ('leaf', 'front...  5.88 us
    select_n x2, other arithmetic, gather_half(): picked = jnp.where(found[:, None, None], picked, jnp.zeros_like(picked))  5.25 us
    gather x2, local copies, waits for them, and re-layouts, gather_half(): picked = jnp.take(blocks, index, axis=0)  3.98 us
  transfers between devices with their start and end apart: 5, of which 1 were waited for; matrix products, arithmetic and copies ran while one was open for 5% of the time, Pallas kernels for 41%

profile of v11, /device:TPU:1, one launch (start us, length us, event | category | flops | bytes accessed | tf_op | source)
XLA Modules:
  0.0 191.3 jit_solution(569460980101403726)
XLA Ops:
  6.5 0.0 copy-start
  6.5 0.0 all-gather.2.cloned.1.call-start
  6.5 1.5 compare_reduce_fusion
  8.1 0.8 compare_reduce_fusion.3
  8.9 0.0 copy-done
  8.9 2.0 %gather_fusion.1 = f32[32,128,128]{2,1,0:T(8,128)} fusion(f32[48,128,128]{2,1,0:T(8,128)S(1)} %bitcast.31, s32[1024]{0:T(1024)S(1)} %pad_clamp_fusion), kind=kCustom, calls=%fused_computation.1.clone | custom fusion | bytes 4194432 | tf_op jit(solution)/shard_map/jit(_take)/gather | solution.py:21
  10.9 0.0 copy-start.4
  10.9 3.2 %select_select_fusion = f32[32,128,128]{2,1,0:T(8,128)} fusion(f32[32,128,128]{2,1,0:T(8,128)} %gather_fusion.1, pred[32]{0:T(512)(128)(4,1)S(1)} %compare_and_fusion, pred[32]{0:T(512)(128)(4,1)S(1)} %get-tuple-element.102), kind=kLoop, calls=%fused_computation.15 | loop fusion | flops 1048576 | bytes 4194368 | tf_op jit(solution)/shard_map/jit(_where)/select_n | solution.py:22
  14.1 1.4 collective-permute-start
  15.6 0.0 copy-done.4
  15.6 0.7 compare_reduce_fusion.2
  16.3 2.0 %gather_fusion = f32[32,128,128]{2,1,0:T(8,128)} fusion(f32[48,128,128]{2,1,0:T(8,128)S(1)} %bitcast.30, s32[1024]{0:T(1024)S(1)} %pad_clamp_fusion.1), kind=kCustom, calls=%fused_computation.clone | custom fusion | bytes 4194432 | tf_op jit(solution)/shard_map/jit(_take)/gather | solution.py:21
  18.3 0.0 copy-start.2
  18.3 2.0 %select_select_fusion.1 = f32[32,128,128]{2,1,0:T(8,128)S(1)} fusion(f32[32,128,128]{2,1,0:T(8,128)} %gather_fusion, pred[32]{0:T(512)(128)(4,1)S(1)} %compare_and_fusion.1, pred[32]{0:T(512)(128)(4,1)S(1)} %get-tuple-element.101), kind=kLoop, calls=%fused_computation.16 | loop fusion | flops 1048576 | bytes 4194368 | tf_op jit(solution)/shard_map/jit(_where)/select_n | solution.py:22
  20.3 0.0 collective-permute-done
  20.3 0.2 copy-done.2
  20.5 1.9 fusion.6
  22.4 0.0 copy-start.1
  22.4 1.4 copy-done.1
  23.8 0.7 fusion.7
  24.5 0.9 fusion.8
  25.4 1.3 collective-permute-start.3
  26.7 1.4 collective-permute-start.2
  28.0 1.3 collective-permute-start.1
  29.3 5.9 %collective-permute-done.3 = f32[64,512]{0,1:T(8,128)} collective-permute-done((f32[64,512]{0,1:T(8,128)}, f32[64,512]{0,1:T(8,128)}, u32[]{:S(2)}, u32[]{:S(2)}) %collective-permute-start.3) | collective-permute-done | bytes 131104 | tf_op jit(solution)/shard_map/ppermute | solution.py:272
  35.2 0.0 collective-permute-done.2
  35.2 1.7 broadcast_select_fusion
  36.9 0.0 collective-permute-done.1
  36.9 0.0 copy-start.3
  36.9 1.8 broadcast_select_fusion.1
  38.7 43.2 %shard_map.39.a_ref = f32[64,32,128]{2,1,0:T(8,128)} custom-call(f32[512,128]{1,0:T(8,128)} %get-tuple-element.64.top_ref), custom_call_target="tpu_custom_call" | custom-call | tf_op jit(solution)/shard_map/pallas_call | solution.py:133
  81.9 0.0 copy-done.3
  82.0 0.8 copy.15
  82.7 0.0 all-gather.2.cloned.1.call-update
  82.8 78.2 %shard_map.40 = (f32[512,512]{1,0:T(8,128)}, f32[512,512]{1,0:T(8,128)}) custom-call(f32[64,32,128]{2,1,0:T(8,128)} %shard_map.39.a_ref), custom_call_target="tpu_custom_call" | custom-call | tf_op jit(solution)/shard_map/pallas_call | solution.py:227
  161.0 2.6 %fusion.10 = f32[128,512]{1,0:T(8,128)S(1)} fusion(f32[128,512]{0,1:T(8,128)} %broadcast_select_fusion.1, f32[512,512]{1,0:T(8,128)} %get-tuple-element.66), kind=kOutput, calls=%fused_computation.35 | convolution fusion | flops 402653184 | bytes 1572864 | tf_op jit(solution)/shard_map/dot_general | solution.py:284
  163.5 0.0 all-gather.2.cloned.1.call-done
  163.5 20.9 %conditional.1 = (f32[4096,128]{1,0:T(8,128)}) conditional(s32[]{:T(128)} %convert_element_type.3, (f32[128,512]{1,0:T(8,128)S(1)}, f32[512,512]{1,0:T(8,128)}, f32[4096,512]{1,0:T(8,128)}, f32[4096,128]{1,0:T(8,128)}, s32[]{:T(128)}) %tuple.44, (s32[]{:T(128)}, f32[512,512]{1,0:T(8,128)}, f32[4096,512]{1,0:T(8,128)}, s32[]{:T(128)}, ...), branch_computations={%region_4.6_spmd, %region_5.7_spmd} | conditional | flops 3624468480 | bytes 23592976 | solution.py:301
  164.0 2.5 %copy.17 = f32[512,512]{0,1:T(8,128)} copy(f32[512,512]{1,0:T(8,128)} %get-tuple-element.99) | data formatting | bytes 2097152 | tf_op jit(solution)/shard_map
  166.5 13.3 %convolution_bitcast_fusion.1 = f32[4096,128]{0,1:T(8,128)} fusion(f32[4096,512]{1,0:T(8,128)} %get-tuple-element.50, f32[512,512]{1,0:T(8,128)} %get-tuple-element.48, s32[]{:T(128)S(6)} %select_n.63), kind=kOutput, calls=%fused_computation.6 | convolution fusion | flops 3221225472 | bytes 10747908 | tf_op jit(solution)/shard_map/cond/branch_1_fun/dot_general | solution.py:291
  179.8 1.8 fusion.2
  181.6 2.9 %copy.20 = f32[4096,128]{1,0:T(8,128)} copy(f32[4096,128]{0,1:T(8,128)} %fusion.2) | data formatting | bytes 4194304 | tf_op jit(solution)/shard_map/cond
  (7 shorter events, 0.0 us)
Async XLA Ops:
  6.5 2.4 %copy-start = (f32[1,6144,128]{2,1,0:T(8,128)S(1)}, f32[1,6144,128]{2,1,0:T(8,128)}, u32[]{:S(2)}) copy-start(f32[1,6144,128]{2,1,0:T(8,128)} %param.8) | copy-start | bytes 9437188
  6.5 157.0 %all-gather.2.cloned.1.call-start = ((), (), s32[]{:S(2)}) async-start(), calls=%async_computation | async-start | bytes 8519680 | tf_op jit(solution)/shard_map/all_gather | solution.py:281
  10.9 4.6 %copy-start.4 = (s32[1,48]{1,0:T(1,128)S(1)}, s32[1,48]{1,0:T(1,128)}, u32[]{:S(2)}) copy-start(s32[1,48]{1,0:T(1,128)} %param.9) | copy-start | bytes 580
  14.1 6.2 %collective-permute-start = (f32[4096,128]{1,0:T(8,128)}, f32[4096,128]{1,0:T(8,128)}, u32[]{:S(2)}, u32[]{:S(2)}) collective-permute-start(f32[4096,128]{1,0:T(8,128)} %bitcast.6), channel_id=1, source_target_pairs={{0,64},{64,0},{1,65},{65,1},{2,66},{66,2},{3,67},{67,3},{4,68},{68... | collective-permute-start | bytes 6291464 | tf_op jit(solution)/shard_map/ppermute | solution.py:254
  18.3 2.2 %copy-start.2 = (f32[4096,128]{1,0:T(8,128)S(1)}, f32[4096,128]{1,0:T(8,128)}, u32[]{:S(2)}) copy-start(f32[4096,128]{1,0:T(8,128)} %param.7) | copy-start | bytes 6291460
  22.4 1.4 copy-start.1
  25.4 9.8 %collective-permute-start.3 = (f32[64,512]{0,1:T(8,128)}, f32[64,512]{0,1:T(8,128)}, u32[]{:S(2)}, u32[]{:S(2)}) collective-permute-start(f32[64,512]{0,1:T(8,128)} %get-tuple-element.105), channel_id=1, source_target_pairs={{0,0},{1,2},{2,4},{3,6},{4,8},{5,10},{6,12},{7,14},{8,16},{9,18},{... | collective-permute-start | bytes 393224 | tf_op jit(solution)/shard_map/ppermute | solution.py:272
  26.7 8.5 %collective-permute-start.2 = (f32[64,512]{0,1:T(8,128)}, f32[64,512]{0,1:T(8,128)}, u32[]{:S(2)}, u32[]{:S(2)}) collective-permute-start(f32[64,512]{0,1:T(8,128)} %get-tuple-element.106), channel_id=1, source_target_pairs={{0,1},{1,3},{2,5},{3,7},{4,9},{5,11},{6,13},{7,15},{8,17},{9,19},{... | collective-permute-start | bytes 393224 | tf_op jit(solution)/shard_map/ppermute | solution.py:272
  28.0 8.9 %collective-permute-start.1 = (f32[128,512]{0,1:T(8,128)S(1)}, f32[128,512]{0,1:T(8,128)}, u32[]{:S(2)}, u32[]{:S(2)}) collective-permute-start(f32[128,512]{0,1:T(8,128)S(1)} %get-tuple-element.104), channel_id=1, source_target_pairs={{0,64},{1,65},{2,66},{3,67},{4,68},{5,69},{6,70},{7,71},{8,72},{9,... | collective-permute-start | bytes 786440 | tf_op jit(solution)/shard_map/ppermute | solution.py:276
  36.9 45.1 %copy-start.3 = (f32[64,512]{0,1:T(8,128)S(1)}, f32[64,512]{0,1:T(8,128)}, u32[]{:S(2)}) copy-start(f32[64,512]{0,1:T(8,128)} %broadcast_select_fusion) | copy-start | bytes 393220
Sparse Core Ops, SparseCore 0:
  82.9 80.2 all-gather.1

commit v12 on v11

--- a/solution.py
+++ b/solution.py
@@ -23,130 +23,94 @@
     return picked.reshape(half_blocks * BLK, blocks.shape[2])
 
 
-def pivot_kernel(n_front, n_src, top_ref, out_ref, chunk, sem_a, sem_b, send_a, send_b, recv_g, send_g):
+def pivot_kernel(dims, top_ref, out_ref, own_sem, peer_sem, send_y, send_z, send_leaf, send_x):
+    n_z, n_y, n_x = dims
     leaf = lax.axis_index("leaf")
     me = lax.axis_index("front")
-    per_src = n_front // n_src
-    rows = chunk.shape[0]
-
-    @pl.when((leaf == 0) & (me < n_src))
-    def _():
-        for k in range(per_src):
-            src = top_ref.at[pl.ds(k * rows, rows)]
-            dst = me * per_src + k
-            if k == 0:
-                @pl.when(me == 0)
-                def _():
-                    pltpu.make_async_copy(src, chunk, sem_a).start()
-
-                @pl.when(me != 0)
-                def _():
-                    pltpu.make_async_remote_copy(
-                        src, chunk, send_a.at[k], sem_a, device_id=(0, dst), device_id_type=MESH
-                    ).start()
-            else:
-                pltpu.make_async_remote_copy(
-                    src, chunk, send_a.at[k], sem_a, device_id=(0, dst), device_id_type=MESH
-                ).start()
-
-    @pl.when((leaf == 0) & (me == 0))
-    def _():
-        pltpu.make_async_copy(top_ref.at[pl.ds(0, rows)], chunk, sem_a).wait()
-
-    @pl.when((leaf == 0) & (me != 0))
-    def _():
+    x = me % n_x
+    y = (me // n_x) % n_y
+    z = me // (n_x * n_y)
+    mine = out_ref.at[x]
+
+    def remote(dst_leaf, dst_front, sem):
+        return pltpu.make_async_remote_copy(
+            mine, mine, sem, own_sem, device_id=(dst_leaf, dst_front), device_id_type=MESH
+        )
+
+    source = (leaf == 0) & (y == 0) & (z == 0)
+
+    @pl.when(source)
+    def _():
+        pltpu.make_async_copy(top_ref, mine, own_sem).start()
+        pltpu.make_async_copy(top_ref, mine, own_sem).wait()
+        for dy in range(1, n_y):
+            remote(0, dy * n_x + x, send_y.at[dy]).start()
+
+    @pl.when(jnp.logical_not(source))
+    def _():
+        remote(0, me, send_y.at[0]).wait_recv()
+
+    @pl.when((leaf == 0) & (z == 0))
+    def _():
+        for dz in range(1, n_z):
+            remote(0, dz * n_x * n_y + y * n_x + x, send_z.at[dz]).start()
+
+    @pl.when(leaf == 0)
+    def _():
+        remote(1, me, send_leaf).start()
+
+    for dx in range(1, n_x):
+        dst = me - x + (x + dx) % n_x
         pltpu.make_async_remote_copy(
-            top_ref.at[pl.ds(0, rows)], chunk, send_a.at[0], sem_a, device_id=(0, me), device_id_type=MESH
+            mine, mine, send_x.at[dx], peer_sem.at[x], device_id=(leaf, dst), device_id_type=MESH
+        ).start()
+
+    for dx in range(1, n_x):
+        src = (x + dx) % n_x
+        pltpu.make_async_remote_copy(
+            out_ref.at[src], out_ref.at[src], send_x.at[dx], peer_sem.at[src],
+            device_id=(leaf, me - x + src), device_id_type=MESH
         ).wait_recv()
 
+    for dx in range(1, n_x):
+        dst = me - x + (x + dx) % n_x
+        pltpu.make_async_remote_copy(
+            mine, mine, send_x.at[dx], peer_sem.at[x], device_id=(leaf, dst), device_id_type=MESH
+        ).wait_send()
+
     @pl.when(leaf == 0)
     def _():
-        pltpu.make_async_remote_copy(
-            chunk, chunk, send_b, sem_b, device_id=(1, me), device_id_type=MESH
-        ).start()
-
-    @pl.when(leaf == 1)
-    def _():
-        pltpu.make_async_remote_copy(
-            chunk, chunk, send_b, sem_b, device_id=(0, me), device_id_type=MESH
-        ).wait_recv()
-
-    pltpu.make_async_copy(chunk, out_ref.at[me], recv_g.at[me]).start()
-
-    def send(j, carry):
-        dst = lax.rem(me + j, n_front)
-        pltpu.make_async_remote_copy(
-            chunk, out_ref.at[me], send_g.at[j], recv_g.at[me], device_id=(leaf, dst), device_id_type=MESH
-        ).start()
-        return carry
-
-    lax.fori_loop(1, n_front, send, 0)
-
-    pltpu.make_async_copy(chunk, out_ref.at[me], recv_g.at[me]).wait()
-
-    def receive(j, carry):
-        src = lax.rem(me + j, n_front)
-        pltpu.make_async_remote_copy(
-            chunk, out_ref.at[src], send_g.at[j], recv_g.at[src], device_id=(leaf, src), device_id_type=MESH
-        ).wait_recv()
-        return carry
-
-    lax.fori_loop(1, n_front, receive, 0)
-
-    def sent(j, carry):
-        dst = lax.rem(me + j, n_front)
-        pltpu.make_async_remote_copy(
-            chunk, out_ref.at[me], send_g.at[j], recv_g.at[me], device_id=(leaf, dst), device_id_type=MESH
-        ).wait_send()
-        return carry
-
-    lax.fori_loop(1, n_front, sent, 0)
-
-    @pl.when(leaf == 0)
-    def _():
-        pltpu.make_async_remote_copy(
-            chunk, chunk, send_b, sem_b, device_id=(1, me), device_id_type=MESH
-        ).wait_send()
-
-    @pl.when((leaf == 0) & (me < n_src))
-    def _():
-        for k in range(per_src):
-            src = top_ref.at[pl.ds(k * rows, rows)]
-            dst = me * per_src + k
-            if k == 0:
-                @pl.when(me != 0)
-                def _():
-                    pltpu.make_async_remote_copy(
-                        src, chunk, send_a.at[k], sem_a, device_id=(0, dst), device_id_type=MESH
-                    ).wait_send()
-            else:
-                pltpu.make_async_remote_copy(
-                    src, chunk, send_a.at[k], sem_a, device_id=(0, dst), device_id_type=MESH
-                ).wait_send()
-
-
-def broadcast_pivot(top, n_front):
-    cols = top.shape[1]
+        remote(1, me, send_leaf).wait_send()
+
+    @pl.when((leaf == 0) & (z == 0))
+    def _():
+        for dz in range(1, n_z):
+            remote(0, dz * n_x * n_y + y * n_x + x, send_z.at[dz]).wait_send()
+
+    @pl.when(source)
+    def _():
+        for dy in range(1, n_y):
+            remote(0, dy * n_x + x, send_y.at[dy]).wait_send()
+
+
+def broadcast_pivot(top, dims):
+    rows, cols = top.shape
     n_src = S // cols
-    per_src = n_front // n_src
-    rows = S // per_src
-    gathered = pl.pallas_call(
-        functools.partial(pivot_kernel, n_front, n_src),
-        out_shape=jax.ShapeDtypeStruct((n_front, rows, cols), jnp.float32),
+    return pl.pallas_call(
+        functools.partial(pivot_kernel, dims),
+        out_shape=jax.ShapeDtypeStruct((n_src, rows, cols), jnp.float32),
         in_specs=[pl.BlockSpec(memory_space=pltpu.VMEM)],
         out_specs=pl.BlockSpec(memory_space=pltpu.VMEM),
         scratch_shapes=[
-            pltpu.VMEM((rows, cols), jnp.float32),
             pltpu.SemaphoreType.DMA,
+            pltpu.SemaphoreType.DMA((n_src,)),
+            pltpu.SemaphoreType.DMA((dims[1],)),
+            pltpu.SemaphoreType.DMA((dims[0],)),
             pltpu.SemaphoreType.DMA,
-            pltpu.SemaphoreType.DMA((per_src,)),
-            pltpu.SemaphoreType.DMA,
-            pltpu.SemaphoreType.DMA((n_front,)),
-            pltpu.SemaphoreType.DMA((n_front,)),
+            pltpu.SemaphoreType.DMA((n_src,)),
         ],
         compiler_params=pltpu.CompilerParams(has_side_effects=True),
     )(top)
-    return gathered
 
 
 PANEL = 8
@@ -168,11 +132,9 @@
     lane = lax.broadcasted_iota(jnp.int32, (PANEL, b), 1)
     sub = lax.broadcasted_iota(jnp.int32, (PANEL, 1), 0)
     eye = (lax.broadcasted_iota(jnp.int32, (b, b), 0) == lax.broadcasted_iota(jnp.int32, (b, b), 1)).astype(jnp.float32)
-    n_slots, rows, cols = a_ref.shape
-    per_src = n_slots // (n // cols)
-    for slot in range(n_slots):
-        c, k = divmod(slot, per_src)
-        w_ref[k * rows:(k + 1) * rows, c * cols:(c + 1) * cols] = a_ref[slot]
+    n_cb, _, cols = a_ref.shape
+    for c in range(n_cb):
+        w_ref[:, c * cols:(c + 1) * cols] = a_ref[c]
     l_ref[...] = jnp.zeros_like(l_ref)
     linv_ref[...] = jnp.zeros_like(linv_ref)
 
@@ -275,8 +237,7 @@
         my_piece = jnp.where(front % per_block == part, pieces[part], my_piece)
     partner_rows = lax.ppermute(panel_rows, "leaf", [(0, 1)])
     col_rows = jnp.where(leaf == 0, panel_rows, partner_rows)
-    col_rows, top = lax.optimization_barrier((col_rows, top))
-    pivot = broadcast_pivot(top, n_front)
+    pivot = broadcast_pivot(top, (4, 4, 4))
     my_piece, pivot = lax.optimization_barrier((my_piece, pivot))
     panel = lax.all_gather(my_piece, "front", tiled=True)
     factor, inverse = chol_inv(pivot, S)

time: 193 us -> 192 us (level)
  the two profiles are of different devices: /device:TPU:1 before, /device:TPU:80 now
where the time goes in v12:
time: 192 us; the launch traced here: 191 us
  Pallas kernels  123 us (64%)
  matrix products  18.2 us (9%)
  local copies, waits for them, and re-layouts  14.6 us (8%)
  other arithmetic  13.6 us (7%)
  between operations  13.5 us (7%)
  starting transfers between devices  8.15 us (4%)
    pallas_call x1, Pallas kernels, chol_inv(): pl.pallas_call(chol_inv_kernel, out_shape=(jax.ShapeDtypeStruct((n, n), j...  78.2 us
    pallas_call x1, Pallas kernels, broadcast_pivot(): pl.pallas_call(functools.partial(pivot_kernel, dims), out_shape=jax.Shape...  44.5 us
    dot_general x1, matrix products, other_columns(): out = assembled - jnp.dot(panel, weights, precision=HIGHEST)  13.7 us
    select_n x2, other arithmetic, gather_half(): picked = jnp.where(found[:, None, None], picked, jnp.zeros_like(picked))  5.25 us
    ppermute x2, starting transfers between devices, per_device(): lax.ppermute(panel_rows[part * piece:(part + 1) * piece], ('leaf', 'front...  4.88 us
    gather x2, local copies, waits for them, and re-layouts, gather_half(): picked = jnp.take(blocks, index, axis=0)  3.98 us
  transfers between devices with their start and end apart: 5, of which 0 were waited for; matrix products, arithmetic and copies ran while one was open for 4% of the time, Pallas kernels for 64%

profile of v12, /device:TPU:80, one launch (start us, length us, event | category | flops | bytes accessed | tf_op | source)
XLA Modules:
  0.0 191.1 jit_solution(18101833875985603396)
XLA Ops:
  6.5 0.0 copy-start
  6.5 0.0 all-gather.2.cloned.1.call-start
  6.5 1.5 compare_reduce_fusion
  8.1 0.8 compare_reduce_fusion.3
  8.9 0.0 copy-done
  8.9 2.0 %gather_fusion.1 = f32[32,128,128]{2,1,0:T(8,128)} fusion(f32[48,128,128]{2,1,0:T(8,128)S(1)} %bitcast.33, s32[1024]{0:T(1024)S(1)} %pad_clamp_fusion), kind=kCustom, calls=%fused_computation.1.clone | custom fusion | bytes 4194432 | tf_op jit(solution)/shard_map/jit(_take)/gather | solution.py:21
  10.9 0.0 copy-start.3
  10.9 3.2 %select_select_fusion = f32[32,128,128]{2,1,0:T(8,128)} fusion(f32[32,128,128]{2,1,0:T(8,128)} %gather_fusion.1, pred[32]{0:T(512)(128)(4,1)S(1)} %compare_and_fusion, pred[32]{0:T(512)(128)(4,1)S(1)} %get-tuple-element.98), kind=kLoop, calls=%fused_computation.15 | loop fusion | flops 1048576 | bytes 4194368 | tf_op jit(solution)/shard_map/jit(_where)/select_n | solution.py:22
  14.1 0.0 collective-permute-start
  14.1 0.0 copy-done.3
  14.1 0.7 compare_reduce_fusion.2
  14.9 2.0 %gather_fusion = f32[32,128,128]{2,1,0:T(8,128)} fusion(f32[48,128,128]{2,1,0:T(8,128)S(1)} %bitcast.32, s32[1024]{0:T(1024)S(1)} %pad_clamp_fusion.1), kind=kCustom, calls=%fused_computation.clone | custom fusion | bytes 4194432 | tf_op jit(solution)/shard_map/jit(_take)/gather | solution.py:21
  16.8 0.0 copy-start.2
  16.9 2.0 %select_select_fusion.1 = f32[32,128,128]{2,1,0:T(8,128)S(1)} fusion(f32[32,128,128]{2,1,0:T(8,128)} %gather_fusion, pred[32]{0:T(512)(128)(4,1)S(1)} %compare_and_fusion.1, pred[32]{0:T(512)(128)(4,1)S(1)} %get-tuple-element.97), kind=kLoop, calls=%fused_computation.16 | loop fusion | flops 1048576 | bytes 4194368 | tf_op jit(solution)/shard_map/jit(_where)/select_n | solution.py:22
  18.9 0.0 collective-permute-done
  18.9 0.2 copy-done.2
  19.1 1.9 fusion.6
  20.9 0.0 copy-start.1
  20.9 1.4 copy-done.1
  22.3 0.7 fusion.12
  23.1 0.9 fusion.13
  23.9 1.9 collective-permute-start.3
  25.8 3.0 %collective-permute-start.2 = (f32[64,512]{0,1:T(8,128)}, f32[64,512]{0,1:T(8,128)}, u32[]{:S(2)}, u32[]{:S(2)}) collective-permute-start(f32[64,512]{0,1:T(8,128)} %get-tuple-element.102), channel_id=1, source_target_pairs={{0,1},{1,3},{2,5},{3,7},{4,9},{5,11},{6,13},{7,15},{8,17},{9,19},{... | collective-permute-start | bytes 393224 | tf_op jit(solution)/shard_map/ppermute | solution.py:234
  28.8 44.5 %shard_map.39.a_ref = f32[4,512,128]{2,1,0:T(8,128)} custom-call(f32[512,128]{1,0:T(8,128)} %get-tuple-element.99.top_ref), custom_call_target="tpu_custom_call" | custom-call | tf_op jit(solution)/shard_map/pallas_call | solution.py:99
  73.3 0.0 collective-permute-done.3
  73.4 0.0 collective-permute-done.2
  73.4 1.7 broadcast_select_fusion
  75.1 1.7 copy.15
  76.8 0.0 all-gather.2.cloned.1.call-update
  76.8 3.3 %collective-permute-start.1 = (f32[128,512]{0,1:T(8,128)S(1)}, f32[128,512]{0,1:T(8,128)}, u32[]{:S(2)}, u32[]{:S(2)}) collective-permute-start(f32[128,512]{0,1:T(8,128)S(1)} %get-tuple-element.100), channel_id=1, source_target_pairs={{0,64},{1,65},{2,66},{3,67},{4,68},{5,69},{6,70},{7,71},{8,72},{9,... | collective-permute-start | bytes 786440 | tf_op jit(solution)/shard_map/ppermute | solution.py:238
  80.1 78.2 %shard_map.40 = (f32[512,512]{1,0:T(8,128)}, f32[512,512]{1,0:T(8,128)}) custom-call(f32[4,512,128]{2,1,0:T(8,128)} %shard_map.39.a_ref), custom_call_target="tpu_custom_call" | custom-call | tf_op jit(solution)/shard_map/pallas_call | solution.py:189
  158.3 0.0 collective-permute-done.1
  158.3 2.6 %fusion.7 = f32[128,512]{1,0:T(8,128)S(1)} fusion(f32[512,512]{1,0:T(8,128)} %get-tuple-element.62, f32[128,512]{0,1:T(8,128)} %collective-permute-done.1, pred[]{:T(512)S(6)} %eq.46, f32[4096,128]{1,0:T(8,128)} %copy-done.1), kind=kOutput, calls=%fused_computation.17 | convolution fusion | flops 402718720 | bytes 1835009 | tf_op jit(solution)/shard_map/dot_general | solution.py:245
  160.8 0.0 all-gather.2.cloned.1.call-done
  160.9 23.4 %conditional.1 = (f32[4096,128]{1,0:T(8,128)}) conditional(s32[]{:T(128)} %convert_element_type.3, (f32[128,512]{1,0:T(8,128)S(1)}, f32[512,512]{1,0:T(8,128)}, f32[4096,512]{1,0:T(8,128)}, f32[4096,128]{1,0:T(8,128)}, s32[]{:T(128)}) %tuple.42, (s32[]{:T(128)}, f32[512,512]{1,0:T(8,128)}, f32[4096,512]{1,0:T(8,128)}, s32[]{:T(128)}, ...), branch_computations={%region_4.6_spmd, %region_5.7_spmd} | conditional | flops 3624468480 | bytes 23592976 | solution.py:262
  161.1 2.9 %copy.16 = f32[4096,128]{0,1:T(8,128)} copy(f32[4096,128]{1,0:T(8,128)} %get-tuple-element.89) | data formatting | bytes 4194304 | tf_op jit(solution)/shard_map
  163.9 1.9 %fusion.14 = f32[128,512]{1,0:T(8,128)S(1)} fusion(f32[128,512]{1,0:T(8,128)S(1)} %get-tuple-element.44, f32[512,512]{1,0:T(8,128)} %get-tuple-element.45), kind=kOutput, calls=%fused_computation.38 | convolution fusion | flops 402653184 | bytes 1572864 | tf_op jit(solution)/shard_map/cond/branch_0_fun/dot_general | solution.py:257
  165.9 13.7 %fusion = f32[4096,128]{0,1:T(8,128)} fusion(f32[4096,128]{0,1:T(8,128)} %copy.16, f32[128,512]{1,0:T(8,128)S(1)} %fusion.14, f32[4096,512]{1,0:T(8,128)} %get-tuple-element.46), kind=kOutput, calls=%fused_computation.3 | convolution fusion | flops 3221749760 | bytes 12845056 | tf_op jit(solution)/shard_map/cond/branch_0_fun/dot_general | solution.py:258
  179.6 1.7 fusion.1
  181.3 2.9 %copy.19 = f32[4096,128]{1,0:T(8,128)} copy(f32[4096,128]{0,1:T(8,128)} %fusion.1) | data formatting | bytes 4194304 | tf_op jit(solution)/shard_map/cond
  (7 shorter events, 0.0 us)
Async XLA Ops:
  6.5 2.4 %copy-start = (f32[1,6144,128]{2,1,0:T(8,128)S(1)}, f32[1,6144,128]{2,1,0:T(8,128)}, u32[]{:S(2)}) copy-start(f32[1,6144,128]{2,1,0:T(8,128)} %param.8) | copy-start | bytes 9437188
  6.5 154.3 %all-gather.2.cloned.1.call-start = ((), (), s32[]{:S(2)}) async-start(), calls=%async_computation | async-start | bytes 8519680 | tf_op jit(solution)/shard_map/all_gather | solution.py:242
  10.9 3.2 %copy-start.3 = (s32[1,48]{1,0:T(1,128)S(1)}, s32[1,48]{1,0:T(1,128)}, u32[]{:S(2)}) copy-start(s32[1,48]{1,0:T(1,128)} %param.9) | copy-start | bytes 580
  14.1 4.8 %collective-permute-start = (f32[4096,128]{1,0:T(8,128)}, f32[4096,128]{1,0:T(8,128)}, u32[]{:S(2)}, u32[]{:S(2)}) collective-permute-start(f32[4096,128]{1,0:T(8,128)} %bitcast.6), channel_id=1, source_target_pairs={{0,64},{64,0},{1,65},{65,1},{2,66},{66,2},{3,67},{67,3},{4,68},{68... | collective-permute-start | bytes 6291464 | tf_op jit(solution)/shard_map/ppermute | solution.py:216
  16.8 2.2 %copy-start.2 = (f32[4096,128]{1,0:T(8,128)S(1)}, f32[4096,128]{1,0:T(8,128)}, u32[]{:S(2)}) copy-start(f32[4096,128]{1,0:T(8,128)} %param.7) | copy-start | bytes 6291460
  20.9 1.4 copy-start.1
  23.9 49.4 %collective-permute-start.3 = (f32[64,512]{0,1:T(8,128)}, f32[64,512]{0,1:T(8,128)}, u32[]{:S(2)}, u32[]{:S(2)}) collective-permute-start(f32[64,512]{0,1:T(8,128)} %get-tuple-element.101), channel_id=1, source_target_pairs={{0,0},{1,2},{2,4},{3,6},{4,8},{5,10},{6,12},{7,14},{8,16},{9,18},{... | collective-permute-start | bytes 393224 | tf_op jit(solution)/shard_map/ppermute | solution.py:234
  25.8 47.5 %collective-permute-start.2 = (f32[64,512]{0,1:T(8,128)}, f32[64,512]{0,1:T(8,128)}, u32[]{:S(2)}, u32[]{:S(2)}) collective-permute-start(f32[64,512]{0,1:T(8,128)} %get-tuple-element.102), channel_id=1, source_target_pairs={{0,1},{1,3},{2,5},{3,7},{4,9},{5,11},{6,13},{7,15},{8,17},{9,19},{... | collective-permute-start | bytes 393224 | tf_op jit(solution)/shard_map/ppermute | solution.py:234
  76.8 81.5 %collective-permute-start.1 = (f32[128,512]{0,1:T(8,128)S(1)}, f32[128,512]{0,1:T(8,128)}, u32[]{:S(2)}, u32[]{:S(2)}) collective-permute-start(f32[128,512]{0,1:T(8,128)S(1)} %get-tuple-element.100), channel_id=1, source_target_pairs={{0,64},{1,65},{2,66},{3,67},{4,68},{5,69},{6,70},{7,71},{8,72},{9,... | collective-permute-start | bytes 786440 | tf_op jit(solution)/shard_map/ppermute | solution.py:238
Sparse Core Ops, SparseCore 0:
  76.9 81.3 all-gather.1

commit v13 on v12

--- a/solution.py
+++ b/solution.py
@@ -238,7 +238,6 @@
     partner_rows = lax.ppermute(panel_rows, "leaf", [(0, 1)])
     col_rows = jnp.where(leaf == 0, panel_rows, partner_rows)
     pivot = broadcast_pivot(top, (4, 4, 4))
-    my_piece, pivot = lax.optimization_barrier((my_piece, pivot))
     panel = lax.all_gather(my_piece, "front", tiled=True)
     factor, inverse = chol_inv(pivot, S)
 

time: 192 us -> 204 us (1.062)
  the two profiles are of different devices: /device:TPU:80 before, /device:TPU:81 now
where the time goes in v13:
time: 204 us
  Pallas kernels  132 us (65%)
  matrix products  18.3 us (9%)
  local copies, waits for them, and re-layouts  14.6 us (7%)
  other arithmetic  13.6 us (7%)
  between operations  13.5 us (7%)
  waiting for transfers between devices  6.47 us (3%)
  starting transfers between devices  4.61 us (2%)
    pallas_call x1, Pallas kernels, chol_inv(): pl.pallas_call(chol_inv_kernel, out_shape=(jax.ShapeDtypeStruct((n, n), j...  78.2 us
    pallas_call x1, Pallas kernels, broadcast_pivot(): pl.pallas_call(functools.partial(pivot_kernel, dims), out_shape=jax.Shape...  54.2 us
    dot_general x1, matrix products, other_columns(): out = assembled - jnp.dot(panel, weights, precision=HIGHEST)  13.7 us
    ppermute x2, waiting for transfers between devices, per_device(): lax.ppermute(panel_rows[part * piece:(part + 1) * piece], ('leaf', 'front...  6.43 us
    select_n x2, other arithmetic, gather_half(): picked = jnp.where(found[:, None, None], picked, jnp.zeros_like(picked))  5.25 us
  transfers between devices with their start and end apart: 5, of which 1 were waited for; matrix products, arithmetic and copies ran while one was open for 4% of the time, Pallas kernels for 65%

profile of v13, /device:TPU:81, one launch (start us, length us, event | category | flops | bytes accessed | tf_op | source)
XLA Modules:
  0.0 203.7 jit_solution(10486937666996696917)
XLA Ops:
  6.5 0.0 copy-start
  6.5 0.0 all-gather.2.cloned.1.call-start
  6.5 1.5 compare_reduce_fusion
  8.1 0.8 compare_reduce_fusion.3
  8.9 0.0 copy-done
  8.9 2.0 gather_fusion.1
  10.9 0.0 copy-start.3
  10.9 3.2 %select_select_fusion = f32[32,128,128]{2,1,0:T(8,128)} fusion(f32[32,128,128]{2,1,0:T(8,128)} %gather_fusion.1, pred[32]{0:T(512)(128)(4,1)S(1)} %compare_and_fusion, pred[32]{0:T(512)(128)(4,1)S(1)} %get-tuple-element.94), kind=kLoop, calls=%fused_computation.15 | loop fusion | flops 1048576 | bytes 4194368 | tf_op jit(solution)/shard_map/jit(_where)/select_n | solution.py:22
  14.1 0.7 collective-permute-start
  14.8 0.0 copy-done.3
  14.8 0.7 compare_reduce_fusion.2
  15.5 2.0 gather_fusion
  17.5 0.0 copy-start.2
  17.5 2.0 select_select_fusion.1
  19.6 0.0 collective-permute-done
  19.6 0.2 copy-done.2
  19.7 1.9 fusion.6
  21.6 0.0 copy-start.1
  21.6 1.4 copy-done.1
  23.0 0.7 slice_bitcast_fusion
  23.7 0.9 fusion.12
  24.6 1.3 collective-permute-start.3
  25.9 1.4 collective-permute-start.2
  27.3 6.4 %collective-permute-done.3 = f32[64,512]{0,1:T(8,128)} collective-permute-done((f32[64,512]{0,1:T(8,128)}, f32[64,512]{0,1:T(8,128)}, u32[]{:S(2)}, u32[]{:S(2)}) %collective-permute-start.3) | collective-permute-done | bytes 131104 | tf_op jit(solution)/shard_map/ppermute | solution.py:234
  33.7 0.0 collective-permute-done.2
  33.7 1.7 broadcast_select_fusion
  35.4 1.7 copy.15
  37.1 0.0 all-gather.2.cloned.1.call-update
  37.1 1.3 collective-permute-start.1
  38.4 54.2 %shard_map.39.a_ref = f32[4,512,128]{2,1,0:T(8,128)} custom-call(f32[512,128]{1,0:T(8,128)} %get-tuple-element.96.top_ref), custom_call_target="tpu_custom_call" | custom-call | tf_op jit(solution)/shard_map/pallas_call | solution.py:99
  92.6 78.2 %shard_map.40 = (f32[512,512]{1,0:T(8,128)}, f32[512,512]{1,0:T(8,128)}) custom-call(f32[4,512,128]{2,1,0:T(8,128)} %shard_map.39.a_ref), custom_call_target="tpu_custom_call" | custom-call | tf_op jit(solution)/shard_map/pallas_call | solution.py:189
  170.9 0.0 collective-permute-done.1
  170.9 2.6 %fusion.7 = f32[128,512]{1,0:T(8,128)S(1)} fusion(f32[512,512]{1,0:T(8,128)} %get-tuple-element.59, f32[128,512]{0,1:T(8,128)} %collective-permute-done.1, pred[]{:T(512)S(6)} %eq.46, f32[4096,128]{1,0:T(8,128)} %copy-done.1), kind=kOutput, calls=%fused_computation.17 | convolution fusion | flops 402718720 | bytes 1835009 | tf_op jit(solution)/shard_map/dot_general | solution.py:244
  173.5 0.0 all-gather.2.cloned.1.call-done
  173.5 23.4 %conditional.1 = (f32[4096,128]{1,0:T(8,128)}) conditional(s32[]{:T(128)} %convert_element_type.3, (f32[128,512]{1,0:T(8,128)S(1)}, f32[512,512]{1,0:T(8,128)}, f32[4096,512]{1,0:T(8,128)}, f32[4096,128]{1,0:T(8,128)}, s32[]{:T(128)}) %tuple.40, (s32[]{:T(128)}, f32[512,512]{1,0:T(8,128)}, f32[4096,512]{1,0:T(8,128)}, s32[]{:T(128)}, ...), branch_computations={%region_4.6_spmd, %region_5.7_spmd} | conditional | flops 3624468480 | bytes 23592976 | solution.py:261
  173.7 2.9 %copy.16 = f32[4096,128]{0,1:T(8,128)} copy(f32[4096,128]{1,0:T(8,128)} %get-tuple-element.85) | data formatting | bytes 4194304 | tf_op jit(solution)/shard_map
  176.6 1.9 fusion.13
  178.6 13.7 %fusion = f32[4096,128]{0,1:T(8,128)} fusion(f32[4096,128]{0,1:T(8,128)} %copy.16, f32[128,512]{1,0:T(8,128)S(1)} %fusion.13, f32[4096,512]{1,0:T(8,128)} %get-tuple-element.46), kind=kOutput, calls=%fused_computation.3 | convolution fusion | flops 3221749760 | bytes 12845056 | tf_op jit(solution)/shard_map/cond/branch_0_fun/dot_general | solution.py:257
  192.3 1.7 fusion.1
  194.0 2.9 %copy.19 = f32[4096,128]{1,0:T(8,128)} copy(f32[4096,128]{0,1:T(8,128)} %fusion.1) | data formatting | bytes 4194304 | tf_op jit(solution)/shard_map/cond
  (7 shorter events, 0.0 us)
Async XLA Ops:
  6.5 2.4 %copy-start = (f32[1,6144,128]{2,1,0:T(8,128)S(1)}, f32[1,6144,128]{2,1,0:T(8,128)}, u32[]{:S(2)}) copy-start(f32[1,6144,128]{2,1,0:T(8,128)} %param.8) | copy-start | bytes 9437188
  6.5 167.0 %all-gather.2.cloned.1.call-start = ((), (), s32[]{:S(2)}) async-start(), calls=%async_computation | async-start | bytes 8519680 | tf_op jit(solution)/shard_map/all_gather | solution.py:241
  10.9 3.9 %copy-start.3 = (s32[1,48]{1,0:T(1,128)S(1)}, s32[1,48]{1,0:T(1,128)}, u32[]{:S(2)}) copy-start(s32[1,48]{1,0:T(1,128)} %param.9) | copy-start | bytes 580
  14.1 5.4 %collective-permute-start = (f32[4096,128]{1,0:T(8,128)}, f32[4096,128]{1,0:T(8,128)}, u32[]{:S(2)}, u32[]{:S(2)}) collective-permute-start(f32[4096,128]{1,0:T(8,128)} %bitcast.6), channel_id=1, source_target_pairs={{0,64},{64,0},{1,65},{65,1},{2,66},{66,2},{3,67},{67,3},{4,68},{68... | collective-permute-start | bytes 6291464 | tf_op jit(solution)/shard_map/ppermute | solution.py:216
  17.5 2.2 %copy-start.2 = (f32[4096,128]{1,0:T(8,128)S(1)}, f32[4096,128]{1,0:T(8,128)}, u32[]{:S(2)}) copy-start(f32[4096,128]{1,0:T(8,128)} %param.7) | copy-start | bytes 6291460
  21.6 1.4 copy-start.1
  24.6 9.1 %collective-permute-start.3 = (f32[64,512]{0,1:T(8,128)}, f32[64,512]{0,1:T(8,128)}, u32[]{:S(2)}, u32[]{:S(2)}) collective-permute-start(f32[64,512]{0,1:T(8,128)} %get-tuple-element.97), channel_id=1, source_target_pairs={{0,0},{1,2},{2,4},{3,6},{4,8},{5,10},{6,12},{7,14},{8,16},{9,18},{... | collective-permute-start | bytes 393224 | tf_op jit(solution)/shard_map/ppermute | solution.py:234
  25.9 7.8 %collective-permute-start.2 = (f32[64,512]{0,1:T(8,128)}, f32[64,512]{0,1:T(8,128)}, u32[]{:S(2)}, u32[]{:S(2)}) collective-permute-start(f32[64,512]{0,1:T(8,128)} %get-tuple-element.98), channel_id=1, source_target_pairs={{0,1},{1,3},{2,5},{3,7},{4,9},{5,11},{6,13},{7,15},{8,17},{9,19},{... | collective-permute-start | bytes 393224 | tf_op jit(solution)/shard_map/ppermute | solution.py:234
  37.1 133.7 %collective-permute-start.1 = (f32[128,512]{0,1:T(8,128)S(1)}, f32[128,512]{0,1:T(8,128)}, u32[]{:S(2)}, u32[]{:S(2)}) collective-permute-start(f32[128,512]{0,1:T(8,128)S(1)} %get-tuple-element.95), channel_id=1, source_target_pairs={{0,64},{1,65},{2,66},{3,67},{4,68},{5,69},{6,70},{7,71},{8,72},{9,... | collective-permute-start | bytes 786440 | tf_op jit(solution)/shard_map/ppermute | solution.py:238
Sparse Core Ops, SparseCore 0:
  37.2 93.6 all-gather.1

commit v14 on v13

--- a/solution.py
+++ b/solution.py
@@ -221,24 +221,32 @@
     top = assembled[:S]
     panel_rows = top.T
 
-    piece = rows // n_front
+    n_parts = 2
+    piece = rows // (n_parts * n_front)
     per_block = BLK // piece
-    pieces = []
-    for part in range(per_block):
-        pairs = []
-        for lf in range(n_leaf):
-            for k in range(n_front // per_block):
-                src = lf * half_blocks + k
-                dst = lf * n_front + per_block * k + part
-                pairs.append((src, dst))
-        pieces.append(lax.ppermute(panel_rows[part * piece:(part + 1) * piece], ("leaf", "front"), pairs))
-    my_piece = pieces[0]
-    for part in range(1, per_block):
-        my_piece = jnp.where(front % per_block == part, pieces[part], my_piece)
+    blocks_per_part = half_blocks // n_parts
+
+    def part_piece(h):
+        received = []
+        for q in range(per_block):
+            pairs = []
+            for lf in range(n_leaf):
+                for k in range(blocks_per_part):
+                    pairs.append((lf * half_blocks + h * blocks_per_part + k, lf * n_front + per_block * k + q))
+            received.append(lax.ppermute(panel_rows[q * piece:(q + 1) * piece], ("leaf", "front"), pairs))
+        mine = received[0]
+        for q in range(1, per_block):
+            mine = jnp.where(front % per_block == q, received[q], mine)
+        return mine
+
+    first_part = lax.all_gather(part_piece(0), "front", tiled=True)
+    pivot = broadcast_pivot(top, (4, 4, 4))
+    second_piece, pivot = lax.optimization_barrier((part_piece(1), pivot))
+    second_part = lax.all_gather(second_piece, "front", tiled=True)
+    parts = (first_part, second_part)
     partner_rows = lax.ppermute(panel_rows, "leaf", [(0, 1)])
     col_rows = jnp.where(leaf == 0, panel_rows, partner_rows)
-    pivot = broadcast_pivot(top, (4, 4, 4))
-    panel = lax.all_gather(my_piece, "front", tiled=True)
+
     factor, inverse = chol_inv(pivot, S)
 
     col_solved = lax.dot_general(col_rows, inverse, (((1,), (1,)), ((), ())), precision=HIGHEST)
@@ -248,13 +256,15 @@
 
     def pivot_columns():
         inv_rows = lax.dynamic_slice_in_dim(inverse, col_at, cols, 0)
-        out = lax.dot_general(panel, inv_rows, (((1,), (1,)), ((), ())), precision=HIGHEST)
+        out = jnp.concatenate(
+            [lax.dot_general(part, inv_rows, (((1,), (1,)), ((), ())), precision=HIGHEST) for part in parts], axis=0
+        )
         top_rows = jnp.where(leaf == 0, lax.dynamic_slice_in_dim(factor, col_at, cols, 1), out[:S])
         return lax.dynamic_update_slice_in_dim(out, top_rows, 0, 0)
 
     def other_columns():
         weights = jnp.dot(col_solved, inverse, precision=HIGHEST).T
-        out = assembled - jnp.dot(panel, weights, precision=HIGHEST)
+        out = assembled - jnp.concatenate([jnp.dot(part, weights, precision=HIGHEST) for part in parts], axis=0)
         top_rows = jnp.where(leaf == 0, col_solved.T, out[:S])
         return lax.dynamic_update_slice_in_dim(out, top_rows, 0, 0)
 

time: 204 us -> 233 us (1.14)
  the two profiles are of different devices: /device:TPU:81 before, /device:TPU:1 now
where the time goes in v14:
time: 233 us; the launch traced here: 232 us
  Pallas kernels  123 us (53%)
  waiting for transfers between devices  34.2 us (15%)
  other arithmetic  16.9 us (7%)
  local copies, waits for them, and re-layouts  16.2 us (7%)
  matrix products  14.7 us (6%)
  between operations  13.6 us (6%)
  starting transfers between devices  13.5 us (6%)
    pallas_call x1, Pallas kernels, chol_inv(): pl.pallas_call(chol_inv_kernel, out_shape=(jax.ShapeDtypeStruct((n, n), j...  78.2 us
    pallas_call x1, Pallas kernels, broadcast_pivot(): pl.pallas_call(functools.partial(pivot_kernel, dims), out_shape=jax.Shape...  44.6 us
    all_gather x1, waiting for transfers between devices, per_device(): second_part = lax.all_gather(second_piece, 'front', tiled=True)  29.7 us
    dot_general x2, matrix products, pivot_columns(): lax.dot_general(part, inv_rows, (((1,), (1,)), ((), ())), precision=HIGHEST)  12.1 us
    ppermute x8, starting transfers between devices, part_piece(): lax.ppermute(panel_rows[q * piece:(q + 1) * piece], ('leaf', 'front'), pa...  10.8 us
    select_n x2, other arithmetic, gather_half(): picked = jnp.where(found[:, None, None], picked, jnp.zeros_like(picked))  5.25 us
  transfers between devices with their start and end apart: 12, of which 2 were waited for; matrix products, arithmetic and copies ran while one was open for 5% of the time, Pallas kernels for 53%

profile of v14, /device:TPU:1, one launch (start us, length us, event | category | flops | bytes accessed | tf_op | source)
XLA Modules:
  0.0 231.8 jit_solution(6602424627132842033)
XLA Ops:
  6.5 1.5 compare_reduce_fusion
  8.1 0.8 compare_reduce_fusion.3
  8.9 2.0 gather_fusion.1
  10.9 3.2 %select_select_fusion = f32[32,128,128]{2,1,0:T(8,128)} fusion(f32[32,128,128]{2,1,0:T(8,128)} %gather_fusion.1, pred[32]{0:T(512)(128)(4,1)S(1)} %compare_and_fusion, pred[32]{0:T(512)(128)(4,1)S(1)} %get-tuple-element.114), kind=kLoop, calls=%fused_computation.20 | loop fusion | flops 1048576 | bytes 4194368 | tf_op jit(solution)/shard_map/jit(_where)/select_n | solution.py:22
  14.1 1.4 collective-permute-start
  15.6 0.8 compare_reduce_fusion.2
  16.3 2.0 gather_fusion
  18.3 2.0 select_select_fusion.1
  20.4 0.0 collective-permute-done
  20.4 0.2 copy-done.5
  20.6 1.9 fusion.7
  22.4 1.3 copy-done.3
  23.8 0.7 fusion.13
  24.5 1.2 fusion.14
  25.7 1.3 collective-permute-start.9
  27.0 1.4 collective-permute-start.8
  28.4 1.4 collective-permute-start.7
  29.7 1.3 collective-permute-start.6
  31.1 4.4 %collective-permute-done.9 = f32[32,512]{0,1:T(8,128)} collective-permute-done((f32[32,512]{0,1:T(8,128)}, f32[32,512]{0,1:T(8,128)}, u32[]{:S(2)}, u32[]{:S(2)}) %collective-permute-start.9) | collective-permute-done | bytes 65568 | tf_op jit(solution)/shard_map/ppermute | solution.py:236
  35.5 0.0 collective-permute-done.8
  35.5 0.0 collective-permute-done.7
  35.5 0.0 collective-permute-done.6
  35.5 1.7 select_select_fusion.2
  37.3 1.7 copy.18
  38.9 0.0 all-gather.3.cloned.1.call-update
  39.0 0.0 all-gather.5.cloned.1.call-start
  39.0 1.3 collective-permute-start.5
  40.3 1.4 collective-permute-start.4
  41.7 1.4 collective-permute-start.3
  43.1 1.3 collective-permute-start.2
  44.4 44.6 %shard_map.39.a_ref = f32[4,512,128]{2,1,0:T(8,128)} custom-call(f32[512,128]{1,0:T(8,128)} %get-tuple-element.115.top_ref), custom_call_target="tpu_custom_call" | custom-call | tf_op jit(solution)/shard_map/pallas_call | solution.py:99
  89.0 0.0 collective-permute-done.5
  89.0 0.0 collective-permute-done.2
  89.0 1.7 select_select_fusion.3
  90.8 1.7 copy.19
  92.4 0.0 all-gather.5.cloned.1.call-update
  92.5 1.3 collective-permute-start.1
  93.8 78.2 %shard_map.40 = (f32[512,512]{1,0:T(8,128)}, f32[512,512]{1,0:T(8,128)}) custom-call(f32[4,512,128]{2,1,0:T(8,128)} %shard_map.39.a_ref), custom_call_target="tpu_custom_call" | custom-call | tf_op jit(solution)/shard_map/pallas_call | solution.py:189
  172.0 2.6 %fusion.8 = f32[128,512]{1,0:T(8,128)S(1)} fusion(f32[512,512]{1,0:T(8,128)} %get-tuple-element.72, f32[128,512]{0,1:T(8,128)} %collective-permute-done.1, pred[]{:T(512)S(6)} %eq.60, f32[4096,128]{1,0:T(8,128)} %copy-done.3), kind=kOutput, calls=%fused_computation.24 | convolution fusion | flops 402718720 | bytes 1835009 | tf_op jit(solution)/shard_map/dot_general | solution.py:252
  174.6 0.0 all-gather.3.cloned.1.call-done
  174.6 29.7 %all-gather.5.cloned.1.call-done = f32[2048,512]{1,0:T(8,128)} async-done(((f32[32,512]{1,0:T(8,128)}), f32[2048,512]{1,0:T(8,128)}) %all-gather.5.cloned.1.call-update) | async-done | bytes 4194320 | tf_op jit(solution)/shard_map/all_gather | solution.py:245
  204.3 20.7 %conditional.1 = (f32[4096,128]{1,0:T(8,128)}) conditional(s32[]{:T(128)} %convert_element_type.3, (f32[128,512]{1,0:T(8,128)S(1)}, f32[512,512]{1,0:T(8,128)}, f32[2048,512]{1,0:T(8,128)}, f32[2048,512]{1,0:T(8,128)}, f32[4096,128]{1,0:T(8,128)}, /*index=5*/s32[]{:T(128)}) %tuple.44, (s32[]{:T(128)}, f32[512,512]{1,0:T(8,128)}, ...), branch_computations={%region_4.6_spmd, %region_5.7_spmd} | conditional | flops 3624992768 | bytes 53215304 | solution.py:271
  204.3 2.5 %copy.21 = f32[512,512]{0,1:T(8,128)} copy(f32[512,512]{1,0:T(8,128)} %get-tuple-element.111) | data formatting | bytes 2097152 | tf_op jit(solution)/shard_map
  206.8 6.7 %convolution_bitcast_fusion.3 = f32[2048,128]{0,1:T(8,128)S(1)} fusion(f32[2048,512]{1,0:T(8,128)} %get-tuple-element.59, f32[512,512]{1,0:T(8,128)} %get-tuple-element.57, s32[]{:T(128)S(6)} %select_n.90), kind=kOutput, calls=%fused_computation.8 | convolution fusion | flops 1610612736 | bytes 5505028 | tf_op jit(solution)/shard_map/cond/branch_1_fun/dot_general | solution.py:260
  213.6 5.4 %convolution_bitcast_fusion.2 = f32[2048,128]{0,1:T(8,128)S(1)} fusion(f32[2048,512]{1,0:T(8,128)S(1)} %copy-done.2, f32[512,512]{1,0:T(8,128)} %get-tuple-element.57, s32[]{:T(128)S(6)} %select_n.90), kind=kOutput, calls=%fused_computation.7 | convolution fusion | flops 1610612736 | bytes 5505028 | tf_op jit(solution)/shard_map/cond/branch_1_fun/dot_general | solution.py:260
  218.9 1.5 pad_maximum_fusion
  220.4 1.7 fusion.1
  222.1 2.9 %copy.24 = f32[4096,128]{1,0:T(8,128)} copy(f32[4096,128]{0,1:T(8,128)} %fusion.1) | data formatting | bytes 4194304 | tf_op jit(solution)/shard_map/cond
  (19 shorter events, 0.1 us)
Async XLA Ops:
  6.5 2.4 %copy-start = (f32[1,6144,128]{2,1,0:T(8,128)S(1)}, f32[1,6144,128]{2,1,0:T(8,128)}, u32[]{:S(2)}) copy-start(f32[1,6144,128]{2,1,0:T(8,128)} %param.8) | copy-start | bytes 9437188
  6.5 168.1 %all-gather.3.cloned.1.call-start = ((), (), s32[]{:S(2)}) async-start(), calls=%async_computation | async-start | bytes 4259840 | tf_op jit(solution)/shard_map/all_gather | solution.py:242
  10.9 4.6 %copy-start.6 = (s32[1,48]{1,0:T(1,128)S(1)}, s32[1,48]{1,0:T(1,128)}, u32[]{:S(2)}) copy-start(s32[1,48]{1,0:T(1,128)} %param.9) | copy-start | bytes 580
  14.1 6.2 %collective-permute-start = (f32[4096,128]{1,0:T(8,128)}, f32[4096,128]{1,0:T(8,128)}, u32[]{:S(2)}, u32[]{:S(2)}) collective-permute-start(f32[4096,128]{1,0:T(8,128)} %bitcast.8), channel_id=1, source_target_pairs={{0,64},{64,0},{1,65},{65,1},{2,66},{66,2},{3,67},{67,3},{4,68},{68... | collective-permute-start | bytes 6291464 | tf_op jit(solution)/shard_map/ppermute | solution.py:216
  18.3 2.2 copy-start.5
  22.4 1.4 copy-start.3
  25.7 9.8 %collective-permute-start.9 = (f32[32,512]{0,1:T(8,128)}, f32[32,512]{0,1:T(8,128)}, u32[]{:S(2)}, u32[]{:S(2)}) collective-permute-start(f32[32,512]{0,1:T(8,128)} %get-tuple-element.117), channel_id=1, source_target_pairs={{0,0},{1,4},{2,8},{3,12},{4,16},{5,20},{6,24},{7,28},{8,32},{9,36}... | collective-permute-start | bytes 196616 | tf_op jit(solution)/shard_map/ppermute | solution.py:236
  27.0 8.5 %collective-permute-start.8 = (f32[32,512]{0,1:T(8,128)}, f32[32,512]{0,1:T(8,128)}, u32[]{:S(2)}, u32[]{:S(2)}) collective-permute-start(f32[32,512]{0,1:T(8,128)} %get-tuple-element.118), channel_id=1, source_target_pairs={{0,1},{1,5},{2,9},{3,13},{4,17},{5,21},{6,25},{7,29},{8,33},{9,37}... | collective-permute-start | bytes 196616 | tf_op jit(solution)/shard_map/ppermute | solution.py:236
  28.4 7.2 %collective-permute-start.7 = (f32[32,512]{0,1:T(8,128)}, f32[32,512]{0,1:T(8,128)}, u32[]{:S(2)}, u32[]{:S(2)}) collective-permute-start(f32[32,512]{0,1:T(8,128)} %get-tuple-element.119), channel_id=1, source_target_pairs={{0,2},{1,6},{2,10},{3,14},{4,18},{5,22},{6,26},{7,30},{8,34},{9,38... | collective-permute-start | bytes 196616 | tf_op jit(solution)/shard_map/ppermute | solution.py:236
  29.7 5.8 %collective-permute-start.6 = (f32[32,512]{0,1:T(8,128)}, f32[32,512]{0,1:T(8,128)}, u32[]{:S(2)}, u32[]{:S(2)}) collective-permute-start(f32[32,512]{0,1:T(8,128)} %get-tuple-element.120), channel_id=1, source_target_pairs={{0,3},{1,7},{2,11},{3,15},{4,19},{5,23},{6,27},{7,31},{8,35},{9,39... | collective-permute-start | bytes 196616 | tf_op jit(solution)/shard_map/ppermute | solution.py:236
  39.0 165.3 %all-gather.5.cloned.1.call-start = ((), (), s32[]{:S(2)}) async-start(), calls=%async_computation.1 | async-start | bytes 4259840 | tf_op jit(solution)/shard_map/all_gather | solution.py:245
  39.0 50.0 %collective-permute-start.5 = (f32[32,512]{0,1:T(8,128)}, f32[32,512]{0,1:T(8,128)}, u32[]{:S(2)}, u32[]{:S(2)}) collective-permute-start(f32[32,512]{0,1:T(8,128)} %get-tuple-element.117), channel_id=1, source_target_pairs={{16,0},{17,4},{18,8},{19,12},{20,16},{21,20},{22,24},{23,28},{24,3... | collective-permute-start | bytes 196616 | tf_op jit(solution)/shard_map/ppermute | solution.py:236
  40.3 48.7 %collective-permute-start.4 = (f32[32,512]{0,1:T(8,128)}, f32[32,512]{0,1:T(8,128)}, u32[]{:S(2)}, u32[]{:S(2)}) collective-permute-start(f32[32,512]{0,1:T(8,128)} %get-tuple-element.118), channel_id=1, source_target_pairs={{16,1},{17,5},{18,9},{19,13},{20,17},{21,21},{22,25},{23,29},{24,3... | collective-permute-start | bytes 196616 | tf_op jit(solution)/shard_map/ppermute | solution.py:236
  41.7 47.3 %collective-permute-start.3 = (f32[32,512]{0,1:T(8,128)}, f32[32,512]{0,1:T(8,128)}, u32[]{:S(2)}, u32[]{:S(2)}) collective-permute-start(f32[32,512]{0,1:T(8,128)} %get-tuple-element.119), channel_id=1, source_target_pairs={{16,2},{17,6},{18,10},{19,14},{20,18},{21,22},{22,26},{23,30},{24,... | collective-permute-start | bytes 196616 | tf_op jit(solution)/shard_map/ppermute | solution.py:236
  43.1 46.0 %collective-permute-start.2 = (f32[32,512]{0,1:T(8,128)}, f32[32,512]{0,1:T(8,128)}, u32[]{:S(2)}, u32[]{:S(2)}) collective-permute-start(f32[32,512]{0,1:T(8,128)} %get-tuple-element.120), channel_id=1, source_target_pairs={{16,3},{17,7},{18,11},{19,15},{20,19},{21,23},{22,27},{23,31},{24,... | collective-permute-start | bytes 196616 | tf_op jit(solution)/shard_map/ppermute | solution.py:236
  92.5 79.5 %collective-permute-start.1 = (f32[128,512]{0,1:T(8,128)S(1)}, f32[128,512]{0,1:T(8,128)}, u32[]{:S(2)}, u32[]{:S(2)}) collective-permute-start(f32[128,512]{0,1:T(8,128)S(1)} %get-tuple-element.116), channel_id=1, source_target_pairs={{0,64},{1,65},{2,66},{3,67},{4,68},{5,69},{6,70},{7,71},{8,72},{9,... | collective-permute-start | bytes 786440 | tf_op jit(solution)/shard_map/ppermute | solution.py:247
  206.8 6.7 %copy-start.2 = (f32[2048,512]{1,0:T(8,128)S(1)}, f32[2048,512]{1,0:T(8,128)}, u32[]{:S(2)}) copy-start(f32[2048,512]{1,0:T(8,128)} %get-tuple-element.60) | copy-start | bytes 12582916 | tf_op jit(solution)/shard_map/cond
Sparse Core Ops, SparseCore 0:
  39.1 92.2 all-gather.2
  134.3 69.9 all-gather.4

commit v15 on v9

--- a/solution.py
+++ b/solution.py
@@ -161,7 +161,7 @@
                            preferred_element_type=jnp.float32)
 
 
-def chol_inv_kernel(a_ref, l_ref, linv_ref, w_ref, d_ref, e_ref, ut_ref, x_ref):
+def chol_inv_kernel(a_ref, l_ref, linvt_ref, w_ref, d_ref, e_ref, ut_ref, x_ref, linv_ref):
     n = a_ref.shape[0]
     b = d_ref.shape[0]
     nb = n // b
@@ -217,6 +217,9 @@
             for k in range(j, i):
                 acc = acc + _mm(l_ref[i * b:(i + 1) * b, k * b:(k + 1) * b], linv_ref[k * b:(k + 1) * b, j * b:(j + 1) * b])
             linv_ref[i * b:(i + 1) * b, j * b:(j + 1) * b] = -_mm(linv_ref[i * b:(i + 1) * b, i * b:(i + 1) * b], acc)
+    for j in range(nb):
+        for i in range(nb):
+            linvt_ref[j * b:(j + 1) * b, i * b:(i + 1) * b] = jnp.transpose(linv_ref[i * b:(i + 1) * b, j * b:(j + 1) * b])
 
 
 def chol_inv(a, b=128):
@@ -232,6 +235,7 @@
             pltpu.VMEM((b, b), jnp.float32),
             pltpu.VMEM((b, b), jnp.float32),
             pltpu.VMEM((b, b), jnp.float32),
+            pltpu.VMEM((n, n), jnp.float32),
         ],
     )(a)
 
@@ -275,21 +279,21 @@
     col_rows = jnp.where(leaf == 0, panel_rows, partner_rows)
     my_piece, pivot = lax.optimization_barrier((my_piece, pivot))
     panel = lax.all_gather(my_piece, "front", tiled=True)
-    factor, inverse = chol_inv(pivot)
-
-    col_solved = lax.dot_general(col_rows, inverse, (((1,), (1,)), ((), ())), precision=HIGHEST)
+    factor, inverse_t = chol_inv(pivot)
+
+    col_solved = jnp.dot(col_rows, inverse_t, precision=HIGHEST)
 
     piv_cols = S // cols
     col_at = jnp.minimum(front, piv_cols - 1) * cols
 
     def pivot_columns():
-        inv_rows = lax.dynamic_slice_in_dim(inverse, col_at, cols, 0)
-        out = lax.dot_general(panel, inv_rows, (((1,), (1,)), ((), ())), precision=HIGHEST)
+        inv_cols = lax.dynamic_slice_in_dim(inverse_t, col_at, cols, 1)
+        out = jnp.dot(panel, inv_cols, precision=HIGHEST)
         top_rows = jnp.where(leaf == 0, lax.dynamic_slice_in_dim(factor, col_at, cols, 1), out[:S])
         return lax.dynamic_update_slice_in_dim(out, top_rows, 0, 0)
 
     def other_columns():
-        weights = jnp.dot(col_solved, inverse, precision=HIGHEST).T
+        weights = lax.dot_general(inverse_t, col_solved, (((1,), (1,)), ((), ())), precision=HIGHEST)
         out = assembled - jnp.dot(panel, weights, precision=HIGHEST)
         top_rows = jnp.where(leaf == 0, col_solved.T, out[:S])
         return lax.dynamic_update_slice_in_dim(out, top_rows, 0, 0)

time: 189 us -> 189 us (level)
  transfers between devices with their start and end apart: 5 -> 5, of which waited for: 0 -> 0; matrix products, arithmetic and copies ran while one was open for 6% -> 5% of each run, Pallas kernels for 65% -> 65%
where the time goes in v15:
time: 189 us; the launch traced here: 186 us
  Pallas kernels  120 us (63%)
  local copies, waits for them, and re-layouts  17.3 us (9%)
  matrix products  15.7 us (8%)
  other arithmetic  13.7 us (7%)
  between operations  13.5 us (7%)
  starting transfers between devices  5.38 us (3%)
    pallas_call x1, Pallas kernels, chol_inv(): pl.pallas_call(chol_inv_kernel, out_shape=(jax.ShapeDtypeStruct((n, n), j...  77.9 us
    pallas_call x1, Pallas kernels, broadcast_pivot(): pl.pallas_call(functools.partial(pivot_kernel, n_front, n_src), out_shape...  42.4 us
    dot_general x1, matrix products, pivot_columns(): out = jnp.dot(panel, inv_cols, precision=HIGHEST)  13.6 us
    select_n x2, other arithmetic, gather_half(): picked = jnp.where(found[:, None, None], picked, jnp.zeros_like(picked))  5.25 us
    gather x2, local copies, waits for them, and re-layouts, gather_half(): picked = jnp.take(blocks, index, axis=0)  3.98 us
  transfers between devices with their start and end apart: 5, of which 0 were waited for; matrix products, arithmetic and copies ran while one was open for 5% of the time, Pallas kernels for 65%

profile of v15, /device:TPU:1, one launch (start us, length us, event | category | flops | bytes accessed | tf_op | source)
XLA Modules:
  0.0 186.4 jit_solution(6984771353764963795)
XLA Ops:
  6.5 0.0 copy-start
  6.5 0.0 all-gather.2.cloned.1.call-start
  6.5 1.5 compare_reduce_fusion
  8.1 0.8 compare_reduce_fusion.3
  8.9 0.0 copy-done
  8.9 2.0 %gather_fusion.1 = f32[32,128,128]{2,1,0:T(8,128)} fusion(f32[48,128,128]{2,1,0:T(8,128)S(1)} %bitcast.40, s32[1024]{0:T(1024)S(1)} %pad_clamp_fusion), kind=kCustom, calls=%fused_computation.1.clone | custom fusion | bytes 4194432 | tf_op jit(solution)/shard_map/jit(_take)/gather | solution.py:21
  10.9 0.0 copy-start.3
  10.9 3.2 %select_select_fusion = f32[32,128,128]{2,1,0:T(8,128)} fusion(f32[32,128,128]{2,1,0:T(8,128)} %gather_fusion.1, pred[32]{0:T(512)(128)(4,1)S(1)} %compare_and_fusion, pred[32]{0:T(512)(128)(4,1)S(1)} %get-tuple-element.98), kind=kLoop, calls=%fused_computation.15 | loop fusion | flops 1048576 | bytes 4194368 | tf_op jit(solution)/shard_map/jit(_where)/select_n | solution.py:22
  14.1 1.4 collective-permute-start
  15.6 0.0 copy-done.3
  15.6 0.7 compare_reduce_fusion.2
  16.3 2.0 %gather_fusion = f32[32,128,128]{2,1,0:T(8,128)} fusion(f32[48,128,128]{2,1,0:T(8,128)S(1)} %bitcast.39, s32[1024]{0:T(1024)S(1)} %pad_clamp_fusion.1), kind=kCustom, calls=%fused_computation.clone | custom fusion | bytes 4194432 | tf_op jit(solution)/shard_map/jit(_take)/gather | solution.py:21
  18.3 0.0 copy-start.2
  18.3 2.0 %select_select_fusion.1 = f32[32,128,128]{2,1,0:T(8,128)S(1)} fusion(f32[32,128,128]{2,1,0:T(8,128)} %gather_fusion, pred[32]{0:T(512)(128)(4,1)S(1)} %compare_and_fusion.1, pred[32]{0:T(512)(128)(4,1)S(1)} %get-tuple-element.97), kind=kLoop, calls=%fused_computation.16 | loop fusion | flops 1048576 | bytes 4194368 | tf_op jit(solution)/shard_map/jit(_where)/select_n | solution.py:22
  20.3 0.0 collective-permute-done
  20.3 0.2 copy-done.2
  20.5 1.9 %fusion.6 = f32[4096,128]{1,0:T(8,128)S(1)} fusion(f32[4096,128]{1,0:T(8,128)S(1)} %copy-done.2, f32[4096,128]{1,0:T(8,128)} %collective-permute-done, f32[32,128,128]{2,1,0:T(8,128)S(1)} %select_select_fusion.1, pred[]{:T(512)S(6)} %eq.47), kind=kLoop, calls=%fused_computation.14 | loop fusion | flops 2097152 | bytes 8388609 | tf_op jit(solution)/shard_map/add | solution.py:258
  22.4 0.0 copy-start.1
  22.4 1.4 copy-done.1
  23.8 0.7 fusion.12
  24.5 0.9 fusion.13
  25.4 1.3 collective-permute-start.2
  26.7 1.4 collective-permute-start.1
  28.0 42.4 %shard_map.39 = f32[64,32,128]{2,1,0:T(8,128)} custom-call(f32[512,128]{1,0:T(8,128)} %get-tuple-element.99.top_ref), custom_call_target="tpu_custom_call" | custom-call | tf_op jit(solution)/shard_map/pallas_call | solution.py:133
  70.4 1.9 %copy.17 = f32[4,16,32,128]{3,0,2,1:T(4,128)S(1)} copy(f32[4,16,32,128]{3,2,1,0:T(8,128)} %bitcast.41) | data formatting | bytes 2097152 | tf_op jit(solution)/shard_map/reshape | solution.py:149
  72.3 1.0 copy.26
  73.4 0.0 collective-permute-done.2
  73.4 0.0 collective-permute-done.1
  73.4 1.7 broadcast_select_fusion
  75.1 1.7 copy.18
  76.8 0.0 all-gather.2.cloned.1.call-update
  76.8 1.3 collective-permute-start.3
  78.1 77.9 %shard_map.40 = (f32[512,512]{1,0:T(8,128)}, f32[512,512]{1,0:T(8,128)}) custom-call(f32[512,512]{1,0:T(8,128)} %bitcast.42), custom_call_target="tpu_custom_call" | custom-call | tf_op jit(solution)/shard_map/pallas_call | solution.py:227
  156.1 0.0 collective-permute-done.3
  156.1 2.2 %fusion.7 = f32[128,512]{1,0:T(8,128)S(1)} fusion(f32[512,512]{1,0:T(8,128)} %get-tuple-element.62, f32[128,512]{0,1:T(8,128)} %collective-permute-done.3, pred[]{:T(512)S(6)} %eq.47, f32[4096,128]{1,0:T(8,128)} %copy-done.1), kind=kOutput, calls=%fused_computation.18 | convolution fusion | flops 402718720 | bytes 1835009 | tf_op jit(solution)/shard_map/dot_general | solution.py:284
  158.2 0.0 all-gather.2.cloned.1.call-done
  158.3 21.2 %conditional.1 = (f32[4096,128]{1,0:T(8,128)}) conditional(s32[]{:T(128)} %convert_element_type.3, (f32[512,512]{1,0:T(8,128)}, f32[128,512]{1,0:T(8,128)S(1)}, f32[4096,512]{1,0:T(8,128)}, f32[4096,128]{1,0:T(8,128)}, s32[]{:T(128)}) %tuple.42, (s32[]{:T(128)}, f32[512,512]{1,0:T(8,128)}, f32[4096,512]{1,0:T(8,128)}, s32[]{:T(128)}, ...), branch_computations={%region_4.6_spmd, %region_5.7_spmd} | conditional | flops 3624468480 | bytes 23592976 | solution.py:301
  158.7 2.5 %copy.20 = f32[512,512]{0,1:T(8,128)} copy(f32[512,512]{1,0:T(8,128)} %get-tuple-element.95) | data formatting | bytes 2097152 | tf_op jit(solution)/shard_map
  161.2 13.6 %convolution_bitcast_fusion.1 = f32[4096,128]{0,1:T(8,128)} fusion(f32[4096,512]{1,0:T(8,128)} %get-tuple-element.50, f32[512,512]{1,0:T(8,128)} %get-tuple-element.48, s32[]{:T(128)S(6)} %select_n.63), kind=kOutput, calls=%fused_computation.6 | convolution fusion | flops 3221225472 | bytes 10747908 | tf_op jit(solution)/shard_map/cond/branch_1_fun/dot_general | solution.py:291
  174.8 1.8 fusion.2
  176.6 2.9 %copy.23 = f32[4096,128]{1,0:T(8,128)} copy(f32[4096,128]{0,1:T(8,128)} %fusion.2) | data formatting | bytes 4194304 | tf_op jit(solution)/shard_map/cond
  (7 shorter events, 0.0 us)
Async XLA Ops:
  6.5 2.4 %copy-start = (f32[1,6144,128]{2,1,0:T(8,128)S(1)}, f32[1,6144,128]{2,1,0:T(8,128)}, u32[]{:S(2)}) copy-start(f32[1,6144,128]{2,1,0:T(8,128)} %param.8) | copy-start | bytes 9437188
  6.5 151.7 %all-gather.2.cloned.1.call-start = ((), (), s32[]{:S(2)}) async-start(), calls=%async_computation | async-start | bytes 8519680 | tf_op jit(solution)/shard_map/all_gather | solution.py:281
  10.9 4.6 %copy-start.3 = (s32[1,48]{1,0:T(1,128)S(1)}, s32[1,48]{1,0:T(1,128)}, u32[]{:S(2)}) copy-start(s32[1,48]{1,0:T(1,128)} %param.9) | copy-start | bytes 580
  14.1 6.2 %collective-permute-start = (f32[4096,128]{1,0:T(8,128)}, f32[4096,128]{1,0:T(8,128)}, u32[]{:S(2)}, u32[]{:S(2)}) collective-permute-start(f32[4096,128]{1,0:T(8,128)} %bitcast.6), channel_id=1, source_target_pairs={{0,64},{64,0},{1,65},{65,1},{2,66},{66,2},{3,67},{67,3},{4,68},{68... | collective-permute-start | bytes 6291464 | tf_op jit(solution)/shard_map/ppermute | solution.py:255
  18.3 2.2 %copy-start.2 = (f32[4096,128]{1,0:T(8,128)S(1)}, f32[4096,128]{1,0:T(8,128)}, u32[]{:S(2)}) copy-start(f32[4096,128]{1,0:T(8,128)} %param.7) | copy-start | bytes 6291460
  22.4 1.4 copy-start.1
  25.4 48.0 %collective-permute-start.2 = (f32[64,512]{0,1:T(8,128)}, f32[64,512]{0,1:T(8,128)}, u32[]{:S(2)}, u32[]{:S(2)}) collective-permute-start(f32[64,512]{0,1:T(8,128)} %get-tuple-element.101), channel_id=1, source_target_pairs={{0,0},{1,2},{2,4},{3,6},{4,8},{5,10},{6,12},{7,14},{8,16},{9,18},{... | collective-permute-start | bytes 393224 | tf_op jit(solution)/shard_map/ppermute | solution.py:273
  26.7 46.7 %collective-permute-start.1 = (f32[64,512]{0,1:T(8,128)}, f32[64,512]{0,1:T(8,128)}, u32[]{:S(2)}, u32[]{:S(2)}) collective-permute-start(f32[64,512]{0,1:T(8,128)} %get-tuple-element.102), channel_id=1, source_target_pairs={{0,1},{1,3},{2,5},{3,7},{4,9},{5,11},{6,13},{7,15},{8,17},{9,19},{... | collective-permute-start | bytes 393224 | tf_op jit(solution)/shard_map/ppermute | solution.py:273
  76.8 79.3 %collective-permute-start.3 = (f32[128,512]{0,1:T(8,128)S(1)}, f32[128,512]{0,1:T(8,128)}, u32[]{:S(2)}, u32[]{:S(2)}) collective-permute-start(f32[128,512]{0,1:T(8,128)S(1)} %get-tuple-element.100), channel_id=1, source_target_pairs={{0,64},{1,65},{2,66},{3,67},{4,68},{5,69},{6,70},{7,71},{8,72},{9,... | collective-permute-start | bytes 786440 | tf_op jit(solution)/shard_map/ppermute | solution.py:278
Sparse Core Ops, SparseCore 0:
  76.9 80.1 all-gather.1

commit v16 on v9

--- a/solution.py
+++ b/solution.py
@@ -236,6 +236,33 @@
     )(a)
 
 
+def panel_product_kernel(subtract, use_top_ref, panel_ref, w_ref, base_ref, top_ref, out_ref):
+    prod = jnp.dot(panel_ref[...], w_ref[...], precision=HIGHEST, preferred_element_type=jnp.float32)
+    result = base_ref[...] - prod if subtract else prod
+    replace = (pl.program_id(0) == 0) & (use_top_ref[0] == 1)
+    out_ref[...] = jnp.where(replace, top_ref[...], result)
+
+
+def panel_product(use_top, panel, weights, base, top_rows, subtract):
+    rows, depth = panel.shape
+    cols = weights.shape[1]
+    return pl.pallas_call(
+        functools.partial(panel_product_kernel, subtract),
+        out_shape=jax.ShapeDtypeStruct((rows, cols), jnp.float32),
+        grid_spec=pltpu.PrefetchScalarGridSpec(
+            num_scalar_prefetch=1,
+            grid=(rows // S,),
+            in_specs=[
+                pl.BlockSpec((S, depth), lambda i, flag: (i, 0)),
+                pl.BlockSpec((depth, cols), lambda i, flag: (0, 0)),
+                pl.BlockSpec((S, cols), lambda i, flag: (i, 0)),
+                pl.BlockSpec((S, cols), lambda i, flag: (0, 0)),
+            ],
+            out_specs=pl.BlockSpec((S, cols), lambda i, flag: (i, 0)),
+        ),
+    )(use_top, panel, weights, base, top_rows)
+
+
 def per_device(front_block, child_update, child_map):
     rows, cols = front_block.shape
     n_leaf = lax.axis_size("leaf")
@@ -282,17 +309,16 @@
     piv_cols = S // cols
     col_at = jnp.minimum(front, piv_cols - 1) * cols
 
+    use_top = (leaf == 0).astype(jnp.int32).reshape(1)
+
     def pivot_columns():
         inv_rows = lax.dynamic_slice_in_dim(inverse, col_at, cols, 0)
-        out = lax.dot_general(panel, inv_rows, (((1,), (1,)), ((), ())), precision=HIGHEST)
-        top_rows = jnp.where(leaf == 0, lax.dynamic_slice_in_dim(factor, col_at, cols, 1), out[:S])
-        return lax.dynamic_update_slice_in_dim(out, top_rows, 0, 0)
+        top_rows = lax.dynamic_slice_in_dim(factor, col_at, cols, 1)
+        return panel_product(use_top, panel, inv_rows.T, assembled, top_rows, False)
 
     def other_columns():
         weights = jnp.dot(col_solved, inverse, precision=HIGHEST).T
-        out = assembled - jnp.dot(panel, weights, precision=HIGHEST)
-        top_rows = jnp.where(leaf == 0, col_solved.T, out[:S])
-        return lax.dynamic_update_slice_in_dim(out, top_rows, 0, 0)
+        return panel_product(use_top, panel, weights, assembled, col_solved.T, True)
 
     return lax.cond(front < piv_cols, pivot_columns, other_columns)
 

time: 189 us -> 185 us (0.979)
  matrix products: 15.9 us -> 2.63 us
  Pallas kernels: 121 us -> 132 us
    dot_general x1 -> x0, matrix products: 13.3 us -> none  [pivot_columns(): lax.dot_general(panel, inv_rows, (((1,), (1,)), ((), ())), precision=HIGH...]
    pallas_call x0 -> x1, Pallas kernels: none -> 11.6 us  [panel_product(): pl.pallas_call(functools.partial(panel_product_kernel, subtract), out_sha...]
    cond x1 -> x0, local copies, waits for them, and re-layouts: 2.88 us -> none
  transfers between devices with their start and end apart: 5 -> 5, of which waited for: 0 -> 0; matrix products, arithmetic and copies ran while one was open for 6% -> 6% of each run, Pallas kernels for 65% -> 66%
where the time goes in v16:
time: 185 us; the launch traced here: 183 us
  Pallas kernels  132 us (71%)
  local copies, waits for them, and re-layouts  17.7 us (10%)
  between operations  13.5 us (7%)
  other arithmetic  11.9 us (6%)
  starting transfers between devices  5.38 us (3%)
  matrix products  2.63 us (1%)
    pallas_call x1, Pallas kernels, chol_inv(): pl.pallas_call(chol_inv_kernel, out_shape=(jax.ShapeDtypeStruct((n, n), j...  78.1 us
    pallas_call x1, Pallas kernels, broadcast_pivot(): pl.pallas_call(functools.partial(pivot_kernel, n_front, n_src), out_shape...  42.4 us
    pallas_call x1, Pallas kernels, panel_product(): pl.pallas_call(functools.partial(panel_product_kernel, subtract), out_sha...  11.6 us
    select_n x2, other arithmetic, gather_half(): picked = jnp.where(found[:, None, None], picked, jnp.zeros_like(picked))  5.25 us
    gather x2, local copies, waits for them, and re-layouts, gather_half(): picked = jnp.take(blocks, index, axis=0)  3.98 us
  transfers between devices with their start and end apart: 5, of which 0 were waited for; matrix products, arithmetic and copies ran while one was open for 6% of the time, Pallas kernels for 66%

profile of v16, /device:TPU:1, one launch (start us, length us, event | category | flops | bytes accessed | tf_op | source)
XLA Modules:
  0.0 183.4 jit_solution(16241254714975534080)
XLA Ops:
  6.5 0.0 copy-start
  6.5 0.0 all-gather.2.cloned.1.call-start
  6.5 1.5 compare_reduce_fusion
  8.1 0.8 compare_reduce_fusion.3
  8.9 0.0 copy-done
  8.9 2.0 %gather_fusion.1 = f32[32,128,128]{2,1,0:T(8,128)} fusion(f32[48,128,128]{2,1,0:T(8,128)S(1)} %bitcast.33, s32[1024]{0:T(1024)S(1)} %pad_clamp_fusion), kind=kCustom, calls=%fused_computation.1.clone | custom fusion | bytes 4194432 | tf_op jit(solution)/shard_map/jit(_take)/gather | solution.py:21
  10.9 0.0 copy-start.3
  10.9 3.2 %select_select_fusion = f32[32,128,128]{2,1,0:T(8,128)} fusion(f32[32,128,128]{2,1,0:T(8,128)} %gather_fusion.1, pred[32]{0:T(512)(128)(4,1)S(1)} %compare_and_fusion, pred[32]{0:T(512)(128)(4,1)S(1)} %get-tuple-element.102), kind=kLoop, calls=%fused_computation.8 | loop fusion | flops 1048576 | bytes 4194368 | tf_op jit(solution)/shard_map/jit(_where)/select_n | solution.py:22
  14.1 1.4 collective-permute-start
  15.6 0.0 copy-done.3
  15.6 0.7 compare_reduce_fusion.2
  16.3 2.0 %gather_fusion = f32[32,128,128]{2,1,0:T(8,128)} fusion(f32[48,128,128]{2,1,0:T(8,128)S(1)} %bitcast.32, s32[1024]{0:T(1024)S(1)} %pad_clamp_fusion.1), kind=kCustom, calls=%fused_computation.clone | custom fusion | bytes 4194432 | tf_op jit(solution)/shard_map/jit(_take)/gather | solution.py:21
  18.3 0.0 copy-start.2
  18.3 2.0 %select_select_fusion.1 = f32[32,128,128]{2,1,0:T(8,128)S(1)} fusion(f32[32,128,128]{2,1,0:T(8,128)} %gather_fusion, pred[32]{0:T(512)(128)(4,1)S(1)} %compare_and_fusion.1, pred[32]{0:T(512)(128)(4,1)S(1)} %get-tuple-element.101), kind=kLoop, calls=%fused_computation.9 | loop fusion | flops 1048576 | bytes 4194368 | tf_op jit(solution)/shard_map/jit(_where)/select_n | solution.py:22
  20.3 0.0 collective-permute-done
  20.3 0.2 copy-done.2
  20.5 1.9 %fusion.1 = f32[4096,128]{1,0:T(8,128)S(1)} fusion(f32[4096,128]{1,0:T(8,128)S(1)} %copy-done.2, f32[4096,128]{1,0:T(8,128)} %collective-permute-done, f32[32,128,128]{2,1,0:T(8,128)S(1)} %select_select_fusion.1, pred[]{:T(512)S(6)} %eq.22), kind=kLoop, calls=%fused_computation.7 | loop fusion | flops 2097152 | bytes 8388609 | tf_op jit(solution)/shard_map/add | solution.py:281
  22.4 0.0 copy-start.1
  22.4 1.4 copy-done.1
  23.8 0.7 fusion.7
  24.5 0.9 fusion.8
  25.4 1.3 collective-permute-start.2
  26.7 1.4 collective-permute-start.1
  28.0 42.4 %shard_map.39 = f32[64,32,128]{2,1,0:T(8,128)} custom-call(f32[512,128]{1,0:T(8,128)} %get-tuple-element.103.top_ref), custom_call_target="tpu_custom_call" | custom-call | tf_op jit(solution)/shard_map/pallas_call | solution.py:133
  70.4 1.9 %copy.15 = f32[4,16,32,128]{3,0,2,1:T(4,128)S(1)} copy(f32[4,16,32,128]{3,2,1,0:T(8,128)} %bitcast.34) | data formatting | bytes 2097152 | tf_op jit(solution)/shard_map/reshape | solution.py:149
  72.3 1.0 copy.22
  73.4 0.0 collective-permute-done.2
  73.4 0.0 collective-permute-done.1
  73.4 1.7 broadcast_select_fusion
  75.1 1.7 copy.16
  76.8 0.0 all-gather.2.cloned.1.call-update
  76.8 1.3 collective-permute-start.3
  78.1 78.1 %shard_map.40 = (f32[512,512]{1,0:T(8,128)}, f32[512,512]{1,0:T(8,128)}) custom-call(f32[512,512]{1,0:T(8,128)} %bitcast.35), custom_call_target="tpu_custom_call" | custom-call | tf_op jit(solution)/shard_map/pallas_call | solution.py:224
  156.2 0.0 collective-permute-done.3
  156.2 2.6 %fusion.2 = f32[128,512]{1,0:T(8,128)S(1)} fusion(f32[512,512]{1,0:T(8,128)} %get-tuple-element.64, f32[128,512]{0,1:T(8,128)} %collective-permute-done.3, pred[]{:T(512)S(6)} %eq.22, f32[4096,128]{1,0:T(8,128)} %copy-done.1), kind=kOutput, calls=%fused_computation.11 | convolution fusion | flops 402718720 | bytes 1835009 | tf_op jit(solution)/shard_map/dot_general | solution.py:307
  158.8 0.0 all-gather.2.cloned.1.call-done
  158.9 17.7 %conditional.1 = (f32[4096,128]{1,0:T(8,128)}) conditional(s32[]{:T(128)} %convert_element_type.4, (f32[512,512]{1,0:T(8,128)}, f32[128,512]{1,0:T(8,128)S(1)}, s32[1]{0:T(128)}, f32[4096,512]{1,0:T(8,128)}, f32[4096,128]{1,0:T(8,128)}) %tuple.40, (s32[]{:T(128)}, f32[512,512]{1,0:T(8,128)}, f32[512,512]{1,0:T(8,128)}, s32[1]{0:T(128)}, ...), branch_computations={%region_4.6_spmd, %region_5.7_spmd} | conditional | flops 402653184 | bytes 3145802 | solution.py:323
  159.1 1.7 constant_dynamic-slice_fusion.top_ref
  160.8 2.5 %copy.18 = f32[512,512]{0,1:T(8,128)} copy(f32[512,512]{1,0:T(8,128)} %get-tuple-element.96) | data formatting | bytes 2097152 | tf_op jit(solution)/shard_map
  163.3 1.7 dynamic-slice_bitcast_fusion.w_ref
  165.0 11.6 %branch_1_fun.2 = f32[4096,128]{1,0:T(8,128)} custom-call(s32[1]{0:T(128)} %get-tuple-element.49.use_top_ref, f32[4096,512]{1,0:T(8,128)} %get-tuple-element.50.panel_ref, f32[512,128]{1,0:T(8,128)} %dynamic-slice_bitcast_fusion.w_ref, f32[4096,128]{1,0:T(8,128)} %get-tuple-element.53.base_ref, f32[512,128]{1,0:T(8,128)} %constant_dynamic-slice_fusion.top_ref), custom_call_target="tpu_custom_call" | custom-call | tf_op jit(solution)/shard_map/cond/branch_1_fun/pallas_call | solution.py:249
  (7 shorter events, 0.0 us)
Async XLA Ops:
  6.5 2.4 %copy-start = (f32[1,6144,128]{2,1,0:T(8,128)S(1)}, f32[1,6144,128]{2,1,0:T(8,128)}, u32[]{:S(2)}) copy-start(f32[1,6144,128]{2,1,0:T(8,128)} %param.8) | copy-start | bytes 9437188
  6.5 152.3 %all-gather.2.cloned.1.call-start = ((), (), s32[]{:S(2)}) async-start(), calls=%async_computation | async-start | bytes 8519680 | tf_op jit(solution)/shard_map/all_gather | solution.py:304
  10.9 4.6 %copy-start.3 = (s32[1,48]{1,0:T(1,128)S(1)}, s32[1,48]{1,0:T(1,128)}, u32[]{:S(2)}) copy-start(s32[1,48]{1,0:T(1,128)} %param.9) | copy-start | bytes 580
  14.1 6.2 %collective-permute-start = (f32[4096,128]{1,0:T(8,128)}, f32[4096,128]{1,0:T(8,128)}, u32[]{:S(2)}, u32[]{:S(2)}) collective-permute-start(f32[4096,128]{1,0:T(8,128)} %bitcast.5), channel_id=1, source_target_pairs={{0,64},{64,0},{1,65},{65,1},{2,66},{66,2},{3,67},{67,3},{4,68},{68... | collective-permute-start | bytes 6291464 | tf_op jit(solution)/shard_map/ppermute | solution.py:278
  18.3 2.2 %copy-start.2 = (f32[4096,128]{1,0:T(8,128)S(1)}, f32[4096,128]{1,0:T(8,128)}, u32[]{:S(2)}) copy-start(f32[4096,128]{1,0:T(8,128)} %param.7) | copy-start | bytes 6291460
  22.4 1.4 copy-start.1
  25.4 48.0 %collective-permute-start.2 = (f32[64,512]{0,1:T(8,128)}, f32[64,512]{0,1:T(8,128)}, u32[]{:S(2)}, u32[]{:S(2)}) collective-permute-start(f32[64,512]{0,1:T(8,128)} %get-tuple-element.105), channel_id=1, source_target_pairs={{0,0},{1,2},{2,4},{3,6},{4,8},{5,10},{6,12},{7,14},{8,16},{9,18},{... | collective-permute-start | bytes 393224 | tf_op jit(solution)/shard_map/ppermute | solution.py:296
  26.7 46.7 %collective-permute-start.1 = (f32[64,512]{0,1:T(8,128)}, f32[64,512]{0,1:T(8,128)}, u32[]{:S(2)}, u32[]{:S(2)}) collective-permute-start(f32[64,512]{0,1:T(8,128)} %get-tuple-element.106), channel_id=1, source_target_pairs={{0,1},{1,3},{2,5},{3,7},{4,9},{5,11},{6,13},{7,15},{8,17},{9,19},{... | collective-permute-start | bytes 393224 | tf_op jit(solution)/shard_map/ppermute | solution.py:296
  76.8 79.4 %collective-permute-start.3 = (f32[128,512]{0,1:T(8,128)S(1)}, f32[128,512]{0,1:T(8,128)}, u32[]{:S(2)}, u32[]{:S(2)}) collective-permute-start(f32[128,512]{0,1:T(8,128)S(1)} %get-tuple-element.104), channel_id=1, source_target_pairs={{0,64},{1,65},{2,66},{3,67},{4,68},{5,69},{6,70},{7,71},{8,72},{9,... | collective-permute-start | bytes 786440 | tf_op jit(solution)/shard_map/ppermute | solution.py:301
Sparse Core Ops, SparseCore 0:
  76.9 80.1 all-gather.1

commit v17 on v16

--- a/solution.py
+++ b/solution.py
@@ -161,7 +161,7 @@
                            preferred_element_type=jnp.float32)
 
 
-def chol_inv_kernel(a_ref, l_ref, linv_ref, w_ref, d_ref, e_ref, ut_ref, x_ref):
+def chol_inv_kernel(a_ref, c_ref, l_ref, linv_ref, cs_ref, wt_ref, w_ref, d_ref, e_ref, ut_ref, x_ref):
     n = a_ref.shape[0]
     b = d_ref.shape[0]
     nb = n // b
@@ -217,15 +217,24 @@
             for k in range(j, i):
                 acc = acc + _mm(l_ref[i * b:(i + 1) * b, k * b:(k + 1) * b], linv_ref[k * b:(k + 1) * b, j * b:(j + 1) * b])
             linv_ref[i * b:(i + 1) * b, j * b:(j + 1) * b] = -_mm(linv_ref[i * b:(i + 1) * b, i * b:(i + 1) * b], acc)
-
-
-def chol_inv(a, b=128):
+    solved = _mm_t(c_ref[...], linv_ref[...])
+    cs_ref[...] = solved
+    wt_ref[...] = jnp.transpose(_mm(solved, linv_ref[...]))
+
+
+def chol_inv(a, c, b=128):
     n = a.shape[0]
+    m = c.shape[0]
     return pl.pallas_call(
         chol_inv_kernel,
-        out_shape=(jax.ShapeDtypeStruct((n, n), jnp.float32), jax.ShapeDtypeStruct((n, n), jnp.float32)),
-        in_specs=[pl.BlockSpec(memory_space=pltpu.VMEM)],
-        out_specs=(pl.BlockSpec(memory_space=pltpu.VMEM), pl.BlockSpec(memory_space=pltpu.VMEM)),
+        out_shape=(
+            jax.ShapeDtypeStruct((n, n), jnp.float32),
+            jax.ShapeDtypeStruct((n, n), jnp.float32),
+            jax.ShapeDtypeStruct((m, n), jnp.float32),
+            jax.ShapeDtypeStruct((n, m), jnp.float32),
+        ),
+        in_specs=[pl.BlockSpec(memory_space=pltpu.VMEM)] * 2,
+        out_specs=tuple(pl.BlockSpec(memory_space=pltpu.VMEM) for _ in range(4)),
         scratch_shapes=[
             pltpu.VMEM((n, n), jnp.float32),
             pltpu.VMEM((b, b), jnp.float32),
@@ -233,7 +242,7 @@
             pltpu.VMEM((b, b), jnp.float32),
             pltpu.VMEM((b, b), jnp.float32),
         ],
-    )(a)
+    )(a, c)
 
 
 def panel_product_kernel(subtract, use_top_ref, panel_ref, w_ref, base_ref, top_ref, out_ref):
@@ -302,9 +311,8 @@
     col_rows = jnp.where(leaf == 0, panel_rows, partner_rows)
     my_piece, pivot = lax.optimization_barrier((my_piece, pivot))
     panel = lax.all_gather(my_piece, "front", tiled=True)
-    factor, inverse = chol_inv(pivot)
-
-    col_solved = lax.dot_general(col_rows, inverse, (((1,), (1,)), ((), ())), precision=HIGHEST)
+    factor, inverse, col_solved, weights = chol_inv(pivot, col_rows)
+
 
     piv_cols = S // cols
     col_at = jnp.minimum(front, piv_cols - 1) * cols
@@ -317,7 +325,6 @@
         return panel_product(use_top, panel, inv_rows.T, assembled, top_rows, False)
 
     def other_columns():
-        weights = jnp.dot(col_solved, inverse, precision=HIGHEST).T
         return panel_product(use_top, panel, weights, assembled, col_solved.T, True)
 
     return lax.cond(front < piv_cols, pivot_columns, other_columns)

time: 185 us -> 198 us (1.070)
  local copies, waits for them, and re-layouts: 17.7 us -> 29.1 us
  matrix products: 2.63 us -> 0 us
  other arithmetic: 11.9 us -> 14.2 us
  waiting for transfers between devices: 0.05 us -> 2.28 us
    reshape x0 -> x2, local copies, waits for them, and re-layouts: none -> 5.8 us  [gather_half(): return picked.reshape(half_blocks * BLK, blocks.shape[2])]
    another operation x1 -> x2, local copies, waits for them, and re-layouts: 2.53 us -> 5.4 us
    unnamed x9 -> x6, local copies, waits for them, and re-layouts: 2.6 us -> 5.33 us
    dot_general x1 -> x0, matrix products: 2.63 us -> none  [per_device(): lax.dot_general(col_rows, inverse, (((1,), (1,)), ((), ())), precision=HI...]
    ppermute x1, waiting for transfers between devices: 0.01 us -> 2.26 us  [per_device(): partner_rows = lax.ppermute(panel_rows, 'leaf', [(0, 1)])]
    select_n x2 -> x1, other arithmetic: 5.25 us -> 4.72 us  [gather_half(): picked = jnp.where(found[:, None, None], picked, jnp.zeros_like(picked))]
  transfers between devices with their start and end apart: 5 -> 5, of which waited for: 0 -> 1; matrix products, arithmetic and copies ran while one was open for 6% -> 6% of each run, Pallas kernels for 66% -> 61%
where the time goes in v17:
time: 198 us; the launch traced here: 197 us
  Pallas kernels  133 us (67%)
  local copies, waits for them, and re-layouts  29.1 us (15%)
  other arithmetic  14.2 us (7%)
  between operations  13.5 us (7%)
  starting transfers between devices  5.31 us (3%)
  waiting for transfers between devices  2.28 us (1%)
    pallas_call x1, Pallas kernels, chol_inv(): pl.pallas_call(chol_inv_kernel, out_shape=(jax.ShapeDtypeStruct((n, n), j...  79.2 us
    pallas_call x1, Pallas kernels, broadcast_pivot(): pl.pallas_call(functools.partial(pivot_kernel, n_front, n_src), out_shape...  41.7 us
    pallas_call x1, Pallas kernels, panel_product(): pl.pallas_call(functools.partial(panel_product_kernel, subtract), out_sha...  11.6 us
    reshape x2, local copies, waits for them, and re-layouts, gather_half(): return picked.reshape(half_blocks * BLK, blocks.shape[2])  5.8 us
    another operation x2, local copies, waits for them, and re-layouts  5.4 us
    unnamed x6, local copies, waits for them, and re-layouts  5.33 us
    select_n x1, other arithmetic, gather_half(): picked = jnp.where(found[:, None, None], picked, jnp.zeros_like(picked))  4.72 us
    gather x2, local copies, waits for them, and re-layouts, gather_half(): picked = jnp.take(blocks, index, axis=0)  4.01 us
  transfers between devices with their start and end apart: 5, of which 1 were waited for; matrix products, arithmetic and copies ran while one was open for 6% of the time, Pallas kernels for 61%

profile of v17, /device:TPU:1, one launch (start us, length us, event | category | flops | bytes accessed | tf_op | source)
XLA Modules:
  0.0 196.9 jit_solution(1059462983429188354)
XLA Ops:
  6.5 0.0 copy-start
  6.5 0.0 all-gather.2.cloned.1.call-start
  6.5 1.5 compare_reduce_fusion
  8.1 0.8 compare_reduce_fusion.3
  8.9 1.4 compare_reduce_fusion.2
  10.3 0.0 copy-done
  10.3 2.0 %gather_fusion.1 = f32[32,128,128]{2,1,0:T(8,128)} fusion(f32[48,128,128]{2,1,0:T(8,128)S(1)} %bitcast.19, s32[1024]{0:T(1024)S(1)} %pad_clamp_fusion), kind=kCustom, calls=%fused_computation.1.clone | custom fusion | bytes 4194432 | tf_op jit(solution)/shard_map/jit(_take)/gather | solution.py:21
  12.3 2.0 %gather_fusion = f32[32,128,128]{2,1,0:T(8,128)} fusion(f32[48,128,128]{2,1,0:T(8,128)S(1)} %bitcast.18, s32[1024]{0:T(1024)S(1)} %pad_clamp_fusion.1), kind=kCustom, calls=%fused_computation.clone | custom fusion | bytes 4194432 | tf_op jit(solution)/shard_map/jit(_take)/gather | solution.py:21
  14.3 4.7 %select_select_fusion = (f32[32,128,128]{2,1,0:T(8,128)}, f32[32,128,128]{2,1,0:T(8,128)}) fusion(f32[32,128,128]{2,1,0:T(8,128)} %gather_fusion.1, pred[32]{0:T(512)(128)(4,1)S(1)} %compare_and_fusion, pred[32]{0:T(512)(128)(4,1)S(1)} %get-tuple-element.106, f32[32,128,128]{2,1,0:T(8,128)} %gather_fusion, pred[32]{0:T(512)(128)(4,1)S(1)} %compare_and_fusion.1, ...), kind=kLoop, calls=%fused_computation.4 | loop fusion | flops 2097152 | bytes 8388736 | tf_op jit(solution)/shard_map/jit(_where)/select_n | solution.py:22
  19.1 2.9 %copy.32 = f32[4096,128]{0,1:T(8,128)} copy(f32[4096,128]{1,0:T(8,128)} %bitcast.21) | data formatting | bytes 4194304 | tf_op jit(solution)/shard_map/reshape | solution.py:23
  22.0 1.4 collective-permute-start
  23.4 2.9 %copy.31 = f32[4096,128]{0,1:T(8,128)} copy(f32[4096,128]{1,0:T(8,128)} %bitcast.20) | data formatting | bytes 4194304 | tf_op jit(solution)/shard_map/reshape | solution.py:23
  26.3 2.9 %copy.24 = f32[4096,128]{0,1:T(8,128)} copy(f32[4096,128]{1,0:T(8,128)} %param.7) | data formatting | bytes 4194304 | tf_op args[0]
  29.2 0.0 collective-permute-done
  29.2 3.3 %select_add_fusion = f32[4096,128]{0,1:T(8,128)S(1)} fusion(f32[4096,128]{0,1:T(8,128)} %collective-permute-done, f32[4096,128]{0,1:T(8,128)} %copy.31, f32[4096,128]{0,1:T(8,128)} %copy.24, pred[]{:T(512)S(6)} %eq.22), kind=kLoop, calls=%fused_computation.6 | loop fusion | flops 2097152 | bytes 8388609 | tf_op jit(solution)/shard_map/add | solution.py:290
  32.5 0.0 copy-start.1
  32.5 1.4 copy-done.1
  33.9 0.8 fusion
  34.6 0.7 fusion.1
  35.3 1.3 collective-permute-start.2
  36.6 1.3 collective-permute-start.1
  38.0 1.8 copy.25.top_ref
  39.8 41.7 %shard_map.39 = f32[64,32,128]{2,1,0:T(8,128)} custom-call(f32[512,128]{1,0:T(8,128)} %copy.25.top_ref), custom_call_target="tpu_custom_call" | custom-call | tf_op jit(solution)/shard_map/pallas_call | solution.py:133
  81.4 1.9 copy.26
  83.3 1.0 copy.35
  84.4 0.0 collective-permute-done.2
  84.4 0.0 collective-permute-done.1
  84.4 0.7 broadcast_select_fusion.1
  85.1 0.0 all-gather.2.cloned.1.call-update
  85.1 1.3 collective-permute-start.3
  86.4 2.3 %collective-permute-done.3 = f32[128,512]{1,0:T(8,128)} collective-permute-done((f32[128,512]{1,0:T(8,128)S(1)}, f32[128,512]{1,0:T(8,128)}, u32[]{:S(2)}, u32[]{:S(2)}) %collective-permute-start.3) | collective-permute-done | bytes 262176 | tf_op jit(solution)/shard_map/ppermute | solution.py:310
  88.7 1.8 broadcast_select_fusion.c_ref
  90.4 79.2 %shard_map.40 = (f32[512,512]{1,0:T(8,128)}, f32[512,512]{1,0:T(8,128)}, f32[128,512]{1,0:T(8,128)}, f32[512,128]{1,0:T(8,128)S(1)}) custom-call(f32[512,512]{1,0:T(8,128)} %bitcast.22, f32[128,512]{1,0:T(8,128)} %broadcast_select_fusion.c_ref), custom_call_target="tpu_custom_call" | custom-call | tf_op jit(solution)/shard_map/pallas_call | solution.py:228
  169.7 0.0 all-gather.2.cloned.1.call-done
  169.7 20.4 %conditional.1 = (f32[4096,128]{1,0:T(8,128)}) conditional(s32[]{:T(128)} %convert_element_type.4, (f32[128,512]{1,0:T(8,128)}, s32[1]{0:T(128)}, f32[4096,512]{1,0:T(8,128)}, f32[512,128]{1,0:T(8,128)S(1)}, f32[4096,128]{0,1:T(8,128)}) %tuple.40, (s32[]{:T(128)}, f32[512,512]{1,0:T(8,128)}, f32[512,512]{1,0:T(8,128)}, s32[1]{0:T(128)}, ...), branch_computations={%region_4.6_spmd, %region_5.7_spmd} | conditional | flops 5 | bytes 7340106 | solution.py:330
  169.7 2.9 %copy.30.base_ref = f32[4096,128]{1,0:T(8,128)} copy(f32[4096,128]{0,1:T(8,128)} %get-tuple-element.104) | data formatting | bytes 4194304 | tf_op jit(solution)/shard_map
  172.6 1.7 constant_dynamic-slice_fusion.top_ref
  174.2 2.5 %copy.29 = f32[512,512]{0,1:T(8,128)} copy(f32[512,512]{1,0:T(8,128)} %get-tuple-element.100) | data formatting | bytes 2097152 | tf_op jit(solution)/shard_map
  176.8 1.7 dynamic-slice_bitcast_fusion.w_ref
  178.5 11.6 %branch_1_fun.2 = f32[4096,128]{1,0:T(8,128)} custom-call(s32[1]{0:T(128)} %get-tuple-element.49.use_top_ref, f32[4096,512]{1,0:T(8,128)} %get-tuple-element.50.panel_ref, f32[512,128]{1,0:T(8,128)} %dynamic-slice_bitcast_fusion.w_ref, f32[4096,128]{1,0:T(8,128)} %copy.30.base_ref, f32[512,128]{1,0:T(8,128)} %constant_dynamic-slice_fusion.top_ref), custom_call_target="tpu_custom_call" | custom-call | tf_op jit(solution)/shard_map/cond/branch_1_fun/pallas_call | solution.py:258
  (8 shorter events, 0.0 us)
Async XLA Ops:
  6.5 3.8 %copy-start = (f32[1,6144,128]{2,1,0:T(8,128)S(1)}, f32[1,6144,128]{2,1,0:T(8,128)}, u32[]{:S(2)}) copy-start(f32[1,6144,128]{2,1,0:T(8,128)} %param.8) | copy-start | bytes 9437188
  6.5 163.2 %all-gather.2.cloned.1.call-start = ((), (), s32[]{:S(2)}) async-start(), calls=%async_computation | async-start | bytes 8519680 | tf_op jit(solution)/shard_map/all_gather | solution.py:313
  22.0 7.2 %collective-permute-start = (f32[4096,128]{0,1:T(8,128)}, f32[4096,128]{0,1:T(8,128)}, u32[]{:S(2)}, u32[]{:S(2)}) collective-permute-start(f32[4096,128]{0,1:T(8,128)} %copy.32), channel_id=1, source_target_pairs={{0,64},{64,0},{1,65},{65,1},{2,66},{66,2},{3,67},{67,3},{4,68},{68... | collective-permute-start | bytes 6291464 | tf_op jit(solution)/shard_map/ppermute | solution.py:287
  32.5 1.4 copy-start.1
  35.3 49.0 %collective-permute-start.2 = (f32[64,512]{1,0:T(8,128)}, f32[64,512]{1,0:T(8,128)S(1)}, u32[]{:S(2)}, u32[]{:S(2)}) collective-permute-start(f32[64,512]{1,0:T(8,128)} %get-tuple-element.109), channel_id=1, source_target_pairs={{0,0},{1,2},{2,4},{3,6},{4,8},{5,10},{6,12},{7,14},{8,16},{9,18},{... | collective-permute-start | bytes 393224 | tf_op jit(solution)/shard_map/ppermute | solution.py:305
  36.6 47.8 %collective-permute-start.1 = (f32[64,512]{1,0:T(8,128)}, f32[64,512]{1,0:T(8,128)}, u32[]{:S(2)}, u32[]{:S(2)}) collective-permute-start(f32[64,512]{1,0:T(8,128)} %get-tuple-element.110), channel_id=1, source_target_pairs={{0,1},{1,3},{2,5},{3,7},{4,9},{5,11},{6,13},{7,15},{8,17},{9,19},{... | collective-permute-start | bytes 393224 | tf_op jit(solution)/shard_map/ppermute | solution.py:305
  85.1 3.6 %collective-permute-start.3 = (f32[128,512]{1,0:T(8,128)S(1)}, f32[128,512]{1,0:T(8,128)}, u32[]{:S(2)}, u32[]{:S(2)}) collective-permute-start(f32[128,512]{1,0:T(8,128)S(1)} %get-tuple-element.108), channel_id=1, source_target_pairs={{0,64},{1,65},{2,66},{3,67},{4,68},{5,69},{6,70},{7,71},{8,72},{9,... | collective-permute-start | bytes 786440 | tf_op jit(solution)/shard_map/ppermute | solution.py:310
Sparse Core Ops, SparseCore 0:
  85.2 82.0 all-gather.1

commit v18 on v16

--- a/solution.py
+++ b/solution.py
@@ -237,7 +237,8 @@
 
 
 def panel_product_kernel(subtract, use_top_ref, panel_ref, w_ref, base_ref, top_ref, out_ref):
-    prod = jnp.dot(panel_ref[...], w_ref[...], precision=HIGHEST, preferred_element_type=jnp.float32)
+    prod = jnp.transpose(lax.dot_general(w_ref[...], panel_ref[...], (((1,), (1,)), ((), ())),
+                                         precision=HIGHEST, preferred_element_type=jnp.float32))
     result = base_ref[...] - prod if subtract else prod
     replace = (pl.program_id(0) == 0) & (use_top_ref[0] == 1)
     out_ref[...] = jnp.where(replace, top_ref[...], result)
@@ -245,7 +246,7 @@
 
 def panel_product(use_top, panel, weights, base, top_rows, subtract):
     rows, depth = panel.shape
-    cols = weights.shape[1]
+    cols = weights.shape[0]
     return pl.pallas_call(
         functools.partial(panel_product_kernel, subtract),
         out_shape=jax.ShapeDtypeStruct((rows, cols), jnp.float32),
@@ -254,7 +255,7 @@
             grid=(rows // S,),
             in_specs=[
                 pl.BlockSpec((S, depth), lambda i, flag: (i, 0)),
-                pl.BlockSpec((depth, cols), lambda i, flag: (0, 0)),
+                pl.BlockSpec((cols, depth), lambda i, flag: (0, 0)),
                 pl.BlockSpec((S, cols), lambda i, flag: (i, 0)),
                 pl.BlockSpec((S, cols), lambda i, flag: (0, 0)),
             ],
@@ -314,10 +315,10 @@
     def pivot_columns():
         inv_rows = lax.dynamic_slice_in_dim(inverse, col_at, cols, 0)
         top_rows = lax.dynamic_slice_in_dim(factor, col_at, cols, 1)
-        return panel_product(use_top, panel, inv_rows.T, assembled, top_rows, False)
+        return panel_product(use_top, panel, inv_rows, assembled, top_rows, False)
 
     def other_columns():
-        weights = jnp.dot(col_solved, inverse, precision=HIGHEST).T
+        weights = jnp.dot(col_solved, inverse, precision=HIGHEST)
         return panel_product(use_top, panel, weights, assembled, col_solved.T, True)
 
     return lax.cond(front < piv_cols, pivot_columns, other_columns)

time: 185 us -> 183 us (0.989)
  local copies, waits for them, and re-layouts: 17.7 us -> 15.2 us
    another operation x1 -> x0, local copies, waits for them, and re-layouts: 2.53 us -> none
where the time goes in v18:
time: 183 us; the launch traced here: 182 us
  Pallas kernels  133 us (73%)
  local copies, waits for them, and re-layouts  15.2 us (8%)
  between operations  13.5 us (7%)
  other arithmetic  11.9 us (7%)
  starting transfers between devices  5.38 us (3%)
  matrix products  2.63 us (1%)
    pallas_call x1, Pallas kernels, chol_inv(): pl.pallas_call(chol_inv_kernel, out_shape=(jax.ShapeDtypeStruct((n, n), j...  78.1 us
    pallas_call x1, Pallas kernels, broadcast_pivot(): pl.pallas_call(functools.partial(pivot_kernel, n_front, n_src), out_shape...  42.4 us
    pallas_call x1, Pallas kernels, panel_product(): pl.pallas_call(functools.partial(panel_product_kernel, subtract), out_sha...  12.6 us
    select_n x2, other arithmetic, gather_half(): picked = jnp.where(found[:, None, None], picked, jnp.zeros_like(picked))  5.25 us
    gather x2, local copies, waits for them, and re-layouts, gather_half(): picked = jnp.take(blocks, index, axis=0)  3.98 us
  transfers between devices with their start and end apart: 5, of which 0 were waited for; matrix products, arithmetic and copies ran while one was open for 6% of the time, Pallas kernels for 66%

profile of v18, /device:TPU:1, one launch (start us, length us, event | category | flops | bytes accessed | tf_op | source)
XLA Modules:
  0.0 181.7 jit_solution(10662404695927259678)
XLA Ops:
  6.5 0.0 copy-start
  6.5 0.0 all-gather.2.cloned.1.call-start
  6.5 1.5 compare_reduce_fusion
  8.1 0.8 compare_reduce_fusion.3
  8.9 0.0 copy-done
  8.9 2.0 %gather_fusion.1 = f32[32,128,128]{2,1,0:T(8,128)} fusion(f32[48,128,128]{2,1,0:T(8,128)S(1)} %bitcast.31, s32[1024]{0:T(1024)S(1)} %pad_clamp_fusion), kind=kCustom, calls=%fused_computation.1.clone | custom fusion | bytes 4194432 | tf_op jit(solution)/shard_map/jit(_take)/gather | solution.py:21
  10.9 0.0 copy-start.3
  10.9 3.2 %select_select_fusion = f32[32,128,128]{2,1,0:T(8,128)} fusion(f32[32,128,128]{2,1,0:T(8,128)} %gather_fusion.1, pred[32]{0:T(512)(128)(4,1)S(1)} %compare_and_fusion, pred[32]{0:T(512)(128)(4,1)S(1)} %get-tuple-element.90), kind=kLoop, calls=%fused_computation.8 | loop fusion | flops 1048576 | bytes 4194368 | tf_op jit(solution)/shard_map/jit(_where)/select_n | solution.py:22
  14.1 1.4 collective-permute-start
  15.6 0.0 copy-done.3
  15.6 0.7 compare_reduce_fusion.2
  16.3 2.0 %gather_fusion = f32[32,128,128]{2,1,0:T(8,128)} fusion(f32[48,128,128]{2,1,0:T(8,128)S(1)} %bitcast.30, s32[1024]{0:T(1024)S(1)} %pad_clamp_fusion.1), kind=kCustom, calls=%fused_computation.clone | custom fusion | bytes 4194432 | tf_op jit(solution)/shard_map/jit(_take)/gather | solution.py:21
  18.3 0.0 copy-start.2
  18.3 2.0 %select_select_fusion.1 = f32[32,128,128]{2,1,0:T(8,128)S(1)} fusion(f32[32,128,128]{2,1,0:T(8,128)} %gather_fusion, pred[32]{0:T(512)(128)(4,1)S(1)} %compare_and_fusion.1, pred[32]{0:T(512)(128)(4,1)S(1)} %get-tuple-element.89), kind=kLoop, calls=%fused_computation.9 | loop fusion | flops 1048576 | bytes 4194368 | tf_op jit(solution)/shard_map/jit(_where)/select_n | solution.py:22
  20.3 0.0 collective-permute-done
  20.3 0.2 copy-done.2
  20.5 1.9 %fusion.1 = f32[4096,128]{1,0:T(8,128)S(1)} fusion(f32[4096,128]{1,0:T(8,128)S(1)} %copy-done.2, f32[4096,128]{1,0:T(8,128)} %collective-permute-done, f32[32,128,128]{2,1,0:T(8,128)S(1)} %select_select_fusion.1, pred[]{:T(512)S(6)} %eq.21), kind=kLoop, calls=%fused_computation.7 | loop fusion | flops 2097152 | bytes 8388609 | tf_op jit(solution)/shard_map/add | solution.py:282
  22.4 0.0 copy-start.1
  22.4 1.4 copy-done.1
  23.8 0.7 fusion.7
  24.5 0.9 fusion.8
  25.4 1.3 collective-permute-start.3
  26.7 1.4 collective-permute-start.2
  28.0 42.4 %shard_map.39 = f32[64,32,128]{2,1,0:T(8,128)} custom-call(f32[512,128]{1,0:T(8,128)} %get-tuple-element.91.top_ref), custom_call_target="tpu_custom_call" | custom-call | tf_op jit(solution)/shard_map/pallas_call | solution.py:133
  70.4 1.9 %copy.13 = f32[4,16,32,128]{3,0,2,1:T(4,128)S(1)} copy(f32[4,16,32,128]{3,2,1,0:T(8,128)} %bitcast.32) | data formatting | bytes 2097152 | tf_op jit(solution)/shard_map/reshape | solution.py:149
  72.3 1.0 copy.19
  73.4 0.0 collective-permute-done.3
  73.4 0.0 collective-permute-done.2
  73.4 1.7 broadcast_select_fusion
  75.1 1.7 copy.14
  76.8 0.0 all-gather.2.cloned.1.call-update
  76.8 1.3 collective-permute-start.1
  78.1 78.1 %shard_map.40 = (f32[512,512]{1,0:T(8,128)}, f32[512,512]{1,0:T(8,128)}) custom-call(f32[512,512]{1,0:T(8,128)} %bitcast.33), custom_call_target="tpu_custom_call" | custom-call | tf_op jit(solution)/shard_map/pallas_call | solution.py:224
  156.2 0.0 collective-permute-done.1
  156.2 2.6 %fusion.2 = f32[128,512]{1,0:T(8,128)S(1)} fusion(f32[512,512]{1,0:T(8,128)} %get-tuple-element.64, f32[128,512]{0,1:T(8,128)} %collective-permute-done.1, pred[]{:T(512)S(6)} %eq.21, f32[4096,128]{1,0:T(8,128)} %copy-done.1), kind=kOutput, calls=%fused_computation.11 | convolution fusion | flops 402718720 | bytes 1835009 | tf_op jit(solution)/shard_map/dot_general | solution.py:308
  158.8 0.0 all-gather.2.cloned.1.call-done
  158.9 16.0 %conditional.1 = (f32[4096,128]{1,0:T(8,128)}) conditional(s32[]{:T(128)} %convert_element_type.4, (f32[128,512]{1,0:T(8,128)S(1)}, f32[512,512]{1,0:T(8,128)}, s32[1]{0:T(128)}, f32[4096,512]{1,0:T(8,128)}, f32[4096,128]{1,0:T(8,128)}) %tuple.38, (s32[]{:T(128)}, f32[512,512]{1,0:T(8,128)}, f32[512,512]{1,0:T(8,128)}, s32[1]{0:T(128)}, ...), branch_computations={%region_4.6_spmd, %region_5.7_spmd} | conditional | flops 402653184 | bytes 2097160 | solution.py:324
  158.9 1.7 constant_dynamic-slice_fusion.1.w_ref
  160.6 1.7 constant_dynamic-slice_fusion.top_ref
  162.2 12.6 %branch_1_fun.2 = f32[4096,128]{1,0:T(8,128)} custom-call(s32[1]{0:T(128)} %get-tuple-element.49.use_top_ref, f32[4096,512]{1,0:T(8,128)} %get-tuple-element.50.panel_ref, f32[128,512]{1,0:T(8,128)} %constant_dynamic-slice_fusion.1.w_ref, f32[4096,128]{1,0:T(8,128)} %get-tuple-element.53.base_ref, f32[512,128]{1,0:T(8,128)} %constant_dynamic-slice_fusion.top_ref), custom_call_target="tpu_custom_call" | custom-call | tf_op jit(solution)/shard_map/cond/branch_1_fun/pallas_call | solution.py:250
  (7 shorter events, 0.0 us)
Async XLA Ops:
  6.5 2.4 %copy-start = (f32[1,6144,128]{2,1,0:T(8,128)S(1)}, f32[1,6144,128]{2,1,0:T(8,128)}, u32[]{:S(2)}) copy-start(f32[1,6144,128]{2,1,0:T(8,128)} %param.8) | copy-start | bytes 9437188
  6.5 152.3 %all-gather.2.cloned.1.call-start = ((), (), s32[]{:S(2)}) async-start(), calls=%async_computation | async-start | bytes 8519680 | tf_op jit(solution)/shard_map/all_gather | solution.py:305
  10.9 4.6 %copy-start.3 = (s32[1,48]{1,0:T(1,128)S(1)}, s32[1,48]{1,0:T(1,128)}, u32[]{:S(2)}) copy-start(s32[1,48]{1,0:T(1,128)} %param.9) | copy-start | bytes 580
  14.1 6.2 %collective-permute-start = (f32[4096,128]{1,0:T(8,128)}, f32[4096,128]{1,0:T(8,128)}, u32[]{:S(2)}, u32[]{:S(2)}) collective-permute-start(f32[4096,128]{1,0:T(8,128)} %bitcast.4), channel_id=1, source_target_pairs={{0,64},{64,0},{1,65},{65,1},{2,66},{66,2},{3,67},{67,3},{4,68},{68... | collective-permute-start | bytes 6291464 | tf_op jit(solution)/shard_map/ppermute | solution.py:279
  18.3 2.2 %copy-start.2 = (f32[4096,128]{1,0:T(8,128)S(1)}, f32[4096,128]{1,0:T(8,128)}, u32[]{:S(2)}) copy-start(f32[4096,128]{1,0:T(8,128)} %param.7) | copy-start | bytes 6291460
  22.4 1.4 copy-start.1
  25.4 48.0 %collective-permute-start.3 = (f32[64,512]{0,1:T(8,128)}, f32[64,512]{0,1:T(8,128)}, u32[]{:S(2)}, u32[]{:S(2)}) collective-permute-start(f32[64,512]{0,1:T(8,128)} %get-tuple-element.93), channel_id=1, source_target_pairs={{0,0},{1,2},{2,4},{3,6},{4,8},{5,10},{6,12},{7,14},{8,16},{9,18},{... | collective-permute-start | bytes 393224 | tf_op jit(solution)/shard_map/ppermute | solution.py:297
  26.7 46.7 %collective-permute-start.2 = (f32[64,512]{0,1:T(8,128)}, f32[64,512]{0,1:T(8,128)}, u32[]{:S(2)}, u32[]{:S(2)}) collective-permute-start(f32[64,512]{0,1:T(8,128)} %get-tuple-element.94), channel_id=1, source_target_pairs={{0,1},{1,3},{2,5},{3,7},{4,9},{5,11},{6,13},{7,15},{8,17},{9,19},{... | collective-permute-start | bytes 393224 | tf_op jit(solution)/shard_map/ppermute | solution.py:297
  76.8 79.4 %collective-permute-start.1 = (f32[128,512]{0,1:T(8,128)S(1)}, f32[128,512]{0,1:T(8,128)}, u32[]{:S(2)}, u32[]{:S(2)}) collective-permute-start(f32[128,512]{0,1:T(8,128)S(1)} %get-tuple-element.92), channel_id=1, source_target_pairs={{0,64},{1,65},{2,66},{3,67},{4,68},{5,69},{6,70},{7,71},{8,72},{9,... | collective-permute-start | bytes 786440 | tf_op jit(solution)/shard_map/ppermute | solution.py:302
Sparse Core Ops, SparseCore 0:
  76.9 80.1 all-gather.1

commit v19 on v18

--- a/solution.py
+++ b/solution.py
@@ -146,7 +146,7 @@
         ],
         compiler_params=pltpu.CompilerParams(has_side_effects=True),
     )(top)
-    return gathered.reshape(n_src, per_src, rows, cols).transpose(1, 2, 0, 3).reshape(S, S)
+    return gathered
 
 
 PANEL = 8
@@ -162,13 +162,17 @@
 
 
 def chol_inv_kernel(a_ref, l_ref, linv_ref, w_ref, d_ref, e_ref, ut_ref, x_ref):
-    n = a_ref.shape[0]
+    n = w_ref.shape[0]
     b = d_ref.shape[0]
     nb = n // b
     lane = lax.broadcasted_iota(jnp.int32, (PANEL, b), 1)
     sub = lax.broadcasted_iota(jnp.int32, (PANEL, 1), 0)
     eye = (lax.broadcasted_iota(jnp.int32, (b, b), 0) == lax.broadcasted_iota(jnp.int32, (b, b), 1)).astype(jnp.float32)
-    w_ref[...] = a_ref[...]
+    n_slots, rows, cols = a_ref.shape
+    per_src = n_slots // (n // cols)
+    for slot in range(n_slots):
+        c, k = divmod(slot, per_src)
+        w_ref[k * rows:(k + 1) * rows, c * cols:(c + 1) * cols] = a_ref[slot]
     l_ref[...] = jnp.zeros_like(l_ref)
     linv_ref[...] = jnp.zeros_like(linv_ref)
 
@@ -219,8 +223,7 @@
             linv_ref[i * b:(i + 1) * b, j * b:(j + 1) * b] = -_mm(linv_ref[i * b:(i + 1) * b, i * b:(i + 1) * b], acc)
 
 
-def chol_inv(a, b=128):
-    n = a.shape[0]
+def chol_inv(a, n, b=128):
     return pl.pallas_call(
         chol_inv_kernel,
         out_shape=(jax.ShapeDtypeStruct((n, n), jnp.float32), jax.ShapeDtypeStruct((n, n), jnp.float32)),
@@ -303,7 +306,7 @@
     col_rows = jnp.where(leaf == 0, panel_rows, partner_rows)
     my_piece, pivot = lax.optimization_barrier((my_piece, pivot))
     panel = lax.all_gather(my_piece, "front", tiled=True)
-    factor, inverse = chol_inv(pivot)
+    factor, inverse = chol_inv(pivot, S)
 
     col_solved = lax.dot_general(col_rows, inverse, (((1,), (1,)), ((), ())), precision=HIGHEST)
 

time: 183 us -> 180 us (0.984)
  local copies, waits for them, and re-layouts: 15.2 us -> 12.2 us
    reshape x1 -> x0, local copies, waits for them, and re-layouts: 1.93 us -> none  [broadcast_pivot(): gathered.reshape(n_src, per_src, rows, cols).transpose(1, 2, 0, 3)]
  transfers between devices with their start and end apart: 5 -> 5, of which waited for: 0 -> 0; matrix products, arithmetic and copies ran while one was open for 6% -> 4% of each run, Pallas kernels for 66% -> 67%
where the time goes in v19:
time: 180 us; the launch traced here: 179 us
  Pallas kernels  133 us (74%)
  between operations  13.5 us (8%)
  local copies, waits for them, and re-layouts  12.2 us (7%)
  other arithmetic  11.9 us (7%)
  starting transfers between devices  5.38 us (3%)
  matrix products  2.63 us (1%)
    pallas_call x1, Pallas kernels, chol_inv(): pl.pallas_call(chol_inv_kernel, out_shape=(jax.ShapeDtypeStruct((n, n), j...  78.1 us
    pallas_call x1, Pallas kernels, broadcast_pivot(): pl.pallas_call(functools.partial(pivot_kernel, n_front, n_src), out_shape...  42.4 us
    pallas_call x1, Pallas kernels, panel_product(): pl.pallas_call(functools.partial(panel_product_kernel, subtract), out_sha...  12.6 us
    select_n x2, other arithmetic, gather_half(): picked = jnp.where(found[:, None, None], picked, jnp.zeros_like(picked))  5.25 us
    gather x2, local copies, waits for them, and re-layouts, gather_half(): picked = jnp.take(blocks, index, axis=0)  3.98 us
  transfers between devices with their start and end apart: 5, of which 0 were waited for; matrix products, arithmetic and copies ran while one was open for 4% of the time, Pallas kernels for 67%

profile of v19, /device:TPU:1, one launch (start us, length us, event | category | flops | bytes accessed | tf_op | source)
XLA Modules:
  0.0 178.9 jit_solution(12364613210278046275)
XLA Ops:
  6.5 0.0 copy-start
  6.5 0.0 all-gather.2.cloned.1.call-start
  6.5 1.5 compare_reduce_fusion
  8.1 0.8 compare_reduce_fusion.3
  8.9 0.0 copy-done
  8.9 2.0 %gather_fusion.1 = f32[32,128,128]{2,1,0:T(8,128)} fusion(f32[48,128,128]{2,1,0:T(8,128)S(1)} %bitcast.24, s32[1024]{0:T(1024)S(1)} %pad_clamp_fusion), kind=kCustom, calls=%fused_computation.1.clone | custom fusion | bytes 4194432 | tf_op jit(solution)/shard_map/jit(_take)/gather | solution.py:21
  10.9 0.0 copy-start.3
  10.9 3.2 %select_select_fusion = f32[32,128,128]{2,1,0:T(8,128)} fusion(f32[32,128,128]{2,1,0:T(8,128)} %gather_fusion.1, pred[32]{0:T(512)(128)(4,1)S(1)} %compare_and_fusion, pred[32]{0:T(512)(128)(4,1)S(1)} %get-tuple-element.90), kind=kLoop, calls=%fused_computation.8 | loop fusion | flops 1048576 | bytes 4194368 | tf_op jit(solution)/shard_map/jit(_where)/select_n | solution.py:22
  14.1 1.4 collective-permute-start
  15.6 0.0 copy-done.3
  15.6 0.7 compare_reduce_fusion.2
  16.3 2.0 %gather_fusion = f32[32,128,128]{2,1,0:T(8,128)} fusion(f32[48,128,128]{2,1,0:T(8,128)S(1)} %bitcast.23, s32[1024]{0:T(1024)S(1)} %pad_clamp_fusion.1), kind=kCustom, calls=%fused_computation.clone | custom fusion | bytes 4194432 | tf_op jit(solution)/shard_map/jit(_take)/gather | solution.py:21
  18.3 0.0 copy-start.2
  18.3 2.0 %select_select_fusion.1 = f32[32,128,128]{2,1,0:T(8,128)S(1)} fusion(f32[32,128,128]{2,1,0:T(8,128)} %gather_fusion, pred[32]{0:T(512)(128)(4,1)S(1)} %compare_and_fusion.1, pred[32]{0:T(512)(128)(4,1)S(1)} %get-tuple-element.89), kind=kLoop, calls=%fused_computation.9 | loop fusion | flops 1048576 | bytes 4194368 | tf_op jit(solution)/shard_map/jit(_where)/select_n | solution.py:22
  20.3 0.0 collective-permute-done
  20.3 0.2 copy-done.2
  20.5 1.9 %fusion.1 = f32[4096,128]{1,0:T(8,128)S(1)} fusion(f32[4096,128]{1,0:T(8,128)S(1)} %copy-done.2, f32[4096,128]{1,0:T(8,128)} %collective-permute-done, f32[32,128,128]{2,1,0:T(8,128)S(1)} %select_select_fusion.1, pred[]{:T(512)S(6)} %eq.21), kind=kLoop, calls=%fused_computation.7 | loop fusion | flops 2097152 | bytes 8388609 | tf_op jit(solution)/shard_map/add | solution.py:285
  22.4 0.0 copy-start.1
  22.4 1.4 copy-done.1
  23.8 0.7 fusion.7
  24.5 0.9 fusion.8
  25.4 1.3 collective-permute-start.3
  26.7 1.4 collective-permute-start.2
  28.1 42.4 %shard_map.39.a_ref = f32[64,32,128]{2,1,0:T(8,128)} custom-call(f32[512,128]{1,0:T(8,128)} %get-tuple-element.91.top_ref), custom_call_target="tpu_custom_call" | custom-call | tf_op jit(solution)/shard_map/pallas_call | solution.py:133
  70.5 0.0 collective-permute-done.3
  70.5 0.0 collective-permute-done.2
  70.5 1.7 broadcast_select_fusion
  72.2 1.7 copy.11
  73.9 0.0 all-gather.2.cloned.1.call-update
  73.9 1.3 collective-permute-start.1
  75.2 78.1 %shard_map.40 = (f32[512,512]{1,0:T(8,128)}, f32[512,512]{1,0:T(8,128)}) custom-call(f32[64,32,128]{2,1,0:T(8,128)} %shard_map.39.a_ref), custom_call_target="tpu_custom_call" | custom-call | tf_op jit(solution)/shard_map/pallas_call | solution.py:227
  153.4 0.0 collective-permute-done.1
  153.4 2.6 %fusion.2 = f32[128,512]{1,0:T(8,128)S(1)} fusion(f32[512,512]{1,0:T(8,128)} %get-tuple-element.64, f32[128,512]{0,1:T(8,128)} %collective-permute-done.1, pred[]{:T(512)S(6)} %eq.21, f32[4096,128]{1,0:T(8,128)} %copy-done.1), kind=kOutput, calls=%fused_computation.10 | convolution fusion | flops 402718720 | bytes 1835009 | tf_op jit(solution)/shard_map/dot_general | solution.py:311
  156.0 0.0 all-gather.2.cloned.1.call-done
  156.0 16.0 %conditional.1 = (f32[4096,128]{1,0:T(8,128)}) conditional(s32[]{:T(128)} %convert_element_type.4, (f32[128,512]{1,0:T(8,128)S(1)}, f32[512,512]{1,0:T(8,128)}, s32[1]{0:T(128)}, f32[4096,512]{1,0:T(8,128)}, f32[4096,128]{1,0:T(8,128)}) %tuple.38, (s32[]{:T(128)}, f32[512,512]{1,0:T(8,128)}, f32[512,512]{1,0:T(8,128)}, s32[1]{0:T(128)}, ...), branch_computations={%region_4.6_spmd, %region_5.7_spmd} | conditional | flops 402653184 | bytes 2097160 | solution.py:327
  156.0 1.7 constant_dynamic-slice_fusion.1.w_ref
  157.7 1.7 constant_dynamic-slice_fusion.top_ref
  159.4 12.6 %branch_1_fun.2 = f32[4096,128]{1,0:T(8,128)} custom-call(s32[1]{0:T(128)} %get-tuple-element.49.use_top_ref, f32[4096,512]{1,0:T(8,128)} %get-tuple-element.50.panel_ref, f32[128,512]{1,0:T(8,128)} %constant_dynamic-slice_fusion.1.w_ref, f32[4096,128]{1,0:T(8,128)} %get-tuple-element.53.base_ref, f32[512,128]{1,0:T(8,128)} %constant_dynamic-slice_fusion.top_ref), custom_call_target="tpu_custom_call" | custom-call | tf_op jit(solution)/shard_map/cond/branch_1_fun/pallas_call | solution.py:253
  (7 shorter events, 0.0 us)
Async XLA Ops:
  6.5 2.4 %copy-start = (f32[1,6144,128]{2,1,0:T(8,128)S(1)}, f32[1,6144,128]{2,1,0:T(8,128)}, u32[]{:S(2)}) copy-start(f32[1,6144,128]{2,1,0:T(8,128)} %param.8) | copy-start | bytes 9437188
  6.5 149.5 %all-gather.2.cloned.1.call-start = ((), (), s32[]{:S(2)}) async-start(), calls=%async_computation | async-start | bytes 8519680 | tf_op jit(solution)/shard_map/all_gather | solution.py:308
  10.9 4.6 %copy-start.3 = (s32[1,48]{1,0:T(1,128)S(1)}, s32[1,48]{1,0:T(1,128)}, u32[]{:S(2)}) copy-start(s32[1,48]{1,0:T(1,128)} %param.9) | copy-start | bytes 580
  14.1 6.2 %collective-permute-start = (f32[4096,128]{1,0:T(8,128)}, f32[4096,128]{1,0:T(8,128)}, u32[]{:S(2)}, u32[]{:S(2)}) collective-permute-start(f32[4096,128]{1,0:T(8,128)} %bitcast.4), channel_id=1, source_target_pairs={{0,64},{64,0},{1,65},{65,1},{2,66},{66,2},{3,67},{67,3},{4,68},{68... | collective-permute-start | bytes 6291464 | tf_op jit(solution)/shard_map/ppermute | solution.py:282
  18.3 2.2 %copy-start.2 = (f32[4096,128]{1,0:T(8,128)S(1)}, f32[4096,128]{1,0:T(8,128)}, u32[]{:S(2)}) copy-start(f32[4096,128]{1,0:T(8,128)} %param.7) | copy-start | bytes 6291460
  22.4 1.4 copy-start.1
  25.4 45.1 %collective-permute-start.3 = (f32[64,512]{0,1:T(8,128)}, f32[64,512]{0,1:T(8,128)}, u32[]{:S(2)}, u32[]{:S(2)}) collective-permute-start(f32[64,512]{0,1:T(8,128)} %get-tuple-element.93), channel_id=1, source_target_pairs={{0,0},{1,2},{2,4},{3,6},{4,8},{5,10},{6,12},{7,14},{8,16},{9,18},{... | collective-permute-start | bytes 393224 | tf_op jit(solution)/shard_map/ppermute | solution.py:300
  26.7 43.8 %collective-permute-start.2 = (f32[64,512]{0,1:T(8,128)}, f32[64,512]{0,1:T(8,128)}, u32[]{:S(2)}, u32[]{:S(2)}) collective-permute-start(f32[64,512]{0,1:T(8,128)} %get-tuple-element.94), channel_id=1, source_target_pairs={{0,1},{1,3},{2,5},{3,7},{4,9},{5,11},{6,13},{7,15},{8,17},{9,19},{... | collective-permute-start | bytes 393224 | tf_op jit(solution)/shard_map/ppermute | solution.py:300
  73.9 79.5 %collective-permute-start.1 = (f32[128,512]{0,1:T(8,128)S(1)}, f32[128,512]{0,1:T(8,128)}, u32[]{:S(2)}, u32[]{:S(2)}) collective-permute-start(f32[128,512]{0,1:T(8,128)S(1)} %get-tuple-element.92), channel_id=1, source_target_pairs={{0,64},{1,65},{2,66},{3,67},{4,68},{5,69},{6,70},{7,71},{8,72},{9,... | collective-permute-start | bytes 786440 | tf_op jit(solution)/shard_map/ppermute | solution.py:305
Sparse Core Ops, SparseCore 0:
  74.0 80.2 all-gather.1

commit v20 on v19

--- a/solution.py
+++ b/solution.py
@@ -287,6 +287,9 @@
     top = assembled[:S]
     panel_rows = top.T
 
+    pivot = broadcast_pivot(top, n_front)
+    piece_rows, pivot = lax.optimization_barrier((panel_rows, pivot))
+
     piece = rows // n_front
     per_block = BLK // piece
     pieces = []
@@ -297,14 +300,12 @@
                 src = lf * half_blocks + k
                 dst = lf * n_front + per_block * k + part
                 pairs.append((src, dst))
-        pieces.append(lax.ppermute(panel_rows[part * piece:(part + 1) * piece], ("leaf", "front"), pairs))
+        pieces.append(lax.ppermute(piece_rows[part * piece:(part + 1) * piece], ("leaf", "front"), pairs))
     my_piece = pieces[0]
     for part in range(1, per_block):
         my_piece = jnp.where(front % per_block == part, pieces[part], my_piece)
-    pivot = broadcast_pivot(top, n_front)
     partner_rows = lax.ppermute(panel_rows, "leaf", [(0, 1)])
     col_rows = jnp.where(leaf == 0, panel_rows, partner_rows)
-    my_piece, pivot = lax.optimization_barrier((my_piece, pivot))
     panel = lax.all_gather(my_piece, "front", tiled=True)
     factor, inverse = chol_inv(pivot, S)
 

time: 180 us -> 186 us (1.033)
  waiting for transfers between devices: 0.05 us -> 11.5 us
  Pallas kernels: 133 us -> 128 us
    ppermute x2, waiting for transfers between devices: 0.01 us -> 6.83 us  [per_device(): lax.ppermute(piece_rows[part * piece:(part + 1) * piece], ('leaf', 'front...]
    pallas_call x1, Pallas kernels: 42.4 us -> 36.8 us  [broadcast_pivot(): pl.pallas_call(functools.partial(pivot_kernel, n_front, n_src), out_shape...]
    all_gather x1, waiting for transfers between devices: 0.02 us -> 4.62 us  [per_device(): panel = lax.all_gather(my_piece, 'front', tiled=True)]
  transfers between devices with their start and end apart: 5 -> 5, of which waited for: 0 -> 2; matrix products, arithmetic and copies ran while one was open for 4% -> 4% of each run, Pallas kernels for 67% -> 42%
where the time goes in v20:
time: 186 us; the launch traced here: 185 us
  Pallas kernels  128 us (69%)
  between operations  13.5 us (7%)
  local copies, waits for them, and re-layouts  12.2 us (7%)
  other arithmetic  11.9 us (6%)
  waiting for transfers between devices  11.5 us (6%)
  starting transfers between devices  5.38 us (3%)
  matrix products  2.73 us (1%)
    pallas_call x1, Pallas kernels, chol_inv(): pl.pallas_call(chol_inv_kernel, out_shape=(jax.ShapeDtypeStruct((n, n), j...  78.1 us
    pallas_call x1, Pallas kernels, broadcast_pivot(): pl.pallas_call(functools.partial(pivot_kernel, n_front, n_src), out_shape...  36.8 us
    pallas_call x1, Pallas kernels, panel_product(): pl.pallas_call(functools.partial(panel_product_kernel, subtract), out_sha...  12.6 us
    ppermute x2, waiting for transfers between devices, per_device(): lax.ppermute(piece_rows[part * piece:(part + 1) * piece], ('leaf', 'front...  6.83 us
    select_n x2, other arithmetic, gather_half(): picked = jnp.where(found[:, None, None], picked, jnp.zeros_like(picked))  5.25 us
    all_gather x1, waiting for transfers between devices, per_device(): panel = lax.all_gather(my_piece, 'front', tiled=True)  4.62 us
    gather x2, local copies, waits for them, and re-layouts, gather_half(): picked = jnp.take(blocks, index, axis=0)  3.98 us
  transfers between devices with their start and end apart: 5, of which 2 were waited for; matrix products, arithmetic and copies ran while one was open for 4% of the time, Pallas kernels for 42%

profile of v20, /device:TPU:1, one launch (start us, length us, event | category | flops | bytes accessed | tf_op | source)
XLA Modules:
  0.0 184.7 jit_solution(4463886597706395366)
XLA Ops:
  6.5 0.0 copy-start
  6.5 0.0 all-gather.2.cloned.1.call-start
  6.5 1.5 compare_reduce_fusion
  8.1 0.8 compare_reduce_fusion.3
  8.9 0.0 copy-done
  8.9 2.0 %gather_fusion.1 = f32[32,128,128]{2,1,0:T(8,128)} fusion(f32[48,128,128]{2,1,0:T(8,128)S(1)} %bitcast.24, s32[1024]{0:T(1024)S(1)} %pad_clamp_fusion), kind=kCustom, calls=%fused_computation.1.clone | custom fusion | bytes 4194432 | tf_op jit(solution)/shard_map/jit(_take)/gather | solution.py:21
  10.9 0.0 copy-start.3
  10.9 3.2 %select_select_fusion = f32[32,128,128]{2,1,0:T(8,128)} fusion(f32[32,128,128]{2,1,0:T(8,128)} %gather_fusion.1, pred[32]{0:T(512)(128)(4,1)S(1)} %compare_and_fusion, pred[32]{0:T(512)(128)(4,1)S(1)} %get-tuple-element.90), kind=kLoop, calls=%fused_computation.8 | loop fusion | flops 1048576 | bytes 4194368 | tf_op jit(solution)/shard_map/jit(_where)/select_n | solution.py:22
  14.1 1.4 collective-permute-start
  15.6 0.0 copy-done.3
  15.6 0.7 compare_reduce_fusion.2
  16.3 2.0 %gather_fusion = f32[32,128,128]{2,1,0:T(8,128)} fusion(f32[48,128,128]{2,1,0:T(8,128)S(1)} %bitcast.23, s32[1024]{0:T(1024)S(1)} %pad_clamp_fusion.1), kind=kCustom, calls=%fused_computation.clone | custom fusion | bytes 4194432 | tf_op jit(solution)/shard_map/jit(_take)/gather | solution.py:21
  18.3 0.0 copy-start.2
  18.3 2.0 %select_select_fusion.1 = f32[32,128,128]{2,1,0:T(8,128)S(1)} fusion(f32[32,128,128]{2,1,0:T(8,128)} %gather_fusion, pred[32]{0:T(512)(128)(4,1)S(1)} %compare_and_fusion.1, pred[32]{0:T(512)(128)(4,1)S(1)} %get-tuple-element.89), kind=kLoop, calls=%fused_computation.9 | loop fusion | flops 1048576 | bytes 4194368 | tf_op jit(solution)/shard_map/jit(_where)/select_n | solution.py:22
  20.3 0.0 collective-permute-done
  20.3 0.2 copy-done.2
  20.5 1.9 %fusion.1 = f32[4096,128]{1,0:T(8,128)S(1)} fusion(f32[4096,128]{1,0:T(8,128)S(1)} %copy-done.2, f32[4096,128]{1,0:T(8,128)} %collective-permute-done, f32[32,128,128]{2,1,0:T(8,128)S(1)} %select_select_fusion.1, pred[]{:T(512)S(6)} %eq.21), kind=kLoop, calls=%fused_computation.7 | loop fusion | flops 2097152 | bytes 8388609 | tf_op jit(solution)/shard_map/add | solution.py:285
  22.4 0.0 copy-start.1
  22.4 1.4 copy-done.1
  23.8 0.7 fusion.7
  24.5 36.8 %shard_map.39.a_ref = f32[64,32,128]{2,1,0:T(8,128)} custom-call(f32[512,128]{1,0:T(8,128)} %get-tuple-element.91.top_ref), custom_call_target="tpu_custom_call" | custom-call | tf_op jit(solution)/shard_map/pallas_call | solution.py:133
  61.3 0.9 fusion.8
  62.2 1.3 collective-permute-start.3
  63.5 1.4 collective-permute-start.2
  64.8 6.8 %collective-permute-done.3 = f32[64,512]{0,1:T(8,128)} collective-permute-done((f32[64,512]{0,1:T(8,128)}, f32[64,512]{0,1:T(8,128)}, u32[]{:S(2)}, u32[]{:S(2)}) %collective-permute-start.3) | collective-permute-done | bytes 131104 | tf_op jit(solution)/shard_map/ppermute | solution.py:303
  71.7 0.0 collective-permute-done.2
  71.7 1.7 broadcast_select_fusion
  73.4 1.7 copy.11
  75.1 0.0 all-gather.2.cloned.1.call-update
  75.1 1.3 collective-permute-start.1
  76.4 78.1 %shard_map.40 = (f32[512,512]{1,0:T(8,128)}, f32[512,512]{1,0:T(8,128)}) custom-call(f32[64,32,128]{2,1,0:T(8,128)} %shard_map.39.a_ref), custom_call_target="tpu_custom_call" | custom-call | tf_op jit(solution)/shard_map/pallas_call | solution.py:227
  154.5 0.0 collective-permute-done.1
  154.5 2.7 %fusion.2 = f32[128,512]{1,0:T(8,128)S(1)} fusion(f32[512,512]{1,0:T(8,128)} %get-tuple-element.64, f32[128,512]{0,1:T(8,128)} %collective-permute-done.1, pred[]{:T(512)S(6)} %eq.21, f32[4096,128]{1,0:T(8,128)} %copy-done.1), kind=kOutput, calls=%fused_computation.10 | convolution fusion | flops 402718720 | bytes 1835009 | tf_op jit(solution)/shard_map/dot_general | solution.py:312
  157.3 4.6 %all-gather.2.cloned.1.call-done = f32[4096,512]{1,0:T(8,128)} async-done(((f32[64,512]{1,0:T(8,128)}), f32[4096,512]{1,0:T(8,128)}) %all-gather.2.cloned.1.call-update) | async-done | bytes 8388624 | tf_op jit(solution)/shard_map/all_gather | solution.py:309
  161.9 16.0 %conditional.1 = (f32[4096,128]{1,0:T(8,128)}) conditional(s32[]{:T(128)} %convert_element_type.4, (f32[128,512]{1,0:T(8,128)S(1)}, f32[512,512]{1,0:T(8,128)}, s32[1]{0:T(128)}, f32[4096,512]{1,0:T(8,128)}, f32[4096,128]{1,0:T(8,128)}) %tuple.38, (s32[]{:T(128)}, f32[512,512]{1,0:T(8,128)}, f32[512,512]{1,0:T(8,128)}, s32[1]{0:T(128)}, ...), branch_computations={%region_4.6_spmd, %region_5.7_spmd} | conditional | flops 402653184 | bytes 2097160 | solution.py:328
  161.9 1.7 constant_dynamic-slice_fusion.1.w_ref
  163.6 1.7 constant_dynamic-slice_fusion.top_ref
  165.2 12.6 %branch_1_fun.2 = f32[4096,128]{1,0:T(8,128)} custom-call(s32[1]{0:T(128)} %get-tuple-element.49.use_top_ref, f32[4096,512]{1,0:T(8,128)} %get-tuple-element.50.panel_ref, f32[128,512]{1,0:T(8,128)} %constant_dynamic-slice_fusion.1.w_ref, f32[4096,128]{1,0:T(8,128)} %get-tuple-element.53.base_ref, f32[512,128]{1,0:T(8,128)} %constant_dynamic-slice_fusion.top_ref), custom_call_target="tpu_custom_call" | custom-call | tf_op jit(solution)/shard_map/cond/branch_1_fun/pallas_call | solution.py:253
  (7 shorter events, 0.0 us)
Async XLA Ops:
  6.5 2.4 %copy-start = (f32[1,6144,128]{2,1,0:T(8,128)S(1)}, f32[1,6144,128]{2,1,0:T(8,128)}, u32[]{:S(2)}) copy-start(f32[1,6144,128]{2,1,0:T(8,128)} %param.8) | copy-start | bytes 9437188
  6.5 155.3 %all-gather.2.cloned.1.call-start = ((), (), s32[]{:S(2)}) async-start(), calls=%async_computation | async-start | bytes 8519680 | tf_op jit(solution)/shard_map/all_gather | solution.py:309
  10.9 4.6 %copy-start.3 = (s32[1,48]{1,0:T(1,128)S(1)}, s32[1,48]{1,0:T(1,128)}, u32[]{:S(2)}) copy-start(s32[1,48]{1,0:T(1,128)} %param.9) | copy-start | bytes 580
  14.1 6.2 %collective-permute-start = (f32[4096,128]{1,0:T(8,128)}, f32[4096,128]{1,0:T(8,128)}, u32[]{:S(2)}, u32[]{:S(2)}) collective-permute-start(f32[4096,128]{1,0:T(8,128)} %bitcast.4), channel_id=1, source_target_pairs={{0,64},{64,0},{1,65},{65,1},{2,66},{66,2},{3,67},{67,3},{4,68},{68... | collective-permute-start | bytes 6291464 | tf_op jit(solution)/shard_map/ppermute | solution.py:282
  18.3 2.2 %copy-start.2 = (f32[4096,128]{1,0:T(8,128)S(1)}, f32[4096,128]{1,0:T(8,128)}, u32[]{:S(2)}) copy-start(f32[4096,128]{1,0:T(8,128)} %param.7) | copy-start | bytes 6291460
  22.4 1.4 copy-start.1
  62.2 9.5 %collective-permute-start.3 = (f32[64,512]{0,1:T(8,128)}, f32[64,512]{0,1:T(8,128)}, u32[]{:S(2)}, u32[]{:S(2)}) collective-permute-start(f32[64,512]{0,1:T(8,128)} %get-tuple-element.93), channel_id=1, source_target_pairs={{0,0},{1,2},{2,4},{3,6},{4,8},{5,10},{6,12},{7,14},{8,16},{9,18},{... | collective-permute-start | bytes 393224 | tf_op jit(solution)/shard_map/ppermute | solution.py:303
  63.5 8.2 %collective-permute-start.2 = (f32[64,512]{0,1:T(8,128)}, f32[64,512]{0,1:T(8,128)}, u32[]{:S(2)}, u32[]{:S(2)}) collective-permute-start(f32[64,512]{0,1:T(8,128)} %get-tuple-element.94), channel_id=1, source_target_pairs={{0,1},{1,3},{2,5},{3,7},{4,9},{5,11},{6,13},{7,15},{8,17},{9,19},{... | collective-permute-start | bytes 393224 | tf_op jit(solution)/shard_map/ppermute | solution.py:303
  75.1 79.5 %collective-permute-start.1 = (f32[128,512]{0,1:T(8,128)S(1)}, f32[128,512]{0,1:T(8,128)}, u32[]{:S(2)}, u32[]{:S(2)}) collective-permute-start(f32[128,512]{0,1:T(8,128)S(1)} %get-tuple-element.65), channel_id=1, source_target_pairs={{0,64},{1,65},{2,66},{3,67},{4,68},{5,69},{6,70},{7,71},{8,72},{9,... | collective-permute-start | bytes 786440 | tf_op jit(solution)/shard_map/ppermute | solution.py:307
Sparse Core Ops, SparseCore 0:
  75.2 86.6 all-gather.1

commit v21 on v19

--- a/solution.py
+++ b/solution.py
@@ -267,6 +267,40 @@
     )(use_top, panel, weights, base, top_rows)
 
 
+def schur_kernel(use_top_ref, rows_ref, inv_ref, panel_ref, base_ref, out_ref, w_ref, top_ref):
+    @pl.when(pl.program_id(0) == 0)
+    def _():
+        solved = _mm_t(rows_ref[...], inv_ref[...])
+        w_ref[...] = _mm(solved, inv_ref[...])
+        top_ref[...] = jnp.transpose(solved)
+
+    prod = jnp.transpose(lax.dot_general(w_ref[...], panel_ref[...], (((1,), (1,)), ((), ())),
+                                         precision=HIGHEST, preferred_element_type=jnp.float32))
+    replace = (pl.program_id(0) == 0) & (use_top_ref[0] == 1)
+    out_ref[...] = jnp.where(replace, top_ref[...], base_ref[...] - prod)
+
+
+def schur_update(use_top, col_rows, inverse, panel, base):
+    rows, depth = panel.shape
+    cols = col_rows.shape[0]
+    return pl.pallas_call(
+        schur_kernel,
+        out_shape=jax.ShapeDtypeStruct((rows, cols), jnp.float32),
+        grid_spec=pltpu.PrefetchScalarGridSpec(
+            num_scalar_prefetch=1,
+            grid=(rows // S,),
+            in_specs=[
+                pl.BlockSpec((cols, depth), lambda i, flag: (0, 0)),
+                pl.BlockSpec((depth, depth), lambda i, flag: (0, 0)),
+                pl.BlockSpec((S, depth), lambda i, flag: (i, 0)),
+                pl.BlockSpec((S, cols), lambda i, flag: (i, 0)),
+            ],
+            out_specs=pl.BlockSpec((S, cols), lambda i, flag: (i, 0)),
+            scratch_shapes=[pltpu.VMEM((cols, depth), jnp.float32), pltpu.VMEM((S, cols), jnp.float32)],
+        ),
+    )(use_top, col_rows, inverse, panel, base)
+
+
 def per_device(front_block, child_update, child_map):
     rows, cols = front_block.shape
     n_leaf = lax.axis_size("leaf")
@@ -308,7 +342,6 @@
     panel = lax.all_gather(my_piece, "front", tiled=True)
     factor, inverse = chol_inv(pivot, S)
 
-    col_solved = lax.dot_general(col_rows, inverse, (((1,), (1,)), ((), ())), precision=HIGHEST)
 
     piv_cols = S // cols
     col_at = jnp.minimum(front, piv_cols - 1) * cols
@@ -321,8 +354,7 @@
         return panel_product(use_top, panel, inv_rows, assembled, top_rows, False)
 
     def other_columns():
-        weights = jnp.dot(col_solved, inverse, precision=HIGHEST)
-        return panel_product(use_top, panel, weights, assembled, col_solved.T, True)
+        return schur_update(use_top, col_rows, inverse, panel, assembled)
 
     return lax.cond(front < piv_cols, pivot_columns, other_columns)
 

time: 180 us -> 180 us (level)
  matrix products: 2.63 us -> 0 us
    dot_general x1 -> x0, matrix products: 2.63 us -> none  [per_device(): lax.dot_general(col_rows, inverse, (((1,), (1,)), ((), ())), precision=HI...]
  transfers between devices with their start and end apart: 5 -> 5, of which waited for: 0 -> 1; matrix products, arithmetic and copies ran while one was open for 4% -> 3% of each run, Pallas kernels for 67% -> 68%
where the time goes in v21:
time: 180 us; the launch traced here: 177 us
  Pallas kernels  133 us (74%)
  between operations  13.5 us (8%)
  local copies, waits for them, and re-layouts  12.2 us (7%)
  other arithmetic  11.9 us (7%)
  starting transfers between devices  5.38 us (3%)
    pallas_call x1, Pallas kernels, chol_inv(): pl.pallas_call(chol_inv_kernel, out_shape=(jax.ShapeDtypeStruct((n, n), j...  78.1 us
    pallas_call x1, Pallas kernels, broadcast_pivot(): pl.pallas_call(functools.partial(pivot_kernel, n_front, n_src), out_shape...  42.4 us
    pallas_call x1, Pallas kernels, panel_product(): pl.pallas_call(functools.partial(panel_product_kernel, subtract), out_sha...  12.6 us
    select_n x2, other arithmetic, gather_half(): picked = jnp.where(found[:, None, None], picked, jnp.zeros_like(picked))  5.25 us
    gather x2, local copies, waits for them, and re-layouts, gather_half(): picked = jnp.take(blocks, index, axis=0)  3.98 us
  transfers between devices with their start and end apart: 5, of which 1 were waited for; matrix products, arithmetic and copies ran while one was open for 3% of the time, Pallas kernels for 68%

profile of v21, /device:TPU:1, one launch (start us, length us, event | category | flops | bytes accessed | tf_op | source)
XLA Modules:
  0.0 177.1 jit_solution(2965358491091680582)
XLA Ops:
  6.5 0.0 copy-start
  6.5 0.0 all-gather.2.cloned.1.call-start
  6.5 1.5 compare_reduce_fusion
  8.1 0.8 compare_reduce_fusion.3
  8.9 0.0 copy-done
  8.9 2.0 %gather_fusion.1 = f32[32,128,128]{2,1,0:T(8,128)} fusion(f32[48,128,128]{2,1,0:T(8,128)S(1)} %bitcast.16, s32[1024]{0:T(1024)S(1)} %pad_clamp_fusion), kind=kCustom, calls=%fused_computation.1.clone | custom fusion | bytes 4194432 | tf_op jit(solution)/shard_map/jit(_take)/gather | solution.py:21
  10.9 0.0 copy-start.3
  10.9 3.2 %select_select_fusion = f32[32,128,128]{2,1,0:T(8,128)} fusion(f32[32,128,128]{2,1,0:T(8,128)} %gather_fusion.1, pred[32]{0:T(512)(128)(4,1)S(1)} %compare_and_fusion, pred[32]{0:T(512)(128)(4,1)S(1)} %get-tuple-element.104), kind=kLoop, calls=%fused_computation.9 | loop fusion | flops 1048576 | bytes 4194368 | tf_op jit(solution)/shard_map/jit(_where)/select_n | solution.py:22
  14.1 1.4 collective-permute-start
  15.6 0.0 copy-done.3
  15.6 0.7 compare_reduce_fusion.2
  16.3 2.0 %gather_fusion = f32[32,128,128]{2,1,0:T(8,128)} fusion(f32[48,128,128]{2,1,0:T(8,128)S(1)} %bitcast.15, s32[1024]{0:T(1024)S(1)} %pad_clamp_fusion.1), kind=kCustom, calls=%fused_computation.clone | custom fusion | bytes 4194432 | tf_op jit(solution)/shard_map/jit(_take)/gather | solution.py:21
  18.3 0.0 copy-start.2
  18.3 2.0 %select_select_fusion.1 = f32[32,128,128]{2,1,0:T(8,128)S(1)} fusion(f32[32,128,128]{2,1,0:T(8,128)} %gather_fusion, pred[32]{0:T(512)(128)(4,1)S(1)} %compare_and_fusion.1, pred[32]{0:T(512)(128)(4,1)S(1)} %get-tuple-element.103), kind=kLoop, calls=%fused_computation.10 | loop fusion | flops 1048576 | bytes 4194368 | tf_op jit(solution)/shard_map/jit(_where)/select_n | solution.py:22
  20.3 0.0 collective-permute-done
  20.3 0.2 copy-done.2
  20.5 1.9 %fusion.1 = f32[4096,128]{1,0:T(8,128)S(1)} fusion(f32[4096,128]{1,0:T(8,128)S(1)} %copy-done.2, f32[4096,128]{1,0:T(8,128)} %collective-permute-done, f32[32,128,128]{2,1,0:T(8,128)S(1)} %select_select_fusion.1, pred[]{:T(512)} %eq.21), kind=kLoop, calls=%fused_computation.8 | loop fusion | flops 2097152 | bytes 8388609 | tf_op jit(solution)/shard_map/add | solution.py:319
  22.4 0.0 copy-start.1
  22.4 1.4 copy-done.1
  23.8 0.7 fusion.2
  24.5 0.9 fusion.3
  25.4 1.3 collective-permute-start.3
  26.7 1.4 collective-permute-start.2
  28.1 42.4 %shard_map.39.a_ref = f32[64,32,128]{2,1,0:T(8,128)} custom-call(f32[512,128]{1,0:T(8,128)} %get-tuple-element.105.top_ref), custom_call_target="tpu_custom_call" | custom-call | tf_op jit(solution)/shard_map/pallas_call | solution.py:133
  70.5 0.0 collective-permute-done.3
  70.5 0.0 collective-permute-done.2
  70.5 1.7 broadcast_select_fusion.1
  72.2 1.7 copy.13
  73.9 0.0 all-gather.2.cloned.1.call-update
  73.9 1.3 collective-permute-start.1
  75.2 78.1 %shard_map.40 = (f32[512,512]{1,0:T(8,128)}, f32[512,512]{1,0:T(8,128)}) custom-call(f32[64,32,128]{2,1,0:T(8,128)} %shard_map.39.a_ref), custom_call_target="tpu_custom_call" | custom-call | tf_op jit(solution)/shard_map/pallas_call | solution.py:227
  153.4 0.9 all-gather.2.cloned.1.call-done
  154.3 0.0 collective-permute-done.1
  154.3 16.0 %conditional.1 = (f32[4096,128]{1,0:T(8,128)}) conditional(s32[]{:T(128)} %convert_element_type.4, (pred[]{:T(512)}, f32[128,512]{0,1:T(8,128)S(1)}, f32[128,512]{0,1:T(8,128)}, s32[1]{0:T(128)}, f32[512,512]{1,0:T(8,128)}, /*index=5*/f32[4096,512]{1,0:T(8,128)}, f32[4096,128]{1,0:T(8,128)}) %tuple.38, (s32[]{:T(128)}, f32[512,512]{1,0:T(8,128)}, ...), branch_computations={%region_4.6_spmd, %region_5.7_spmd} | conditional | flops 65536 | bytes 1835017 | solution.py:359
  154.3 1.7 constant_dynamic-slice_fusion.1.w_ref
  156.0 1.7 constant_dynamic-slice_fusion.top_ref
  157.6 12.6 %branch_1_fun.2 = f32[4096,128]{1,0:T(8,128)} custom-call(s32[1]{0:T(128)} %get-tuple-element.57.use_top_ref, f32[4096,512]{1,0:T(8,128)} %get-tuple-element.58.panel_ref, f32[128,512]{1,0:T(8,128)} %constant_dynamic-slice_fusion.1.w_ref, f32[4096,128]{1,0:T(8,128)} %get-tuple-element.61.base_ref, f32[512,128]{1,0:T(8,128)} %constant_dynamic-slice_fusion.top_ref), custom_call_target="tpu_custom_call" | custom-call | tf_op jit(solution)/shard_map/cond/branch_1_fun/pallas_call | solution.py:253
  (7 shorter events, 0.0 us)
Async XLA Ops:
  6.5 2.4 %copy-start = (f32[1,6144,128]{2,1,0:T(8,128)S(1)}, f32[1,6144,128]{2,1,0:T(8,128)}, u32[]{:S(2)}) copy-start(f32[1,6144,128]{2,1,0:T(8,128)} %param.8) | copy-start | bytes 9437188
  6.5 147.7 %all-gather.2.cloned.1.call-start = ((), (), s32[]{:S(2)}) async-start(), calls=%async_computation | async-start | bytes 8519680 | tf_op jit(solution)/shard_map/all_gather | solution.py:342
  10.9 4.6 %copy-start.3 = (s32[1,48]{1,0:T(1,128)S(1)}, s32[1,48]{1,0:T(1,128)}, u32[]{:S(2)}) copy-start(s32[1,48]{1,0:T(1,128)} %param.9) | copy-start | bytes 580
  14.1 6.2 %collective-permute-start = (f32[4096,128]{1,0:T(8,128)}, f32[4096,128]{1,0:T(8,128)}, u32[]{:S(2)}, u32[]{:S(2)}) collective-permute-start(f32[4096,128]{1,0:T(8,128)} %bitcast.3), channel_id=1, source_target_pairs={{0,64},{64,0},{1,65},{65,1},{2,66},{66,2},{3,67},{67,3},{4,68},{68... | collective-permute-start | bytes 6291464 | tf_op jit(solution)/shard_map/ppermute | solution.py:316
  18.3 2.2 %copy-start.2 = (f32[4096,128]{1,0:T(8,128)S(1)}, f32[4096,128]{1,0:T(8,128)}, u32[]{:S(2)}) copy-start(f32[4096,128]{1,0:T(8,128)} %param.7) | copy-start | bytes 6291460
  22.4 1.4 copy-start.1
  25.4 45.1 %collective-permute-start.3 = (f32[64,512]{0,1:T(8,128)}, f32[64,512]{0,1:T(8,128)}, u32[]{:S(2)}, u32[]{:S(2)}) collective-permute-start(f32[64,512]{0,1:T(8,128)} %get-tuple-element.107), channel_id=1, source_target_pairs={{0,0},{1,2},{2,4},{3,6},{4,8},{5,10},{6,12},{7,14},{8,16},{9,18},{... | collective-permute-start | bytes 393224 | tf_op jit(solution)/shard_map/ppermute | solution.py:334
  26.7 43.8 %collective-permute-start.2 = (f32[64,512]{0,1:T(8,128)}, f32[64,512]{0,1:T(8,128)}, u32[]{:S(2)}, u32[]{:S(2)}) collective-permute-start(f32[64,512]{0,1:T(8,128)} %get-tuple-element.108), channel_id=1, source_target_pairs={{0,1},{1,3},{2,5},{3,7},{4,9},{5,11},{6,13},{7,15},{8,17},{9,19},{... | collective-permute-start | bytes 393224 | tf_op jit(solution)/shard_map/ppermute | solution.py:334
  73.9 80.4 %collective-permute-start.1 = (f32[128,512]{0,1:T(8,128)S(1)}, f32[128,512]{0,1:T(8,128)}, u32[]{:S(2)}, u32[]{:S(2)}) collective-permute-start(f32[128,512]{0,1:T(8,128)S(1)} %get-tuple-element.106), channel_id=1, source_target_pairs={{0,64},{1,65},{2,66},{3,67},{4,68},{5,69},{6,70},{7,71},{8,72},{9,... | collective-permute-start | bytes 786440 | tf_op jit(solution)/shard_map/ppermute | solution.py:339
Sparse Core Ops, SparseCore 0:
  74.0 80.2 all-gather.1

commit v22 on v19

--- a/solution.py
+++ b/solution.py
@@ -23,7 +23,7 @@
     return picked.reshape(half_blocks * BLK, blocks.shape[2])
 
 
-def pivot_kernel(n_front, n_src, top_ref, out_ref, chunk, sem_a, sem_b, send_a, send_b, recv_g, send_g):
+def pivot_kernel(n_front, n_src, top_ref, out_ref, cols_ref, chunk, sem_a, sem_b, send_a, send_b, recv_g, send_g, sem_t, send_t):
     leaf = lax.axis_index("leaf")
     me = lax.axis_index("front")
     per_src = n_front // n_src
@@ -61,6 +61,13 @@
 
     @pl.when(leaf == 0)
     def _():
+        pltpu.make_async_copy(top_ref, cols_ref, sem_t).start()
+        pltpu.make_async_remote_copy(
+            top_ref, cols_ref, send_t, sem_t, device_id=(1, me), device_id_type=MESH
+        ).start()
+
+    @pl.when(leaf == 0)
+    def _():
         pltpu.make_async_remote_copy(
             chunk, chunk, send_b, sem_b, device_id=(1, me), device_id_type=MESH
         ).start()
@@ -107,6 +114,19 @@
         pltpu.make_async_remote_copy(
             chunk, chunk, send_b, sem_b, device_id=(1, me), device_id_type=MESH
         ).wait_send()
+
+    @pl.when(leaf == 0)
+    def _():
+        pltpu.make_async_copy(top_ref, cols_ref, sem_t).wait()
+        pltpu.make_async_remote_copy(
+            top_ref, cols_ref, send_t, sem_t, device_id=(1, me), device_id_type=MESH
+        ).wait_send()
+
+    @pl.when(leaf == 1)
+    def _():
+        pltpu.make_async_remote_copy(
+            top_ref, cols_ref, send_t, sem_t, device_id=(0, me), device_id_type=MESH
+        ).wait_recv()
 
     @pl.when((leaf == 0) & (me < n_src))
     def _():
@@ -130,11 +150,11 @@
     n_src = S // cols
     per_src = n_front // n_src
     rows = S // per_src
-    gathered = pl.pallas_call(
+    gathered, own_cols = pl.pallas_call(
         functools.partial(pivot_kernel, n_front, n_src),
-        out_shape=jax.ShapeDtypeStruct((n_front, rows, cols), jnp.float32),
+        out_shape=(jax.ShapeDtypeStruct((n_front, rows, cols), jnp.float32), jax.ShapeDtypeStruct(top.shape, jnp.float32)),
         in_specs=[pl.BlockSpec(memory_space=pltpu.VMEM)],
-        out_specs=pl.BlockSpec(memory_space=pltpu.VMEM),
+        out_specs=(pl.BlockSpec(memory_space=pltpu.VMEM), pl.BlockSpec(memory_space=pltpu.VMEM)),
         scratch_shapes=[
             pltpu.VMEM((rows, cols), jnp.float32),
             pltpu.SemaphoreType.DMA,
@@ -143,10 +163,12 @@
             pltpu.SemaphoreType.DMA,
             pltpu.SemaphoreType.DMA((n_front,)),
             pltpu.SemaphoreType.DMA((n_front,)),
+            pltpu.SemaphoreType.DMA,
+            pltpu.SemaphoreType.DMA,
         ],
         compiler_params=pltpu.CompilerParams(has_side_effects=True),
     )(top)
-    return gathered
+    return gathered, own_cols
 
 
 PANEL = 8
@@ -301,9 +323,8 @@
     my_piece = pieces[0]
     for part in range(1, per_block):
         my_piece = jnp.where(front % per_block == part, pieces[part], my_piece)
-    pivot = broadcast_pivot(top, n_front)
-    partner_rows = lax.ppermute(panel_rows, "leaf", [(0, 1)])
-    col_rows = jnp.where(leaf == 0, panel_rows, partner_rows)
+    pivot, own_cols = broadcast_pivot(top, n_front)
+    col_rows = own_cols.T
     my_piece, pivot = lax.optimization_barrier((my_piece, pivot))
     panel = lax.all_gather(my_piece, "front", tiled=True)
     factor, inverse = chol_inv(pivot, S)

time: 180 us -> 178 us (0.989)
  transfers between devices with their start and end apart: 5 -> 4, of which waited for: 0 -> 1; matrix products, arithmetic and copies ran while one was open for 4% -> 4% of each run, Pallas kernels for 67% -> 68%
where the time goes in v22:
time: 178 us; the launch traced here: 177 us
  Pallas kernels  134 us (75%)
  between operations  13.5 us (8%)
  local copies, waits for them, and re-layouts  11.2 us (6%)
  other arithmetic  11.2 us (6%)
  starting transfers between devices  4.09 us (2%)
  matrix products  2.56 us (1%)
    pallas_call x1, Pallas kernels, chol_inv(): pl.pallas_call(chol_inv_kernel, out_shape=(jax.ShapeDtypeStruct((n, n), j...  78.1 us
    pallas_call x1, Pallas kernels, broadcast_pivot(): pl.pallas_call(functools.partial(pivot_kernel, n_front, n_src), out_shape...  43 us
    pallas_call x1, Pallas kernels, panel_product(): pl.pallas_call(functools.partial(panel_product_kernel, subtract), out_sha...  12.6 us
    select_n x2, other arithmetic, gather_half(): picked = jnp.where(found[:, None, None], picked, jnp.zeros_like(picked))  5.25 us
    gather x2, local copies, waits for them, and re-layouts, gather_half(): picked = jnp.take(blocks, index, axis=0)  3.98 us
  transfers between devices with their start and end apart: 4, of which 1 were waited for; matrix products, arithmetic and copies ran while one was open for 4% of the time, Pallas kernels for 68%

profile of v22, /device:TPU:1, one launch (start us, length us, event | category | flops | bytes accessed | tf_op | source)
XLA Modules:
  0.0 176.8 jit_solution(10368070266915431798)
XLA Ops:
  6.5 0.0 copy-start
  6.5 0.0 all-gather.2.cloned.1.call-start
  6.5 1.5 compare_reduce_fusion
  8.1 0.8 compare_reduce_fusion.3
  8.9 0.0 copy-done
  8.9 2.0 %gather_fusion.1 = f32[32,128,128]{2,1,0:T(8,128)} fusion(f32[48,128,128]{2,1,0:T(8,128)S(1)} %bitcast.21, s32[1024]{0:T(1024)S(1)} %pad_clamp_fusion), kind=kCustom, calls=%fused_computation.1.clone | custom fusion | bytes 4194432 | tf_op jit(solution)/shard_map/jit(_take)/gather | solution.py:21
  10.9 0.0 copy-start.3
  10.9 3.2 %select_select_fusion = f32[32,128,128]{2,1,0:T(8,128)} fusion(f32[32,128,128]{2,1,0:T(8,128)} %gather_fusion.1, pred[32]{0:T(512)(128)(4,1)S(1)} %compare_and_fusion, pred[32]{0:T(512)(128)(4,1)S(1)} %get-tuple-element.94), kind=kLoop, calls=%fused_computation.8 | loop fusion | flops 1048576 | bytes 4194368 | tf_op jit(solution)/shard_map/jit(_where)/select_n | solution.py:22
  14.1 1.4 collective-permute-start
  15.6 0.0 copy-done.3
  15.6 0.7 compare_reduce_fusion.2
  16.3 2.0 %gather_fusion = f32[32,128,128]{2,1,0:T(8,128)} fusion(f32[48,128,128]{2,1,0:T(8,128)S(1)} %bitcast.20, s32[1024]{0:T(1024)S(1)} %pad_clamp_fusion.1), kind=kCustom, calls=%fused_computation.clone | custom fusion | bytes 4194432 | tf_op jit(solution)/shard_map/jit(_take)/gather | solution.py:21
  18.3 0.0 copy-start.2
  18.3 2.0 %select_select_fusion.1 = f32[32,128,128]{2,1,0:T(8,128)S(1)} fusion(f32[32,128,128]{2,1,0:T(8,128)} %gather_fusion, pred[32]{0:T(512)(128)(4,1)S(1)} %compare_and_fusion.1, pred[32]{0:T(512)(128)(4,1)S(1)} %get-tuple-element.93), kind=kLoop, calls=%fused_computation.9 | loop fusion | flops 1048576 | bytes 4194368 | tf_op jit(solution)/shard_map/jit(_where)/select_n | solution.py:22
  20.3 0.0 collective-permute-done
  20.3 0.2 copy-done.2
  20.5 1.9 %fusion.1 = f32[4096,128]{1,0:T(8,128)S(1)} fusion(f32[4096,128]{1,0:T(8,128)S(1)} %copy-done.2, f32[4096,128]{1,0:T(8,128)} %collective-permute-done, f32[32,128,128]{2,1,0:T(8,128)S(1)} %select_select_fusion.1, pred[]{:T(512)S(6)} %eq.21), kind=kLoop, calls=%fused_computation.7 | loop fusion | flops 2097152 | bytes 8388609 | tf_op jit(solution)/shard_map/add | solution.py:307
  22.4 0.0 copy-start.1
  22.4 1.4 copy-done.1
  23.8 0.7 slice_bitcast_fusion
  24.5 0.8 fusion.2
  25.3 1.3 collective-permute-start.2
  26.6 1.4 collective-permute-start.1
  28.0 43.0 %shard_map.39 = (f32[64,32,128]{2,1,0:T(8,128)}, f32[512,128]{1,0:T(8,128)}) custom-call(f32[512,128]{1,0:T(8,128)} %get-tuple-element.96.top_ref), custom_call_target="tpu_custom_call" | custom-call | tf_op jit(solution)/shard_map/pallas_call | solution.py:153
  70.9 0.0 collective-permute-done.2
  70.9 0.0 collective-permute-done.1
  70.9 1.0 broadcast_select_fusion
  71.9 0.8 copy.11
  72.7 0.0 all-gather.2.cloned.1.call-update
  72.7 78.1 %shard_map.40 = (f32[512,512]{1,0:T(8,128)}, f32[512,512]{1,0:T(8,128)}) custom-call(f32[64,32,128]{2,1,0:T(8,128)} %get-tuple-element.67.a_ref), custom_call_target="tpu_custom_call" | custom-call | tf_op jit(solution)/shard_map/pallas_call | solution.py:249
  150.9 2.6 %fusion.4 = f32[128,512]{1,0:T(8,128)S(1)} fusion(f32[512,128]{1,0:T(8,128)} %get-tuple-element.65, f32[512,512]{1,0:T(8,128)} %get-tuple-element.68), kind=kOutput, calls=%fused_computation.26 | convolution fusion | flops 402653184 | bytes 1572864 | tf_op jit(solution)/shard_map/dot_general | solution.py:332
  153.4 0.5 all-gather.2.cloned.1.call-done
  154.0 16.0 %conditional.1 = (f32[4096,128]{1,0:T(8,128)}) conditional(s32[]{:T(128)} %convert_element_type.4, (f32[128,512]{1,0:T(8,128)S(1)}, f32[512,512]{1,0:T(8,128)}, s32[1]{0:T(128)}, f32[4096,512]{1,0:T(8,128)}, f32[4096,128]{1,0:T(8,128)}) %tuple.38, (s32[]{:T(128)}, f32[512,512]{1,0:T(8,128)}, f32[512,512]{1,0:T(8,128)}, s32[1]{0:T(128)}, ...), branch_computations={%region_4.6_spmd, %region_5.7_spmd} | conditional | flops 402653184 | bytes 2097160 | solution.py:348
  154.0 1.7 constant_dynamic-slice_fusion.1.w_ref
  155.6 1.7 constant_dynamic-slice_fusion.top_ref
  157.3 12.6 %branch_1_fun.2 = f32[4096,128]{1,0:T(8,128)} custom-call(s32[1]{0:T(128)} %get-tuple-element.49.use_top_ref, f32[4096,512]{1,0:T(8,128)} %get-tuple-element.50.panel_ref, f32[128,512]{1,0:T(8,128)} %constant_dynamic-slice_fusion.1.w_ref, f32[4096,128]{1,0:T(8,128)} %get-tuple-element.53.base_ref, f32[512,128]{1,0:T(8,128)} %constant_dynamic-slice_fusion.top_ref), custom_call_target="tpu_custom_call" | custom-call | tf_op jit(solution)/shard_map/cond/branch_1_fun/pallas_call | solution.py:275
  (7 shorter events, 0.0 us)
Async XLA Ops:
  6.5 2.4 %copy-start = (f32[1,6144,128]{2,1,0:T(8,128)S(1)}, f32[1,6144,128]{2,1,0:T(8,128)}, u32[]{:S(2)}) copy-start(f32[1,6144,128]{2,1,0:T(8,128)} %param.8) | copy-start | bytes 9437188
  6.5 147.4 %all-gather.2.cloned.1.call-start = ((), (), s32[]{:S(2)}) async-start(), calls=%async_computation | async-start | bytes 8519680 | tf_op jit(solution)/shard_map/all_gather | solution.py:329
  10.9 4.6 %copy-start.3 = (s32[1,48]{1,0:T(1,128)S(1)}, s32[1,48]{1,0:T(1,128)}, u32[]{:S(2)}) copy-start(s32[1,48]{1,0:T(1,128)} %param.9) | copy-start | bytes 580
  14.1 6.2 %collective-permute-start = (f32[4096,128]{1,0:T(8,128)}, f32[4096,128]{1,0:T(8,128)}, u32[]{:S(2)}, u32[]{:S(2)}) collective-permute-start(f32[4096,128]{1,0:T(8,128)} %bitcast.4), channel_id=1, source_target_pairs={{0,64},{64,0},{1,65},{65,1},{2,66},{66,2},{3,67},{67,3},{4,68},{68... | collective-permute-start | bytes 6291464 | tf_op jit(solution)/shard_map/ppermute | solution.py:304
  18.3 2.2 %copy-start.2 = (f32[4096,128]{1,0:T(8,128)S(1)}, f32[4096,128]{1,0:T(8,128)}, u32[]{:S(2)}) copy-start(f32[4096,128]{1,0:T(8,128)} %param.7) | copy-start | bytes 6291460
  22.4 1.4 copy-start.1
  25.3 45.6 %collective-permute-start.2 = (f32[64,512]{0,1:T(8,128)}, f32[64,512]{0,1:T(8,128)}, u32[]{:S(2)}, u32[]{:S(2)}) collective-permute-start(f32[64,512]{0,1:T(8,128)} %get-tuple-element.97), channel_id=1, source_target_pairs={{0,0},{1,2},{2,4},{3,6},{4,8},{5,10},{6,12},{7,14},{8,16},{9,18},{... | collective-permute-start | bytes 393224 | tf_op jit(solution)/shard_map/ppermute | solution.py:322
  26.6 44.4 %collective-permute-start.1 = (f32[64,512]{0,1:T(8,128)S(1)}, f32[64,512]{0,1:T(8,128)}, u32[]{:S(2)}, u32[]{:S(2)}) collective-permute-start(f32[64,512]{0,1:T(8,128)S(1)} %get-tuple-element.98), channel_id=1, source_target_pairs={{0,1},{1,3},{2,5},{3,7},{4,9},{5,11},{6,13},{7,15},{8,17},{9,19},{... | collective-permute-start | bytes 393224 | tf_op jit(solution)/shard_map/ppermute | solution.py:322
Sparse Core Ops, SparseCore 0:
  72.9 81.0 all-gather.1

commit v23 on v22

--- a/solution.py
+++ b/solution.py
@@ -172,6 +172,7 @@
 
 
 PANEL = 8
+TILE = 1024
 
 
 def _mm(a, b):
@@ -265,8 +266,11 @@
     prod = jnp.transpose(lax.dot_general(w_ref[...], panel_ref[...], (((1,), (1,)), ((), ())),
                                          precision=HIGHEST, preferred_element_type=jnp.float32))
     result = base_ref[...] - prod if subtract else prod
-    replace = (pl.program_id(0) == 0) & (use_top_ref[0] == 1)
-    out_ref[...] = jnp.where(replace, top_ref[...], result)
+    out_ref[...] = result
+
+    @pl.when((pl.program_id(0) == 0) & (use_top_ref[0] == 1))
+    def _():
+        out_ref[0:S, :] = top_ref[...]
 
 
 def panel_product(use_top, panel, weights, base, top_rows, subtract):
@@ -277,14 +281,14 @@
         out_shape=jax.ShapeDtypeStruct((rows, cols), jnp.float32),
         grid_spec=pltpu.PrefetchScalarGridSpec(
             num_scalar_prefetch=1,
-            grid=(rows // S,),
+            grid=(rows // TILE,),
             in_specs=[
-                pl.BlockSpec((S, depth), lambda i, flag: (i, 0)),
+                pl.BlockSpec((TILE, depth), lambda i, flag: (i, 0)),
                 pl.BlockSpec((cols, depth), lambda i, flag: (0, 0)),
-                pl.BlockSpec((S, cols), lambda i, flag: (i, 0)),
+                pl.BlockSpec((TILE, cols), lambda i, flag: (i, 0)),
                 pl.BlockSpec((S, cols), lambda i, flag: (0, 0)),
             ],
-            out_specs=pl.BlockSpec((S, cols), lambda i, flag: (i, 0)),
+            out_specs=pl.BlockSpec((TILE, cols), lambda i, flag: (i, 0)),
         ),
     )(use_top, panel, weights, base, top_rows)
 

time: 178 us -> 176 us (0.989)
  transfers between devices with their start and end apart: 4 -> 4, of which waited for: 1 -> 1; matrix products, arithmetic and copies ran while one was open for 4% -> 4% of each run, Pallas kernels for 68% -> 69%
where the time goes in v23:
time: 176 us
  Pallas kernels  133 us (76%)
  between operations  13.5 us (8%)
  local copies, waits for them, and re-layouts  11.2 us (6%)
  other arithmetic  11.2 us (6%)
  starting transfers between devices  4.09 us (2%)
  matrix products  2.56 us (1%)
    pallas_call x1, Pallas kernels, chol_inv(): pl.pallas_call(chol_inv_kernel, out_shape=(jax.ShapeDtypeStruct((n, n), j...  78.1 us
    pallas_call x1, Pallas kernels, broadcast_pivot(): pl.pallas_call(functools.partial(pivot_kernel, n_front, n_src), out_shape...  42.8 us
    pallas_call x1, Pallas kernels, panel_product(): pl.pallas_call(functools.partial(panel_product_kernel, subtract), out_sha...  11.8 us
    select_n x2, other arithmetic, gather_half(): picked = jnp.where(found[:, None, None], picked, jnp.zeros_like(picked))  5.25 us
    gather x2, local copies, waits for them, and re-layouts, gather_half(): picked = jnp.take(blocks, index, axis=0)  3.98 us
  transfers between devices with their start and end apart: 4, of which 1 were waited for; matrix products, arithmetic and copies ran while one was open for 4% of the time, Pallas kernels for 69%

profile of v23, /device:TPU:1, one launch (start us, length us, event | category | flops | bytes accessed | tf_op | source)
XLA Modules:
  0.0 175.8 jit_solution(9221323677019714143)
XLA Ops:
  6.5 0.0 copy-start
  6.5 0.0 all-gather.2.cloned.1.call-start
  6.5 1.5 compare_reduce_fusion
  8.1 0.8 compare_reduce_fusion.3
  8.9 0.0 copy-done
  8.9 2.0 %gather_fusion.1 = f32[32,128,128]{2,1,0:T(8,128)} fusion(f32[48,128,128]{2,1,0:T(8,128)S(1)} %bitcast.21, s32[1024]{0:T(1024)S(1)} %pad_clamp_fusion), kind=kCustom, calls=%fused_computation.1.clone | custom fusion | bytes 4194432 | tf_op jit(solution)/shard_map/jit(_take)/gather | solution.py:21
  10.9 0.0 copy-start.3
  10.9 3.2 %select_select_fusion = f32[32,128,128]{2,1,0:T(8,128)} fusion(f32[32,128,128]{2,1,0:T(8,128)} %gather_fusion.1, pred[32]{0:T(512)(128)(4,1)S(1)} %compare_and_fusion, pred[32]{0:T(512)(128)(4,1)S(1)} %get-tuple-element.94), kind=kLoop, calls=%fused_computation.8 | loop fusion | flops 1048576 | bytes 4194368 | tf_op jit(solution)/shard_map/jit(_where)/select_n | solution.py:22
  14.1 1.4 collective-permute-start
  15.6 0.0 copy-done.3
  15.6 0.7 compare_reduce_fusion.2
  16.3 2.0 %gather_fusion = f32[32,128,128]{2,1,0:T(8,128)} fusion(f32[48,128,128]{2,1,0:T(8,128)S(1)} %bitcast.20, s32[1024]{0:T(1024)S(1)} %pad_clamp_fusion.1), kind=kCustom, calls=%fused_computation.clone | custom fusion | bytes 4194432 | tf_op jit(solution)/shard_map/jit(_take)/gather | solution.py:21
  18.3 0.0 copy-start.2
  18.3 2.0 %select_select_fusion.1 = f32[32,128,128]{2,1,0:T(8,128)S(1)} fusion(f32[32,128,128]{2,1,0:T(8,128)} %gather_fusion, pred[32]{0:T(512)(128)(4,1)S(1)} %compare_and_fusion.1, pred[32]{0:T(512)(128)(4,1)S(1)} %get-tuple-element.93), kind=kLoop, calls=%fused_computation.9 | loop fusion | flops 1048576 | bytes 4194368 | tf_op jit(solution)/shard_map/jit(_where)/select_n | solution.py:22
  20.3 0.0 collective-permute-done
  20.3 0.2 copy-done.2
  20.5 1.9 %fusion.1 = f32[4096,128]{1,0:T(8,128)S(1)} fusion(f32[4096,128]{1,0:T(8,128)S(1)} %copy-done.2, f32[4096,128]{1,0:T(8,128)} %collective-permute-done, f32[32,128,128]{2,1,0:T(8,128)S(1)} %select_select_fusion.1, pred[]{:T(512)S(6)} %eq.21), kind=kLoop, calls=%fused_computation.7 | loop fusion | flops 2097152 | bytes 8388609 | tf_op jit(solution)/shard_map/add | solution.py:311
  22.4 0.0 copy-start.1
  22.4 1.4 copy-done.1
  23.8 0.7 slice_bitcast_fusion
  24.5 0.8 fusion.2
  25.3 1.3 collective-permute-start.2
  26.6 1.4 collective-permute-start.1
  28.0 42.8 %shard_map.39 = (f32[64,32,128]{2,1,0:T(8,128)}, f32[512,128]{1,0:T(8,128)}) custom-call(f32[512,128]{1,0:T(8,128)} %get-tuple-element.96.top_ref), custom_call_target="tpu_custom_call" | custom-call | tf_op jit(solution)/shard_map/pallas_call | solution.py:153
  70.8 0.0 collective-permute-done.2
  70.8 0.0 collective-permute-done.1
  70.8 1.0 broadcast_select_fusion
  71.8 0.8 copy.11
  72.6 0.0 all-gather.2.cloned.1.call-update
  72.6 78.1 %shard_map.40 = (f32[512,512]{1,0:T(8,128)}, f32[512,512]{1,0:T(8,128)}) custom-call(f32[64,32,128]{2,1,0:T(8,128)} %get-tuple-element.67.a_ref), custom_call_target="tpu_custom_call" | custom-call | tf_op jit(solution)/shard_map/pallas_call | solution.py:250
  150.7 2.6 %fusion.4 = f32[128,512]{1,0:T(8,128)S(1)} fusion(f32[512,128]{1,0:T(8,128)} %get-tuple-element.65, f32[512,512]{1,0:T(8,128)} %get-tuple-element.68), kind=kOutput, calls=%fused_computation.26 | convolution fusion | flops 402653184 | bytes 1572864 | tf_op jit(solution)/shard_map/dot_general | solution.py:336
  153.3 0.5 all-gather.2.cloned.1.call-done
  153.8 15.2 %conditional.1 = (f32[4096,128]{1,0:T(8,128)}) conditional(s32[]{:T(128)} %convert_element_type.4, (f32[128,512]{1,0:T(8,128)S(1)}, f32[512,512]{1,0:T(8,128)}, s32[1]{0:T(128)}, f32[4096,512]{1,0:T(8,128)}, f32[4096,128]{1,0:T(8,128)}) %tuple.38, (s32[]{:T(128)}, f32[512,512]{1,0:T(8,128)}, f32[512,512]{1,0:T(8,128)}, s32[1]{0:T(128)}, ...), branch_computations={%region_4.6_spmd, %region_5.7_spmd} | conditional | flops 402653184 | bytes 2097160 | solution.py:352
  153.8 1.7 constant_dynamic-slice_fusion.1.w_ref
  155.5 1.7 constant_dynamic-slice_fusion.top_ref
  157.2 11.8 %branch_1_fun.2 = f32[4096,128]{1,0:T(8,128)} custom-call(s32[1]{0:T(128)} %get-tuple-element.49.use_top_ref, f32[4096,512]{1,0:T(8,128)} %get-tuple-element.50.panel_ref, f32[128,512]{1,0:T(8,128)} %constant_dynamic-slice_fusion.1.w_ref, f32[4096,128]{1,0:T(8,128)} %get-tuple-element.53.base_ref, f32[512,128]{1,0:T(8,128)} %constant_dynamic-slice_fusion.top_ref), custom_call_target="tpu_custom_call" | custom-call | tf_op jit(solution)/shard_map/cond/branch_1_fun/pallas_call | solution.py:279
  (7 shorter events, 0.0 us)
Async XLA Ops:
  6.5 2.4 %copy-start = (f32[1,6144,128]{2,1,0:T(8,128)S(1)}, f32[1,6144,128]{2,1,0:T(8,128)}, u32[]{:S(2)}) copy-start(f32[1,6144,128]{2,1,0:T(8,128)} %param.8) | copy-start | bytes 9437188
  6.5 147.3 %all-gather.2.cloned.1.call-start = ((), (), s32[]{:S(2)}) async-start(), calls=%async_computation | async-start | bytes 8519680 | tf_op jit(solution)/shard_map/all_gather | solution.py:333
  10.9 4.6 %copy-start.3 = (s32[1,48]{1,0:T(1,128)S(1)}, s32[1,48]{1,0:T(1,128)}, u32[]{:S(2)}) copy-start(s32[1,48]{1,0:T(1,128)} %param.9) | copy-start | bytes 580
  14.1 6.2 %collective-permute-start = (f32[4096,128]{1,0:T(8,128)}, f32[4096,128]{1,0:T(8,128)}, u32[]{:S(2)}, u32[]{:S(2)}) collective-permute-start(f32[4096,128]{1,0:T(8,128)} %bitcast.4), channel_id=1, source_target_pairs={{0,64},{64,0},{1,65},{65,1},{2,66},{66,2},{3,67},{67,3},{4,68},{68... | collective-permute-start | bytes 6291464 | tf_op jit(solution)/shard_map/ppermute | solution.py:308
  18.3 2.2 %copy-start.2 = (f32[4096,128]{1,0:T(8,128)S(1)}, f32[4096,128]{1,0:T(8,128)}, u32[]{:S(2)}) copy-start(f32[4096,128]{1,0:T(8,128)} %param.7) | copy-start | bytes 6291460
  22.4 1.4 copy-start.1
  25.3 45.5 %collective-permute-start.2 = (f32[64,512]{0,1:T(8,128)}, f32[64,512]{0,1:T(8,128)}, u32[]{:S(2)}, u32[]{:S(2)}) collective-permute-start(f32[64,512]{0,1:T(8,128)} %get-tuple-element.97), channel_id=1, source_target_pairs={{0,0},{1,2},{2,4},{3,6},{4,8},{5,10},{6,12},{7,14},{8,16},{9,18},{... | collective-permute-start | bytes 393224 | tf_op jit(solution)/shard_map/ppermute | solution.py:326
  26.6 44.2 %collective-permute-start.1 = (f32[64,512]{0,1:T(8,128)S(1)}, f32[64,512]{0,1:T(8,128)}, u32[]{:S(2)}, u32[]{:S(2)}) collective-permute-start(f32[64,512]{0,1:T(8,128)S(1)} %get-tuple-element.98), channel_id=1, source_target_pairs={{0,1},{1,3},{2,5},{3,7},{4,9},{5,11},{6,13},{7,15},{8,17},{9,19},{... | collective-permute-start | bytes 393224 | tf_op jit(solution)/shard_map/ppermute | solution.py:326
Sparse Core Ops, SparseCore 0:
  72.7 81.0 all-gather.1

commit v24 on v23

--- a/solution.py
+++ b/solution.py
@@ -184,7 +184,7 @@
                            preferred_element_type=jnp.float32)
 
 
-def chol_inv_kernel(a_ref, l_ref, linv_ref, w_ref, d_ref, e_ref, ut_ref, x_ref):
+def chol_inv_kernel(a_ref, c_ref, l_ref, linv_ref, st_ref, wt_ref, w_ref, d_ref, e_ref, ut_ref, x_ref):
     n = w_ref.shape[0]
     b = d_ref.shape[0]
     nb = n // b
@@ -244,14 +244,20 @@
             for k in range(j, i):
                 acc = acc + _mm(l_ref[i * b:(i + 1) * b, k * b:(k + 1) * b], linv_ref[k * b:(k + 1) * b, j * b:(j + 1) * b])
             linv_ref[i * b:(i + 1) * b, j * b:(j + 1) * b] = -_mm(linv_ref[i * b:(i + 1) * b, i * b:(i + 1) * b], acc)
-
-
-def chol_inv(a, n, b=128):
+    solved_t = _mm(linv_ref[...], c_ref[...])
+    st_ref[...] = solved_t
+    wt_ref[...] = lax.dot_general(solved_t, linv_ref[...], (((0,), (0,)), ((), ())), precision=HIGHEST,
+                                  preferred_element_type=jnp.float32)
+
+
+def chol_inv(a, c, n, b=128):
+    m = c.shape[1]
     return pl.pallas_call(
         chol_inv_kernel,
-        out_shape=(jax.ShapeDtypeStruct((n, n), jnp.float32), jax.ShapeDtypeStruct((n, n), jnp.float32)),
-        in_specs=[pl.BlockSpec(memory_space=pltpu.VMEM)],
-        out_specs=(pl.BlockSpec(memory_space=pltpu.VMEM), pl.BlockSpec(memory_space=pltpu.VMEM)),
+        out_shape=(jax.ShapeDtypeStruct((n, n), jnp.float32), jax.ShapeDtypeStruct((n, n), jnp.float32),
+                   jax.ShapeDtypeStruct((n, m), jnp.float32), jax.ShapeDtypeStruct((m, n), jnp.float32)),
+        in_specs=[pl.BlockSpec(memory_space=pltpu.VMEM)] * 2,
+        out_specs=tuple(pl.BlockSpec(memory_space=pltpu.VMEM) for _ in range(4)),
         scratch_shapes=[
             pltpu.VMEM((n, n), jnp.float32),
             pltpu.VMEM((b, b), jnp.float32),
@@ -259,7 +265,7 @@
             pltpu.VMEM((b, b), jnp.float32),
             pltpu.VMEM((b, b), jnp.float32),
         ],
-    )(a)
+    )(a, c)
 
 
 def panel_product_kernel(subtract, use_top_ref, panel_ref, w_ref, base_ref, top_ref, out_ref):
@@ -328,12 +334,10 @@
     for part in range(1, per_block):
         my_piece = jnp.where(front % per_block == part, pieces[part], my_piece)
     pivot, own_cols = broadcast_pivot(top, n_front)
-    col_rows = own_cols.T
     my_piece, pivot = lax.optimization_barrier((my_piece, pivot))
     panel = lax.all_gather(my_piece, "front", tiled=True)
-    factor, inverse = chol_inv(pivot, S)
-
-    col_solved = lax.dot_general(col_rows, inverse, (((1,), (1,)), ((), ())), precision=HIGHEST)
+    factor, inverse, solved_t, weights = chol_inv(pivot, own_cols, S)
+
 
     piv_cols = S // cols
     col_at = jnp.minimum(front, piv_cols - 1) * cols
@@ -346,8 +350,7 @@
         return panel_product(use_top, panel, inv_rows, assembled, top_rows, False)
 
     def other_columns():
-        weights = jnp.dot(col_solved, inverse, precision=HIGHEST)
-        return panel_product(use_top, panel, weights, assembled, col_solved.T, True)
+        return panel_product(use_top, panel, weights, assembled, solved_t, True)
 
     return lax.cond(front < piv_cols, pivot_columns, other_columns)
 

time: 176 us -> 176 us (level)
  matrix products: 2.56 us -> 0 us
  Pallas kernels: 133 us -> 135 us
    dot_general x1 -> x0, matrix products: 2.56 us -> none  [per_device(): lax.dot_general(col_rows, inverse, (((1,), (1,)), ((), ())), precision=HI...]
    pallas_call x1, Pallas kernels: 78.1 us -> 80 us  [chol_inv(): pl.pallas_call(chol_inv_kernel, out_shape=(jax.ShapeDtypeStruct((n, n), j...]
  transfers between devices with their start and end apart: 4 -> 4, of which waited for: 1 -> 1; matrix products, arithmetic and copies ran while one was open for 4% -> 3% of each run, Pallas kernels for 69% -> 70%
where the time goes in v24:
time: 176 us
  Pallas kernels  135 us (77%)
  between operations  13.5 us (8%)
  local copies, waits for them, and re-layouts  11.2 us (6%)
  other arithmetic  11.2 us (6%)
  starting transfers between devices  4.09 us (2%)
    pallas_call x1, Pallas kernels, chol_inv(): pl.pallas_call(chol_inv_kernel, out_shape=(jax.ShapeDtypeStruct((n, n), j...  80 us
    pallas_call x1, Pallas kernels, broadcast_pivot(): pl.pallas_call(functools.partial(pivot_kernel, n_front, n_src), out_shape...  42.9 us
    pallas_call x1, Pallas kernels, panel_product(): pl.pallas_call(functools.partial(panel_product_kernel, subtract), out_sha...  11.8 us
    select_n x2, other arithmetic, gather_half(): picked = jnp.where(found[:, None, None], picked, jnp.zeros_like(picked))  5.25 us
    gather x2, local copies, waits for them, and re-layouts, gather_half(): picked = jnp.take(blocks, index, axis=0)  3.98 us
  transfers between devices with their start and end apart: 4, of which 1 were waited for; matrix products, arithmetic and copies ran while one was open for 3% of the time, Pallas kernels for 70%

profile of v24, /device:TPU:1, one launch (start us, length us, event | category | flops | bytes accessed | tf_op | source)
XLA Modules:
  0.0 176.0 jit_solution(2341558873451092412)
XLA Ops:
  6.5 0.0 copy-start
  6.5 0.0 all-gather.2.cloned.1.call-start
  6.5 1.5 compare_reduce_fusion
  8.1 0.8 compare_reduce_fusion.3
  8.9 0.0 copy-done
  8.9 2.0 %gather_fusion.1 = f32[32,128,128]{2,1,0:T(8,128)} fusion(f32[48,128,128]{2,1,0:T(8,128)S(1)} %bitcast.16, s32[1024]{0:T(1024)S(1)} %pad_clamp_fusion), kind=kCustom, calls=%fused_computation.1.clone | custom fusion | bytes 4194432 | tf_op jit(solution)/shard_map/jit(_take)/gather | solution.py:21
  10.9 0.0 copy-start.3
  10.9 3.2 %select_select_fusion = f32[32,128,128]{2,1,0:T(8,128)} fusion(f32[32,128,128]{2,1,0:T(8,128)} %gather_fusion.1, pred[32]{0:T(512)(128)(4,1)S(1)} %compare_and_fusion, pred[32]{0:T(512)(128)(4,1)S(1)} %get-tuple-element.88), kind=kLoop, calls=%fused_computation.8 | loop fusion | flops 1048576 | bytes 4194368 | tf_op jit(solution)/shard_map/jit(_where)/select_n | solution.py:22
  14.1 1.4 collective-permute-start
  15.6 0.0 copy-done.3
  15.6 0.7 compare_reduce_fusion.2
  16.3 2.0 %gather_fusion = f32[32,128,128]{2,1,0:T(8,128)} fusion(f32[48,128,128]{2,1,0:T(8,128)S(1)} %bitcast.15, s32[1024]{0:T(1024)S(1)} %pad_clamp_fusion.1), kind=kCustom, calls=%fused_computation.clone | custom fusion | bytes 4194432 | tf_op jit(solution)/shard_map/jit(_take)/gather | solution.py:21
  18.3 0.0 copy-start.2
  18.3 2.0 %select_select_fusion.1 = f32[32,128,128]{2,1,0:T(8,128)S(1)} fusion(f32[32,128,128]{2,1,0:T(8,128)} %gather_fusion, pred[32]{0:T(512)(128)(4,1)S(1)} %compare_and_fusion.1, pred[32]{0:T(512)(128)(4,1)S(1)} %get-tuple-element.87), kind=kLoop, calls=%fused_computation.9 | loop fusion | flops 1048576 | bytes 4194368 | tf_op jit(solution)/shard_map/jit(_where)/select_n | solution.py:22
  20.3 0.0 collective-permute-done
  20.3 0.2 copy-done.2
  20.5 1.9 %fusion.1 = f32[4096,128]{1,0:T(8,128)S(1)} fusion(f32[4096,128]{1,0:T(8,128)S(1)} %copy-done.2, f32[4096,128]{1,0:T(8,128)} %collective-permute-done, f32[32,128,128]{2,1,0:T(8,128)S(1)} %select_select_fusion.1, pred[]{:T(512)S(6)} %eq.21), kind=kLoop, calls=%fused_computation.7 | loop fusion | flops 2097152 | bytes 8388609 | tf_op jit(solution)/shard_map/add | solution.py:317
  22.4 0.0 copy-start.1
  22.4 1.4 copy-done.1
  23.8 0.7 fusion.2
  24.5 0.8 fusion.3
  25.3 1.3 collective-permute-start.2
  26.5 1.4 collective-permute-start.1
  27.9 42.9 %shard_map.39 = (f32[64,32,128]{2,1,0:T(8,128)}, f32[512,128]{1,0:T(8,128)}) custom-call(f32[512,128]{1,0:T(8,128)} %get-tuple-element.89.top_ref), custom_call_target="tpu_custom_call" | custom-call | tf_op jit(solution)/shard_map/pallas_call | solution.py:153
  70.9 0.0 collective-permute-done.2
  70.9 0.0 collective-permute-done.1
  70.9 1.0 broadcast_select_fusion
  71.9 0.8 copy.9
  72.7 0.0 all-gather.2.cloned.1.call-update
  72.7 80.0 %shard_map.40 = (f32[512,512]{1,0:T(8,128)}, f32[512,512]{1,0:T(8,128)}, f32[512,128]{1,0:T(8,128)S(1)}, f32[128,512]{1,0:T(8,128)}) custom-call(f32[64,32,128]{2,1,0:T(8,128)} %get-tuple-element.69.a_ref, f32[512,128]{1,0:T(8,128)} %get-tuple-element.70.c_ref), custom_call_target="tpu_custom_call" | custom-call | tf_op jit(solution)/shard_map/pallas_call | solution.py:255
  152.7 1.3 all-gather.2.cloned.1.call-done
  154.0 15.2 %conditional.1 = (f32[4096,128]{1,0:T(8,128)}) conditional(s32[]{:T(128)} %convert_element_type.4, (s32[1]{0:T(128)}, f32[4096,512]{1,0:T(8,128)}, f32[128,512]{1,0:T(8,128)}, f32[4096,128]{1,0:T(8,128)}, f32[512,128]{1,0:T(8,128)S(1)}) %tuple.36, (s32[]{:T(128)}, f32[512,512]{1,0:T(8,128)}, f32[512,512]{1,0:T(8,128)}, s32[1]{0:T(128)}, ...), branch_computations={%region_4.6_spmd, %region_5.7_spmd} | conditional | flops 5 | bytes 1048650 | solution.py:355
  154.0 1.7 constant_dynamic-slice_fusion.1.w_ref
  155.6 1.7 constant_dynamic-slice_fusion.top_ref
  157.3 11.8 %branch_1_fun.2 = f32[4096,128]{1,0:T(8,128)} custom-call(s32[1]{0:T(128)} %get-tuple-element.49.use_top_ref, f32[4096,512]{1,0:T(8,128)} %get-tuple-element.50.panel_ref, f32[128,512]{1,0:T(8,128)} %constant_dynamic-slice_fusion.1.w_ref, f32[4096,128]{1,0:T(8,128)} %get-tuple-element.53.base_ref, f32[512,128]{1,0:T(8,128)} %constant_dynamic-slice_fusion.top_ref), custom_call_target="tpu_custom_call" | custom-call | tf_op jit(solution)/shard_map/cond/branch_1_fun/pallas_call | solution.py:285
  (7 shorter events, 0.0 us)
Async XLA Ops:
  6.5 2.4 %copy-start = (f32[1,6144,128]{2,1,0:T(8,128)S(1)}, f32[1,6144,128]{2,1,0:T(8,128)}, u32[]{:S(2)}) copy-start(f32[1,6144,128]{2,1,0:T(8,128)} %param.8) | copy-start | bytes 9437188
  6.5 147.4 %all-gather.2.cloned.1.call-start = ((), (), s32[]{:S(2)}) async-start(), calls=%async_computation | async-start | bytes 8519680 | tf_op jit(solution)/shard_map/all_gather | solution.py:338
  10.9 4.6 %copy-start.3 = (s32[1,48]{1,0:T(1,128)S(1)}, s32[1,48]{1,0:T(1,128)}, u32[]{:S(2)}) copy-start(s32[1,48]{1,0:T(1,128)} %param.9) | copy-start | bytes 580
  14.1 6.2 %collective-permute-start = (f32[4096,128]{1,0:T(8,128)}, f32[4096,128]{1,0:T(8,128)}, u32[]{:S(2)}, u32[]{:S(2)}) collective-permute-start(f32[4096,128]{1,0:T(8,128)} %bitcast.4), channel_id=1, source_target_pairs={{0,64},{64,0},{1,65},{65,1},{2,66},{66,2},{3,67},{67,3},{4,68},{68... | collective-permute-start | bytes 6291464 | tf_op jit(solution)/shard_map/ppermute | solution.py:314
  18.3 2.2 %copy-start.2 = (f32[4096,128]{1,0:T(8,128)S(1)}, f32[4096,128]{1,0:T(8,128)}, u32[]{:S(2)}) copy-start(f32[4096,128]{1,0:T(8,128)} %param.7) | copy-start | bytes 6291460
  22.4 1.4 copy-start.1
  25.3 45.6 %collective-permute-start.2 = (f32[64,512]{0,1:T(8,128)}, f32[64,512]{0,1:T(8,128)}, u32[]{:S(2)}, u32[]{:S(2)}) collective-permute-start(f32[64,512]{0,1:T(8,128)} %get-tuple-element.91), channel_id=1, source_target_pairs={{0,0},{1,2},{2,4},{3,6},{4,8},{5,10},{6,12},{7,14},{8,16},{9,18},{... | collective-permute-start | bytes 393224 | tf_op jit(solution)/shard_map/ppermute | solution.py:332
  26.5 44.3 %collective-permute-start.1 = (f32[64,512]{0,1:T(8,128)S(1)}, f32[64,512]{0,1:T(8,128)}, u32[]{:S(2)}, u32[]{:S(2)}) collective-permute-start(f32[64,512]{0,1:T(8,128)S(1)} %get-tuple-element.92), channel_id=1, source_target_pairs={{0,1},{1,3},{2,5},{3,7},{4,9},{5,11},{6,13},{7,15},{8,17},{9,19},{... | collective-permute-start | bytes 393224 | tf_op jit(solution)/shard_map/ppermute | solution.py:332
Sparse Core Ops, SparseCore 0:
  72.8 81.1 all-gather.1

commit v25 on v23

--- a/solution.py
+++ b/solution.py
@@ -327,6 +327,7 @@
     my_piece = pieces[0]
     for part in range(1, per_block):
         my_piece = jnp.where(front % per_block == part, pieces[part], my_piece)
+    my_piece, top = lax.optimization_barrier((my_piece, top))
     pivot, own_cols = broadcast_pivot(top, n_front)
     col_rows = own_cols.T
     my_piece, pivot = lax.optimization_barrier((my_piece, pivot))

time: 176 us -> 184 us (1.045)
  waiting for transfers between devices: 0.55 us -> 7.57 us
    ppermute x2, waiting for transfers between devices: 0.01 us -> 7.03 us  [per_device(): lax.ppermute(panel_rows[part * piece:(part + 1) * piece], ('leaf', 'front...]
  transfers between devices with their start and end apart: 4 -> 4, of which waited for: 1 -> 2; matrix products, arithmetic and copies ran while one was open for 4% -> 4% of each run, Pallas kernels for 69% -> 42%
where the time goes in v25:
time: 184 us
  Pallas kernels  134 us (73%)
  between operations  13.5 us (7%)
  local copies, waits for them, and re-layouts  11.2 us (6%)
  other arithmetic  11.2 us (6%)
  waiting for transfers between devices  7.57 us (4%)
  starting transfers between devices  4.07 us (2%)
  matrix products  2.56 us (1%)
    pallas_call x1, Pallas kernels, chol_inv(): pl.pallas_call(chol_inv_kernel, out_shape=(jax.ShapeDtypeStruct((n, n), j...  78.1 us
    pallas_call x1, Pallas kernels, broadcast_pivot(): pl.pallas_call(functools.partial(pivot_kernel, n_front, n_src), out_shape...  44 us
    pallas_call x1, Pallas kernels, panel_product(): pl.pallas_call(functools.partial(panel_product_kernel, subtract), out_sha...  11.8 us
    ppermute x2, waiting for transfers between devices, per_device(): lax.ppermute(panel_rows[part * piece:(part + 1) * piece], ('leaf', 'front...  7.03 us
    select_n x2, other arithmetic, gather_half(): picked = jnp.where(found[:, None, None], picked, jnp.zeros_like(picked))  5.25 us
    gather x2, local copies, waits for them, and re-layouts, gather_half(): picked = jnp.take(blocks, index, axis=0)  3.98 us
  transfers between devices with their start and end apart: 4, of which 2 were waited for; matrix products, arithmetic and copies ran while one was open for 4% of the time, Pallas kernels for 42%

profile of v25, /device:TPU:1, one launch (start us, length us, event | category | flops | bytes accessed | tf_op | source)
XLA Modules:
  0.0 183.9 jit_solution(11681556786320653918)
XLA Ops:
  6.5 0.0 copy-start
  6.5 0.0 all-gather.2.cloned.1.call-start
  6.5 1.5 compare_reduce_fusion
  8.1 0.8 compare_reduce_fusion.3
  8.9 0.0 copy-done
  8.9 2.0 %gather_fusion.1 = f32[32,128,128]{2,1,0:T(8,128)} fusion(f32[48,128,128]{2,1,0:T(8,128)S(1)} %bitcast.21, s32[1024]{0:T(1024)S(1)} %pad_clamp_fusion), kind=kCustom, calls=%fused_computation.1.clone | custom fusion | bytes 4194432 | tf_op jit(solution)/shard_map/jit(_take)/gather | solution.py:21
  10.9 0.0 copy-start.3
  10.9 3.2 %select_select_fusion = f32[32,128,128]{2,1,0:T(8,128)} fusion(f32[32,128,128]{2,1,0:T(8,128)} %gather_fusion.1, pred[32]{0:T(512)(128)(4,1)S(1)} %compare_and_fusion, pred[32]{0:T(512)(128)(4,1)S(1)} %get-tuple-element.98), kind=kLoop, calls=%fused_computation.8 | loop fusion | flops 1048576 | bytes 4194368 | tf_op jit(solution)/shard_map/jit(_where)/select_n | solution.py:22
  14.1 1.4 collective-permute-start
  15.6 0.0 copy-done.3
  15.6 0.7 compare_reduce_fusion.2
  16.3 2.0 %gather_fusion = f32[32,128,128]{2,1,0:T(8,128)} fusion(f32[48,128,128]{2,1,0:T(8,128)S(1)} %bitcast.20, s32[1024]{0:T(1024)S(1)} %pad_clamp_fusion.1), kind=kCustom, calls=%fused_computation.clone | custom fusion | bytes 4194432 | tf_op jit(solution)/shard_map/jit(_take)/gather | solution.py:21
  18.3 0.0 copy-start.2
  18.3 2.0 %select_select_fusion.1 = f32[32,128,128]{2,1,0:T(8,128)S(1)} fusion(f32[32,128,128]{2,1,0:T(8,128)} %gather_fusion, pred[32]{0:T(512)(128)(4,1)S(1)} %compare_and_fusion.1, pred[32]{0:T(512)(128)(4,1)S(1)} %get-tuple-element.97), kind=kLoop, calls=%fused_computation.9 | loop fusion | flops 1048576 | bytes 4194368 | tf_op jit(solution)/shard_map/jit(_where)/select_n | solution.py:22
  20.3 0.0 collective-permute-done
  20.3 0.2 copy-done.2
  20.5 1.9 %fusion.1 = f32[4096,128]{1,0:T(8,128)S(1)} fusion(f32[4096,128]{1,0:T(8,128)S(1)} %copy-done.2, f32[4096,128]{1,0:T(8,128)} %collective-permute-done, f32[32,128,128]{2,1,0:T(8,128)S(1)} %select_select_fusion.1, pred[]{:T(512)S(6)} %eq.40), kind=kLoop, calls=%fused_computation.7 | loop fusion | flops 2097152 | bytes 8388609 | tf_op jit(solution)/shard_map/add | solution.py:311
  22.4 0.0 copy-start.1
  22.4 1.4 copy-done.1
  23.8 0.7 fusion.2
  24.5 0.8 fusion.3
  25.3 1.3 collective-permute-start.2
  26.5 1.4 collective-permute-start.1
  27.9 7.0 %collective-permute-done.2 = f32[64,512]{0,1:T(8,128)} collective-permute-done((f32[64,512]{0,1:T(8,128)}, f32[64,512]{0,1:T(8,128)}, u32[]{:S(2)}, u32[]{:S(2)}) %collective-permute-start.2) | collective-permute-done | bytes 131104 | tf_op jit(solution)/shard_map/ppermute | solution.py:326
  34.9 0.0 collective-permute-done.1
  34.9 1.0 broadcast_select_fusion
  35.9 44.0 %shard_map.39 = (f32[64,32,128]{2,1,0:T(8,128)}, f32[512,128]{1,0:T(8,128)}) custom-call(f32[512,128]{1,0:T(8,128)} %get-tuple-element.67.top_ref), custom_call_target="tpu_custom_call" | custom-call | tf_op jit(solution)/shard_map/pallas_call | solution.py:153
  79.9 0.8 copy.11
  80.7 0.0 all-gather.2.cloned.1.call-update
  80.7 78.1 %shard_map.40 = (f32[512,512]{1,0:T(8,128)}, f32[512,512]{1,0:T(8,128)}) custom-call(f32[64,32,128]{2,1,0:T(8,128)} %get-tuple-element.71.a_ref), custom_call_target="tpu_custom_call" | custom-call | tf_op jit(solution)/shard_map/pallas_call | solution.py:250
  158.8 2.6 %fusion.5 = f32[128,512]{1,0:T(8,128)S(1)} fusion(f32[512,128]{1,0:T(8,128)} %get-tuple-element.68, f32[512,512]{1,0:T(8,128)} %get-tuple-element.72), kind=kOutput, calls=%fused_computation.27 | convolution fusion | flops 402653184 | bytes 1572864 | tf_op jit(solution)/shard_map/dot_general | solution.py:337
  161.4 0.5 all-gather.2.cloned.1.call-done
  161.9 15.2 %conditional.1 = (f32[4096,128]{1,0:T(8,128)}) conditional(s32[]{:T(128)} %convert_element_type.4, (f32[128,512]{1,0:T(8,128)S(1)}, f32[512,512]{1,0:T(8,128)}, s32[1]{0:T(128)}, f32[4096,512]{1,0:T(8,128)}, f32[4096,128]{1,0:T(8,128)}) %tuple.40, (s32[]{:T(128)}, f32[512,512]{1,0:T(8,128)}, f32[512,512]{1,0:T(8,128)}, s32[1]{0:T(128)}, ...), branch_computations={%region_4.6_spmd, %region_5.7_spmd} | conditional | flops 402653184 | bytes 2097160 | solution.py:353
  161.9 1.7 constant_dynamic-slice_fusion.1.w_ref
  163.6 1.7 constant_dynamic-slice_fusion.top_ref
  165.3 11.8 %branch_1_fun.2 = f32[4096,128]{1,0:T(8,128)} custom-call(s32[1]{0:T(128)} %get-tuple-element.49.use_top_ref, f32[4096,512]{1,0:T(8,128)} %get-tuple-element.50.panel_ref, f32[128,512]{1,0:T(8,128)} %constant_dynamic-slice_fusion.1.w_ref, f32[4096,128]{1,0:T(8,128)} %get-tuple-element.53.base_ref, f32[512,128]{1,0:T(8,128)} %constant_dynamic-slice_fusion.top_ref), custom_call_target="tpu_custom_call" | custom-call | tf_op jit(solution)/shard_map/cond/branch_1_fun/pallas_call | solution.py:279
  (7 shorter events, 0.0 us)
Async XLA Ops:
  6.5 2.4 %copy-start = (f32[1,6144,128]{2,1,0:T(8,128)S(1)}, f32[1,6144,128]{2,1,0:T(8,128)}, u32[]{:S(2)}) copy-start(f32[1,6144,128]{2,1,0:T(8,128)} %param.8) | copy-start | bytes 9437188
  6.5 155.4 %all-gather.2.cloned.1.call-start = ((), (), s32[]{:S(2)}) async-start(), calls=%async_computation | async-start | bytes 8519680 | tf_op jit(solution)/shard_map/all_gather | solution.py:334
  10.9 4.6 %copy-start.3 = (s32[1,48]{1,0:T(1,128)S(1)}, s32[1,48]{1,0:T(1,128)}, u32[]{:S(2)}) copy-start(s32[1,48]{1,0:T(1,128)} %param.9) | copy-start | bytes 580
  14.1 6.2 %collective-permute-start = (f32[4096,128]{1,0:T(8,128)}, f32[4096,128]{1,0:T(8,128)}, u32[]{:S(2)}, u32[]{:S(2)}) collective-permute-start(f32[4096,128]{1,0:T(8,128)} %bitcast.4), channel_id=1, source_target_pairs={{0,64},{64,0},{1,65},{65,1},{2,66},{66,2},{3,67},{67,3},{4,68},{68... | collective-permute-start | bytes 6291464 | tf_op jit(solution)/shard_map/ppermute | solution.py:308
  18.3 2.2 %copy-start.2 = (f32[4096,128]{1,0:T(8,128)S(1)}, f32[4096,128]{1,0:T(8,128)}, u32[]{:S(2)}) copy-start(f32[4096,128]{1,0:T(8,128)} %param.7) | copy-start | bytes 6291460
  22.4 1.4 copy-start.1
  25.3 9.7 %collective-permute-start.2 = (f32[64,512]{0,1:T(8,128)}, f32[64,512]{0,1:T(8,128)}, u32[]{:S(2)}, u32[]{:S(2)}) collective-permute-start(f32[64,512]{0,1:T(8,128)} %get-tuple-element.101), channel_id=1, source_target_pairs={{0,0},{1,2},{2,4},{3,6},{4,8},{5,10},{6,12},{7,14},{8,16},{9,18},{... | collective-permute-start | bytes 393224 | tf_op jit(solution)/shard_map/ppermute | solution.py:326
  26.5 8.4 %collective-permute-start.1 = (f32[64,512]{0,1:T(8,128)S(1)}, f32[64,512]{0,1:T(8,128)}, u32[]{:S(2)}, u32[]{:S(2)}) collective-permute-start(f32[64,512]{0,1:T(8,128)S(1)} %get-tuple-element.102), channel_id=1, source_target_pairs={{0,1},{1,3},{2,5},{3,7},{4,9},{5,11},{6,13},{7,15},{8,17},{9,19},{... | collective-permute-start | bytes 393224 | tf_op jit(solution)/shard_map/ppermute | solution.py:326
Sparse Core Ops, SparseCore 0:
  80.8 81.0 all-gather.1
